TPU v7x, 32 devices: a whole 2x2x4 slice. The times are simulated.
32 devices in a mesh: rows: 16 (over z, y, x), cols: 2 (over core).
Axes of the slice: x: 2, y: 2, z: 4, core: 2. Of those that a mesh axis runs over, the one named last changes fastest.
Arguments:
- snapshots: bfloat16 [16384, 2, 2, 128], P('rows', 'cols'), may hold values from -12 to 12
- scales: float32 [32, 2, 2], P('rows'), may hold values from 0.2 to 9
Outputs:
- coefficients: float32 [128, 2, 2, 128], P(None, 'cols')
- updated: bfloat16 [16384, 2, 2, 128], P('rows', 'cols')
All inputs are finite; a program needn't handle non-finite values.
Results may differ from a plain program's by a relative error of at most 0.012.
Values may be sent and summed in bfloat16 or wider, within the bound.
No kernel may reach another device: no remote copies, remote signals or barrier semaphores. Data moves between devices by JAX's collectives and lax.ppermute only.
A program may use at most 64 MiB of HBM per device.

v0:
```python
import math

import jax
import jax.numpy as jnp
from jax import lax
from jax.sharding import PartitionSpec as P

HIGH = lax.Precision.HIGHEST


def spread(shard, axis, root):
    mine = lax.axis_index(axis) == root
    return lax.psum(jnp.where(mine, shard, jnp.zeros_like(shard)), axis)


def product(left, right):
    return jnp.dot(left, right, precision=HIGH, preferred_element_type=jnp.float32)


def scaled_values(snapshots, scales, group):
    points, _, rounds, width = snapshots.shape
    nblock = scales.shape[0]
    own_scales = lax.dynamic_slice_in_dim(scales, group, 1, 1)[:, 0, :]
    shaped = snapshots.astype(jnp.float32).reshape(nblock, points // nblock, rounds, width)
    return (shaped * own_scales[:, None, :, None]).reshape(points, rounds * width)


def upper_inverse(gram):
    width = gram.shape[0]
    positions = jnp.arange(width, dtype=jnp.int32)

    def factor_step(column_index, state_pair):
        remaining, lower_factor = state_pair
        picker = (positions == column_index).astype(jnp.float32)
        column = jnp.sum(remaining * picker[None, :], axis=1)
        pivot_value = jnp.sum(column * picker)
        column = jnp.where(positions >= column_index, column / jnp.sqrt(pivot_value), 0.0)
        lower_factor = lower_factor + column[:, None] * picker[None, :]
        remaining = remaining - column[:, None] * column[None, :]
        return (remaining, lower_factor)

    start_lower = jnp.zeros((width, width), jnp.float32)
    _, lower_factor = lax.fori_loop(0, width, factor_step, (gram, start_lower))

    def solve_step(row_index, inverse_rows):
        picker = (positions == row_index).astype(jnp.float32)
        lower_row = jnp.sum(lower_factor * picker[:, None], axis=0)
        diagonal_entry = jnp.sum(lower_row * picker)
        earlier = jnp.where(positions < row_index, lower_row, 0.0)
        new_row = (picker - product(earlier[None, :], inverse_rows)[0]) / diagonal_entry
        return inverse_rows + picker[:, None] * new_row[None, :]

    lower_inverse = lax.fori_loop(0, width, solve_step, jnp.zeros((width, width), jnp.float32))
    return lower_inverse.T


def shards(snapshots, scales):
    points, _, rounds, width = snapshots.shape
    group = lax.axis_index("cols")
    values = scaled_values(snapshots, scales, group)
    panel = values[:, :width]
    gram = lax.psum(product(panel.T, panel), "rows")
    inverse = upper_inverse(gram)
    basis = spread(product(panel, inverse).astype(jnp.bfloat16), "cols", 0).astype(jnp.float32)
    raw = lax.psum(product(basis.T, values), "rows")
    root = math.sqrt(points * lax.axis_size("rows"))
    remainder = values - product(basis, raw)
    leading = jnp.where(group == 0, root * basis, remainder[:, :width])
    whole = jnp.concatenate([leading, remainder[:, width:]], axis=1)
    updated = whole.astype(jnp.bfloat16).reshape(points, 1, rounds, width)
    coefficients = (raw / root).reshape(width, 1, rounds, width)
    return (coefficients, updated)


def solution(mesh):
    return jax.shard_map(
        shards,
        mesh=mesh,
        in_specs=(P("rows", "cols", None, None), P("rows", None, None)),
        out_specs=(P(None, "cols", None, None), P("rows", "cols", None, None)),
        check_vma=False,
    )
```

profile of v0, /device:TPU:0, one launch (start us, length us, event | category | flops | bytes accessed | tf_op | source)
XLA Modules:
  0.0 862.3 jit_solution(12025838508278605038)
XLA Ops:
  7.2 1.1 bitcast_convert_fusion
  8.9 1.7 fusion.19
  10.6 108.1 %all-reduce.4.cloned.1.call-done = f32[128,128]{1,0:T(8,128)} async-done(((f32[128,128]{1,0:T(8,128)}), f32[128,128]{1,0:T(8,128)}) %all-reduce.4.cloned.1.call-update) | async-done | bytes 65552 | tf_op jit(solution)/shard_map/psum | solution.py:62
  118.8 393.0 %while.32 = (s32[]{:T(128)}, f32[128,128]{1,0:T(8,128)}, f32[128,128]{1,0:T(8,128)S(1)}, s32[]{:T(128)}, s32[]{:T(128)}) while((s32[]{:T(128)}, f32[128,128]{1,0:T(8,128)}, f32[128,128]{1,0:T(8,128)S(1)}, s32[]{:T(128)}, s32[]{:T(128)}) %tuple.74), condition=%wide.region_4.5_spmd.clone.clone, body=%wide.region_1.4_spmd.clone.clone.sunk | while | flops 115586 | bytes 856219 | solution.py:43
  118.8 1.0 multiply_reduce_fusion.4
  121.8 1.0 multiply_reduce_fusion.4
  124.9 1.0 multiply_reduce_fusion.4
  128.0 1.0 multiply_reduce_fusion.4
  131.1 1.0 multiply_reduce_fusion.4
  134.1 1.0 multiply_reduce_fusion.4
  137.2 1.0 multiply_reduce_fusion.4
  140.3 1.0 multiply_reduce_fusion.4
  143.3 1.0 multiply_reduce_fusion.4
  146.4 1.0 multiply_reduce_fusion.4
  149.5 1.0 multiply_reduce_fusion.4
  152.5 1.0 multiply_reduce_fusion.4
  155.6 1.0 multiply_reduce_fusion.4
  158.7 1.0 multiply_reduce_fusion.4
  511.7 210.5 %while.33 = (s32[]{:T(128)}, f32[128,128]{1,0:T(8,128)S(1)}, f32[128,128]{1,0:T(8,128)S(1)}, s32[]{:T(128)}, s32[]{:T(128)}) while((s32[]{:T(128)}, f32[128,128]{1,0:T(8,128)S(1)}, f32[128,128]{1,0:T(8,128)S(1)}, s32[]{:T(128)}, s32[]{:T(128)}) %tuple.77), condition=%wide.region_8.9_spmd.clone.clone, body=%wide.region_5.8_spmd.clone.clone.sunk | while | flops 296194 | bytes 266332 | solution.py:53
  722.2 1.3 fusion.16
  723.6 17.4 %all-reduce.6.cloned.1.call-done = bf16[1024,128]{1,0:T(8,128)(2,1)} async-done(((bf16[1024,128]{1,0:T(8,128)(2,1)}), bf16[1024,128]{1,0:T(8,128)(2,1)}) %all-reduce.6.cloned.1.call-update) | async-done | bytes 262160 | tf_op jit(solution)/shard_map/psum | solution.py:13
  741.0 2.3 fusion.21
  743.3 109.1 %all-reduce.8.cloned.1.call-done = f32[128,256]{1,0:T(8,128)} async-done(((f32[128,256]{1,0:T(8,128)}), f32[128,256]{1,0:T(8,128)}) %all-reduce.8.cloned.1.call-update) | async-done | bytes 131088 | tf_op jit(solution)/shard_map/psum | solution.py:65
  852.4 1.5 convolution_subtract_fusion
  (1800 shorter events, 493.1 us)
Async XLA Ops:
  7.2 111.6 %all-reduce.4.cloned.1.call-start = ((), (), s32[]{:S(2)}) async-start(), calls=%async_computation | async-start | bytes 131072 | tf_op jit(solution)/shard_map/psum | solution.py:62
  10.6 730.5 %all-reduce.6.cloned.1.call-start = ((), (), s32[]{:S(2)}) async-start(), calls=%async_computation.1 | async-start | bytes 524288 | tf_op jit(solution)/shard_map/psum | solution.py:13
  118.8 2.3 copy-start.1
  121.8 2.3 copy-start.1
  124.9 2.3 copy-start.1
  128.0 2.3 copy-start.1
  131.1 2.3 copy-start.1
  134.1 2.3 copy-start.1
  137.2 2.3 copy-start.1
  140.3 2.3 copy-start.1
  143.3 2.3 copy-start.1
  146.4 2.3 copy-start.1
  149.5 2.3 copy-start.1
  152.5 2.3 copy-start.1
  155.6 2.3 copy-start.1
  158.7 2.3 copy-start.1
  161.8 2.3 copy-start.1
  164.8 2.3 copy-start.1
  167.9 2.3 copy-start.1
  171.0 2.3 copy-start.1
  174.0 2.3 copy-start.1
  177.1 2.3 copy-start.1
  723.6 128.9 %all-reduce.8.cloned.1.call-start = ((), (), s32[]{:S(2)}) async-start(), calls=%async_computation.2 | async-start | bytes 262144 | tf_op jit(solution)/shard_map/psum | solution.py:65
  741.0 111.4 %copy-start.3 = (bf16[1024,128]{1,0:T(8,128)(2,1)S(1)}, bf16[1024,128]{1,0:T(8,128)(2,1)}, u32[]{:S(2)}) copy-start(bf16[1024,128]{1,0:T(8,128)(2,1)} %all-reduce.6.cloned.1.call-done) | copy-start | bytes 786436
  (238 other events, 334.5 us)
Sparse Core Ops, SparseCore 0:
  14.1 104.6 all-reduce.3
  723.7 17.3 all-reduce.5
  747.1 105.3 all-reduce.7
where the time goes:
time: 871 us; the launch traced here: 862 us
  other arithmetic  326 us (37%)
  waiting for transfers between devices  235 us (27%)
  matrix products  109 us (13%)
  loops' own time  98.7 us (11%)
  local copies, waits for them, and re-layouts  80.3 us (9%)
  between operations  13.9 us (2%)
    reduce_sum x128, other arithmetic, factor_step(): column = jnp.sum(remaining * picker[None, :], axis=1)  129 us
    psum x1, waiting for transfers between devices, shards(): raw = lax.psum(product(basis.T, values), 'rows')  109 us
    dot_general x132, matrix products, product(): jnp.dot(left, right, precision=HIGH, preferred_element_type=jnp.float32)  109 us
    psum x1, waiting for transfers between devices, shards(): gram = lax.psum(product(panel.T, panel), 'rows')  108 us
    another operation x1, loops' own time, upper_inverse(): _, lower_factor = lax.fori_loop(0, width, factor_step, (gram, start_lower))  94.7 us
    while x512, local copies, waits for them, and re-layouts  78.3 us
    reduce_sum x128, other arithmetic, factor_step(): pivot_value = jnp.sum(column * picker)  78.3 us
    reduce_sum x128, other arithmetic, solve_step(): diagonal_entry = jnp.sum(lower_row * picker)  78.1 us
  transfers between devices with their start and end apart: 3, of which 3 were waited for; matrix products, arithmetic and copies ran while one was open for 0% of the time, Pallas kernels for 0%

commit v1 on v0

v1 whole, which is shorter than its diff:
```python
import functools
import math

import jax
import jax.numpy as jnp
from jax import lax
from jax.experimental import pallas as pl
from jax.experimental.pallas import tpu as pltpu
from jax.sharding import PartitionSpec as P

F32 = jnp.float32
BF16 = jnp.bfloat16
HIGH = lax.Precision.HIGHEST
VMEM = pl.BlockSpec(memory_space=pltpu.VMEM)
SMEM = pl.BlockSpec(memory_space=pltpu.SMEM)


def partner(x, axis, count, offset):
    return lax.ppermute(x, axis, [(i, i ^ offset) for i in range(count)])


def total(x, axis, count):
    if count & (count - 1):
        return lax.psum(x, axis)
    stride = 1
    while stride < count:
        radix = 4 if (count // stride) % 4 == 0 else 2
        others = [partner(x, axis, count, b * stride) for b in range(1, radix)]
        for other in others:
            x = x + other
        stride *= radix
    return x


def from_leader(x, axis, count, mine):
    if count & (count - 1):
        return lax.psum(jnp.where(mine == 0, x, jnp.zeros_like(x)), axis)
    stride = 1
    while 2 * stride < count:
        x = jnp.where((mine & stride) != 0, partner(x, axis, count, stride), x)
        stride *= 2
    return x, partner(x, axis, count, stride), stride


def lanes(x, p):
    return jnp.broadcast_to(x[:, p : p + 1], x.shape)


def sublanes(x, j):
    return jnp.broadcast_to(x[j : j + 1, :], x.shape)


def lower_inverse(rows, width):
    n = len(rows)
    rid = lax.broadcasted_iota(jnp.int32, (8, width), 0)
    cid = lax.broadcasted_iota(jnp.int32, (8, width), 1)
    done = []
    for k in range(n):
        base = 8 * k
        held = rows[k]
        columns = [lanes(held, base + j) for j in range(8)]
        inside = (cid >= base) & (cid < base + 8)
        eye = jnp.where(cid - base == rid, 1.0, 0.0).astype(F32)
        full = jnp.where(inside, eye, held)
        forward = full
        root_scale = jnp.zeros((8, width), F32)
        scale = jnp.zeros((8, width), F32)
        for j in range(8):
            pivot = sublanes(columns[j], j)
            inverse = 1.0 / pivot
            root_scale = jnp.where(rid == j, lax.rsqrt(pivot), root_scale)
            scale = jnp.where(rid == j, inverse, scale)
            ratio = columns[j] * inverse
            ratio_all = jnp.where(rid == j, 0.0, ratio)
            ratio_below = jnp.where(rid > j, ratio, 0.0)
            for m in range(j + 1, 8):
                columns[m] = columns[m] - ratio_all * sublanes(columns[m], j)
            full = full - ratio_all * sublanes(full, j)
            forward = forward - ratio_below * sublanes(forward, j)
        done.append(jnp.where(cid <= rid + base, forward * root_scale, 0.0))
        full = full * scale
        if k + 1 < n:
            spread = [sublanes(full, j) for j in range(8)]
            for i in range(k + 1, n):
                terms = [lanes(rows[i], base + j) * spread[j] for j in range(8)]
                while len(terms) > 1:
                    terms = [terms[q] + terms[q + 1] for q in range(0, len(terms), 2)]
                rows[i] = jnp.where(inside, 0.0, rows[i]) - terms[0]
    return done


def leading(z_ref, recv_ref, stride):
    mine = lax.axis_index("cols")
    return jnp.where((mine & stride) == 0, z_ref[...], recv_ref[...])


def products_kernel(rounds, nblock, stride, scale_ref, z_ref, kept_ref, recv_ref, out_ref, own, lead):
    group = lax.axis_index("cols")
    width = z_ref.shape[1]
    points = z_ref.shape[0] // rounds // nblock
    own[...] = z_ref[...].astype(F32)
    lead[...] = leading(kept_ref, recv_ref, stride).astype(F32)
    out = jnp.zeros(out_ref.shape, F32)
    for b in range(nblock):
        start = b * points * rounds
        panel = lead[pl.ds(start, points, stride=rounds), :].astype(BF16)
        parts = [panel] + [own[pl.ds(start + r, points, stride=rounds), :].astype(BF16) for r in range(rounds)]
        block = lax.dot_general(
            panel, jnp.concatenate(parts, axis=1), (((0,), (0,)), ((), ())), preferred_element_type=F32
        )
        first = scale_ref[b, 0]
        pieces = [block[:, :width] * (first * first)]
        for r in range(rounds):
            factor = first * scale_ref[b, group * rounds + r]
            pieces.append(block[:, (r + 1) * width : (r + 2) * width] * factor)
        out = out + jnp.concatenate(pieces, axis=1)
    out_ref[...] = out


def spread_kernel(rounds, stride, kept_ref, recv_ref, out_ref):
    width = kept_ref.shape[1]
    rows = lax.broadcasted_iota(jnp.int32, kept_ref.shape, 0) % rounds
    lead = leading(kept_ref, recv_ref, stride).astype(F32)
    for r in range(rounds):
        moved = lead if r == 0 else pltpu.roll(lead, r, 0)
        out_ref[:, r * width : (r + 1) * width] = jnp.where(rows == r, moved, 0.0).astype(BF16)


def factor_kernel(rounds, root, sums_ref, coef_ref, weight_ref):
    group = lax.axis_index("cols")
    width = sums_ref.shape[0]
    rows = [sums_ref[8 * i : 8 * i + 8, :width] for i in range(width // 8)]
    inverse = jnp.concatenate(lower_inverse(rows, width), axis=0)
    across = inverse.T
    for r in range(rounds):
        cross = sums_ref[:, (r + 1) * width : (r + 2) * width]
        raw = jnp.dot(inverse, cross, precision=HIGH, preferred_element_type=F32)
        coef_ref[pl.ds(r, width, stride=rounds), :] = raw * (1.0 / root)
        weight = jnp.dot(across, raw, precision=HIGH, preferred_element_type=F32)
        if r == 0:
            weight = jnp.where(group == 0, -root * across, weight)
        upper = weight.astype(BF16)
        weight_ref[r * width : (r + 1) * width, :width] = upper
        weight_ref[r * width : (r + 1) * width, width:] = (weight - upper.astype(F32)).astype(BF16)


def update_kernel(rounds, nblock, scale_ref, z_ref, lead_ref, weight_ref, out_ref):
    group = lax.axis_index("cols")
    width = z_ref.shape[1]
    span = z_ref.shape[0] // nblock
    row = lax.broadcasted_iota(jnp.int32, (span, width), 0) % rounds
    for b in range(nblock):
        at = slice(b * span, (b + 1) * span)
        acc = jnp.dot(lead_ref[at, :], weight_ref[...], preferred_element_type=F32)
        acc = (acc[:, :width] + acc[:, width:]) * scale_ref[b, 0]
        factor = jnp.zeros((span, width), F32)
        for r in range(rounds):
            own = scale_ref[b, group * rounds + r]
            if r == 0:
                own = jnp.where(group == 0, 0.0, own)
            factor = jnp.where(row == r, own, factor)
        out_ref[at, :] = (z_ref[at, :].astype(F32) * factor - acc).astype(BF16)


def shards(snapshots, scales):
    points, _, rounds, width = snapshots.shape
    nblock = scales.shape[0]
    n_rows, n_cols = lax.axis_size("rows"), lax.axis_size("cols")
    root = math.sqrt(points * n_rows)
    long = points * rounds
    z = snapshots.reshape(long, width)
    flat = scales.reshape(nblock, -1)
    kept, recv, stride = from_leader(z, "cols", n_cols, lax.axis_index("cols"))
    params = pltpu.CompilerParams(vmem_limit_bytes=48 << 20)
    partial = pl.pallas_call(
        functools.partial(products_kernel, rounds, nblock, stride),
        out_shape=jax.ShapeDtypeStruct((width, (rounds + 1) * width), F32),
        in_specs=[SMEM, VMEM, VMEM, VMEM],
        out_specs=VMEM,
        scratch_shapes=[pltpu.VMEM((long, width), F32)] * 2,
        compiler_params=params,
        name="products",
    )(flat, z, kept, recv)
    lead = pl.pallas_call(
        functools.partial(spread_kernel, rounds, stride),
        out_shape=jax.ShapeDtypeStruct((long, rounds * width), BF16),
        in_specs=[VMEM, VMEM],
        out_specs=VMEM,
        compiler_params=params,
        name="spread",
    )(kept, recv)
    sums = total(partial, "rows", n_rows)
    coef, weight = pl.pallas_call(
        functools.partial(factor_kernel, rounds, root),
        out_shape=[
            jax.ShapeDtypeStruct((width * rounds, width), F32),
            jax.ShapeDtypeStruct((rounds * width, 2 * width), BF16),
        ],
        in_specs=[VMEM],
        out_specs=[VMEM, VMEM],
        compiler_params=params,
        name="factor",
    )(sums)
    updated = pl.pallas_call(
        functools.partial(update_kernel, rounds, nblock),
        out_shape=jax.ShapeDtypeStruct((long, width), BF16),
        in_specs=[SMEM, VMEM, VMEM, VMEM],
        out_specs=VMEM,
        compiler_params=params,
        name="update",
    )(flat, z, lead, weight)
    return coef.reshape(width, 1, rounds, width), updated.reshape(snapshots.shape)


def solution(mesh):
    return jax.shard_map(
        shards,
        mesh=mesh,
        in_specs=(P("rows", "cols", None, None), P("rows", None, None)),
        out_specs=(P(None, "cols", None, None), P("rows", "cols", None, None)),
        check_vma=False,
    )
```

time: 871 us -> 46.9 us (0.05)
  other arithmetic: 326 us -> 0.1 us
  waiting for transfers between devices: 235 us -> 25.6 us
  matrix products: 109 us -> 0 us
  loops' own time: 98.7 us -> 0 us
  local copies, waits for them, and re-layouts: 80.3 us -> 1.81 us
  between operations: 13.9 us -> 0.66 us
  starting transfers between devices: 0.12 us -> 9.49 us
  Pallas kernels: 0 us -> 9.03 us
    reduce_sum x512 -> x0, other arithmetic: 298 us -> none  [the longest x128 129 us: factor_step(): column = jnp.sum(remaining * picker[None, :], axis=1)]
    psum x3 -> x0, waiting for transfers between devices: 235 us -> none  [the longest x1 109 us: shards(): raw = lax.psum(product(basis.T, values), 'rows')]
    dot_general x132 -> x0, matrix products: 109 us -> none  [product(): jnp.dot(left, right, precision=HIGH, preferred_element_type=jnp.float32)]
    another operation x2 -> x0, loops' own time: 98.7 us -> none  [the longest x1 94.7 us: upper_inverse(): _, lower_factor = lax.fori_loop(0, width, factor_step, (gram, start_lower))]
    while x512 -> x0, local copies, waits for them, and re-layouts: 78.3 us -> none
    ppermute x0 -> x7, waiting for transfers between devices: none -> 25.6 us  [partner(): return lax.ppermute(x, axis, [(i, i ^ offset) for i in range(count)])]
    add x256 -> x2, other arithmetic: 25 us -> 0.1 us  [total(): x = x + other]
    ppermute x0 -> x7, starting transfers between devices: none -> 9.49 us  [partner(): return lax.ppermute(x, axis, [(i, i ^ offset) for i in range(count)])]
  transfers between devices with their start and end apart: 3 -> 7, of which waited for: 3 -> 6; matrix products, arithmetic and copies ran while one was open for 0% -> 2% of each run, Pallas kernels for 0% -> 1%
where the time goes in v1:
time: 46.9 us; the launch traced here: 46.7 us
  waiting for transfers between devices  25.6 us (55%)
  starting transfers between devices  9.49 us (20%)
  Pallas kernels  9.03 us (19%)
  local copies, waits for them, and re-layouts  1.81 us (4%)
  between operations  0.66 us (1%)
    ppermute x7, waiting for transfers between devices, partner(): return lax.ppermute(x, axis, [(i, i ^ offset) for i in range(count)])  25.6 us
    ppermute x7, starting transfers between devices, partner(): return lax.ppermute(x, axis, [(i, i ^ offset) for i in range(count)])  9.49 us
    pallas_call x1, Pallas kernels, shards(): pl.pallas_call(functools.partial(factor_kernel, rounds, root), out_shape=...  5.71 us
    pallas_call x1, Pallas kernels, shards(): pl.pallas_call(functools.partial(update_kernel, rounds, nblock), out_shap...  1.81 us
    pallas_call x1, Pallas kernels, shards(): pl.pallas_call(functools.partial(products_kernel, rounds, nblock, stride)...  1.06 us
    unnamed x4, local copies, waits for them, and re-layouts  1.05 us
  transfers between devices with their start and end apart: 7, of which 6 were waited for; matrix products, arithmetic and copies ran while one was open for 2% of the time, Pallas kernels for 1%

profile of v1, /device:TPU:0, one launch (start us, length us, event | category | flops | bytes accessed | tf_op | source)
XLA Modules:
  0.0 46.7 jit_solution(3338640318835300873)
XLA Ops:
  0.6 0.5 %collective-permute-start = (bf16[2048,128]{1,0:T(8,128)(2,1)}, bf16[2048,128]{1,0:T(8,128)(2,1)S(1)}, u32[]{:S(2)}, u32[]{:S(2)}) collective-permute-start(bf16[2048,128]{1,0:T(8,128)(2,1)} %bitcast.7), channel_id=1, source_target_pairs={{0,1},{1,0},{2,3},{3,2},{4,5},{5,4},{6,7},{7,6},{8,9},{9,8},{10,11... | collective-permute-start | bytes 1572872 | tf_op jit(solution)/shard_map/ppermute | solution.py:19
  1.1 0.8 %reshape.16.scale_ref = f32[2,4]{1,0:T(2,128)S(1)} reshape(f32[2,2,2]{2,1,0:T(2,128)} %param.3) | data formatting | bytes 64 | tf_op jit(solution)/shard_map/reshape | solution.py:172
  1.9 1.0 %collective-permute-done.recv_ref = bf16[2048,128]{1,0:T(8,128)(2,1)S(1)} collective-permute-done((bf16[2048,128]{1,0:T(8,128)(2,1)}, bf16[2048,128]{1,0:T(8,128)(2,1)S(1)}, u32[]{:S(2)}, u32[]{:S(2)}) %collective-permute-start) | collective-permute-done | bytes 524320 | tf_op jit(solution)/shard_map/ppermute | solution.py:19
  2.9 0.0 copy-start
  2.9 1.0 %copy-done = bf16[1024,1,2,128]{3,2,1,0:T(2,128)(2,1)S(1)} copy-done((bf16[1024,1,2,128]{3,2,1,0:T(2,128)(2,1)S(1)}, bf16[1024,1,2,128]{3,2,1,0:T(2,128)(2,1)}, u32[]{:S(2)}) %copy-start) | copy-done | bytes 524312
  3.9 1.1 %products.1 = f32[128,384]{1,0:T(8,128)S(1)} custom-call(f32[2,4]{1,0:T(2,128)S(1)} %reshape.16.scale_ref, bf16[2048,128]{1,0:T(8,128)(2,1)S(1)} %bitcast.8, bf16[2048,128]{1,0:T(8,128)(2,1)S(1)} %bitcast.9, bf16[2048,128]{1,0:T(8,128)(2,1)S(1)} %collective-permute-done.recv_ref), custom_call_target="tpu_custom_call" | custom-call | tf_op jit(solution)/shard_map/products/pallas_call | solution.py:175
  5.0 0.0 copy-start.1
  5.0 3.9 %collective-permute-start.3 = (f32[128,384]{1,0:T(8,128)S(1)}, f32[128,384]{1,0:T(8,128)S(1)}, u32[]{:S(2)}, u32[]{:S(2)}) collective-permute-start(f32[128,384]{1,0:T(8,128)S(1)} %products.1), channel_id=1, source_target_pairs={{0,6},{2,4},{4,2},{6,0},{8,14},{10,12},{12,10},{14,8},{16,22},{18,... | collective-permute-start | bytes 589832 | tf_op jit(solution)/shard_map/ppermute | solution.py:19
  8.9 0.5 %collective-permute-start.2 = (f32[128,384]{1,0:T(8,128)S(1)}, f32[128,384]{1,0:T(8,128)S(1)}, u32[]{:S(2)}, u32[]{:S(2)}) collective-permute-start(f32[128,384]{1,0:T(8,128)S(1)} %products.1), channel_id=1, source_target_pairs={{0,4},{2,6},{4,0},{6,2},{8,12},{10,14},{12,8},{14,10},{16,20},{18,... | collective-permute-start | bytes 589832 | tf_op jit(solution)/shard_map/ppermute | solution.py:19
  9.4 0.1 collective-permute-start.1
  9.5 5.1 %collective-permute-done.3 = f32[128,384]{1,0:T(8,128)S(1)} collective-permute-done((f32[128,384]{1,0:T(8,128)S(1)}, f32[128,384]{1,0:T(8,128)S(1)}, u32[]{:S(2)}, u32[]{:S(2)}) %collective-permute-start.3) | collective-permute-done | bytes 196640 | tf_op jit(solution)/shard_map/ppermute | solution.py:19
  14.6 3.7 %collective-permute-done.2 = f32[128,384]{1,0:T(8,128)S(1)} collective-permute-done((f32[128,384]{1,0:T(8,128)S(1)}, f32[128,384]{1,0:T(8,128)S(1)}, u32[]{:S(2)}, u32[]{:S(2)}) %collective-permute-start.2) | collective-permute-done | bytes 196640 | tf_op jit(solution)/shard_map/ppermute | solution.py:19
  18.3 0.3 collective-permute-done.1
  18.6 3.7 %collective-permute-start.6 = (f32[128,384]{1,0:T(8,128)S(1)}, f32[128,384]{1,0:T(8,128)S(1)}, u32[]{:S(2)}, u32[]{:S(2)}) collective-permute-start(f32[128,384]{1,0:T(8,128)S(1)} %add_add_fusion.1), channel_id=1, source_target_pairs={{0,24},{2,26},{4,28},{6,30},{8,16},{10,18},{12,20},{14,22},{16,8},... | collective-permute-start | bytes 589832 | tf_op jit(solution)/shard_map/ppermute | solution.py:19
  22.3 0.0 collective-permute-start.5
  22.3 0.8 %collective-permute-start.4 = (f32[128,384]{1,0:T(8,128)S(1)}, f32[128,384]{1,0:T(8,128)S(1)}, u32[]{:S(2)}, u32[]{:S(2)}) collective-permute-start(f32[128,384]{1,0:T(8,128)S(1)} %add_add_fusion.1), channel_id=1, source_target_pairs={{0,8},{2,10},{4,12},{6,14},{8,0},{10,2},{12,4},{14,6},{16,24},{18,... | collective-permute-start | bytes 589832 | tf_op jit(solution)/shard_map/ppermute | solution.py:19
  23.1 0.0 copy-done.1
  23.1 0.4 spread.1.lead_ref
  23.6 4.8 %collective-permute-done.6 = f32[128,384]{1,0:T(8,128)S(1)} collective-permute-done((f32[128,384]{1,0:T(8,128)S(1)}, f32[128,384]{1,0:T(8,128)S(1)}, u32[]{:S(2)}, u32[]{:S(2)}) %collective-permute-start.6) | collective-permute-done | bytes 196640 | tf_op jit(solution)/shard_map/ppermute | solution.py:19
  28.4 10.7 %collective-permute-done.5 = f32[128,384]{1,0:T(8,128)S(1)} collective-permute-done((f32[128,384]{1,0:T(8,128)S(1)}, f32[128,384]{1,0:T(8,128)S(1)}, u32[]{:S(2)}, u32[]{:S(2)}) %collective-permute-start.5) | collective-permute-done | bytes 196640 | tf_op jit(solution)/shard_map/ppermute | solution.py:19
  39.1 0.0 collective-permute-done.4
  39.1 0.1 add_add_fusion.sums_ref
  39.2 5.7 %factor.1 = (f32[256,128]{1,0:T(8,128)}, bf16[256,256]{1,0:T(8,128)(2,1)S(1)}) custom-call(f32[128,384]{1,0:T(8,128)S(1)} %add_add_fusion.sums_ref), custom_call_target="tpu_custom_call" | custom-call | tf_op jit(solution)/shard_map/factor/pallas_call | solution.py:193
  44.9 1.8 %update.1 = bf16[2048,128]{1,0:T(8,128)(2,1)} custom-call(f32[2,4]{1,0:T(2,128)S(1)} %reshape.16.scale_ref, bf16[2048,128]{1,0:T(8,128)(2,1)S(1)} %bitcast.11, bf16[2048,256]{1,0:T(8,128)(2,1)S(1)} %spread.1.lead_ref, bf16[256,256]{1,0:T(8,128)(2,1)S(1)} %get-tuple-element.5.weight_ref), custom_call_target="tpu_custom_call" | custom-call | tf_op jit(solution)/shard_map/update/pallas_call | solution.py:204
  (1 shorter events, 0.0 us)
Async XLA Ops:
  0.6 2.3 %collective-permute-start = (bf16[2048,128]{1,0:T(8,128)(2,1)}, bf16[2048,128]{1,0:T(8,128)(2,1)S(1)}, u32[]{:S(2)}, u32[]{:S(2)}) collective-permute-start(bf16[2048,128]{1,0:T(8,128)(2,1)} %bitcast.7), channel_id=1, source_target_pairs={{0,1},{1,0},{2,3},{3,2},{4,5},{5,4},{6,7},{7,6},{8,9},{9,8},{10,11... | collective-permute-start | bytes 1572872 | tf_op jit(solution)/shard_map/ppermute | solution.py:19
  2.9 1.0 %copy-start = (bf16[1024,1,2,128]{3,2,1,0:T(2,128)(2,1)S(1)}, bf16[1024,1,2,128]{3,2,1,0:T(2,128)(2,1)}, u32[]{:S(2)}) copy-start(bf16[1024,1,2,128]{3,2,1,0:T(2,128)(2,1)} %param.2) | copy-start | bytes 1572868
  5.0 18.1 %copy-start.1 = (bf16[1024,1,2,128]{3,2,1,0:T(2,128)(2,1)S(1)}, bf16[1024,1,2,128]{3,2,1,0:T(2,128)(2,1)}, u32[]{:S(2)}) copy-start(bf16[1024,1,2,128]{3,2,1,0:T(2,128)(2,1)} %param.2) | copy-start | bytes 1572868
  5.0 9.6 %collective-permute-start.3 = (f32[128,384]{1,0:T(8,128)S(1)}, f32[128,384]{1,0:T(8,128)S(1)}, u32[]{:S(2)}, u32[]{:S(2)}) collective-permute-start(f32[128,384]{1,0:T(8,128)S(1)} %products.1), channel_id=1, source_target_pairs={{0,6},{2,4},{4,2},{6,0},{8,14},{10,12},{12,10},{14,8},{16,22},{18,... | collective-permute-start | bytes 589832 | tf_op jit(solution)/shard_map/ppermute | solution.py:19
  8.9 9.4 %collective-permute-start.2 = (f32[128,384]{1,0:T(8,128)S(1)}, f32[128,384]{1,0:T(8,128)S(1)}, u32[]{:S(2)}, u32[]{:S(2)}) collective-permute-start(f32[128,384]{1,0:T(8,128)S(1)} %products.1), channel_id=1, source_target_pairs={{0,4},{2,6},{4,0},{6,2},{8,12},{10,14},{12,8},{14,10},{16,20},{18,... | collective-permute-start | bytes 589832 | tf_op jit(solution)/shard_map/ppermute | solution.py:19
  9.4 9.2 %collective-permute-start.1 = (f32[128,384]{1,0:T(8,128)S(1)}, f32[128,384]{1,0:T(8,128)S(1)}, u32[]{:S(2)}, u32[]{:S(2)}) collective-permute-start(f32[128,384]{1,0:T(8,128)S(1)} %products.1), channel_id=1, source_target_pairs={{0,2},{2,0},{4,6},{6,4},{8,10},{10,8},{12,14},{14,12},{16,18},{18,... | collective-permute-start | bytes 589832 | tf_op jit(solution)/shard_map/ppermute | solution.py:19
  18.6 9.8 %collective-permute-start.6 = (f32[128,384]{1,0:T(8,128)S(1)}, f32[128,384]{1,0:T(8,128)S(1)}, u32[]{:S(2)}, u32[]{:S(2)}) collective-permute-start(f32[128,384]{1,0:T(8,128)S(1)} %add_add_fusion.1), channel_id=1, source_target_pairs={{0,24},{2,26},{4,28},{6,30},{8,16},{10,18},{12,20},{14,22},{16,8},... | collective-permute-start | bytes 589832 | tf_op jit(solution)/shard_map/ppermute | solution.py:19
  22.3 16.8 %collective-permute-start.5 = (f32[128,384]{1,0:T(8,128)S(1)}, f32[128,384]{1,0:T(8,128)S(1)}, u32[]{:S(2)}, u32[]{:S(2)}) collective-permute-start(f32[128,384]{1,0:T(8,128)S(1)} %add_add_fusion.1), channel_id=1, source_target_pairs={{0,16},{2,18},{4,20},{6,22},{8,24},{10,26},{12,28},{14,30},{16,0},... | collective-permute-start | bytes 589832 | tf_op jit(solution)/shard_map/ppermute | solution.py:19
  22.3 16.8 %collective-permute-start.4 = (f32[128,384]{1,0:T(8,128)S(1)}, f32[128,384]{1,0:T(8,128)S(1)}, u32[]{:S(2)}, u32[]{:S(2)}) collective-permute-start(f32[128,384]{1,0:T(8,128)S(1)} %add_add_fusion.1), channel_id=1, source_target_pairs={{0,8},{2,10},{4,12},{6,14},{8,0},{10,2},{12,4},{14,6},{16,24},{18,... | collective-permute-start | bytes 589832 | tf_op jit(solution)/shard_map/ppermute | solution.py:19

commit v2 on v1

v2 whole, which is shorter than its diff:
```python
import functools
import math

import jax
import jax.numpy as jnp
from jax import lax
from jax.experimental import pallas as pl
from jax.experimental.pallas import tpu as pltpu
from jax.sharding import PartitionSpec as P

F32 = jnp.float32
BF16 = jnp.bfloat16
HIGH = lax.Precision.HIGHEST
VMEM = pl.BlockSpec(memory_space=pltpu.VMEM)
SMEM = pl.BlockSpec(memory_space=pltpu.SMEM)


def partner(x, axis, count, offset):
    return lax.ppermute(x, axis, [(i, i ^ offset) for i in range(count)])


def radices(count):
    found = []
    stride = 1
    while stride < count:
        radix = 4 if (count // stride) % 4 == 0 else 2
        found.append((stride, radix))
        stride *= radix
    return found


def from_leader(x, count, mine):
    stride = 1
    while 2 * stride < count:
        x = jnp.where((mine & stride) != 0, partner(x, "cols", count, stride), x)
        stride *= 2
    return x, partner(x, "cols", count, stride), stride


def lanes(x, p):
    return jnp.broadcast_to(x[:, p : p + 1], x.shape)


def sublanes(x, j):
    return jnp.broadcast_to(x[j : j + 1, :], x.shape)


def lower_inverse(rows, width):
    n = len(rows)
    rid = lax.broadcasted_iota(jnp.int32, (8, width), 0)
    cid = lax.broadcasted_iota(jnp.int32, (8, width), 1)
    done = []
    for k in range(n):
        base = 8 * k
        held = rows[k]
        columns = [lanes(held, base + j) for j in range(8)]
        inside = (cid >= base) & (cid < base + 8)
        eye = jnp.where(cid - base == rid, 1.0, 0.0).astype(F32)
        full = jnp.where(inside, eye, held)
        forward = full
        root_scale = jnp.zeros((8, width), F32)
        scale = jnp.zeros((8, width), F32)
        for j in range(8):
            pivot = sublanes(columns[j], j)
            inverse = 1.0 / pivot
            root_scale = jnp.where(rid == j, lax.rsqrt(pivot), root_scale)
            scale = jnp.where(rid == j, inverse, scale)
            ratio = columns[j] * inverse
            ratio_all = jnp.where(rid == j, 0.0, ratio)
            ratio_below = jnp.where(rid > j, ratio, 0.0)
            for m in range(j + 1, 8):
                columns[m] = columns[m] - ratio_all * sublanes(columns[m], j)
            full = full - ratio_all * sublanes(full, j)
            forward = forward - ratio_below * sublanes(forward, j)
        done.append(jnp.where(cid <= rid + base, forward * root_scale, 0.0))
        full = full * scale
        if k + 1 < n:
            spread = [sublanes(full, j) for j in range(8)]
            for i in range(k + 1, n):
                terms = [lanes(rows[i], base + j) * spread[j] for j in range(8)]
                while len(terms) > 1:
                    terms = [terms[q] + terms[q + 1] for q in range(0, len(terms), 2)]
                rows[i] = jnp.where(inside, 0.0, rows[i]) - terms[0]
    return done


def pack(gram):
    width = gram.shape[0]
    half = width // 2
    row = lax.broadcasted_iota(jnp.int32, (half, width), 0)
    col = lax.broadcasted_iota(jnp.int32, (half, width), 1)
    turned = pltpu.roll(gram[half:, :], half, 1)
    both = jnp.where((col < half) & (row < col), turned, gram[:half, :])
    diagonal = jnp.sum(jnp.where(row + half == col, gram[half:, :], 0.0), axis=0, keepdims=True)
    return jnp.concatenate([both, jnp.broadcast_to(diagonal, (8, width))], axis=0)


def unpack(packed):
    width = packed.shape[1]
    half = width // 2
    row = lax.broadcasted_iota(jnp.int32, (width, width), 0)
    col = lax.broadcasted_iota(jnp.int32, (width, width), 1)
    both = packed[:half, :]
    square = jnp.concatenate([both, pltpu.roll(both, half, 1)], axis=0)
    direct = ((row < half) & ((col >= half) | (col <= row))) | ((row >= half) & (col >= half) & (col > row))
    gram = jnp.where(direct, square, square.T)
    return jnp.where((row == col) & (row >= half), jnp.broadcast_to(packed[half : half + 1, :], gram.shape), gram)


def leading(z_ref, recv_ref, stride):
    mine = lax.axis_index("cols")
    return jnp.where((mine & stride) == 0, z_ref[...], recv_ref[...])


def split_kernel(rounds, z_ref, out_ref, own):
    width = z_ref.shape[1]
    points = z_ref.shape[0] // rounds
    own[...] = z_ref[...].astype(F32)
    for r in range(rounds):
        out_ref[:, r * width : (r + 1) * width] = own[pl.ds(r, points, stride=rounds), :].astype(BF16)


def products_kernel(rounds, nblock, stride, radix, scale_ref, own_ref, kept_ref, recv_ref, *rest):
    outs, (lead, cross) = rest[:radix], rest[radix:]
    group = lax.axis_index("cols")
    digit = lax.axis_index("rows") % radix
    width = kept_ref.shape[1]
    points = own_ref.shape[0] // nblock
    part = width // radix
    lead[...] = leading(kept_ref, recv_ref, stride).astype(F32)
    out = jnp.zeros((width, (rounds + 1) * width), F32)
    for b in range(nblock):
        panel = lead[pl.ds(b * points * rounds, points, stride=rounds), :].astype(BF16)
        own = own_ref[b * points : (b + 1) * points, :]
        block = lax.dot_general(
            panel, jnp.concatenate([panel, own], axis=1), (((0,), (0,)), ((), ())), preferred_element_type=F32
        )
        first = scale_ref[b, 0, 0]
        pieces = [block[:, :width] * (first * first)]
        for r in range(rounds):
            pieces.append(block[:, (r + 1) * width : (r + 2) * width] * (first * scale_ref[b, group, r]))
        out = out + jnp.concatenate(pieces, axis=1)
    packed = pack(out[:, :width])
    height = packed.shape[0]
    for r in range(rounds):
        cross[r * width : (r + 1) * width, :] = out[:, (r + 1) * width : (r + 2) * width]
    for b in range(radix):
        outs[b][:height, :] = packed
        for r in range(rounds):
            at = pl.multiple_of(r * width + (digit ^ b) * part, part)
            outs[b][height + r * part : height + (r + 1) * part, :] = cross[pl.ds(at, part), :]


def spread_kernel(rounds, stride, kept_ref, recv_ref, out_ref):
    width = kept_ref.shape[1]
    rows = lax.broadcasted_iota(jnp.int32, kept_ref.shape, 0) % rounds
    lead = leading(kept_ref, recv_ref, stride).astype(F32)
    for r in range(rounds):
        moved = lead if r == 0 else pltpu.roll(lead, r, 0)
        out_ref[:, r * width : (r + 1) * width] = jnp.where(rows == r, moved, 0.0).astype(BF16)


def factor_kernel(packed_ref, inverse_ref):
    width = packed_ref.shape[1]
    gram = unpack(packed_ref[...])
    rows = [gram[8 * i : 8 * i + 8, :] for i in range(width // 8)]
    for i, row in enumerate(lower_inverse(rows, width)):
        inverse_ref[8 * i : 8 * i + 8, :] = row


def finish_kernel(rounds, nblock, radix, root, chunks, scale_ref, z_ref, lead_ref, inverse_ref, *rest):
    parts, (coef_ref, out_ref, cross, held, sems) = rest[:radix], rest[radix:]
    group = lax.axis_index("cols")
    digit = lax.axis_index("rows") % radix
    width = z_ref.shape[1]
    part = width // radix
    for b in range(radix):
        for r in range(rounds):
            at = pl.multiple_of((digit ^ b) * part, part)
            cross[pl.ds(at, part), r * width : (r + 1) * width] = parts[b][r * part : (r + 1) * part, :]
    inverse = inverse_ref[...]
    across = inverse.T
    raw = jnp.dot(inverse, cross[...], precision=HIGH, preferred_element_type=F32)
    weights = jnp.dot(across, raw, precision=HIGH, preferred_element_type=F32)
    stacked = []
    for r in range(rounds):
        coef_ref[pl.ds(r, width, stride=rounds), :] = raw[:, r * width : (r + 1) * width] * (1.0 / root)
        weight = weights[:, r * width : (r + 1) * width]
        if r == 0:
            weight = jnp.where(group == 0, -root * across, weight)
        upper = weight.astype(BF16)
        stacked.append(jnp.concatenate([upper, (weight - upper.astype(F32)).astype(BF16)], axis=1))
    weight = jnp.concatenate(stacked, axis=0)
    span = z_ref.shape[0] // chunks
    row = lax.broadcasted_iota(jnp.int32, (span, width), 0) % rounds
    copies = []
    for c in range(chunks):
        block = c * nblock // chunks
        at = slice(c * span, (c + 1) * span)
        acc = jnp.dot(lead_ref[at, :], weight, preferred_element_type=F32)
        acc = (acc[:, :width] + acc[:, width:]) * scale_ref[block, 0, 0]
        factor = jnp.zeros((span, width), F32)
        for r in range(rounds):
            own = scale_ref[block, group, r]
            if r == 0:
                own = jnp.where(group == 0, 0.0, own)
            factor = jnp.where(row == r, own, factor)
        held[at, :] = (z_ref[at, :].astype(F32) * factor - acc).astype(BF16)
        copies.append(pltpu.make_async_copy(held.at[at, :], out_ref.at[at, :], sems.at[c]))
        copies[-1].start()
    for copy in copies:
        copy.wait()


def shards(snapshots, scales):
    points, _, rounds, width = snapshots.shape
    nblock = scales.shape[0]
    n_rows, n_cols = lax.axis_size("rows"), lax.axis_size("cols")
    root = math.sqrt(points * n_rows)
    long = points * rounds
    z = snapshots.reshape(long, width)
    kept, recv, stride = from_leader(z, n_cols, lax.axis_index("cols"))
    phases = radices(n_rows)
    radix = phases[0][1]
    height = width // 2 + 8
    payload = height + rounds * width // radix
    params = pltpu.CompilerParams(vmem_limit_bytes=48 << 20)
    own = pl.pallas_call(
        functools.partial(split_kernel, rounds),
        out_shape=jax.ShapeDtypeStruct((points, rounds * width), BF16),
        in_specs=[VMEM],
        out_specs=VMEM,
        scratch_shapes=[pltpu.VMEM((long, width), F32)],
        compiler_params=params,
        name="split",
    )(z)
    sent = pl.pallas_call(
        functools.partial(products_kernel, rounds, nblock, stride, radix),
        out_shape=[jax.ShapeDtypeStruct((payload, width), F32)] * radix,
        in_specs=[SMEM, VMEM, VMEM, VMEM],
        out_specs=[VMEM] * radix,
        scratch_shapes=[pltpu.VMEM((long, width), F32), pltpu.VMEM((rounds * width, width), F32)],
        compiler_params=params,
        name="products",
    )(scales, own, kept, recv)
    lead = pl.pallas_call(
        functools.partial(spread_kernel, rounds, stride),
        out_shape=jax.ShapeDtypeStruct((long, rounds * width), BF16),
        in_specs=[VMEM, VMEM],
        out_specs=VMEM,
        compiler_params=params,
        name="spread",
    )(kept, recv)
    sums = sent[0]
    for step, (hop, base) in enumerate(phases):
        source = sent if step == 0 else [sums] * base
        others = [partner(source[b], "rows", n_rows, b * hop) for b in range(1, base)]
        for other in others:
            sums = sums + other
    mine = sums[height:]
    parts = [mine] + [partner(mine, "rows", n_rows, b) for b in range(1, radix)]
    inverse = pl.pallas_call(
        factor_kernel,
        out_shape=jax.ShapeDtypeStruct((width, width), F32),
        in_specs=[VMEM],
        out_specs=VMEM,
        compiler_params=params,
        cost_estimate=pl.CostEstimate(flops=1 << 30, bytes_accessed=1 << 23, transcendentals=0),
        name="factor",
    )(sums[:height])
    chunks = 2 * nblock
    coef, updated = pl.pallas_call(
        functools.partial(finish_kernel, rounds, nblock, radix, root, chunks),
        out_shape=[
            jax.ShapeDtypeStruct((width * rounds, width), F32),
            jax.ShapeDtypeStruct((long, width), BF16),
        ],
        in_specs=[SMEM] + [VMEM] * (3 + radix),
        out_specs=[VMEM, pl.BlockSpec(memory_space=pl.ANY)],
        scratch_shapes=[
            pltpu.VMEM((width, rounds * width), F32),
            pltpu.VMEM((long, width), BF16),
            pltpu.SemaphoreType.DMA((chunks,)),
        ],
        compiler_params=params,
        name="finish",
    )(scales, z, lead, inverse, *parts)
    return coef.reshape(width, 1, rounds, width), updated.reshape(snapshots.shape)


def solution(mesh):
    return jax.shard_map(
        shards,
        mesh=mesh,
        in_specs=(P("rows", "cols", None, None), P("rows", None, None)),
        out_specs=(P(None, "cols", None, None), P("rows", "cols", None, None)),
        check_vma=False,
    )
```

time: 46.9 us -> 34.1 us (0.73)
  waiting for transfers between devices: 25.6 us -> 9.72 us
  starting transfers between devices: 9.49 us -> 13 us
  local copies, waits for them, and re-layouts: 1.81 us -> 1.06 us
    ppermute x7 -> x10, waiting for transfers between devices: 25.6 us -> 9.72 us  [partner(): return lax.ppermute(x, axis, [(i, i ^ offset) for i in range(count)])]
    ppermute x7 -> x10, starting transfers between devices: 9.49 us -> 13 us  [partner(): return lax.ppermute(x, axis, [(i, i ^ offset) for i in range(count)])]
    reshape x1 -> x0, local copies, waits for them, and re-layouts: 0.76 us -> none  [shards(): flat = scales.reshape(nblock, -1)]
    pallas_call x3 -> x4, Pallas kernels: 8.58 us -> 8.92 us  [the longest x1 4.6 us: shards(): pl.pallas_call(factor_kernel, out_shape=jax.ShapeDtypeStruct((width, widt...]
    unnamed x4 -> x6, local copies, waits for them, and re-layouts: 1.05 us -> 1.05 us
  transfers between devices with their start and end apart: 7 -> 10, of which waited for: 6 -> 6; matrix products, arithmetic and copies ran while one was open for 2% -> 0% of each run, Pallas kernels for 1% -> 15%
where the time goes in v2:
time: 34.1 us; the launch traced here: 33.9 us
  starting transfers between devices  13 us (38%)
  waiting for transfers between devices  9.72 us (29%)
  Pallas kernels  9.37 us (27%)
  local copies, waits for them, and re-layouts  1.06 us (3%)
  between operations  0.72 us (2%)
    ppermute x10, starting transfers between devices, partner(): return lax.ppermute(x, axis, [(i, i ^ offset) for i in range(count)])  13 us
    ppermute x10, waiting for transfers between devices, partner(): return lax.ppermute(x, axis, [(i, i ^ offset) for i in range(count)])  9.72 us
    pallas_call x1, Pallas kernels, shards(): pl.pallas_call(factor_kernel, out_shape=jax.ShapeDtypeStruct((width, widt...  4.6 us
    pallas_call x1, Pallas kernels, shards(): pl.pallas_call(functools.partial(finish_kernel, rounds, nblock, radix, ro...  3.1 us
    pallas_call x1, Pallas kernels, shards(): pl.pallas_call(functools.partial(products_kernel, rounds, nblock, stride,...  1.07 us
    unnamed x6, local copies, waits for them, and re-layouts  1.05 us
  transfers between devices with their start and end apart: 10, of which 6 were waited for; matrix products, arithmetic and copies ran while one was open for 0% of the time, Pallas kernels for 15%

profile of v2, /device:TPU:0, one launch (start us, length us, event | category | flops | bytes accessed | tf_op | source)
XLA Modules:
  0.0 33.9 jit_solution(7271215240832762005)
XLA Ops:
  0.6 0.5 %collective-permute-start = (bf16[2048,128]{1,0:T(8,128)(2,1)}, bf16[2048,128]{1,0:T(8,128)(2,1)S(1)}, u32[]{:S(2)}, u32[]{:S(2)}) collective-permute-start(bf16[2048,128]{1,0:T(8,128)(2,1)} %bitcast.7), channel_id=1, source_target_pairs={{0,1},{1,0},{2,3},{3,2},{4,5},{5,4},{6,7},{7,6},{8,9},{9,8},{10,11... | collective-permute-start | bytes 1572872 | tf_op jit(solution)/shard_map/ppermute | solution.py:19
  1.1 1.0 %copy-done = bf16[1024,1,2,128]{3,2,1,0:T(2,128)(2,1)S(1)} copy-done((bf16[1024,1,2,128]{3,2,1,0:T(2,128)(2,1)S(1)}, bf16[1024,1,2,128]{3,2,1,0:T(2,128)(2,1)}, u32[]{:S(2)}) %copy-start) | copy-done | bytes 524312
  2.2 0.2 split.1.own_ref
  2.3 0.5 %collective-permute-done.recv_ref = bf16[2048,128]{1,0:T(8,128)(2,1)S(1)} collective-permute-done((bf16[2048,128]{1,0:T(8,128)(2,1)}, bf16[2048,128]{1,0:T(8,128)(2,1)S(1)}, u32[]{:S(2)}, u32[]{:S(2)}) %collective-permute-start) | collective-permute-done | bytes 524320 | tf_op jit(solution)/shard_map/ppermute | solution.py:19
  2.9 1.1 %products.1 = (f32[136,128]{1,0:T(8,128)S(1)}, f32[136,128]{1,0:T(8,128)S(1)}, f32[136,128]{1,0:T(8,128)S(1)}, f32[136,128]{1,0:T(8,128)S(1)}) custom-call(f32[2,2,2]{2,1,0:T(2,128)S(1)} %copy-done.2, bf16[1024,256]{1,0:T(8,128)(2,1)S(1)} %split.1.own_ref, bf16[2048,128]{1,0:T(8,128)(2,1)S(1)} %bitcast.9, bf16[2048,128]{1,0:T(8,128)(2,1)S(1)} %collective-permute-done.recv_ref), custom_call_target="tpu_custom_call" | custom-call | tf_op jit(solution)/shard_map/products/pallas_call | solution.py:237
  4.0 2.9 %collective-permute-start.1 = (f32[136,128]{1,0:T(8,128)S(1)}, f32[136,128]{1,0:T(8,128)S(1)}, u32[]{:S(2)}, u32[]{:S(2)}) collective-permute-start(f32[136,128]{1,0:T(8,128)S(1)} %get-tuple-element.9), channel_id=1, source_target_pairs={{0,2},{2,0},{4,6},{6,4},{8,10},{10,8},{12,14},{14,12},{16,18},{18,... | collective-permute-start | bytes 208904 | tf_op jit(solution)/shard_map/ppermute | solution.py:19
  6.9 1.5 %collective-permute-start.2 = (f32[136,128]{1,0:T(8,128)S(1)}, f32[136,128]{1,0:T(8,128)S(1)}, u32[]{:S(2)}, u32[]{:S(2)}) collective-permute-start(f32[136,128]{1,0:T(8,128)S(1)} %get-tuple-element.10), channel_id=1, source_target_pairs={{0,4},{2,6},{4,0},{6,2},{8,12},{10,14},{12,8},{14,10},{16,20},{18,... | collective-permute-start | bytes 208904 | tf_op jit(solution)/shard_map/ppermute | solution.py:19
  8.4 0.0 collective-permute-start.3
  8.4 0.9 %collective-permute-done.1 = f32[136,128]{1,0:T(8,128)S(1)} collective-permute-done((f32[136,128]{1,0:T(8,128)S(1)}, f32[136,128]{1,0:T(8,128)S(1)}, u32[]{:S(2)}, u32[]{:S(2)}) %collective-permute-start.1) | collective-permute-done | bytes 69664 | tf_op jit(solution)/shard_map/ppermute | solution.py:19
  9.4 1.8 %collective-permute-done.2 = f32[136,128]{1,0:T(8,128)S(1)} collective-permute-done((f32[136,128]{1,0:T(8,128)S(1)}, f32[136,128]{1,0:T(8,128)S(1)}, u32[]{:S(2)}, u32[]{:S(2)}) %collective-permute-start.2) | collective-permute-done | bytes 69664 | tf_op jit(solution)/shard_map/ppermute | solution.py:19
  11.2 2.4 %collective-permute-done.3 = f32[136,128]{1,0:T(8,128)S(1)} collective-permute-done((f32[136,128]{1,0:T(8,128)S(1)}, f32[136,128]{1,0:T(8,128)S(1)}, u32[]{:S(2)}, u32[]{:S(2)}) %collective-permute-start.3) | collective-permute-done | bytes 69664 | tf_op jit(solution)/shard_map/ppermute | solution.py:19
  13.7 3.7 %collective-permute-start.6 = (f32[136,128]{1,0:T(8,128)S(1)}, f32[136,128]{1,0:T(8,128)S(1)}, u32[]{:S(2)}, u32[]{:S(2)}) collective-permute-start(f32[136,128]{1,0:T(8,128)S(1)} %add_add_fusion.1), channel_id=1, source_target_pairs={{0,24},{2,26},{4,28},{6,30},{8,16},{10,18},{12,20},{14,22},{16,8},... | collective-permute-start | bytes 208904 | tf_op jit(solution)/shard_map/ppermute | solution.py:19
  17.3 0.0 collective-permute-start.5
  17.3 0.8 %collective-permute-start.4 = (f32[136,128]{1,0:T(8,128)S(1)}, f32[136,128]{1,0:T(8,128)S(1)}, u32[]{:S(2)}, u32[]{:S(2)}) collective-permute-start(f32[136,128]{1,0:T(8,128)S(1)} %add_add_fusion.1), channel_id=1, source_target_pairs={{0,8},{2,10},{4,12},{6,14},{8,0},{10,2},{12,4},{14,6},{16,24},{18,... | collective-permute-start | bytes 208904 | tf_op jit(solution)/shard_map/ppermute | solution.py:19
  18.1 0.4 %spread.1.lead_ref = bf16[2048,256]{1,0:T(8,128)(2,1)S(1)} custom-call(bf16[2048,128]{1,0:T(8,128)(2,1)S(1)} %bitcast.10, bf16[2048,128]{1,0:T(8,128)(2,1)S(1)} %collective-permute-done.recv_ref), custom_call_target="tpu_custom_call" | custom-call | tf_op jit(solution)/shard_map/spread/pallas_call | solution.py:246
  18.6 1.3 %collective-permute-done.6 = f32[136,128]{1,0:T(8,128)S(1)} collective-permute-done((f32[136,128]{1,0:T(8,128)S(1)}, f32[136,128]{1,0:T(8,128)S(1)}, u32[]{:S(2)}, u32[]{:S(2)}) %collective-permute-start.6) | collective-permute-done | bytes 69664 | tf_op jit(solution)/shard_map/ppermute | solution.py:19
  19.8 2.7 %collective-permute-done.5 = f32[136,128]{1,0:T(8,128)S(1)} collective-permute-done((f32[136,128]{1,0:T(8,128)S(1)}, f32[136,128]{1,0:T(8,128)S(1)}, u32[]{:S(2)}, u32[]{:S(2)}) %collective-permute-start.5) | collective-permute-done | bytes 69664 | tf_op jit(solution)/shard_map/ppermute | solution.py:19
  22.6 0.0 copy-start.1
  22.6 0.6 %collective-permute-start.9 = (f32[64,128]{1,0:T(8,128)S(1)}, f32[64,128]{1,0:T(8,128)S(1)}, u32[]{:S(2)}, u32[]{:S(2)}) collective-permute-start(f32[64,128]{1,0:T(8,128)S(1)} %slice.9.rest_0_), channel_id=1, source_target_pairs={{0,6},{2,4},{4,2},{6,0},{8,14},{10,12},{12,10},{14,8},{16,22},{18,... | collective-permute-start | bytes 98312 | tf_op jit(solution)/shard_map/ppermute | solution.py:19
  23.2 1.5 %collective-permute-start.8 = (f32[64,128]{1,0:T(8,128)S(1)}, f32[64,128]{1,0:T(8,128)S(1)}, u32[]{:S(2)}, u32[]{:S(2)}) collective-permute-start(f32[64,128]{1,0:T(8,128)S(1)} %slice.9.rest_0_), channel_id=1, source_target_pairs={{0,4},{2,6},{4,0},{6,2},{8,12},{10,14},{12,8},{14,10},{16,20},{18,... | collective-permute-start | bytes 98312 | tf_op jit(solution)/shard_map/ppermute | solution.py:19
  24.7 1.4 %collective-permute-start.7 = (f32[64,128]{1,0:T(8,128)S(1)}, f32[64,128]{1,0:T(8,128)S(1)}, u32[]{:S(2)}, u32[]{:S(2)}) collective-permute-start(f32[64,128]{1,0:T(8,128)S(1)} %slice.9.rest_0_), channel_id=1, source_target_pairs={{0,2},{2,0},{4,6},{6,4},{8,10},{10,8},{12,14},{14,12},{16,18},{18,... | collective-permute-start | bytes 98312 | tf_op jit(solution)/shard_map/ppermute | solution.py:19
  26.1 4.6 %factor.1.inverse_ref = f32[128,128]{1,0:T(8,128)S(1)} custom-call(f32[72,128]{1,0:T(8,128)S(1)} %slice.8.packed_ref), custom_call_target="tpu_custom_call" | custom-call | flops 1073741824 | bytes 8388608 | tf_op jit(solution)/shard_map/factor/pallas_call | solution.py:262
  30.8 0.0 collective-permute-done.9.rest_3_
  30.8 3.1 %finish.1 = (f32[256,128]{1,0:T(8,128)}, bf16[2048,128]{1,0:T(8,128)(2,1)}) custom-call(f32[2,2,2]{2,1,0:T(2,128)S(1)} %copy-done.2, bf16[2048,128]{1,0:T(8,128)(2,1)S(1)} %bitcast.11, bf16[2048,256]{1,0:T(8,128)(2,1)S(1)} %spread.1.lead_ref, f32[128,128]{1,0:T(8,128)S(1)} %factor.1.inverse_ref, f32[64,128]{1,0:T(8,128)S(1)} %slice.9.rest_0_, ...), custom_call_target="tpu_custom_call" | custom-call | tf_op jit(solution)/shard_map/finish/pallas_call | solution.py:272
  (11 shorter events, 0.1 us)
Async XLA Ops:
  0.6 2.3 %collective-permute-start = (bf16[2048,128]{1,0:T(8,128)(2,1)}, bf16[2048,128]{1,0:T(8,128)(2,1)S(1)}, u32[]{:S(2)}, u32[]{:S(2)}) collective-permute-start(bf16[2048,128]{1,0:T(8,128)(2,1)} %bitcast.7), channel_id=1, source_target_pairs={{0,1},{1,0},{2,3},{3,2},{4,5},{5,4},{6,7},{7,6},{8,9},{9,8},{10,11... | collective-permute-start | bytes 1572872 | tf_op jit(solution)/shard_map/ppermute | solution.py:19
  1.1 1.0 %copy-start = (bf16[1024,1,2,128]{3,2,1,0:T(2,128)(2,1)S(1)}, bf16[1024,1,2,128]{3,2,1,0:T(2,128)(2,1)}, u32[]{:S(2)}) copy-start(bf16[1024,1,2,128]{3,2,1,0:T(2,128)(2,1)} %param.2) | copy-start | bytes 1572868
  2.2 0.7 %copy-start.2 = (f32[2,2,2]{2,1,0:T(2,128)S(1)}, f32[2,2,2]{2,1,0:T(2,128)}, u32[]{:S(2)}) copy-start(f32[2,2,2]{2,1,0:T(2,128)} %scale_ref.3) | copy-start | bytes 100
  4.0 5.4 %collective-permute-start.1 = (f32[136,128]{1,0:T(8,128)S(1)}, f32[136,128]{1,0:T(8,128)S(1)}, u32[]{:S(2)}, u32[]{:S(2)}) collective-permute-start(f32[136,128]{1,0:T(8,128)S(1)} %get-tuple-element.9), channel_id=1, source_target_pairs={{0,2},{2,0},{4,6},{6,4},{8,10},{10,8},{12,14},{14,12},{16,18},{18,... | collective-permute-start | bytes 208904 | tf_op jit(solution)/shard_map/ppermute | solution.py:19
  6.9 4.3 %collective-permute-start.2 = (f32[136,128]{1,0:T(8,128)S(1)}, f32[136,128]{1,0:T(8,128)S(1)}, u32[]{:S(2)}, u32[]{:S(2)}) collective-permute-start(f32[136,128]{1,0:T(8,128)S(1)} %get-tuple-element.10), channel_id=1, source_target_pairs={{0,4},{2,6},{4,0},{6,2},{8,12},{10,14},{12,8},{14,10},{16,20},{18,... | collective-permute-start | bytes 208904 | tf_op jit(solution)/shard_map/ppermute | solution.py:19
  8.4 5.2 %collective-permute-start.3 = (f32[136,128]{1,0:T(8,128)S(1)}, f32[136,128]{1,0:T(8,128)S(1)}, u32[]{:S(2)}, u32[]{:S(2)}) collective-permute-start(f32[136,128]{1,0:T(8,128)S(1)} %get-tuple-element.11), channel_id=1, source_target_pairs={{0,6},{2,4},{4,2},{6,0},{8,14},{10,12},{12,10},{14,8},{16,22},{18,... | collective-permute-start | bytes 208904 | tf_op jit(solution)/shard_map/ppermute | solution.py:19
  13.7 6.2 %collective-permute-start.6 = (f32[136,128]{1,0:T(8,128)S(1)}, f32[136,128]{1,0:T(8,128)S(1)}, u32[]{:S(2)}, u32[]{:S(2)}) collective-permute-start(f32[136,128]{1,0:T(8,128)S(1)} %add_add_fusion.1), channel_id=1, source_target_pairs={{0,24},{2,26},{4,28},{6,30},{8,16},{10,18},{12,20},{14,22},{16,8},... | collective-permute-start | bytes 208904 | tf_op jit(solution)/shard_map/ppermute | solution.py:19
  17.3 5.2 %collective-permute-start.5 = (f32[136,128]{1,0:T(8,128)S(1)}, f32[136,128]{1,0:T(8,128)S(1)}, u32[]{:S(2)}, u32[]{:S(2)}) collective-permute-start(f32[136,128]{1,0:T(8,128)S(1)} %add_add_fusion.1), channel_id=1, source_target_pairs={{0,16},{2,18},{4,20},{6,22},{8,24},{10,26},{12,28},{14,30},{16,0},... | collective-permute-start | bytes 208904 | tf_op jit(solution)/shard_map/ppermute | solution.py:19
  17.3 5.2 %collective-permute-start.4 = (f32[136,128]{1,0:T(8,128)S(1)}, f32[136,128]{1,0:T(8,128)S(1)}, u32[]{:S(2)}, u32[]{:S(2)}) collective-permute-start(f32[136,128]{1,0:T(8,128)S(1)} %add_add_fusion.1), channel_id=1, source_target_pairs={{0,8},{2,10},{4,12},{6,14},{8,0},{10,2},{12,4},{14,6},{16,24},{18,... | collective-permute-start | bytes 208904 | tf_op jit(solution)/shard_map/ppermute | solution.py:19
  22.6 8.2 %copy-start.1 = (bf16[1024,1,2,128]{3,2,1,0:T(2,128)(2,1)S(1)}, bf16[1024,1,2,128]{3,2,1,0:T(2,128)(2,1)}, u32[]{:S(2)}) copy-start(bf16[1024,1,2,128]{3,2,1,0:T(2,128)(2,1)} %param.2) | copy-start | bytes 1572868
  22.6 8.2 %collective-permute-start.9 = (f32[64,128]{1,0:T(8,128)S(1)}, f32[64,128]{1,0:T(8,128)S(1)}, u32[]{:S(2)}, u32[]{:S(2)}) collective-permute-start(f32[64,128]{1,0:T(8,128)S(1)} %slice.9.rest_0_), channel_id=1, source_target_pairs={{0,6},{2,4},{4,2},{6,0},{8,14},{10,12},{12,10},{14,8},{16,22},{18,... | collective-permute-start | bytes 98312 | tf_op jit(solution)/shard_map/ppermute | solution.py:19
  23.2 7.5 %collective-permute-start.8 = (f32[64,128]{1,0:T(8,128)S(1)}, f32[64,128]{1,0:T(8,128)S(1)}, u32[]{:S(2)}, u32[]{:S(2)}) collective-permute-start(f32[64,128]{1,0:T(8,128)S(1)} %slice.9.rest_0_), channel_id=1, source_target_pairs={{0,4},{2,6},{4,0},{6,2},{8,12},{10,14},{12,8},{14,10},{16,20},{18,... | collective-permute-start | bytes 98312 | tf_op jit(solution)/shard_map/ppermute | solution.py:19
  24.7 6.1 %collective-permute-start.7 = (f32[64,128]{1,0:T(8,128)S(1)}, f32[64,128]{1,0:T(8,128)S(1)}, u32[]{:S(2)}, u32[]{:S(2)}) collective-permute-start(f32[64,128]{1,0:T(8,128)S(1)} %slice.9.rest_0_), channel_id=1, source_target_pairs={{0,2},{2,0},{4,6},{6,4},{8,10},{10,8},{12,14},{14,12},{16,18},{18,... | collective-permute-start | bytes 98312 | tf_op jit(solution)/shard_map/ppermute | solution.py:19

commit v3 on v2

--- a/solution.py
+++ b/solution.py
@@ -15,8 +15,8 @@
 SMEM = pl.BlockSpec(memory_space=pltpu.SMEM)
 
 
-def partner(x, axis, count, offset):
-    return lax.ppermute(x, axis, [(i, i ^ offset) for i in range(count)])
+def partner(x, count, offset):
+    return lax.ppermute(x, "cols", [(i, i ^ offset) for i in range(count)])
 
 
 def radices(count):
@@ -29,12 +29,34 @@
     return found
 
 
+def exchange(x, phases, step, b, n_rows, n_cols):
+    pairs = []
+    for row in range(n_rows):
+        for col in range(n_cols):
+            stride = phases[(step + turn(phases, col)) % len(phases)][0]
+            pairs.append((row * n_cols + col, (row ^ (b * stride)) * n_cols + col))
+    return lax.ppermute(x, ("rows", "cols"), pairs)
+
+
+def turn(phases, col):
+    return col % 2 if len({radix for _, radix in phases}) == 1 else 0
+
+
+def row_digit(phases, n_cols):
+    row, digit = lax.axis_index("rows"), None
+    for col in range(min(n_cols, 2)):
+        stride, radix = phases[turn(phases, col) % len(phases)]
+        own = (row // stride) % radix
+        digit = own if digit is None else jnp.where(lax.axis_index("cols") % 2 == 0, digit, own)
+    return digit
+
+
 def from_leader(x, count, mine):
     stride = 1
     while 2 * stride < count:
-        x = jnp.where((mine & stride) != 0, partner(x, "cols", count, stride), x)
+        x = jnp.where((mine & stride) != 0, partner(x, count, stride), x)
         stride *= 2
-    return x, partner(x, "cols", count, stride), stride
+    return x, partner(x, count, stride), stride
 
 
 def lanes(x, p):
@@ -120,10 +142,10 @@
         out_ref[:, r * width : (r + 1) * width] = own[pl.ds(r, points, stride=rounds), :].astype(BF16)
 
 
-def products_kernel(rounds, nblock, stride, radix, scale_ref, own_ref, kept_ref, recv_ref, *rest):
+def products_kernel(rounds, nblock, stride, phases, radix, scale_ref, own_ref, kept_ref, recv_ref, *rest):
     outs, (lead, cross) = rest[:radix], rest[radix:]
     group = lax.axis_index("cols")
-    digit = lax.axis_index("rows") % radix
+    digit = row_digit(phases, lax.axis_size("cols"))
     width = kept_ref.shape[1]
     points = own_ref.shape[0] // nblock
     part = width // radix
@@ -168,10 +190,10 @@
         inverse_ref[8 * i : 8 * i + 8, :] = row
 
 
-def finish_kernel(rounds, nblock, radix, root, chunks, scale_ref, z_ref, lead_ref, inverse_ref, *rest):
+def finish_kernel(rounds, nblock, phases, radix, root, chunks, scale_ref, z_ref, lead_ref, inverse_ref, *rest):
     parts, (coef_ref, out_ref, cross, held, sems) = rest[:radix], rest[radix:]
     group = lax.axis_index("cols")
-    digit = lax.axis_index("rows") % radix
+    digit = row_digit(phases, lax.axis_size("cols"))
     width = z_ref.shape[1]
     part = width // radix
     for b in range(radix):
@@ -235,7 +257,7 @@
         name="split",
     )(z)
     sent = pl.pallas_call(
-        functools.partial(products_kernel, rounds, nblock, stride, radix),
+        functools.partial(products_kernel, rounds, nblock, stride, phases, radix),
         out_shape=[jax.ShapeDtypeStruct((payload, width), F32)] * radix,
         in_specs=[SMEM, VMEM, VMEM, VMEM],
         out_specs=[VMEM] * radix,
@@ -252,13 +274,13 @@
         name="spread",
     )(kept, recv)
     sums = sent[0]
-    for step, (hop, base) in enumerate(phases):
+    for step, (_, base) in enumerate(phases):
         source = sent if step == 0 else [sums] * base
-        others = [partner(source[b], "rows", n_rows, b * hop) for b in range(1, base)]
+        others = [exchange(source[b], phases, step, b, n_rows, n_cols) for b in range(1, base)]
         for other in others:
             sums = sums + other
     mine = sums[height:]
-    parts = [mine] + [partner(mine, "rows", n_rows, b) for b in range(1, radix)]
+    parts = [mine] + [exchange(mine, phases, 0, b, n_rows, n_cols) for b in range(1, radix)]
     inverse = pl.pallas_call(
         factor_kernel,
         out_shape=jax.ShapeDtypeStruct((width, width), F32),
@@ -270,7 +292,7 @@
     )(sums[:height])
     chunks = 2 * nblock
     coef, updated = pl.pallas_call(
-        functools.partial(finish_kernel, rounds, nblock, radix, root, chunks),
+        functools.partial(finish_kernel, rounds, nblock, phases, radix, root, chunks),
         out_shape=[
             jax.ShapeDtypeStruct((width * rounds, width), F32),
             jax.ShapeDtypeStruct((long, width), BF16),

time: 34.1 us -> 34.4 us (level)
  no operation moved by 1% of the time
where the time goes in v3:
time: 34.4 us; the launch traced here: 34.2 us
  starting transfers between devices  13 us (38%)
  waiting for transfers between devices  10 us (29%)
  Pallas kernels  9.38 us (27%)
  local copies, waits for them, and re-layouts  1.06 us (3%)
  between operations  0.71 us (2%)
    ppermute x9, starting transfers between devices, exchange(): return lax.ppermute(x, ('rows', 'cols'), pairs)  12.5 us
    ppermute x9, waiting for transfers between devices, exchange(): return lax.ppermute(x, ('rows', 'cols'), pairs)  9.45 us
    pallas_call x1, Pallas kernels, shards(): pl.pallas_call(factor_kernel, out_shape=jax.ShapeDtypeStruct((width, widt...  4.6 us
    pallas_call x1, Pallas kernels, shards(): pl.pallas_call(functools.partial(finish_kernel, rounds, nblock, phases, r...  3.11 us
    pallas_call x1, Pallas kernels, shards(): pl.pallas_call(functools.partial(products_kernel, rounds, nblock, stride,...  1.08 us
    unnamed x6, local copies, waits for them, and re-layouts  1.05 us
  transfers between devices with their start and end apart: 10, of which 6 were waited for; matrix products, arithmetic and copies ran while one was open for 0% of the time, Pallas kernels for 15%

profile of v3, /device:TPU:0, one launch (start us, length us, event | category | flops | bytes accessed | tf_op | source)
XLA Modules:
  0.0 34.2 jit_solution(12965653202483317172)
XLA Ops:
  0.6 0.5 %collective-permute-start = (bf16[2048,128]{1,0:T(8,128)(2,1)}, bf16[2048,128]{1,0:T(8,128)(2,1)S(1)}, u32[]{:S(2)}, u32[]{:S(2)}) collective-permute-start(bf16[2048,128]{1,0:T(8,128)(2,1)} %bitcast.7), channel_id=1, source_target_pairs={{0,1},{1,0},{2,3},{3,2},{4,5},{5,4},{6,7},{7,6},{8,9},{9,8},{10,11... | collective-permute-start | bytes 1572872 | tf_op jit(solution)/shard_map/ppermute | solution.py:19
  1.1 1.0 %copy-done = bf16[1024,1,2,128]{3,2,1,0:T(2,128)(2,1)S(1)} copy-done((bf16[1024,1,2,128]{3,2,1,0:T(2,128)(2,1)S(1)}, bf16[1024,1,2,128]{3,2,1,0:T(2,128)(2,1)}, u32[]{:S(2)}) %copy-start) | copy-done | bytes 524312
  2.2 0.2 split.1.own_ref
  2.3 0.5 %collective-permute-done.recv_ref = bf16[2048,128]{1,0:T(8,128)(2,1)S(1)} collective-permute-done((bf16[2048,128]{1,0:T(8,128)(2,1)}, bf16[2048,128]{1,0:T(8,128)(2,1)S(1)}, u32[]{:S(2)}, u32[]{:S(2)}) %collective-permute-start) | collective-permute-done | bytes 524320 | tf_op jit(solution)/shard_map/ppermute | solution.py:19
  2.9 1.1 %products.1 = (f32[136,128]{1,0:T(8,128)S(1)}, f32[136,128]{1,0:T(8,128)S(1)}, f32[136,128]{1,0:T(8,128)S(1)}, f32[136,128]{1,0:T(8,128)S(1)}) custom-call(f32[2,2,2]{2,1,0:T(2,128)S(1)} %copy-done.2, bf16[1024,256]{1,0:T(8,128)(2,1)S(1)} %split.1.own_ref, bf16[2048,128]{1,0:T(8,128)(2,1)S(1)} %bitcast.9, bf16[2048,128]{1,0:T(8,128)(2,1)S(1)} %collective-permute-done.recv_ref), custom_call_target="tpu_custom_call" | custom-call | tf_op jit(solution)/shard_map/products/pallas_call | solution.py:259
  4.0 2.9 %collective-permute-start.1 = (f32[136,128]{1,0:T(8,128)S(1)}, f32[136,128]{1,0:T(8,128)S(1)}, u32[]{:S(2)}, u32[]{:S(2)}) collective-permute-start(f32[136,128]{1,0:T(8,128)S(1)} %get-tuple-element.9), channel_id=1, source_target_pairs={{0,2},{1,9},{2,0},{3,11},{4,6},{5,13},{6,4},{7,15},{8,10},{9,1},{1... | collective-permute-start | bytes 208904 | tf_op jit(solution)/shard_map/ppermute | solution.py:38
  6.9 1.5 %collective-permute-start.2 = (f32[136,128]{1,0:T(8,128)S(1)}, f32[136,128]{1,0:T(8,128)S(1)}, u32[]{:S(2)}, u32[]{:S(2)}) collective-permute-start(f32[136,128]{1,0:T(8,128)S(1)} %get-tuple-element.10), channel_id=1, source_target_pairs={{0,4},{1,17},{2,6},{3,19},{4,0},{5,21},{6,2},{7,23},{8,12},{9,25},... | collective-permute-start | bytes 208904 | tf_op jit(solution)/shard_map/ppermute | solution.py:38
  8.4 0.0 collective-permute-start.3
  8.4 0.7 %collective-permute-done.1 = f32[136,128]{1,0:T(8,128)S(1)} collective-permute-done((f32[136,128]{1,0:T(8,128)S(1)}, f32[136,128]{1,0:T(8,128)S(1)}, u32[]{:S(2)}, u32[]{:S(2)}) %collective-permute-start.1) | collective-permute-done | bytes 69664 | tf_op jit(solution)/shard_map/ppermute | solution.py:38
  9.2 2.0 %collective-permute-done.2 = f32[136,128]{1,0:T(8,128)S(1)} collective-permute-done((f32[136,128]{1,0:T(8,128)S(1)}, f32[136,128]{1,0:T(8,128)S(1)}, u32[]{:S(2)}, u32[]{:S(2)}) %collective-permute-start.2) | collective-permute-done | bytes 69664 | tf_op jit(solution)/shard_map/ppermute | solution.py:38
  11.2 2.4 %collective-permute-done.3 = f32[136,128]{1,0:T(8,128)S(1)} collective-permute-done((f32[136,128]{1,0:T(8,128)S(1)}, f32[136,128]{1,0:T(8,128)S(1)}, u32[]{:S(2)}, u32[]{:S(2)}) %collective-permute-start.3) | collective-permute-done | bytes 69664 | tf_op jit(solution)/shard_map/ppermute | solution.py:38
  13.7 3.7 %collective-permute-start.6 = (f32[136,128]{1,0:T(8,128)S(1)}, f32[136,128]{1,0:T(8,128)S(1)}, u32[]{:S(2)}, u32[]{:S(2)}) collective-permute-start(f32[136,128]{1,0:T(8,128)S(1)} %add_add_fusion.1), channel_id=1, source_target_pairs={{0,24},{1,7},{2,26},{3,5},{4,28},{5,3},{6,30},{7,1},{8,16},{9,15},... | collective-permute-start | bytes 208904 | tf_op jit(solution)/shard_map/ppermute | solution.py:38
  17.3 0.0 collective-permute-start.5
  17.3 0.8 %collective-permute-start.4 = (f32[136,128]{1,0:T(8,128)S(1)}, f32[136,128]{1,0:T(8,128)S(1)}, u32[]{:S(2)}, u32[]{:S(2)}) collective-permute-start(f32[136,128]{1,0:T(8,128)S(1)} %add_add_fusion.1), channel_id=1, source_target_pairs={{0,8},{1,3},{2,10},{3,1},{4,12},{5,7},{6,14},{7,5},{8,0},{9,11},{1... | collective-permute-start | bytes 208904 | tf_op jit(solution)/shard_map/ppermute | solution.py:38
  18.1 0.4 %spread.1.lead_ref = bf16[2048,256]{1,0:T(8,128)(2,1)S(1)} custom-call(bf16[2048,128]{1,0:T(8,128)(2,1)S(1)} %bitcast.10, bf16[2048,128]{1,0:T(8,128)(2,1)S(1)} %collective-permute-done.recv_ref), custom_call_target="tpu_custom_call" | custom-call | tf_op jit(solution)/shard_map/spread/pallas_call | solution.py:268
  18.6 1.3 %collective-permute-done.6 = f32[136,128]{1,0:T(8,128)S(1)} collective-permute-done((f32[136,128]{1,0:T(8,128)S(1)}, f32[136,128]{1,0:T(8,128)S(1)}, u32[]{:S(2)}, u32[]{:S(2)}) %collective-permute-start.6) | collective-permute-done | bytes 69664 | tf_op jit(solution)/shard_map/ppermute | solution.py:38
  19.8 3.0 %collective-permute-done.5 = f32[136,128]{1,0:T(8,128)S(1)} collective-permute-done((f32[136,128]{1,0:T(8,128)S(1)}, f32[136,128]{1,0:T(8,128)S(1)}, u32[]{:S(2)}, u32[]{:S(2)}) %collective-permute-start.5) | collective-permute-done | bytes 69664 | tf_op jit(solution)/shard_map/ppermute | solution.py:38
  22.8 0.0 collective-permute-done.4
  22.9 0.0 copy-start.1
  22.9 0.3 collective-permute-start.9
  23.1 1.9 %collective-permute-start.8 = (f32[64,128]{1,0:T(8,128)S(1)}, f32[64,128]{1,0:T(8,128)S(1)}, u32[]{:S(2)}, u32[]{:S(2)}) collective-permute-start(f32[64,128]{1,0:T(8,128)S(1)} %slice.9.rest_0_), channel_id=1, source_target_pairs={{0,4},{1,17},{2,6},{3,19},{4,0},{5,21},{6,2},{7,23},{8,12},{9,25},... | collective-permute-start | bytes 98312 | tf_op jit(solution)/shard_map/ppermute | solution.py:38
  25.0 1.4 %collective-permute-start.7 = (f32[64,128]{1,0:T(8,128)S(1)}, f32[64,128]{1,0:T(8,128)S(1)}, u32[]{:S(2)}, u32[]{:S(2)}) collective-permute-start(f32[64,128]{1,0:T(8,128)S(1)} %slice.9.rest_0_), channel_id=1, source_target_pairs={{0,2},{1,9},{2,0},{3,11},{4,6},{5,13},{6,4},{7,15},{8,10},{9,1},{1... | collective-permute-start | bytes 98312 | tf_op jit(solution)/shard_map/ppermute | solution.py:38
  26.4 4.6 %factor.1.inverse_ref = f32[128,128]{1,0:T(8,128)S(1)} custom-call(f32[72,128]{1,0:T(8,128)S(1)} %slice.8.packed_ref), custom_call_target="tpu_custom_call" | custom-call | flops 1073741824 | bytes 8388608 | tf_op jit(solution)/shard_map/factor/pallas_call | solution.py:284
  31.1 3.1 %finish.1 = (f32[256,128]{1,0:T(8,128)}, bf16[2048,128]{1,0:T(8,128)(2,1)}) custom-call(f32[2,2,2]{2,1,0:T(2,128)S(1)} %copy-done.2, bf16[2048,128]{1,0:T(8,128)(2,1)S(1)} %bitcast.11, bf16[2048,256]{1,0:T(8,128)(2,1)S(1)} %spread.1.lead_ref, f32[128,128]{1,0:T(8,128)S(1)} %factor.1.inverse_ref, f32[64,128]{1,0:T(8,128)S(1)} %slice.9.rest_0_, ...), custom_call_target="tpu_custom_call" | custom-call | tf_op jit(solution)/shard_map/finish/pallas_call | solution.py:294
  (11 shorter events, 0.1 us)
Async XLA Ops:
  0.6 2.3 %collective-permute-start = (bf16[2048,128]{1,0:T(8,128)(2,1)}, bf16[2048,128]{1,0:T(8,128)(2,1)S(1)}, u32[]{:S(2)}, u32[]{:S(2)}) collective-permute-start(bf16[2048,128]{1,0:T(8,128)(2,1)} %bitcast.7), channel_id=1, source_target_pairs={{0,1},{1,0},{2,3},{3,2},{4,5},{5,4},{6,7},{7,6},{8,9},{9,8},{10,11... | collective-permute-start | bytes 1572872 | tf_op jit(solution)/shard_map/ppermute | solution.py:19
  1.1 1.0 %copy-start = (bf16[1024,1,2,128]{3,2,1,0:T(2,128)(2,1)S(1)}, bf16[1024,1,2,128]{3,2,1,0:T(2,128)(2,1)}, u32[]{:S(2)}) copy-start(bf16[1024,1,2,128]{3,2,1,0:T(2,128)(2,1)} %param.2) | copy-start | bytes 1572868
  2.2 0.7 %copy-start.2 = (f32[2,2,2]{2,1,0:T(2,128)S(1)}, f32[2,2,2]{2,1,0:T(2,128)}, u32[]{:S(2)}) copy-start(f32[2,2,2]{2,1,0:T(2,128)} %scale_ref.3) | copy-start | bytes 100
  4.0 5.2 %collective-permute-start.1 = (f32[136,128]{1,0:T(8,128)S(1)}, f32[136,128]{1,0:T(8,128)S(1)}, u32[]{:S(2)}, u32[]{:S(2)}) collective-permute-start(f32[136,128]{1,0:T(8,128)S(1)} %get-tuple-element.9), channel_id=1, source_target_pairs={{0,2},{1,9},{2,0},{3,11},{4,6},{5,13},{6,4},{7,15},{8,10},{9,1},{1... | collective-permute-start | bytes 208904 | tf_op jit(solution)/shard_map/ppermute | solution.py:38
  6.9 4.3 %collective-permute-start.2 = (f32[136,128]{1,0:T(8,128)S(1)}, f32[136,128]{1,0:T(8,128)S(1)}, u32[]{:S(2)}, u32[]{:S(2)}) collective-permute-start(f32[136,128]{1,0:T(8,128)S(1)} %get-tuple-element.10), channel_id=1, source_target_pairs={{0,4},{1,17},{2,6},{3,19},{4,0},{5,21},{6,2},{7,23},{8,12},{9,25},... | collective-permute-start | bytes 208904 | tf_op jit(solution)/shard_map/ppermute | solution.py:38
  8.4 5.2 %collective-permute-start.3 = (f32[136,128]{1,0:T(8,128)S(1)}, f32[136,128]{1,0:T(8,128)S(1)}, u32[]{:S(2)}, u32[]{:S(2)}) collective-permute-start(f32[136,128]{1,0:T(8,128)S(1)} %get-tuple-element.11), channel_id=1, source_target_pairs={{0,6},{1,25},{2,4},{3,27},{4,2},{5,29},{6,0},{7,31},{8,14},{9,17},... | collective-permute-start | bytes 208904 | tf_op jit(solution)/shard_map/ppermute | solution.py:38
  13.7 6.2 %collective-permute-start.6 = (f32[136,128]{1,0:T(8,128)S(1)}, f32[136,128]{1,0:T(8,128)S(1)}, u32[]{:S(2)}, u32[]{:S(2)}) collective-permute-start(f32[136,128]{1,0:T(8,128)S(1)} %add_add_fusion.1), channel_id=1, source_target_pairs={{0,24},{1,7},{2,26},{3,5},{4,28},{5,3},{6,30},{7,1},{8,16},{9,15},... | collective-permute-start | bytes 208904 | tf_op jit(solution)/shard_map/ppermute | solution.py:38
  17.3 5.5 %collective-permute-start.5 = (f32[136,128]{1,0:T(8,128)S(1)}, f32[136,128]{1,0:T(8,128)S(1)}, u32[]{:S(2)}, u32[]{:S(2)}) collective-permute-start(f32[136,128]{1,0:T(8,128)S(1)} %add_add_fusion.1), channel_id=1, source_target_pairs={{0,16},{1,5},{2,18},{3,7},{4,20},{5,1},{6,22},{7,3},{8,24},{9,13},... | collective-permute-start | bytes 208904 | tf_op jit(solution)/shard_map/ppermute | solution.py:38
  17.3 5.5 %collective-permute-start.4 = (f32[136,128]{1,0:T(8,128)S(1)}, f32[136,128]{1,0:T(8,128)S(1)}, u32[]{:S(2)}, u32[]{:S(2)}) collective-permute-start(f32[136,128]{1,0:T(8,128)S(1)} %add_add_fusion.1), channel_id=1, source_target_pairs={{0,8},{1,3},{2,10},{3,1},{4,12},{5,7},{6,14},{7,5},{8,0},{9,11},{1... | collective-permute-start | bytes 208904 | tf_op jit(solution)/shard_map/ppermute | solution.py:38
  22.9 8.2 %copy-start.1 = (bf16[1024,1,2,128]{3,2,1,0:T(2,128)(2,1)S(1)}, bf16[1024,1,2,128]{3,2,1,0:T(2,128)(2,1)}, u32[]{:S(2)}) copy-start(bf16[1024,1,2,128]{3,2,1,0:T(2,128)(2,1)} %param.2) | copy-start | bytes 1572868
  22.9 8.2 %collective-permute-start.9 = (f32[64,128]{1,0:T(8,128)S(1)}, f32[64,128]{1,0:T(8,128)S(1)}, u32[]{:S(2)}, u32[]{:S(2)}) collective-permute-start(f32[64,128]{1,0:T(8,128)S(1)} %slice.9.rest_0_), channel_id=1, source_target_pairs={{0,6},{1,25},{2,4},{3,27},{4,2},{5,29},{6,0},{7,31},{8,14},{9,17},... | collective-permute-start | bytes 98312 | tf_op jit(solution)/shard_map/ppermute | solution.py:38
  23.1 7.9 %collective-permute-start.8 = (f32[64,128]{1,0:T(8,128)S(1)}, f32[64,128]{1,0:T(8,128)S(1)}, u32[]{:S(2)}, u32[]{:S(2)}) collective-permute-start(f32[64,128]{1,0:T(8,128)S(1)} %slice.9.rest_0_), channel_id=1, source_target_pairs={{0,4},{1,17},{2,6},{3,19},{4,0},{5,21},{6,2},{7,23},{8,12},{9,25},... | collective-permute-start | bytes 98312 | tf_op jit(solution)/shard_map/ppermute | solution.py:38
  25.0 6.1 %collective-permute-start.7 = (f32[64,128]{1,0:T(8,128)S(1)}, f32[64,128]{1,0:T(8,128)S(1)}, u32[]{:S(2)}, u32[]{:S(2)}) collective-permute-start(f32[64,128]{1,0:T(8,128)S(1)} %slice.9.rest_0_), channel_id=1, source_target_pairs={{0,2},{1,9},{2,0},{3,11},{4,6},{5,13},{6,4},{7,15},{8,10},{9,1},{1... | collective-permute-start | bytes 98312 | tf_op jit(solution)/shard_map/ppermute | solution.py:38

commit v4 on v2

--- a/solution.py
+++ b/solution.py
@@ -120,35 +120,33 @@
         out_ref[:, r * width : (r + 1) * width] = own[pl.ds(r, points, stride=rounds), :].astype(BF16)
 
 
-def products_kernel(rounds, nblock, stride, radix, scale_ref, own_ref, kept_ref, recv_ref, *rest):
-    outs, (lead, cross) = rest[:radix], rest[radix:]
+def products_kernel(rounds, nblock, stride, scale_ref, own_ref, kept_ref, recv_ref, same_ref, other_ref, lead, cross):
     group = lax.axis_index("cols")
-    digit = lax.axis_index("rows") % radix
+    digit = lax.axis_index("rows") % 2
     width = kept_ref.shape[1]
     points = own_ref.shape[0] // nblock
-    part = width // radix
+    half = width // 2
     lead[...] = leading(kept_ref, recv_ref, stride).astype(F32)
-    out = jnp.zeros((width, (rounds + 1) * width), F32)
+    out = jnp.zeros((width, rounds * width), F32)
     for b in range(nblock):
         panel = lead[pl.ds(b * points * rounds, points, stride=rounds), :].astype(BF16)
         own = own_ref[b * points : (b + 1) * points, :]
-        block = lax.dot_general(
-            panel, jnp.concatenate([panel, own], axis=1), (((0,), (0,)), ((), ())), preferred_element_type=F32
-        )
+        block = lax.dot_general(panel, own, (((0,), (0,)), ((), ())), preferred_element_type=F32)
         first = scale_ref[b, 0, 0]
-        pieces = [block[:, :width] * (first * first)]
-        for r in range(rounds):
-            pieces.append(block[:, (r + 1) * width : (r + 2) * width] * (first * scale_ref[b, group, r]))
+        pieces = [block[:, r * width : (r + 1) * width] * (first * scale_ref[b, group, r]) for r in range(rounds)]
         out = out + jnp.concatenate(pieces, axis=1)
     packed = pack(out[:, :width])
     height = packed.shape[0]
     for r in range(rounds):
-        cross[r * width : (r + 1) * width, :] = out[:, (r + 1) * width : (r + 2) * width]
-    for b in range(radix):
-        outs[b][:height, :] = packed
+        cross[r * width : (r + 1) * width, :] = out[:, r * width : (r + 1) * width]
+    for ref, place in ((same_ref, digit), (other_ref, 1 - digit)):
         for r in range(rounds):
-            at = pl.multiple_of(r * width + (digit ^ b) * part, part)
-            outs[b][height + r * part : height + (r + 1) * part, :] = cross[pl.ds(at, part), :]
+            rows = cross[pl.ds(pl.multiple_of(r * width + place * half, half), half), :]
+            if r == 0:
+                ref[:half, :] = jnp.where(group == 0, packed[:half, :], rows)
+                ref[half:height, :] = packed[half:, :]
+            else:
+                ref[height + (r - 1) * half : height + r * half, :] = rows
 
 
 def spread_kernel(rounds, stride, kept_ref, recv_ref, out_ref):
@@ -160,24 +158,32 @@
         out_ref[:, r * width : (r + 1) * width] = jnp.where(rows == r, moved, 0.0).astype(BF16)
 
 
-def factor_kernel(packed_ref, inverse_ref):
-    width = packed_ref.shape[1]
-    gram = unpack(packed_ref[...])
+def factor_kernel(stride, kept_ref, recv_ref, inverse_ref, gram_ref):
+    width = kept_ref.shape[1]
+    mine = lax.axis_index("cols")
+    height = width // 2 + 8
+    packed = jnp.where((mine & stride) == 0, kept_ref[:height, :], recv_ref[:height, :])
+    gram = unpack(packed)
+    gram_ref[...] = gram
     rows = [gram[8 * i : 8 * i + 8, :] for i in range(width // 8)]
     for i, row in enumerate(lower_inverse(rows, width)):
         inverse_ref[8 * i : 8 * i + 8, :] = row
 
 
-def finish_kernel(rounds, nblock, radix, root, chunks, scale_ref, z_ref, lead_ref, inverse_ref, *rest):
-    parts, (coef_ref, out_ref, cross, held, sems) = rest[:radix], rest[radix:]
+def finish_kernel(rounds, nblock, root, chunks, scale_ref, z_ref, lead_ref, inverse_ref, gram_ref, same_ref, other_ref, coef_ref, out_ref, cross, held, sems):
     group = lax.axis_index("cols")
-    digit = lax.axis_index("rows") % radix
+    digit = lax.axis_index("rows") % 2
     width = z_ref.shape[1]
-    part = width // radix
-    for b in range(radix):
+    half = width // 2
+    height = half + 8
+    for ref, place in ((same_ref, digit), (other_ref, 1 - digit)):
+        at = pl.ds(pl.multiple_of(place * half, half), half)
         for r in range(rounds):
-            at = pl.multiple_of((digit ^ b) * part, part)
-            cross[pl.ds(at, part), r * width : (r + 1) * width] = parts[b][r * part : (r + 1) * part, :]
+            if r == 0:
+                rows = jnp.where(group == 0, gram_ref[at, :], ref[:half, :])
+            else:
+                rows = ref[height + (r - 1) * half : height + r * half, :]
+            cross[at, r * width : (r + 1) * width] = rows
     inverse = inverse_ref[...]
     across = inverse.T
     raw = jnp.dot(inverse, cross[...], precision=HIGH, preferred_element_type=F32)
@@ -221,9 +227,7 @@
     z = snapshots.reshape(long, width)
     kept, recv, stride = from_leader(z, n_cols, lax.axis_index("cols"))
     phases = radices(n_rows)
-    radix = phases[0][1]
-    height = width // 2 + 8
-    payload = height + rounds * width // radix
+    payload = (rounds * width) // 2 + 8
     params = pltpu.CompilerParams(vmem_limit_bytes=48 << 20)
     own = pl.pallas_call(
         functools.partial(split_kernel, rounds),
@@ -235,10 +239,10 @@
         name="split",
     )(z)
     sent = pl.pallas_call(
-        functools.partial(products_kernel, rounds, nblock, stride, radix),
-        out_shape=[jax.ShapeDtypeStruct((payload, width), F32)] * radix,
+        functools.partial(products_kernel, rounds, nblock, stride),
+        out_shape=[jax.ShapeDtypeStruct((payload, width), F32)] * 2,
         in_specs=[SMEM, VMEM, VMEM, VMEM],
-        out_specs=[VMEM] * radix,
+        out_specs=[VMEM] * 2,
         scratch_shapes=[pltpu.VMEM((long, width), F32), pltpu.VMEM((rounds * width, width), F32)],
         compiler_params=params,
         name="products",
@@ -253,29 +257,29 @@
     )(kept, recv)
     sums = sent[0]
     for step, (hop, base) in enumerate(phases):
-        source = sent if step == 0 else [sums] * base
-        others = [partner(source[b], "rows", n_rows, b * hop) for b in range(1, base)]
+        source = sent if step == 0 else [sums] * 2
+        others = [partner(source[b % 2], "rows", n_rows, b * hop) for b in range(1, base)]
         for other in others:
             sums = sums + other
-    mine = sums[height:]
-    parts = [mine] + [partner(mine, "rows", n_rows, b) for b in range(1, radix)]
-    inverse = pl.pallas_call(
-        factor_kernel,
-        out_shape=jax.ShapeDtypeStruct((width, width), F32),
-        in_specs=[VMEM],
-        out_specs=VMEM,
+    first, second, bit = from_leader(sums, n_cols, lax.axis_index("cols"))
+    gathered = partner(sums, "rows", n_rows, 1)
+    inverse, gram = pl.pallas_call(
+        functools.partial(factor_kernel, bit),
+        out_shape=[jax.ShapeDtypeStruct((width, width), F32)] * 2,
+        in_specs=[VMEM] * 2,
+        out_specs=[VMEM] * 2,
         compiler_params=params,
         cost_estimate=pl.CostEstimate(flops=1 << 30, bytes_accessed=1 << 23, transcendentals=0),
         name="factor",
-    )(sums[:height])
+    )(first, second)
     chunks = 2 * nblock
     coef, updated = pl.pallas_call(
-        functools.partial(finish_kernel, rounds, nblock, radix, root, chunks),
+        functools.partial(finish_kernel, rounds, nblock, root, chunks),
         out_shape=[
             jax.ShapeDtypeStruct((width * rounds, width), F32),
             jax.ShapeDtypeStruct((long, width), BF16),
         ],
-        in_specs=[SMEM] + [VMEM] * (3 + radix),
+        in_specs=[SMEM] + [VMEM] * 6,
         out_specs=[VMEM, pl.BlockSpec(memory_space=pl.ANY)],
         scratch_shapes=[
             pltpu.VMEM((width, rounds * width), F32),
@@ -284,7 +288,7 @@
         ],
         compiler_params=params,
         name="finish",
-    )(scales, z, lead, inverse, *parts)
+    )(scales, z, lead, inverse, gram, sums, gathered)
     return coef.reshape(width, 1, rounds, width), updated.reshape(snapshots.shape)
 
 

time: 34.1 us -> 31.5 us (0.924)
  starting transfers between devices: 13 us -> 10.5 us
    ppermute x10 -> x9, starting transfers between devices: 13 us -> 10.5 us  [partner(): return lax.ppermute(x, axis, [(i, i ^ offset) for i in range(count)])]
    ppermute x10 -> x9, waiting for transfers between devices: 9.72 us -> 9.65 us  [partner(): return lax.ppermute(x, axis, [(i, i ^ offset) for i in range(count)])]
  transfers between devices with their start and end apart: 10 -> 9, of which waited for: 6 -> 6; matrix products, arithmetic and copies ran while one was open for 0% -> 0% of each run, Pallas kernels for 15% -> 17%
where the time goes in v4:
time: 31.5 us; the launch traced here: 31.3 us
  starting transfers between devices  10.5 us (33%)
  waiting for transfers between devices  9.65 us (31%)
  Pallas kernels  9.37 us (30%)
  local copies, waits for them, and re-layouts  1.05 us (3%)
  between operations  0.7 us (2%)
    ppermute x9, starting transfers between devices, partner(): return lax.ppermute(x, axis, [(i, i ^ offset) for i in range(count)])  10.5 us
    ppermute x9, waiting for transfers between devices, partner(): return lax.ppermute(x, axis, [(i, i ^ offset) for i in range(count)])  9.65 us
    pallas_call x1, Pallas kernels, shards(): pl.pallas_call(functools.partial(factor_kernel, bit), out_shape=[jax.Shap...  4.61 us
    pallas_call x1, Pallas kernels, shards(): pl.pallas_call(functools.partial(finish_kernel, rounds, nblock, root, chu...  3.12 us
    pallas_call x1, Pallas kernels, shards(): pl.pallas_call(functools.partial(products_kernel, rounds, nblock, stride)...  1.05 us
    unnamed x6, local copies, waits for them, and re-layouts  1.05 us
  transfers between devices with their start and end apart: 9, of which 6 were waited for; matrix products, arithmetic and copies ran while one was open for 0% of the time, Pallas kernels for 17%

profile of v4, /device:TPU:0, one launch (start us, length us, event | category | flops | bytes accessed | tf_op | source)
XLA Modules:
  0.0 31.3 jit_solution(15633279867247048677)
XLA Ops:
  0.6 0.5 %collective-permute-start = (bf16[2048,128]{1,0:T(8,128)(2,1)}, bf16[2048,128]{1,0:T(8,128)(2,1)S(1)}, u32[]{:S(2)}, u32[]{:S(2)}) collective-permute-start(bf16[2048,128]{1,0:T(8,128)(2,1)} %bitcast.7), channel_id=1, source_target_pairs={{0,1},{1,0},{2,3},{3,2},{4,5},{5,4},{6,7},{7,6},{8,9},{9,8},{10,11... | collective-permute-start | bytes 1572872 | tf_op jit(solution)/shard_map/ppermute | solution.py:19
  1.1 1.0 %copy-done = bf16[1024,1,2,128]{3,2,1,0:T(2,128)(2,1)S(1)} copy-done((bf16[1024,1,2,128]{3,2,1,0:T(2,128)(2,1)S(1)}, bf16[1024,1,2,128]{3,2,1,0:T(2,128)(2,1)}, u32[]{:S(2)}) %copy-start) | copy-done | bytes 524312
  2.2 0.2 split.1.own_ref
  2.3 0.5 %collective-permute-done.recv_ref = bf16[2048,128]{1,0:T(8,128)(2,1)S(1)} collective-permute-done((bf16[2048,128]{1,0:T(8,128)(2,1)}, bf16[2048,128]{1,0:T(8,128)(2,1)S(1)}, u32[]{:S(2)}, u32[]{:S(2)}) %collective-permute-start) | collective-permute-done | bytes 524320 | tf_op jit(solution)/shard_map/ppermute | solution.py:19
  2.9 1.1 %products.1 = (f32[136,128]{1,0:T(8,128)S(1)}, f32[136,128]{1,0:T(8,128)S(1)}) custom-call(f32[2,2,2]{2,1,0:T(2,128)S(1)} %copy-done.2, bf16[1024,256]{1,0:T(8,128)(2,1)S(1)} %split.1.own_ref, bf16[2048,128]{1,0:T(8,128)(2,1)S(1)} %bitcast.9, bf16[2048,128]{1,0:T(8,128)(2,1)S(1)} %collective-permute-done.recv_ref), custom_call_target="tpu_custom_call" | custom-call | tf_op jit(solution)/shard_map/products/pallas_call | solution.py:241
  4.0 3.0 %collective-permute-start.2 = (f32[136,128]{1,0:T(8,128)S(1)}, f32[136,128]{1,0:T(8,128)S(1)}, u32[]{:S(2)}, u32[]{:S(2)}) collective-permute-start(f32[136,128]{1,0:T(8,128)S(1)} %get-tuple-element.8), channel_id=1, source_target_pairs={{0,4},{2,6},{4,0},{6,2},{8,12},{10,14},{12,8},{14,10},{16,20},{18,... | collective-permute-start | bytes 208904 | tf_op jit(solution)/shard_map/ppermute | solution.py:19
  6.9 1.4 %collective-permute-start.3 = (f32[136,128]{1,0:T(8,128)S(1)}, f32[136,128]{1,0:T(8,128)S(1)}, u32[]{:S(2)}, u32[]{:S(2)}) collective-permute-start(f32[136,128]{1,0:T(8,128)S(1)} %get-tuple-element.9), channel_id=1, source_target_pairs={{0,6},{2,4},{4,2},{6,0},{8,14},{10,12},{12,10},{14,8},{16,22},{18,... | collective-permute-start | bytes 208904 | tf_op jit(solution)/shard_map/ppermute | solution.py:19
  8.3 0.1 collective-permute-start.1
  8.5 1.8 %collective-permute-done.2 = f32[136,128]{1,0:T(8,128)S(1)} collective-permute-done((f32[136,128]{1,0:T(8,128)S(1)}, f32[136,128]{1,0:T(8,128)S(1)}, u32[]{:S(2)}, u32[]{:S(2)}) %collective-permute-start.2) | collective-permute-done | bytes 69664 | tf_op jit(solution)/shard_map/ppermute | solution.py:19
  10.3 2.5 %collective-permute-done.3 = f32[136,128]{1,0:T(8,128)S(1)} collective-permute-done((f32[136,128]{1,0:T(8,128)S(1)}, f32[136,128]{1,0:T(8,128)S(1)}, u32[]{:S(2)}, u32[]{:S(2)}) %collective-permute-start.3) | collective-permute-done | bytes 69664 | tf_op jit(solution)/shard_map/ppermute | solution.py:19
  12.8 0.0 collective-permute-done.1
  12.8 3.7 %collective-permute-start.6 = (f32[136,128]{1,0:T(8,128)S(1)}, f32[136,128]{1,0:T(8,128)S(1)}, u32[]{:S(2)}, u32[]{:S(2)}) collective-permute-start(f32[136,128]{1,0:T(8,128)S(1)} %add_add_fusion.1), channel_id=1, source_target_pairs={{0,24},{2,26},{4,28},{6,30},{8,16},{10,18},{12,20},{14,22},{16,8},... | collective-permute-start | bytes 208904 | tf_op jit(solution)/shard_map/ppermute | solution.py:19
  16.5 0.0 collective-permute-start.5
  16.5 0.8 %collective-permute-start.4 = (f32[136,128]{1,0:T(8,128)S(1)}, f32[136,128]{1,0:T(8,128)S(1)}, u32[]{:S(2)}, u32[]{:S(2)}) collective-permute-start(f32[136,128]{1,0:T(8,128)S(1)} %add_add_fusion.1), channel_id=1, source_target_pairs={{0,8},{2,10},{4,12},{6,14},{8,0},{10,2},{12,4},{14,6},{16,24},{18,... | collective-permute-start | bytes 208904 | tf_op jit(solution)/shard_map/ppermute | solution.py:19
  17.2 2.3 %collective-permute-done.6 = f32[136,128]{1,0:T(8,128)S(1)} collective-permute-done((f32[136,128]{1,0:T(8,128)S(1)}, f32[136,128]{1,0:T(8,128)S(1)}, u32[]{:S(2)}, u32[]{:S(2)}) %collective-permute-start.6) | collective-permute-done | bytes 69664 | tf_op jit(solution)/shard_map/ppermute | solution.py:19
  19.5 2.4 %collective-permute-done.5 = f32[136,128]{1,0:T(8,128)S(1)} collective-permute-done((f32[136,128]{1,0:T(8,128)S(1)}, f32[136,128]{1,0:T(8,128)S(1)}, u32[]{:S(2)}, u32[]{:S(2)}) %collective-permute-start.5) | collective-permute-done | bytes 69664 | tf_op jit(solution)/shard_map/ppermute | solution.py:19
  22.0 0.1 collective-permute-done.4
  22.0 0.1 collective-permute-start.7
  22.1 0.4 %spread.1.lead_ref = bf16[2048,256]{1,0:T(8,128)(2,1)S(1)} custom-call(bf16[2048,128]{1,0:T(8,128)(2,1)S(1)} %bitcast.10, bf16[2048,128]{1,0:T(8,128)(2,1)S(1)} %collective-permute-done.recv_ref), custom_call_target="tpu_custom_call" | custom-call | tf_op jit(solution)/shard_map/spread/pallas_call | solution.py:250
  22.6 0.0 copy-start.1
  22.6 0.9 %collective-permute-start.8 = (f32[136,128]{1,0:T(8,128)S(1)}, f32[136,128]{1,0:T(8,128)S(1)}, u32[]{:S(2)}, u32[]{:S(2)}) collective-permute-start(f32[136,128]{1,0:T(8,128)S(1)} %add_add_fusion.kept_ref.same_ref), channel_id=1, source_target_pairs={{0,2},{2,0},{4,6},{6,4},{8,10},{10,8},{12,14},{14,12},{16,18},{18,... | collective-permute-start | bytes 208904 | tf_op jit(solution)/shard_map/ppermute | solution.py:19
  23.5 0.0 collective-permute-done.7.recv_ref
  23.5 4.6 %factor.1 = (f32[128,128]{1,0:T(8,128)S(1)}, f32[128,128]{1,0:T(8,128)S(1)}) custom-call(f32[136,128]{1,0:T(8,128)S(1)} %add_add_fusion.kept_ref.same_ref, f32[136,128]{1,0:T(8,128)S(1)} %collective-permute-done.7.recv_ref), custom_call_target="tpu_custom_call" | custom-call | flops 1073741824 | bytes 8388608 | tf_op jit(solution)/shard_map/factor/pallas_call | solution.py:266
  28.2 3.1 %finish.1 = (f32[256,128]{1,0:T(8,128)}, bf16[2048,128]{1,0:T(8,128)(2,1)}) custom-call(f32[2,2,2]{2,1,0:T(2,128)S(1)} %copy-done.2, bf16[2048,128]{1,0:T(8,128)(2,1)S(1)} %bitcast.11, bf16[2048,256]{1,0:T(8,128)(2,1)S(1)} %spread.1.lead_ref, f32[128,128]{1,0:T(8,128)S(1)} %get-tuple-element.10.inverse_ref, f32[128,128]{1,0:T(8,128)S(1)} %get-tuple-element.11.gram_ref, ...), custom_call_target="tpu_custom_call" | custom-call | tf_op jit(solution)/shard_map/finish/pallas_call | solution.py:276
  (7 shorter events, 0.1 us)
Async XLA Ops:
  0.6 2.3 %collective-permute-start = (bf16[2048,128]{1,0:T(8,128)(2,1)}, bf16[2048,128]{1,0:T(8,128)(2,1)S(1)}, u32[]{:S(2)}, u32[]{:S(2)}) collective-permute-start(bf16[2048,128]{1,0:T(8,128)(2,1)} %bitcast.7), channel_id=1, source_target_pairs={{0,1},{1,0},{2,3},{3,2},{4,5},{5,4},{6,7},{7,6},{8,9},{9,8},{10,11... | collective-permute-start | bytes 1572872 | tf_op jit(solution)/shard_map/ppermute | solution.py:19
  1.1 1.0 %copy-start = (bf16[1024,1,2,128]{3,2,1,0:T(2,128)(2,1)S(1)}, bf16[1024,1,2,128]{3,2,1,0:T(2,128)(2,1)}, u32[]{:S(2)}) copy-start(bf16[1024,1,2,128]{3,2,1,0:T(2,128)(2,1)} %param.2) | copy-start | bytes 1572868
  2.2 0.7 %copy-start.2 = (f32[2,2,2]{2,1,0:T(2,128)S(1)}, f32[2,2,2]{2,1,0:T(2,128)}, u32[]{:S(2)}) copy-start(f32[2,2,2]{2,1,0:T(2,128)} %scale_ref.3) | copy-start | bytes 100
  4.0 6.3 %collective-permute-start.2 = (f32[136,128]{1,0:T(8,128)S(1)}, f32[136,128]{1,0:T(8,128)S(1)}, u32[]{:S(2)}, u32[]{:S(2)}) collective-permute-start(f32[136,128]{1,0:T(8,128)S(1)} %get-tuple-element.8), channel_id=1, source_target_pairs={{0,4},{2,6},{4,0},{6,2},{8,12},{10,14},{12,8},{14,10},{16,20},{18,... | collective-permute-start | bytes 208904 | tf_op jit(solution)/shard_map/ppermute | solution.py:19
  6.9 5.9 %collective-permute-start.3 = (f32[136,128]{1,0:T(8,128)S(1)}, f32[136,128]{1,0:T(8,128)S(1)}, u32[]{:S(2)}, u32[]{:S(2)}) collective-permute-start(f32[136,128]{1,0:T(8,128)S(1)} %get-tuple-element.9), channel_id=1, source_target_pairs={{0,6},{2,4},{4,2},{6,0},{8,14},{10,12},{12,10},{14,8},{16,22},{18,... | collective-permute-start | bytes 208904 | tf_op jit(solution)/shard_map/ppermute | solution.py:19
  8.3 4.4 %collective-permute-start.1 = (f32[136,128]{1,0:T(8,128)S(1)}, f32[136,128]{1,0:T(8,128)S(1)}, u32[]{:S(2)}, u32[]{:S(2)}) collective-permute-start(f32[136,128]{1,0:T(8,128)S(1)} %get-tuple-element.9), channel_id=1, source_target_pairs={{0,2},{2,0},{4,6},{6,4},{8,10},{10,8},{12,14},{14,12},{16,18},{18,... | collective-permute-start | bytes 208904 | tf_op jit(solution)/shard_map/ppermute | solution.py:19
  12.8 6.7 %collective-permute-start.6 = (f32[136,128]{1,0:T(8,128)S(1)}, f32[136,128]{1,0:T(8,128)S(1)}, u32[]{:S(2)}, u32[]{:S(2)}) collective-permute-start(f32[136,128]{1,0:T(8,128)S(1)} %add_add_fusion.1), channel_id=1, source_target_pairs={{0,24},{2,26},{4,28},{6,30},{8,16},{10,18},{12,20},{14,22},{16,8},... | collective-permute-start | bytes 208904 | tf_op jit(solution)/shard_map/ppermute | solution.py:19
  16.5 5.5 %collective-permute-start.5 = (f32[136,128]{1,0:T(8,128)S(1)}, f32[136,128]{1,0:T(8,128)S(1)}, u32[]{:S(2)}, u32[]{:S(2)}) collective-permute-start(f32[136,128]{1,0:T(8,128)S(1)} %add_add_fusion.1), channel_id=1, source_target_pairs={{0,16},{2,18},{4,20},{6,22},{8,24},{10,26},{12,28},{14,30},{16,0},... | collective-permute-start | bytes 208904 | tf_op jit(solution)/shard_map/ppermute | solution.py:19
  16.5 5.6 %collective-permute-start.4 = (f32[136,128]{1,0:T(8,128)S(1)}, f32[136,128]{1,0:T(8,128)S(1)}, u32[]{:S(2)}, u32[]{:S(2)}) collective-permute-start(f32[136,128]{1,0:T(8,128)S(1)} %add_add_fusion.1), channel_id=1, source_target_pairs={{0,8},{2,10},{4,12},{6,14},{8,0},{10,2},{12,4},{14,6},{16,24},{18,... | collective-permute-start | bytes 208904 | tf_op jit(solution)/shard_map/ppermute | solution.py:19
  22.0 1.5 %collective-permute-start.7 = (f32[136,128]{1,0:T(8,128)S(1)}, f32[136,128]{1,0:T(8,128)S(1)}, u32[]{:S(2)}, u32[]{:S(2)}) collective-permute-start(f32[136,128]{1,0:T(8,128)S(1)} %add_add_fusion.kept_ref.same_ref), channel_id=1, source_target_pairs={{0,1},{1,0},{2,3},{3,2},{4,5},{5,4},{6,7},{7,6},{8,9},{9,8},{10,11... | collective-permute-start | bytes 208904 | tf_op jit(solution)/shard_map/ppermute | solution.py:19
  22.6 5.6 %copy-start.1 = (bf16[1024,1,2,128]{3,2,1,0:T(2,128)(2,1)S(1)}, bf16[1024,1,2,128]{3,2,1,0:T(2,128)(2,1)}, u32[]{:S(2)}) copy-start(bf16[1024,1,2,128]{3,2,1,0:T(2,128)(2,1)} %param.2) | copy-start | bytes 1572868
  22.6 5.6 %collective-permute-start.8 = (f32[136,128]{1,0:T(8,128)S(1)}, f32[136,128]{1,0:T(8,128)S(1)}, u32[]{:S(2)}, u32[]{:S(2)}) collective-permute-start(f32[136,128]{1,0:T(8,128)S(1)} %add_add_fusion.kept_ref.same_ref), channel_id=1, source_target_pairs={{0,2},{2,0},{4,6},{6,4},{8,10},{10,8},{12,14},{14,12},{16,18},{18,... | collective-permute-start | bytes 208904 | tf_op jit(solution)/shard_map/ppermute | solution.py:19

commit v5 on v4

--- a/solution.py
+++ b/solution.py
@@ -29,12 +29,12 @@
     return found
 
 
-def from_leader(x, count, mine):
-    stride = 1
-    while 2 * stride < count:
-        x = jnp.where((mine & stride) != 0, partner(x, "cols", count, stride), x)
+def among_pairs(x, count, mine, root):
+    stride = 2
+    while stride < count:
+        x = jnp.where(((mine ^ root) & stride) != 0, partner(x, "cols", count, stride), x)
         stride *= 2
-    return x, partner(x, "cols", count, stride), stride
+    return x
 
 
 def lanes(x, p):
@@ -107,84 +107,108 @@
     return jnp.where((row == col) & (row >= half), jnp.broadcast_to(packed[half : half + 1, :], gram.shape), gram)
 
 
-def leading(z_ref, recv_ref, stride):
-    mine = lax.axis_index("cols")
-    return jnp.where((mine & stride) == 0, z_ref[...], recv_ref[...])
-
-
-def split_kernel(rounds, z_ref, out_ref, own):
-    width = z_ref.shape[1]
+def leading(even_ref, odd_ref):
+    return jnp.where(lax.axis_index("cols") % 2 == 0, even_ref[...], odd_ref[...])
+
+
+def split_kernel(rounds, z_ref, first_ref, own_ref, wide):
     points = z_ref.shape[0] // rounds
-    own[...] = z_ref[...].astype(F32)
-    for r in range(rounds):
-        out_ref[:, r * width : (r + 1) * width] = own[pl.ds(r, points, stride=rounds), :].astype(BF16)
-
-
-def products_kernel(rounds, nblock, stride, scale_ref, own_ref, kept_ref, recv_ref, same_ref, other_ref, lead, cross):
+    wide[...] = z_ref[...].astype(F32)
+    first = wide[pl.ds(0, points, stride=rounds), :].astype(BF16)
+    last = wide[pl.ds(1, points, stride=rounds), :].astype(BF16)
+    first_ref[...] = first
+    own_ref[...] = jnp.where(lax.axis_index("cols") % 2 == 1, first, last)
+
+
+def products_kernel(rounds, nblock, scale_ref, first_ref, own_ref, recv_ref, *rest):
+    lead_ref = rest[:-4] if len(rest) == 4 else (*rest[:2], rest[-1])
+    same_ref, other_ref, wide, cross = rest if len(rest) == 4 else rest[2:-1]
     group = lax.axis_index("cols")
+    odd = group % 2
+    place_round = 1 - odd
     digit = lax.axis_index("rows") % 2
-    width = kept_ref.shape[1]
+    width = recv_ref.shape[1]
     points = own_ref.shape[0] // nblock
     half = width // 2
-    lead[...] = leading(kept_ref, recv_ref, stride).astype(F32)
-    out = jnp.zeros((width, rounds * width), F32)
+    height = half + 8
+    wide[...] = recv_ref[...].astype(F32)
+    if lead_ref:
+        lead_ref[2][...] = leading(*lead_ref[:2]).astype(F32)
+    out = jnp.zeros((width, 2 * width), F32)
     for b in range(nblock):
-        panel = lead[pl.ds(b * points * rounds, points, stride=rounds), :].astype(BF16)
-        own = own_ref[b * points : (b + 1) * points, :]
-        block = lax.dot_general(panel, own, (((0,), (0,)), ((), ())), preferred_element_type=F32)
+        at = slice(b * points, (b + 1) * points)
+        start = b * points * rounds
+        near = wide[pl.ds(start, points, stride=rounds), :]
+        far = wide[pl.ds(start + 1, points, stride=rounds), :]
+        theirs = jnp.where(odd == 1, near, far).astype(BF16)
+        if lead_ref:
+            panel = lead_ref[2][pl.ds(start, points, stride=rounds), :].astype(BF16)
+        else:
+            panel = jnp.where(odd == 1, theirs, first_ref[at, :])
+        block = lax.dot_general(
+            panel, jnp.concatenate([theirs, own_ref[at, :]], axis=1), (((0,), (0,)), ((), ())), preferred_element_type=F32
+        )
         first = scale_ref[b, 0, 0]
-        pieces = [block[:, r * width : (r + 1) * width] * (first * scale_ref[b, group, r]) for r in range(rounds)]
-        out = out + jnp.concatenate(pieces, axis=1)
+        left = block[:, :width] * (first * scale_ref[b, group + 1 - 2 * odd, place_round])
+        right = block[:, width:] * (first * scale_ref[b, group, place_round])
+        out = out + jnp.concatenate([left, right], axis=1)
     packed = pack(out[:, :width])
-    height = packed.shape[0]
-    for r in range(rounds):
-        cross[r * width : (r + 1) * width, :] = out[:, r * width : (r + 1) * width]
+    cross[:width, :] = out[:, :width]
+    cross[width:, :] = out[:, width:]
     for ref, place in ((same_ref, digit), (other_ref, 1 - digit)):
-        for r in range(rounds):
-            rows = cross[pl.ds(pl.multiple_of(r * width + place * half, half), half), :]
-            if r == 0:
-                ref[:half, :] = jnp.where(group == 0, packed[:half, :], rows)
-                ref[half:height, :] = packed[half:, :]
-            else:
-                ref[height + (r - 1) * half : height + r * half, :] = rows
-
-
-def spread_kernel(rounds, stride, kept_ref, recv_ref, out_ref):
-    width = kept_ref.shape[1]
-    rows = lax.broadcasted_iota(jnp.int32, kept_ref.shape, 0) % rounds
-    lead = leading(kept_ref, recv_ref, stride).astype(F32)
+        theirs = cross[pl.ds(pl.multiple_of(place * half, half), half), :]
+        ref[:half, :] = jnp.where(group == 1, packed[:half, :], theirs)
+        ref[half:height, :] = packed[half:, :]
+        ref[height:, :] = cross[pl.ds(pl.multiple_of(width + place * half, half), half), :]
+
+
+def spread_kernel(rounds, even_ref, odd_ref, out_ref):
+    width = even_ref.shape[1]
+    rows = lax.broadcasted_iota(jnp.int32, even_ref.shape, 0) % rounds
+    lead = leading(even_ref, odd_ref).astype(F32)
     for r in range(rounds):
         moved = lead if r == 0 else pltpu.roll(lead, r, 0)
         out_ref[:, r * width : (r + 1) * width] = jnp.where(rows == r, moved, 0.0).astype(BF16)
 
 
-def factor_kernel(stride, kept_ref, recv_ref, inverse_ref, gram_ref):
-    width = kept_ref.shape[1]
-    mine = lax.axis_index("cols")
+def factor_kernel(sums_ref, out_ref):
+    width = sums_ref.shape[1]
     height = width // 2 + 8
-    packed = jnp.where((mine & stride) == 0, kept_ref[:height, :], recv_ref[:height, :])
-    gram = unpack(packed)
-    gram_ref[...] = gram
-    rows = [gram[8 * i : 8 * i + 8, :] for i in range(width // 8)]
-    for i, row in enumerate(lower_inverse(rows, width)):
-        inverse_ref[8 * i : 8 * i + 8, :] = row
-
-
-def finish_kernel(rounds, nblock, root, chunks, scale_ref, z_ref, lead_ref, inverse_ref, gram_ref, same_ref, other_ref, coef_ref, out_ref, cross, held, sems):
     group = lax.axis_index("cols")
+
+    @pl.when(group == 1)
+    def _():
+        gram = unpack(sums_ref[:height, :])
+        out_ref[width:, :] = gram
+        rows = [gram[8 * i : 8 * i + 8, :] for i in range(width // 8)]
+        for i, row in enumerate(lower_inverse(rows, width)):
+            out_ref[8 * i : 8 * i + 8, :] = row
+
+    @pl.when(group != 1)
+    def _():
+        out_ref[:width, :] = jnp.zeros((width, width), F32)
+        out_ref[width : width + height, :] = sums_ref[:height, :]
+        out_ref[width + height :, :] = jnp.zeros((width - height, width), F32)
+
+
+def finish_kernel(
+    rounds, nblock, root, chunks, scale_ref, z_ref, lead_ref, kept_ref, recv_ref, same_ref, other_ref, across_ref,
+    coef_ref, out_ref, cross, held, sems,
+):
+    group = lax.axis_index("cols")
+    odd = group % 2 == 1
     digit = lax.axis_index("rows") % 2
     width = z_ref.shape[1]
     half = width // 2
     height = half + 8
-    for ref, place in ((same_ref, digit), (other_ref, 1 - digit)):
+    for place, own_ref, theirs in ((digit, same_ref, recv_ref[width : width + half, :]), (1 - digit, other_ref, across_ref[:half, :])):
         at = pl.ds(pl.multiple_of(place * half, half), half)
-        for r in range(rounds):
-            if r == 0:
-                rows = jnp.where(group == 0, gram_ref[at, :], ref[:half, :])
-            else:
-                rows = ref[height + (r - 1) * half : height + r * half, :]
-            cross[at, r * width : (r + 1) * width] = rows
-    inverse = inverse_ref[...]
+        gram = recv_ref[pl.ds(pl.multiple_of(width + place * half, half), half), :]
+        mine = own_ref[height:, :]
+        theirs = jnp.where(group == 0, gram, theirs)
+        cross[at, :width] = jnp.where(odd, mine, theirs)
+        cross[at, width:] = jnp.where(odd, theirs, mine)
+    inverse = jnp.where(odd, kept_ref[:width, :], recv_ref[:width, :])
     across = inverse.T
     raw = jnp.dot(inverse, cross[...], precision=HIGH, preferred_element_type=F32)
     weights = jnp.dot(across, raw, precision=HIGH, preferred_element_type=F32)
@@ -225,53 +249,64 @@
     root = math.sqrt(points * n_rows)
     long = points * rounds
     z = snapshots.reshape(long, width)
-    kept, recv, stride = from_leader(z, n_cols, lax.axis_index("cols"))
+    group = lax.axis_index("cols")
+    recv = partner(z, "cols", n_cols, 1)
+    even = among_pairs(z, n_cols, group, 0)
+    leads = (even, recv) if n_cols == 2 else (even, partner(even, "cols", n_cols, 1))
     phases = radices(n_rows)
-    payload = (rounds * width) // 2 + 8
+    payload = width + 8
     params = pltpu.CompilerParams(vmem_limit_bytes=48 << 20)
-    own = pl.pallas_call(
+    first, own = pl.pallas_call(
         functools.partial(split_kernel, rounds),
-        out_shape=jax.ShapeDtypeStruct((points, rounds * width), BF16),
+        out_shape=[jax.ShapeDtypeStruct((points, width), BF16)] * 2,
         in_specs=[VMEM],
-        out_specs=VMEM,
+        out_specs=[VMEM] * 2,
         scratch_shapes=[pltpu.VMEM((long, width), F32)],
         compiler_params=params,
         name="split",
     )(z)
+    extra = () if n_cols == 2 else leads
     sent = pl.pallas_call(
-        functools.partial(products_kernel, rounds, nblock, stride),
+        functools.partial(products_kernel, rounds, nblock),
         out_shape=[jax.ShapeDtypeStruct((payload, width), F32)] * 2,
-        in_specs=[SMEM, VMEM, VMEM, VMEM],
+        in_specs=[SMEM] + [VMEM] * (3 + len(extra)),
         out_specs=[VMEM] * 2,
-        scratch_shapes=[pltpu.VMEM((long, width), F32), pltpu.VMEM((rounds * width, width), F32)],
+        scratch_shapes=[pltpu.VMEM((long, width), F32), pltpu.VMEM((2 * width, width), F32)]
+        + [pltpu.VMEM((long, width), F32)] * (len(extra) // 2),
         compiler_params=params,
         name="products",
-    )(scales, own, kept, recv)
-    lead = pl.pallas_call(
-        functools.partial(spread_kernel, rounds, stride),
-        out_shape=jax.ShapeDtypeStruct((long, rounds * width), BF16),
-        in_specs=[VMEM, VMEM],
-        out_specs=VMEM,
-        compiler_params=params,
-        name="spread",
-    )(kept, recv)
+    )(scales, first, own, recv, *extra)
     sums = sent[0]
     for step, (hop, base) in enumerate(phases):
         source = sent if step == 0 else [sums] * 2
         others = [partner(source[b % 2], "rows", n_rows, b * hop) for b in range(1, base)]
+        if step == len(phases) - 1:
+            lead = pl.pallas_call(
+                functools.partial(spread_kernel, rounds),
+                out_shape=jax.ShapeDtypeStruct((long, rounds * width), BF16),
+                in_specs=[VMEM, VMEM],
+                out_specs=VMEM,
+                compiler_params=params,
+                name="spread",
+            )(*leads)
+            *others, lead = lax.optimization_barrier((*others, lead))
         for other in others:
             sums = sums + other
-    first, second, bit = from_leader(sums, n_cols, lax.axis_index("cols"))
     gathered = partner(sums, "rows", n_rows, 1)
-    inverse, gram = pl.pallas_call(
-        functools.partial(factor_kernel, bit),
-        out_shape=[jax.ShapeDtypeStruct((width, width), F32)] * 2,
-        in_specs=[VMEM] * 2,
-        out_specs=[VMEM] * 2,
+    factored = pl.pallas_call(
+        factor_kernel,
+        out_shape=jax.ShapeDtypeStruct((2 * width, width), F32),
+        in_specs=[VMEM],
+        out_specs=VMEM,
         compiler_params=params,
         cost_estimate=pl.CostEstimate(flops=1 << 30, bytes_accessed=1 << 23, transcendentals=0),
         name="factor",
-    )(first, second)
+    )(sums)
+    if n_cols > 2:
+        shared = among_pairs(factored[:width], n_cols, group, 1)
+        factored = jnp.concatenate([shared, factored[width:]], axis=0)
+    crossed = partner(gathered, "cols", n_cols, 1)
+    swapped = partner(factored, "cols", n_cols, 1)
     chunks = 2 * nblock
     coef, updated = pl.pallas_call(
         functools.partial(finish_kernel, rounds, nblock, root, chunks),
@@ -279,7 +314,7 @@
             jax.ShapeDtypeStruct((width * rounds, width), F32),
             jax.ShapeDtypeStruct((long, width), BF16),
         ],
-        in_specs=[SMEM] + [VMEM] * 6,
+        in_specs=[SMEM] + [VMEM] * 7,
         out_specs=[VMEM, pl.BlockSpec(memory_space=pl.ANY)],
         scratch_shapes=[
             pltpu.VMEM((width, rounds * width), F32),
@@ -288,7 +323,7 @@
         ],
         compiler_params=params,
         name="finish",
-    )(scales, z, lead, inverse, gram, sums, gathered)
+    )(scales, z, lead, factored, swapped, sums, gathered, crossed)
     return coef.reshape(width, 1, rounds, width), updated.reshape(snapshots.shape)
 
 

time: 31.5 us -> 31.1 us (0.987)
  Pallas kernels: 9.37 us -> 4.77 us
  starting transfers between devices: 10.5 us -> 14.1 us
  waiting for transfers between devices: 9.65 us -> 10.2 us
    pallas_call x4, Pallas kernels: 6.26 us -> 1.66 us  [the longest x1 1 us: shards(): pl.pallas_call(functools.partial(products_kernel, rounds, nblock), out_sh...]
    ppermute x9 -> x10, starting transfers between devices: 10.5 us -> 14.1 us  [partner(): return lax.ppermute(x, axis, [(i, i ^ offset) for i in range(count)])]
    ppermute x9 -> x10, waiting for transfers between devices: 9.65 us -> 10.2 us  [partner(): return lax.ppermute(x, axis, [(i, i ^ offset) for i in range(count)])]
  transfers between devices with their start and end apart: 9 -> 10, of which waited for: 6 -> 8; matrix products, arithmetic and copies ran while one was open for 0% -> 0% of each run, Pallas kernels for 17% -> 2%
where the time goes in v5:
time: 31.1 us; the launch traced here: 30.9 us
  starting transfers between devices  14.1 us (45%)
  waiting for transfers between devices  10.2 us (33%)
  Pallas kernels  4.77 us (15%)
  local copies, waits for them, and re-layouts  1.2 us (4%)
  between operations  0.67 us (2%)
    ppermute x10, starting transfers between devices, partner(): return lax.ppermute(x, axis, [(i, i ^ offset) for i in range(count)])  14.1 us
    ppermute x10, waiting for transfers between devices, partner(): return lax.ppermute(x, axis, [(i, i ^ offset) for i in range(count)])  10.2 us
    pallas_call x1, Pallas kernels, shards(): pl.pallas_call(functools.partial(finish_kernel, rounds, nblock, root, chu...  3.11 us
    unnamed x6, local copies, waits for them, and re-layouts  1.2 us
    pallas_call x1, Pallas kernels, shards(): pl.pallas_call(functools.partial(products_kernel, rounds, nblock), out_sh...  1 us
  transfers between devices with their start and end apart: 10, of which 8 were waited for; matrix products, arithmetic and copies ran while one was open for 0% of the time, Pallas kernels for 2%

profile of v5, /device:TPU:0, one launch (start us, length us, event | category | flops | bytes accessed | tf_op | source)
XLA Modules:
  0.0 30.9 jit_solution(17845822401900939297)
XLA Ops:
  0.6 0.5 %collective-permute-start = (bf16[2048,128]{1,0:T(8,128)(2,1)}, bf16[2048,128]{1,0:T(8,128)(2,1)S(1)}, u32[]{:S(2)}, u32[]{:S(2)}) collective-permute-start(bf16[2048,128]{1,0:T(8,128)(2,1)} %bitcast.7), channel_id=1, source_target_pairs={{0,1},{1,0},{2,3},{3,2},{4,5},{5,4},{6,7},{7,6},{8,9},{9,8},{10,11... | collective-permute-start | bytes 1572872 | tf_op jit(solution)/shard_map/ppermute | solution.py:19
  1.1 1.0 %copy-done = bf16[1024,1,2,128]{3,2,1,0:T(2,128)(2,1)S(1)} copy-done((bf16[1024,1,2,128]{3,2,1,0:T(2,128)(2,1)S(1)}, bf16[1024,1,2,128]{3,2,1,0:T(2,128)(2,1)}, u32[]{:S(2)}) %copy-start) | copy-done | bytes 524312
  2.2 0.2 split.1
  2.4 0.5 %collective-permute-done.recv_ref.odd_ref = bf16[2048,128]{1,0:T(8,128)(2,1)S(1)} collective-permute-done((bf16[2048,128]{1,0:T(8,128)(2,1)}, bf16[2048,128]{1,0:T(8,128)(2,1)S(1)}, u32[]{:S(2)}, u32[]{:S(2)}) %collective-permute-start) | collective-permute-done | bytes 524320 | tf_op jit(solution)/shard_map/ppermute | solution.py:19
  2.9 0.2 copy-done.2
  3.1 1.0 %products.1 = (f32[136,128]{1,0:T(8,128)S(1)}, f32[136,128]{1,0:T(8,128)S(1)}) custom-call(f32[2,2,2]{2,1,0:T(2,128)S(1)} %copy-done.2, bf16[1024,128]{1,0:T(8,128)(2,1)S(1)} %get-tuple-element.12.first_ref, bf16[1024,128]{1,0:T(8,128)(2,1)S(1)} %get-tuple-element.13.own_ref, bf16[2048,128]{1,0:T(8,128)(2,1)S(1)} %collective-permute-done.recv_ref.odd_ref), custom_call_target="tpu_custom_call" | custom-call | tf_op jit(solution)/shard_map/products/pallas_call | solution.py:269
  4.1 2.8 %collective-permute-start.2 = (f32[136,128]{1,0:T(8,128)S(1)}, f32[136,128]{1,0:T(8,128)S(1)}, u32[]{:S(2)}, u32[]{:S(2)}) collective-permute-start(f32[136,128]{1,0:T(8,128)S(1)} %get-tuple-element.14), channel_id=1, source_target_pairs={{0,4},{2,6},{4,0},{6,2},{8,12},{10,14},{12,8},{14,10},{16,20},{18,... | collective-permute-start | bytes 208904 | tf_op jit(solution)/shard_map/ppermute | solution.py:19
  6.9 1.4 %collective-permute-start.3 = (f32[136,128]{1,0:T(8,128)S(1)}, f32[136,128]{1,0:T(8,128)S(1)}, u32[]{:S(2)}, u32[]{:S(2)}) collective-permute-start(f32[136,128]{1,0:T(8,128)S(1)} %get-tuple-element.15), channel_id=1, source_target_pairs={{0,6},{2,4},{4,2},{6,0},{8,14},{10,12},{12,10},{14,8},{16,22},{18,... | collective-permute-start | bytes 208904 | tf_op jit(solution)/shard_map/ppermute | solution.py:19
  8.3 0.1 collective-permute-start.1
  8.4 1.9 %collective-permute-done.2 = f32[136,128]{1,0:T(8,128)S(1)} collective-permute-done((f32[136,128]{1,0:T(8,128)S(1)}, f32[136,128]{1,0:T(8,128)S(1)}, u32[]{:S(2)}, u32[]{:S(2)}) %collective-permute-start.2) | collective-permute-done | bytes 69664 | tf_op jit(solution)/shard_map/ppermute | solution.py:19
  10.3 2.3 %collective-permute-done.3 = f32[136,128]{1,0:T(8,128)S(1)} collective-permute-done((f32[136,128]{1,0:T(8,128)S(1)}, f32[136,128]{1,0:T(8,128)S(1)}, u32[]{:S(2)}, u32[]{:S(2)}) %collective-permute-start.3) | collective-permute-done | bytes 69664 | tf_op jit(solution)/shard_map/ppermute | solution.py:19
  12.6 0.0 collective-permute-done.1
  12.6 3.7 %collective-permute-start.6 = (f32[136,128]{1,0:T(8,128)S(1)}, f32[136,128]{1,0:T(8,128)S(1)}, u32[]{:S(2)}, u32[]{:S(2)}) collective-permute-start(f32[136,128]{1,0:T(8,128)S(1)} %add_add_fusion.1), channel_id=1, source_target_pairs={{0,24},{2,26},{4,28},{6,30},{8,16},{10,18},{12,20},{14,22},{16,8},... | collective-permute-start | bytes 208904 | tf_op jit(solution)/shard_map/ppermute | solution.py:19
  16.3 0.8 %collective-permute-start.4 = (f32[136,128]{1,0:T(8,128)S(1)}, f32[136,128]{1,0:T(8,128)S(1)}, u32[]{:S(2)}, u32[]{:S(2)}) collective-permute-start(f32[136,128]{1,0:T(8,128)S(1)} %add_add_fusion.1), channel_id=1, source_target_pairs={{0,8},{2,10},{4,12},{6,14},{8,0},{10,2},{12,4},{14,6},{16,24},{18,... | collective-permute-start | bytes 208904 | tf_op jit(solution)/shard_map/ppermute | solution.py:19
  17.1 0.5 %spread.1.lead_ref = bf16[2048,256]{1,0:T(8,128)(2,1)S(1)} custom-call(bf16[2048,128]{1,0:T(8,128)(2,1)S(1)} %bitcast.9, bf16[2048,128]{1,0:T(8,128)(2,1)S(1)} %collective-permute-done.recv_ref.odd_ref), custom_call_target="tpu_custom_call" | custom-call | tf_op jit(solution)/shard_map/spread/pallas_call | solution.py:284
  17.6 1.9 %collective-permute-done.6 = f32[136,128]{1,0:T(8,128)S(1)} collective-permute-done((f32[136,128]{1,0:T(8,128)S(1)}, f32[136,128]{1,0:T(8,128)S(1)}, u32[]{:S(2)}, u32[]{:S(2)}) %collective-permute-start.6) | collective-permute-done | bytes 69664 | tf_op jit(solution)/shard_map/ppermute | solution.py:19
  19.5 2.3 %collective-permute-done.5 = f32[136,128]{1,0:T(8,128)S(1)} collective-permute-done((f32[136,128]{1,0:T(8,128)S(1)}, f32[136,128]{1,0:T(8,128)S(1)}, u32[]{:S(2)}, u32[]{:S(2)}) %collective-permute-start.5) | collective-permute-done | bytes 69664 | tf_op jit(solution)/shard_map/ppermute | solution.py:19
  21.8 0.1 collective-permute-done.4
  21.9 1.4 %collective-permute-start.8 = (f32[136,128]{1,0:T(8,128)S(1)}, f32[136,128]{1,0:T(8,128)S(1)}, u32[]{:S(2)}, u32[]{:S(2)}) collective-permute-start(f32[136,128]{1,0:T(8,128)S(1)} %add_add_fusion.sums_ref.same_ref), channel_id=1, source_target_pairs={{0,2},{2,0},{4,6},{6,4},{8,10},{10,8},{12,14},{14,12},{16,18},{18,... | collective-permute-start | bytes 208904 | tf_op jit(solution)/shard_map/ppermute | solution.py:19
  23.3 3.2 %collective-permute-start.7 = (f32[256,128]{1,0:T(8,128)S(1)}, f32[256,128]{1,0:T(8,128)S(1)}, u32[]{:S(2)}, u32[]{:S(2)}) collective-permute-start(f32[256,128]{1,0:T(8,128)S(1)} %factor.1.kept_ref), channel_id=1, source_target_pairs={{0,1},{1,0},{2,3},{3,2},{4,5},{5,4},{6,7},{7,6},{8,9},{9,8},{10,11... | collective-permute-start | bytes 393224 | tf_op jit(solution)/shard_map/ppermute | solution.py:19
  26.6 0.1 collective-permute-start.9
  26.7 0.9 %collective-permute-done.7.recv_ref = f32[256,128]{1,0:T(8,128)S(1)} collective-permute-done((f32[256,128]{1,0:T(8,128)S(1)}, f32[256,128]{1,0:T(8,128)S(1)}, u32[]{:S(2)}, u32[]{:S(2)}) %collective-permute-start.7) | collective-permute-done | bytes 131104 | tf_op jit(solution)/shard_map/ppermute | solution.py:19
  27.6 0.3 collective-permute-done.9.across_ref
  27.8 3.1 %finish.1 = (f32[256,128]{1,0:T(8,128)}, bf16[2048,128]{1,0:T(8,128)(2,1)}) custom-call(f32[2,2,2]{2,1,0:T(2,128)S(1)} %copy-done.2, bf16[2048,128]{1,0:T(8,128)(2,1)S(1)} %bitcast.10, bf16[2048,256]{1,0:T(8,128)(2,1)S(1)} %spread.1.lead_ref, f32[256,128]{1,0:T(8,128)S(1)} %factor.1.kept_ref, f32[256,128]{1,0:T(8,128)S(1)} %collective-permute-done.7.recv_ref, ...), custom_call_target="tpu_custom_call" | custom-call | tf_op jit(solution)/shard_map/finish/pallas_call | solution.py:311
  (9 shorter events, 0.1 us)
Async XLA Ops:
  0.6 2.3 %collective-permute-start = (bf16[2048,128]{1,0:T(8,128)(2,1)}, bf16[2048,128]{1,0:T(8,128)(2,1)S(1)}, u32[]{:S(2)}, u32[]{:S(2)}) collective-permute-start(bf16[2048,128]{1,0:T(8,128)(2,1)} %bitcast.7), channel_id=1, source_target_pairs={{0,1},{1,0},{2,3},{3,2},{4,5},{5,4},{6,7},{7,6},{8,9},{9,8},{10,11... | collective-permute-start | bytes 1572872 | tf_op jit(solution)/shard_map/ppermute | solution.py:19
  1.1 1.0 %copy-start = (bf16[1024,1,2,128]{3,2,1,0:T(2,128)(2,1)S(1)}, bf16[1024,1,2,128]{3,2,1,0:T(2,128)(2,1)}, u32[]{:S(2)}) copy-start(bf16[1024,1,2,128]{3,2,1,0:T(2,128)(2,1)} %param.2) | copy-start | bytes 1572868
  2.4 0.7 %copy-start.2 = (f32[2,2,2]{2,1,0:T(2,128)S(1)}, f32[2,2,2]{2,1,0:T(2,128)}, u32[]{:S(2)}) copy-start(f32[2,2,2]{2,1,0:T(2,128)} %scale_ref.3) | copy-start | bytes 100
  3.1 14.0 %copy-start.1 = (bf16[1024,1,2,128]{3,2,1,0:T(2,128)(2,1)S(1)}, bf16[1024,1,2,128]{3,2,1,0:T(2,128)(2,1)}, u32[]{:S(2)}) copy-start(bf16[1024,1,2,128]{3,2,1,0:T(2,128)(2,1)} %param.2) | copy-start | bytes 1572868
  4.1 6.2 %collective-permute-start.2 = (f32[136,128]{1,0:T(8,128)S(1)}, f32[136,128]{1,0:T(8,128)S(1)}, u32[]{:S(2)}, u32[]{:S(2)}) collective-permute-start(f32[136,128]{1,0:T(8,128)S(1)} %get-tuple-element.14), channel_id=1, source_target_pairs={{0,4},{2,6},{4,0},{6,2},{8,12},{10,14},{12,8},{14,10},{16,20},{18,... | collective-permute-start | bytes 208904 | tf_op jit(solution)/shard_map/ppermute | solution.py:19
  6.9 5.7 %collective-permute-start.3 = (f32[136,128]{1,0:T(8,128)S(1)}, f32[136,128]{1,0:T(8,128)S(1)}, u32[]{:S(2)}, u32[]{:S(2)}) collective-permute-start(f32[136,128]{1,0:T(8,128)S(1)} %get-tuple-element.15), channel_id=1, source_target_pairs={{0,6},{2,4},{4,2},{6,0},{8,14},{10,12},{12,10},{14,8},{16,22},{18,... | collective-permute-start | bytes 208904 | tf_op jit(solution)/shard_map/ppermute | solution.py:19
  8.3 4.3 %collective-permute-start.1 = (f32[136,128]{1,0:T(8,128)S(1)}, f32[136,128]{1,0:T(8,128)S(1)}, u32[]{:S(2)}, u32[]{:S(2)}) collective-permute-start(f32[136,128]{1,0:T(8,128)S(1)} %get-tuple-element.15), channel_id=1, source_target_pairs={{0,2},{2,0},{4,6},{6,4},{8,10},{10,8},{12,14},{14,12},{16,18},{18,... | collective-permute-start | bytes 208904 | tf_op jit(solution)/shard_map/ppermute | solution.py:19
  12.6 6.8 %collective-permute-start.6 = (f32[136,128]{1,0:T(8,128)S(1)}, f32[136,128]{1,0:T(8,128)S(1)}, u32[]{:S(2)}, u32[]{:S(2)}) collective-permute-start(f32[136,128]{1,0:T(8,128)S(1)} %add_add_fusion.1), channel_id=1, source_target_pairs={{0,24},{2,26},{4,28},{6,30},{8,16},{10,18},{12,20},{14,22},{16,8},... | collective-permute-start | bytes 208904 | tf_op jit(solution)/shard_map/ppermute | solution.py:19
  16.3 5.5 %collective-permute-start.5 = (f32[136,128]{1,0:T(8,128)S(1)}, f32[136,128]{1,0:T(8,128)S(1)}, u32[]{:S(2)}, u32[]{:S(2)}) collective-permute-start(f32[136,128]{1,0:T(8,128)S(1)} %add_add_fusion.1), channel_id=1, source_target_pairs={{0,16},{2,18},{4,20},{6,22},{8,24},{10,26},{12,28},{14,30},{16,0},... | collective-permute-start | bytes 208904 | tf_op jit(solution)/shard_map/ppermute | solution.py:19
  16.3 5.6 %collective-permute-start.4 = (f32[136,128]{1,0:T(8,128)S(1)}, f32[136,128]{1,0:T(8,128)S(1)}, u32[]{:S(2)}, u32[]{:S(2)}) collective-permute-start(f32[136,128]{1,0:T(8,128)S(1)} %add_add_fusion.1), channel_id=1, source_target_pairs={{0,8},{2,10},{4,12},{6,14},{8,0},{10,2},{12,4},{14,6},{16,24},{18,... | collective-permute-start | bytes 208904 | tf_op jit(solution)/shard_map/ppermute | solution.py:19
  21.9 4.7 %collective-permute-start.8 = (f32[136,128]{1,0:T(8,128)S(1)}, f32[136,128]{1,0:T(8,128)S(1)}, u32[]{:S(2)}, u32[]{:S(2)}) collective-permute-start(f32[136,128]{1,0:T(8,128)S(1)} %add_add_fusion.sums_ref.same_ref), channel_id=1, source_target_pairs={{0,2},{2,0},{4,6},{6,4},{8,10},{10,8},{12,14},{14,12},{16,18},{18,... | collective-permute-start | bytes 208904 | tf_op jit(solution)/shard_map/ppermute | solution.py:19
  23.3 4.2 %collective-permute-start.7 = (f32[256,128]{1,0:T(8,128)S(1)}, f32[256,128]{1,0:T(8,128)S(1)}, u32[]{:S(2)}, u32[]{:S(2)}) collective-permute-start(f32[256,128]{1,0:T(8,128)S(1)} %factor.1.kept_ref), channel_id=1, source_target_pairs={{0,1},{1,0},{2,3},{3,2},{4,5},{5,4},{6,7},{7,6},{8,9},{9,8},{10,11... | collective-permute-start | bytes 393224 | tf_op jit(solution)/shard_map/ppermute | solution.py:19
  26.6 1.3 %collective-permute-start.9 = (f32[136,128]{1,0:T(8,128)S(1)}, f32[136,128]{1,0:T(8,128)S(1)}, u32[]{:S(2)}, u32[]{:S(2)}) collective-permute-start(f32[136,128]{1,0:T(8,128)S(1)} %collective-permute-done.8.other_ref), channel_id=1, source_target_pairs={{0,1},{1,0},{2,3},{3,2},{4,5},{5,4},{6,7},{7,6},{8,9},{9,8},{10,11... | collective-permute-start | bytes 208904 | tf_op jit(solution)/shard_map/ppermute | solution.py:19

commit v6 on v5

--- a/solution.py
+++ b/solution.py
@@ -10,7 +10,6 @@
 
 F32 = jnp.float32
 BF16 = jnp.bfloat16
-HIGH = lax.Precision.HIGHEST
 VMEM = pl.BlockSpec(memory_space=pltpu.VMEM)
 SMEM = pl.BlockSpec(memory_space=pltpu.SMEM)
 
@@ -43,6 +42,31 @@
 
 def sublanes(x, j):
     return jnp.broadcast_to(x[j : j + 1, :], x.shape)
+
+
+def thirds(x):
+    high = x.astype(BF16)
+    rest = x - high.astype(F32)
+    middle = rest.astype(BF16)
+    return high, middle, (rest - middle.astype(F32)).astype(BF16)
+
+
+def product(left, right):
+    return product_of_thirds(thirds(left), thirds(right))
+
+
+def product_of_thirds(left, right):
+    columns = right[0].shape[1]
+    wide = jnp.concatenate(right[:2], axis=1)
+    both = jnp.dot(
+        jnp.concatenate(left[:2], axis=1), jnp.concatenate([wide, wide], axis=0), preferred_element_type=F32
+    )
+    small = jnp.dot(
+        jnp.concatenate([left[0], left[2]], axis=1),
+        jnp.concatenate([right[2], right[0]], axis=0),
+        preferred_element_type=F32,
+    )
+    return (both[:, :columns] + both[:, columns:]) + small
 
 
 def lower_inverse(rows, width):
@@ -58,29 +82,53 @@
         eye = jnp.where(cid - base == rid, 1.0, 0.0).astype(F32)
         full = jnp.where(inside, eye, held)
         forward = full
-        root_scale = jnp.zeros((8, width), F32)
         scale = jnp.zeros((8, width), F32)
+        inverses = []
+        for j in range(0, 8, 2):
+            left, right = columns[j], columns[j + 1]
+            a, b, c = sublanes(left, j), sublanes(right, j), sublanes(right, j + 1)
+            det = a * c - b * b
+            inverse, inverse_a = 1.0 / det, 1.0 / a
+            pair = (rid == j) | (rid == j + 1)
+            left, right = jnp.where(pair, 0.0, left), jnp.where(pair, 0.0, right)
+            first, second = (left * c - right * b) * inverse, (right * a - left * b) * inverse
+            for m in range(j + 2, 8):
+                columns[m] = columns[m] - (first * sublanes(columns[m], j) + second * sublanes(columns[m], j + 1))
+            full = full - (first * sublanes(full, j) + second * sublanes(full, j + 1))
+            below = rid > j + 1
+            first = jnp.where(below, first, jnp.where(rid == j + 1, b * inverse_a, 0.0))
+            second = jnp.where(below, second, 0.0)
+            forward = forward - (first * sublanes(forward, j) + second * sublanes(forward, j + 1))
+            scale = jnp.where(rid == j, lax.rsqrt(a), jnp.where(rid == j + 1, lax.rsqrt(det * inverse_a), scale))
+            inverses.append((a * inverse, b * inverse, c * inverse))
+        done.append(jnp.where(cid <= rid + base, forward * scale, 0.0))
+        if k + 1 == n:
+            break
+        spread = []
+        for j, (a, b, c) in enumerate(inverses):
+            above, under = sublanes(full, 2 * j), sublanes(full, 2 * j + 1)
+            spread += [above * c - under * b, under * a - above * b]
+        terms = [lanes(rows[k + 1], base + j) * spread[j] for j in range(8)]
+        while len(terms) > 1:
+            terms = [terms[q] + terms[q + 1] for q in range(0, len(terms), 2)]
+        rows[k + 1] = jnp.where(inside, 0.0, rows[k + 1]) - terms[0]
+        if k + 2 == n:
+            continue
+        solved = jnp.zeros((8, width), F32)
         for j in range(8):
-            pivot = sublanes(columns[j], j)
-            inverse = 1.0 / pivot
-            root_scale = jnp.where(rid == j, lax.rsqrt(pivot), root_scale)
-            scale = jnp.where(rid == j, inverse, scale)
-            ratio = columns[j] * inverse
-            ratio_all = jnp.where(rid == j, 0.0, ratio)
-            ratio_below = jnp.where(rid > j, ratio, 0.0)
-            for m in range(j + 1, 8):
-                columns[m] = columns[m] - ratio_all * sublanes(columns[m], j)
-            full = full - ratio_all * sublanes(full, j)
-            forward = forward - ratio_below * sublanes(forward, j)
-        done.append(jnp.where(cid <= rid + base, forward * root_scale, 0.0))
-        full = full * scale
-        if k + 1 < n:
-            spread = [sublanes(full, j) for j in range(8)]
-            for i in range(k + 1, n):
-                terms = [lanes(rows[i], base + j) * spread[j] for j in range(8)]
-                while len(terms) > 1:
-                    terms = [terms[q] + terms[q + 1] for q in range(0, len(terms), 2)]
-                rows[i] = jnp.where(inside, 0.0, rows[i]) - terms[0]
+            solved = jnp.where(rid == j, spread[j], solved)
+        far = jnp.concatenate(rows[k + 2 :], axis=0)
+        column = lax.broadcasted_iota(jnp.int32, far.shape, 1)
+        within = (column >= base) & (column < base + 8)
+        placed = []
+        for third in thirds(solved):
+            blocks = [jnp.zeros((base, width), F32)] if base else []
+            blocks += [third.astype(F32), jnp.zeros((width - base - 8, width), F32)]
+            placed.append(jnp.concatenate(blocks, axis=0).astype(BF16))
+        update = product_of_thirds(thirds(jnp.where(within, far, 0.0)), placed)
+        far = jnp.where(within, 0.0, far) - update
+        for i in range(k + 2, n):
+            rows[i] = far[8 * (i - k - 2) : 8 * (i - k - 1)]
     return done
 
 
@@ -193,7 +241,7 @@
 
 def finish_kernel(
     rounds, nblock, root, chunks, scale_ref, z_ref, lead_ref, kept_ref, recv_ref, same_ref, other_ref, across_ref,
-    coef_ref, out_ref, cross, held, sems,
+    coef_ref, out_ref, cross, coef, held, sems,
 ):
     group = lax.axis_index("cols")
     odd = group % 2 == 1
@@ -210,11 +258,14 @@
         cross[at, width:] = jnp.where(odd, theirs, mine)
     inverse = jnp.where(odd, kept_ref[:width, :], recv_ref[:width, :])
     across = inverse.T
-    raw = jnp.dot(inverse, cross[...], precision=HIGH, preferred_element_type=F32)
-    weights = jnp.dot(across, raw, precision=HIGH, preferred_element_type=F32)
+    raw = product(inverse, cross[...])
+    for r in range(rounds):
+        coef[pl.ds(r, width, stride=rounds), :] = raw[:, r * width : (r + 1) * width] * (1.0 / root)
+    copies = [pltpu.make_async_copy(coef, coef_ref, sems.at[chunks])]
+    copies[0].start()
+    weights = product(across, raw)
     stacked = []
     for r in range(rounds):
-        coef_ref[pl.ds(r, width, stride=rounds), :] = raw[:, r * width : (r + 1) * width] * (1.0 / root)
         weight = weights[:, r * width : (r + 1) * width]
         if r == 0:
             weight = jnp.where(group == 0, -root * across, weight)
@@ -223,18 +274,13 @@
     weight = jnp.concatenate(stacked, axis=0)
     span = z_ref.shape[0] // chunks
     row = lax.broadcasted_iota(jnp.int32, (span, width), 0) % rounds
-    copies = []
     for c in range(chunks):
         block = c * nblock // chunks
         at = slice(c * span, (c + 1) * span)
         acc = jnp.dot(lead_ref[at, :], weight, preferred_element_type=F32)
         acc = (acc[:, :width] + acc[:, width:]) * scale_ref[block, 0, 0]
-        factor = jnp.zeros((span, width), F32)
-        for r in range(rounds):
-            own = scale_ref[block, group, r]
-            if r == 0:
-                own = jnp.where(group == 0, 0.0, own)
-            factor = jnp.where(row == r, own, factor)
+        first = jnp.where(group == 0, 0.0, scale_ref[block, group, 0])
+        factor = jnp.where(row == 0, first, scale_ref[block, group, 1])
         held[at, :] = (z_ref[at, :].astype(F32) * factor - acc).astype(BF16)
         copies.append(pltpu.make_async_copy(held.at[at, :], out_ref.at[at, :], sems.at[c]))
         copies[-1].start()
@@ -315,11 +361,12 @@
             jax.ShapeDtypeStruct((long, width), BF16),
         ],
         in_specs=[SMEM] + [VMEM] * 7,
-        out_specs=[VMEM, pl.BlockSpec(memory_space=pl.ANY)],
+        out_specs=[pl.BlockSpec(memory_space=pl.ANY)] * 2,
         scratch_shapes=[
             pltpu.VMEM((width, rounds * width), F32),
+            pltpu.VMEM((width * rounds, width), F32),
             pltpu.VMEM((long, width), BF16),
-            pltpu.SemaphoreType.DMA((chunks,)),
+            pltpu.SemaphoreType.DMA((chunks + 1,)),
         ],
         compiler_params=params,
         name="finish",

time: 31.1 us -> 30 us (0.965)
  starting transfers between devices: 14.1 us -> 12.7 us
  waiting for transfers between devices: 10.2 us -> 11.2 us
  Pallas kernels: 4.77 us -> 3.93 us
    ppermute x10, starting transfers between devices: 14.1 us -> 12.7 us  [partner(): return lax.ppermute(x, axis, [(i, i ^ offset) for i in range(count)])]
    ppermute x10, waiting for transfers between devices: 10.2 us -> 11.2 us  [partner(): return lax.ppermute(x, axis, [(i, i ^ offset) for i in range(count)])]
    pallas_call x1, Pallas kernels: 3.11 us -> 2.27 us  [shards(): pl.pallas_call(functools.partial(finish_kernel, rounds, nblock, root, chu...]
where the time goes in v6:
time: 30 us; the launch traced here: 29.8 us
  starting transfers between devices  12.7 us (42%)
  waiting for transfers between devices  11.2 us (37%)
  Pallas kernels  3.93 us (13%)
  local copies, waits for them, and re-layouts  1.2 us (4%)
  between operations  0.67 us (2%)
    ppermute x10, starting transfers between devices, partner(): return lax.ppermute(x, axis, [(i, i ^ offset) for i in range(count)])  12.7 us
    ppermute x10, waiting for transfers between devices, partner(): return lax.ppermute(x, axis, [(i, i ^ offset) for i in range(count)])  11.2 us
    pallas_call x1, Pallas kernels, shards(): pl.pallas_call(functools.partial(finish_kernel, rounds, nblock, root, chu...  2.27 us
    unnamed x6, local copies, waits for them, and re-layouts  1.2 us
    pallas_call x1, Pallas kernels, shards(): pl.pallas_call(functools.partial(products_kernel, rounds, nblock), out_sh...  1 us
  transfers between devices with their start and end apart: 10, of which 8 were waited for; matrix products, arithmetic and copies ran while one was open for 0% of the time, Pallas kernels for 2%

profile of v6, /device:TPU:0, one launch (start us, length us, event | category | flops | bytes accessed | tf_op | source)
XLA Modules:
  0.0 29.8 jit_solution(6223021632049108024)
XLA Ops:
  0.6 0.5 %collective-permute-start = (bf16[2048,128]{1,0:T(8,128)(2,1)}, bf16[2048,128]{1,0:T(8,128)(2,1)S(1)}, u32[]{:S(2)}, u32[]{:S(2)}) collective-permute-start(bf16[2048,128]{1,0:T(8,128)(2,1)} %bitcast.7), channel_id=1, source_target_pairs={{0,1},{1,0},{2,3},{3,2},{4,5},{5,4},{6,7},{7,6},{8,9},{9,8},{10,11... | collective-permute-start | bytes 1572872 | tf_op jit(solution)/shard_map/ppermute | solution.py:18
  1.1 1.0 %copy-done = bf16[1024,1,2,128]{3,2,1,0:T(2,128)(2,1)S(1)} copy-done((bf16[1024,1,2,128]{3,2,1,0:T(2,128)(2,1)S(1)}, bf16[1024,1,2,128]{3,2,1,0:T(2,128)(2,1)}, u32[]{:S(2)}) %copy-start) | copy-done | bytes 524312
  2.2 0.2 split.1
  2.4 0.5 %collective-permute-done.recv_ref.odd_ref = bf16[2048,128]{1,0:T(8,128)(2,1)S(1)} collective-permute-done((bf16[2048,128]{1,0:T(8,128)(2,1)}, bf16[2048,128]{1,0:T(8,128)(2,1)S(1)}, u32[]{:S(2)}, u32[]{:S(2)}) %collective-permute-start) | collective-permute-done | bytes 524320 | tf_op jit(solution)/shard_map/ppermute | solution.py:18
  2.9 0.2 copy-done.2
  3.1 1.0 %products.1 = (f32[136,128]{1,0:T(8,128)S(1)}, f32[136,128]{1,0:T(8,128)S(1)}) custom-call(f32[2,2,2]{2,1,0:T(2,128)S(1)} %copy-done.2, bf16[1024,128]{1,0:T(8,128)(2,1)S(1)} %get-tuple-element.12.first_ref, bf16[1024,128]{1,0:T(8,128)(2,1)S(1)} %get-tuple-element.13.own_ref, bf16[2048,128]{1,0:T(8,128)(2,1)S(1)} %collective-permute-done.recv_ref.odd_ref), custom_call_target="tpu_custom_call" | custom-call | tf_op jit(solution)/shard_map/products/pallas_call | solution.py:315
  4.1 2.8 %collective-permute-start.2 = (f32[136,128]{1,0:T(8,128)S(1)}, f32[136,128]{1,0:T(8,128)S(1)}, u32[]{:S(2)}, u32[]{:S(2)}) collective-permute-start(f32[136,128]{1,0:T(8,128)S(1)} %get-tuple-element.14), channel_id=1, source_target_pairs={{0,4},{2,6},{4,0},{6,2},{8,12},{10,14},{12,8},{14,10},{16,20},{18,... | collective-permute-start | bytes 208904 | tf_op jit(solution)/shard_map/ppermute | solution.py:18
  6.9 1.4 %collective-permute-start.3 = (f32[136,128]{1,0:T(8,128)S(1)}, f32[136,128]{1,0:T(8,128)S(1)}, u32[]{:S(2)}, u32[]{:S(2)}) collective-permute-start(f32[136,128]{1,0:T(8,128)S(1)} %get-tuple-element.15), channel_id=1, source_target_pairs={{0,6},{2,4},{4,2},{6,0},{8,14},{10,12},{12,10},{14,8},{16,22},{18,... | collective-permute-start | bytes 208904 | tf_op jit(solution)/shard_map/ppermute | solution.py:18
  8.3 0.1 collective-permute-start.1
  8.4 1.9 %collective-permute-done.2 = f32[136,128]{1,0:T(8,128)S(1)} collective-permute-done((f32[136,128]{1,0:T(8,128)S(1)}, f32[136,128]{1,0:T(8,128)S(1)}, u32[]{:S(2)}, u32[]{:S(2)}) %collective-permute-start.2) | collective-permute-done | bytes 69664 | tf_op jit(solution)/shard_map/ppermute | solution.py:18
  10.3 2.3 %collective-permute-done.3 = f32[136,128]{1,0:T(8,128)S(1)} collective-permute-done((f32[136,128]{1,0:T(8,128)S(1)}, f32[136,128]{1,0:T(8,128)S(1)}, u32[]{:S(2)}, u32[]{:S(2)}) %collective-permute-start.3) | collective-permute-done | bytes 69664 | tf_op jit(solution)/shard_map/ppermute | solution.py:18
  12.6 0.0 collective-permute-done.1
  12.6 3.7 %collective-permute-start.6 = (f32[136,128]{1,0:T(8,128)S(1)}, f32[136,128]{1,0:T(8,128)S(1)}, u32[]{:S(2)}, u32[]{:S(2)}) collective-permute-start(f32[136,128]{1,0:T(8,128)S(1)} %add_add_fusion.1), channel_id=1, source_target_pairs={{0,24},{2,26},{4,28},{6,30},{8,16},{10,18},{12,20},{14,22},{16,8},... | collective-permute-start | bytes 208904 | tf_op jit(solution)/shard_map/ppermute | solution.py:18
  16.3 0.8 %collective-permute-start.4 = (f32[136,128]{1,0:T(8,128)S(1)}, f32[136,128]{1,0:T(8,128)S(1)}, u32[]{:S(2)}, u32[]{:S(2)}) collective-permute-start(f32[136,128]{1,0:T(8,128)S(1)} %add_add_fusion.1), channel_id=1, source_target_pairs={{0,8},{2,10},{4,12},{6,14},{8,0},{10,2},{12,4},{14,6},{16,24},{18,... | collective-permute-start | bytes 208904 | tf_op jit(solution)/shard_map/ppermute | solution.py:18
  17.1 0.5 %spread.1.lead_ref = bf16[2048,256]{1,0:T(8,128)(2,1)S(1)} custom-call(bf16[2048,128]{1,0:T(8,128)(2,1)S(1)} %bitcast.9, bf16[2048,128]{1,0:T(8,128)(2,1)S(1)} %collective-permute-done.recv_ref.odd_ref), custom_call_target="tpu_custom_call" | custom-call | tf_op jit(solution)/shard_map/spread/pallas_call | solution.py:330
  17.6 1.9 %collective-permute-done.6 = f32[136,128]{1,0:T(8,128)S(1)} collective-permute-done((f32[136,128]{1,0:T(8,128)S(1)}, f32[136,128]{1,0:T(8,128)S(1)}, u32[]{:S(2)}, u32[]{:S(2)}) %collective-permute-start.6) | collective-permute-done | bytes 69664 | tf_op jit(solution)/shard_map/ppermute | solution.py:18
  19.5 2.3 %collective-permute-done.5 = f32[136,128]{1,0:T(8,128)S(1)} collective-permute-done((f32[136,128]{1,0:T(8,128)S(1)}, f32[136,128]{1,0:T(8,128)S(1)}, u32[]{:S(2)}, u32[]{:S(2)}) %collective-permute-start.5) | collective-permute-done | bytes 69664 | tf_op jit(solution)/shard_map/ppermute | solution.py:18
  21.8 0.1 collective-permute-done.4
  21.9 1.4 %collective-permute-start.8 = (f32[136,128]{1,0:T(8,128)S(1)}, f32[136,128]{1,0:T(8,128)S(1)}, u32[]{:S(2)}, u32[]{:S(2)}) collective-permute-start(f32[136,128]{1,0:T(8,128)S(1)} %add_add_fusion.sums_ref.same_ref), channel_id=1, source_target_pairs={{0,2},{2,0},{4,6},{6,4},{8,10},{10,8},{12,14},{14,12},{16,18},{18,... | collective-permute-start | bytes 208904 | tf_op jit(solution)/shard_map/ppermute | solution.py:18
  23.3 1.9 %collective-permute-start.7 = (f32[256,128]{1,0:T(8,128)S(1)}, f32[256,128]{1,0:T(8,128)S(1)}, u32[]{:S(2)}, u32[]{:S(2)}) collective-permute-start(f32[256,128]{1,0:T(8,128)S(1)} %factor.1.kept_ref), channel_id=1, source_target_pairs={{0,1},{1,0},{2,3},{3,2},{4,5},{5,4},{6,7},{7,6},{8,9},{9,8},{10,11... | collective-permute-start | bytes 393224 | tf_op jit(solution)/shard_map/ppermute | solution.py:18
  25.3 1.0 %collective-permute-done.8.other_ref = f32[136,128]{1,0:T(8,128)S(1)} collective-permute-done((f32[136,128]{1,0:T(8,128)S(1)}, f32[136,128]{1,0:T(8,128)S(1)}, u32[]{:S(2)}, u32[]{:S(2)}) %collective-permute-start.8) | collective-permute-done | bytes 69664 | tf_op jit(solution)/shard_map/ppermute | solution.py:18
  26.3 0.0 collective-permute-done.7.recv_ref
  26.3 1.2 %collective-permute-done.9.across_ref = f32[136,128]{1,0:T(8,128)S(1)} collective-permute-done((f32[136,128]{1,0:T(8,128)S(1)}, f32[136,128]{1,0:T(8,128)S(1)}, u32[]{:S(2)}, u32[]{:S(2)}) %collective-permute-start.9) | collective-permute-done | bytes 69664 | tf_op jit(solution)/shard_map/ppermute | solution.py:18
  27.5 2.3 %finish.1 = (f32[256,128]{1,0:T(8,128)}, bf16[2048,128]{1,0:T(8,128)(2,1)}) custom-call(f32[2,2,2]{2,1,0:T(2,128)S(1)} %copy-done.2, bf16[2048,128]{1,0:T(8,128)(2,1)S(1)} %bitcast.10, bf16[2048,256]{1,0:T(8,128)(2,1)S(1)} %spread.1.lead_ref, f32[256,128]{1,0:T(8,128)S(1)} %factor.1.kept_ref, f32[256,128]{1,0:T(8,128)S(1)} %collective-permute-done.7.recv_ref, ...), custom_call_target="tpu_custom_call" | custom-call | tf_op jit(solution)/shard_map/finish/pallas_call | solution.py:357
  (9 shorter events, 0.1 us)
Async XLA Ops:
  0.6 2.3 %collective-permute-start = (bf16[2048,128]{1,0:T(8,128)(2,1)}, bf16[2048,128]{1,0:T(8,128)(2,1)S(1)}, u32[]{:S(2)}, u32[]{:S(2)}) collective-permute-start(bf16[2048,128]{1,0:T(8,128)(2,1)} %bitcast.7), channel_id=1, source_target_pairs={{0,1},{1,0},{2,3},{3,2},{4,5},{5,4},{6,7},{7,6},{8,9},{9,8},{10,11... | collective-permute-start | bytes 1572872 | tf_op jit(solution)/shard_map/ppermute | solution.py:18
  1.1 1.0 %copy-start = (bf16[1024,1,2,128]{3,2,1,0:T(2,128)(2,1)S(1)}, bf16[1024,1,2,128]{3,2,1,0:T(2,128)(2,1)}, u32[]{:S(2)}) copy-start(bf16[1024,1,2,128]{3,2,1,0:T(2,128)(2,1)} %param.2) | copy-start | bytes 1572868
  2.4 0.7 %copy-start.2 = (f32[2,2,2]{2,1,0:T(2,128)S(1)}, f32[2,2,2]{2,1,0:T(2,128)}, u32[]{:S(2)}) copy-start(f32[2,2,2]{2,1,0:T(2,128)} %scale_ref.3) | copy-start | bytes 100
  3.1 14.0 %copy-start.1 = (bf16[1024,1,2,128]{3,2,1,0:T(2,128)(2,1)S(1)}, bf16[1024,1,2,128]{3,2,1,0:T(2,128)(2,1)}, u32[]{:S(2)}) copy-start(bf16[1024,1,2,128]{3,2,1,0:T(2,128)(2,1)} %param.2) | copy-start | bytes 1572868
  4.1 6.2 %collective-permute-start.2 = (f32[136,128]{1,0:T(8,128)S(1)}, f32[136,128]{1,0:T(8,128)S(1)}, u32[]{:S(2)}, u32[]{:S(2)}) collective-permute-start(f32[136,128]{1,0:T(8,128)S(1)} %get-tuple-element.14), channel_id=1, source_target_pairs={{0,4},{2,6},{4,0},{6,2},{8,12},{10,14},{12,8},{14,10},{16,20},{18,... | collective-permute-start | bytes 208904 | tf_op jit(solution)/shard_map/ppermute | solution.py:18
  6.9 5.7 %collective-permute-start.3 = (f32[136,128]{1,0:T(8,128)S(1)}, f32[136,128]{1,0:T(8,128)S(1)}, u32[]{:S(2)}, u32[]{:S(2)}) collective-permute-start(f32[136,128]{1,0:T(8,128)S(1)} %get-tuple-element.15), channel_id=1, source_target_pairs={{0,6},{2,4},{4,2},{6,0},{8,14},{10,12},{12,10},{14,8},{16,22},{18,... | collective-permute-start | bytes 208904 | tf_op jit(solution)/shard_map/ppermute | solution.py:18
  8.3 4.3 %collective-permute-start.1 = (f32[136,128]{1,0:T(8,128)S(1)}, f32[136,128]{1,0:T(8,128)S(1)}, u32[]{:S(2)}, u32[]{:S(2)}) collective-permute-start(f32[136,128]{1,0:T(8,128)S(1)} %get-tuple-element.15), channel_id=1, source_target_pairs={{0,2},{2,0},{4,6},{6,4},{8,10},{10,8},{12,14},{14,12},{16,18},{18,... | collective-permute-start | bytes 208904 | tf_op jit(solution)/shard_map/ppermute | solution.py:18
  12.6 6.8 %collective-permute-start.6 = (f32[136,128]{1,0:T(8,128)S(1)}, f32[136,128]{1,0:T(8,128)S(1)}, u32[]{:S(2)}, u32[]{:S(2)}) collective-permute-start(f32[136,128]{1,0:T(8,128)S(1)} %add_add_fusion.1), channel_id=1, source_target_pairs={{0,24},{2,26},{4,28},{6,30},{8,16},{10,18},{12,20},{14,22},{16,8},... | collective-permute-start | bytes 208904 | tf_op jit(solution)/shard_map/ppermute | solution.py:18
  16.3 5.5 %collective-permute-start.5 = (f32[136,128]{1,0:T(8,128)S(1)}, f32[136,128]{1,0:T(8,128)S(1)}, u32[]{:S(2)}, u32[]{:S(2)}) collective-permute-start(f32[136,128]{1,0:T(8,128)S(1)} %add_add_fusion.1), channel_id=1, source_target_pairs={{0,16},{2,18},{4,20},{6,22},{8,24},{10,26},{12,28},{14,30},{16,0},... | collective-permute-start | bytes 208904 | tf_op jit(solution)/shard_map/ppermute | solution.py:18
  16.3 5.6 %collective-permute-start.4 = (f32[136,128]{1,0:T(8,128)S(1)}, f32[136,128]{1,0:T(8,128)S(1)}, u32[]{:S(2)}, u32[]{:S(2)}) collective-permute-start(f32[136,128]{1,0:T(8,128)S(1)} %add_add_fusion.1), channel_id=1, source_target_pairs={{0,8},{2,10},{4,12},{6,14},{8,0},{10,2},{12,4},{14,6},{16,24},{18,... | collective-permute-start | bytes 208904 | tf_op jit(solution)/shard_map/ppermute | solution.py:18
  21.9 4.4 %collective-permute-start.8 = (f32[136,128]{1,0:T(8,128)S(1)}, f32[136,128]{1,0:T(8,128)S(1)}, u32[]{:S(2)}, u32[]{:S(2)}) collective-permute-start(f32[136,128]{1,0:T(8,128)S(1)} %add_add_fusion.sums_ref.same_ref), channel_id=1, source_target_pairs={{0,2},{2,0},{4,6},{6,4},{8,10},{10,8},{12,14},{14,12},{16,18},{18,... | collective-permute-start | bytes 208904 | tf_op jit(solution)/shard_map/ppermute | solution.py:18
  23.3 2.9 %collective-permute-start.7 = (f32[256,128]{1,0:T(8,128)S(1)}, f32[256,128]{1,0:T(8,128)S(1)}, u32[]{:S(2)}, u32[]{:S(2)}) collective-permute-start(f32[256,128]{1,0:T(8,128)S(1)} %factor.1.kept_ref), channel_id=1, source_target_pairs={{0,1},{1,0},{2,3},{3,2},{4,5},{5,4},{6,7},{7,6},{8,9},{9,8},{10,11... | collective-permute-start | bytes 393224 | tf_op jit(solution)/shard_map/ppermute | solution.py:18
  26.3 1.3 %collective-permute-start.9 = (f32[136,128]{1,0:T(8,128)S(1)}, f32[136,128]{1,0:T(8,128)S(1)}, u32[]{:S(2)}, u32[]{:S(2)}) collective-permute-start(f32[136,128]{1,0:T(8,128)S(1)} %collective-permute-done.8.other_ref), channel_id=1, source_target_pairs={{0,1},{1,0},{2,3},{3,2},{4,5},{5,4},{6,7},{7,6},{8,9},{9,8},{10,11... | collective-permute-start | bytes 208904 | tf_op jit(solution)/shard_map/ppermute | solution.py:18

commit v7 on v6

--- a/solution.py
+++ b/solution.py
@@ -11,7 +11,6 @@
 F32 = jnp.float32
 BF16 = jnp.bfloat16
 VMEM = pl.BlockSpec(memory_space=pltpu.VMEM)
-SMEM = pl.BlockSpec(memory_space=pltpu.SMEM)
 
 
 def partner(x, axis, count, offset):
@@ -159,21 +158,37 @@
     return jnp.where(lax.axis_index("cols") % 2 == 0, even_ref[...], odd_ref[...])
 
 
-def split_kernel(rounds, z_ref, first_ref, own_ref, wide):
+def tall(tile, rows):
+    return jnp.broadcast_to(tile[None], (rows // 8, *tile.shape)).reshape(rows, tile.shape[1])
+
+
+def split_kernel(rounds, nblock, scale_ref, z_ref, first_ref, own_ref, factor_ref, wide):
+    group = lax.axis_index("cols")
+    odd = group % 2
+    width = z_ref.shape[1]
     points = z_ref.shape[0] // rounds
+    row = lax.broadcasted_iota(jnp.int32, (8, width), 0)
+    for b in range(nblock):
+        lead = jnp.broadcast_to(scale_ref[b, 0:1, 0:1], (8, width))
+        mine = scale_ref[b, pl.ds(group, 1), :]
+        theirs = scale_ref[b, pl.ds(group + 1 - 2 * odd, 1), :]
+        mine, theirs = [[jnp.broadcast_to(x[:, r : r + 1], (8, width)) for r in range(2)] for x in (mine, theirs)]
+        factor_ref[4 * b] = lead * jnp.where(odd == 1, theirs[0], theirs[1])
+        factor_ref[4 * b + 1] = lead * jnp.where(odd == 1, mine[0], mine[1])
+        factor_ref[4 * b + 2] = lead
+        factor_ref[4 * b + 3] = jnp.where(row % rounds == 0, jnp.where(group == 0, 0.0, mine[0]), mine[1])
     wide[...] = z_ref[...].astype(F32)
     first = wide[pl.ds(0, points, stride=rounds), :].astype(BF16)
     last = wide[pl.ds(1, points, stride=rounds), :].astype(BF16)
     first_ref[...] = first
-    own_ref[...] = jnp.where(lax.axis_index("cols") % 2 == 1, first, last)
-
-
-def products_kernel(rounds, nblock, scale_ref, first_ref, own_ref, recv_ref, *rest):
+    own_ref[...] = jnp.where(odd == 1, first, last)
+
+
+def products_kernel(rounds, nblock, factor_ref, first_ref, own_ref, recv_ref, *rest):
     lead_ref = rest[:-4] if len(rest) == 4 else (*rest[:2], rest[-1])
     same_ref, other_ref, wide, cross = rest if len(rest) == 4 else rest[2:-1]
     group = lax.axis_index("cols")
     odd = group % 2
-    place_round = 1 - odd
     digit = lax.axis_index("rows") % 2
     width = recv_ref.shape[1]
     points = own_ref.shape[0] // nblock
@@ -186,9 +201,7 @@
     for b in range(nblock):
         at = slice(b * points, (b + 1) * points)
         start = b * points * rounds
-        near = wide[pl.ds(start, points, stride=rounds), :]
-        far = wide[pl.ds(start + 1, points, stride=rounds), :]
-        theirs = jnp.where(odd == 1, near, far).astype(BF16)
+        theirs = wide[pl.ds(start + 1 - odd, points, stride=rounds), :].astype(BF16)
         if lead_ref:
             panel = lead_ref[2][pl.ds(start, points, stride=rounds), :].astype(BF16)
         else:
@@ -196,9 +209,8 @@
         block = lax.dot_general(
             panel, jnp.concatenate([theirs, own_ref[at, :]], axis=1), (((0,), (0,)), ((), ())), preferred_element_type=F32
         )
-        first = scale_ref[b, 0, 0]
-        left = block[:, :width] * (first * scale_ref[b, group + 1 - 2 * odd, place_round])
-        right = block[:, width:] * (first * scale_ref[b, group, place_round])
+        left = block[:, :width] * tall(factor_ref[4 * b], width)
+        right = block[:, width:] * tall(factor_ref[4 * b + 1], width)
         out = out + jnp.concatenate([left, right], axis=1)
     packed = pack(out[:, :width])
     cross[:width, :] = out[:, :width]
@@ -240,7 +252,7 @@
 
 
 def finish_kernel(
-    rounds, nblock, root, chunks, scale_ref, z_ref, lead_ref, kept_ref, recv_ref, same_ref, other_ref, across_ref,
+    rounds, nblock, root, chunks, factor_ref, z_ref, lead_ref, kept_ref, recv_ref, same_ref, other_ref, across_ref,
     coef_ref, out_ref, cross, coef, held, sems,
 ):
     group = lax.axis_index("cols")
@@ -273,14 +285,12 @@
         stacked.append(jnp.concatenate([upper, (weight - upper.astype(F32)).astype(BF16)], axis=1))
     weight = jnp.concatenate(stacked, axis=0)
     span = z_ref.shape[0] // chunks
-    row = lax.broadcasted_iota(jnp.int32, (span, width), 0) % rounds
     for c in range(chunks):
         block = c * nblock // chunks
         at = slice(c * span, (c + 1) * span)
         acc = jnp.dot(lead_ref[at, :], weight, preferred_element_type=F32)
-        acc = (acc[:, :width] + acc[:, width:]) * scale_ref[block, 0, 0]
-        first = jnp.where(group == 0, 0.0, scale_ref[block, group, 0])
-        factor = jnp.where(row == 0, first, scale_ref[block, group, 1])
+        acc = (acc[:, :width] + acc[:, width:]) * tall(factor_ref[4 * block + 2], span)
+        factor = tall(factor_ref[4 * block + 3], span)
         held[at, :] = (z_ref[at, :].astype(F32) * factor - acc).astype(BF16)
         copies.append(pltpu.make_async_copy(held.at[at, :], out_ref.at[at, :], sems.at[c]))
         copies[-1].start()
@@ -302,26 +312,26 @@
     phases = radices(n_rows)
     payload = width + 8
     params = pltpu.CompilerParams(vmem_limit_bytes=48 << 20)
-    first, own = pl.pallas_call(
-        functools.partial(split_kernel, rounds),
-        out_shape=[jax.ShapeDtypeStruct((points, width), BF16)] * 2,
-        in_specs=[VMEM],
-        out_specs=[VMEM] * 2,
+    first, own, factors = pl.pallas_call(
+        functools.partial(split_kernel, rounds, nblock),
+        out_shape=[jax.ShapeDtypeStruct((points, width), BF16)] * 2 + [jax.ShapeDtypeStruct((4 * nblock, 8, width), F32)],
+        in_specs=[VMEM] * 2,
+        out_specs=[VMEM] * 3,
         scratch_shapes=[pltpu.VMEM((long, width), F32)],
         compiler_params=params,
         name="split",
-    )(z)
+    )(scales, z)
     extra = () if n_cols == 2 else leads
     sent = pl.pallas_call(
         functools.partial(products_kernel, rounds, nblock),
         out_shape=[jax.ShapeDtypeStruct((payload, width), F32)] * 2,
-        in_specs=[SMEM] + [VMEM] * (3 + len(extra)),
+        in_specs=[VMEM] * (4 + len(extra)),
         out_specs=[VMEM] * 2,
         scratch_shapes=[pltpu.VMEM((long, width), F32), pltpu.VMEM((2 * width, width), F32)]
         + [pltpu.VMEM((long, width), F32)] * (len(extra) // 2),
         compiler_params=params,
         name="products",
-    )(scales, first, own, recv, *extra)
+    )(factors, first, own, recv, *extra)
     sums = sent[0]
     for step, (hop, base) in enumerate(phases):
         source = sent if step == 0 else [sums] * 2
@@ -360,7 +370,7 @@
             jax.ShapeDtypeStruct((width * rounds, width), F32),
             jax.ShapeDtypeStruct((long, width), BF16),
         ],
-        in_specs=[SMEM] + [VMEM] * 7,
+        in_specs=[VMEM] * 8,
         out_specs=[pl.BlockSpec(memory_space=pl.ANY)] * 2,
         scratch_shapes=[
             pltpu.VMEM((width, rounds * width), F32),
@@ -370,7 +380,7 @@
         ],
         compiler_params=params,
         name="finish",
-    )(scales, z, lead, factored, swapped, sums, gathered, crossed)
+    )(factors, z, lead, factored, swapped, sums, gathered, crossed)
     return coef.reshape(width, 1, rounds, width), updated.reshape(snapshots.shape)
 
 

time: 30 us -> 28.9 us (0.963)
  Pallas kernels: 3.93 us -> 2.89 us
  waiting for transfers between devices: 11.2 us -> 10.6 us
  local copies, waits for them, and re-layouts: 1.2 us -> 1.73 us
    ppermute x10, waiting for transfers between devices: 11.2 us -> 10.6 us  [partner(): return lax.ppermute(x, axis, [(i, i ^ offset) for i in range(count)])]
    pallas_call x1, Pallas kernels: 2.27 us -> 1.69 us  [shards(): pl.pallas_call(functools.partial(finish_kernel, rounds, nblock, root, chu...]
    unnamed x6, local copies, waits for them, and re-layouts: 1.2 us -> 1.73 us
    pallas_call x1, Pallas kernels: 1 us -> 0.48 us  [shards(): pl.pallas_call(functools.partial(products_kernel, rounds, nblock), out_sh...]
  transfers between devices with their start and end apart: 10 -> 10, of which waited for: 8 -> 9; matrix products, arithmetic and copies ran while one was open for 0% -> 0% of each run, Pallas kernels for 2% -> 3%
where the time goes in v7:
time: 28.9 us; the launch traced here: 28.7 us
  starting transfers between devices  12.7 us (44%)
  waiting for transfers between devices  10.6 us (37%)
  Pallas kernels  2.89 us (10%)
  local copies, waits for them, and re-layouts  1.73 us (6%)
  between operations  0.68 us (2%)
    ppermute x10, starting transfers between devices, partner(): return lax.ppermute(x, axis, [(i, i ^ offset) for i in range(count)])  12.7 us
    ppermute x10, waiting for transfers between devices, partner(): return lax.ppermute(x, axis, [(i, i ^ offset) for i in range(count)])  10.6 us
    unnamed x6, local copies, waits for them, and re-layouts  1.73 us
    pallas_call x1, Pallas kernels, shards(): pl.pallas_call(functools.partial(finish_kernel, rounds, nblock, root, chu...  1.69 us
  transfers between devices with their start and end apart: 10, of which 9 were waited for; matrix products, arithmetic and copies ran while one was open for 0% of the time, Pallas kernels for 3%

profile of v7, /device:TPU:0, one launch (start us, length us, event | category | flops | bytes accessed | tf_op | source)
XLA Modules:
  0.0 28.7 jit_solution(9181134002978327685)
XLA Ops:
  0.6 0.5 %collective-permute-start = (bf16[2048,128]{1,0:T(8,128)(2,1)}, bf16[2048,128]{1,0:T(8,128)(2,1)S(1)}, u32[]{:S(2)}, u32[]{:S(2)}) collective-permute-start(bf16[2048,128]{1,0:T(8,128)(2,1)} %bitcast.7), channel_id=1, source_target_pairs={{0,1},{1,0},{2,3},{3,2},{4,5},{5,4},{6,7},{7,6},{8,9},{9,8},{10,11... | collective-permute-start | bytes 1572872 | tf_op jit(solution)/shard_map/ppermute | solution.py:17
  1.1 1.0 %copy-done = bf16[1024,1,2,128]{3,2,1,0:T(2,128)(2,1)S(1)} copy-done((bf16[1024,1,2,128]{3,2,1,0:T(2,128)(2,1)S(1)}, bf16[1024,1,2,128]{3,2,1,0:T(2,128)(2,1)}, u32[]{:S(2)}) %copy-start) | copy-done | bytes 524312
  2.2 0.7 %copy-done.2 = f32[2,2,2]{2,1,0:T(2,128)S(1)} copy-done((f32[2,2,2]{2,1,0:T(2,128)S(1)}, f32[2,2,2]{2,1,0:T(2,128)}, u32[]{:S(2)}) %copy-start.2) | copy-done | bytes 56
  2.9 0.2 split.1
  3.1 0.0 copy-start.1
  3.1 0.5 %products.1 = (f32[136,128]{1,0:T(8,128)S(1)}, f32[136,128]{1,0:T(8,128)S(1)}) custom-call(f32[8,8,128]{2,1,0:T(8,128)S(1)} %get-tuple-element.13.factor_ref, bf16[1024,128]{1,0:T(8,128)(2,1)S(1)} %get-tuple-element.14.first_ref, bf16[1024,128]{1,0:T(8,128)(2,1)S(1)} %get-tuple-element.15.own_ref, bf16[2048,128]{1,0:T(8,128)(2,1)S(1)} %collective-permute-done.recv_ref.odd_ref), custom_call_target="tpu_custom_call" | custom-call | tf_op jit(solution)/shard_map/products/pallas_call | solution.py:325
  3.6 2.7 %collective-permute-start.2 = (f32[136,128]{1,0:T(8,128)S(1)}, f32[136,128]{1,0:T(8,128)S(1)}, u32[]{:S(2)}, u32[]{:S(2)}) collective-permute-start(f32[136,128]{1,0:T(8,128)S(1)} %get-tuple-element.16), channel_id=1, source_target_pairs={{0,4},{2,6},{4,0},{6,2},{8,12},{10,14},{12,8},{14,10},{16,20},{18,... | collective-permute-start | bytes 208904 | tf_op jit(solution)/shard_map/ppermute | solution.py:17
  6.3 1.4 %collective-permute-start.3 = (f32[136,128]{1,0:T(8,128)S(1)}, f32[136,128]{1,0:T(8,128)S(1)}, u32[]{:S(2)}, u32[]{:S(2)}) collective-permute-start(f32[136,128]{1,0:T(8,128)S(1)} %get-tuple-element.17), channel_id=1, source_target_pairs={{0,6},{2,4},{4,2},{6,0},{8,14},{10,12},{12,10},{14,8},{16,22},{18,... | collective-permute-start | bytes 208904 | tf_op jit(solution)/shard_map/ppermute | solution.py:17
  7.8 0.1 collective-permute-start.1
  7.9 1.9 %collective-permute-done.2 = f32[136,128]{1,0:T(8,128)S(1)} collective-permute-done((f32[136,128]{1,0:T(8,128)S(1)}, f32[136,128]{1,0:T(8,128)S(1)}, u32[]{:S(2)}, u32[]{:S(2)}) %collective-permute-start.2) | collective-permute-done | bytes 69664 | tf_op jit(solution)/shard_map/ppermute | solution.py:17
  9.8 2.1 %collective-permute-done.3 = f32[136,128]{1,0:T(8,128)S(1)} collective-permute-done((f32[136,128]{1,0:T(8,128)S(1)}, f32[136,128]{1,0:T(8,128)S(1)}, u32[]{:S(2)}, u32[]{:S(2)}) %collective-permute-start.3) | collective-permute-done | bytes 69664 | tf_op jit(solution)/shard_map/ppermute | solution.py:17
  12.0 0.1 collective-permute-done.1
  12.1 3.7 %collective-permute-start.6 = (f32[136,128]{1,0:T(8,128)S(1)}, f32[136,128]{1,0:T(8,128)S(1)}, u32[]{:S(2)}, u32[]{:S(2)}) collective-permute-start(f32[136,128]{1,0:T(8,128)S(1)} %add_add_fusion.1), channel_id=1, source_target_pairs={{0,24},{2,26},{4,28},{6,30},{8,16},{10,18},{12,20},{14,22},{16,8},... | collective-permute-start | bytes 208904 | tf_op jit(solution)/shard_map/ppermute | solution.py:17
  15.8 0.8 %collective-permute-start.4 = (f32[136,128]{1,0:T(8,128)S(1)}, f32[136,128]{1,0:T(8,128)S(1)}, u32[]{:S(2)}, u32[]{:S(2)}) collective-permute-start(f32[136,128]{1,0:T(8,128)S(1)} %add_add_fusion.1), channel_id=1, source_target_pairs={{0,8},{2,10},{4,12},{6,14},{8,0},{10,2},{12,4},{14,6},{16,24},{18,... | collective-permute-start | bytes 208904 | tf_op jit(solution)/shard_map/ppermute | solution.py:17
  16.6 0.5 %spread.1.lead_ref = bf16[2048,256]{1,0:T(8,128)(2,1)S(1)} custom-call(bf16[2048,128]{1,0:T(8,128)(2,1)S(1)} %bitcast.9, bf16[2048,128]{1,0:T(8,128)(2,1)S(1)} %collective-permute-done.recv_ref.odd_ref), custom_call_target="tpu_custom_call" | custom-call | tf_op jit(solution)/shard_map/spread/pallas_call | solution.py:340
  17.1 1.9 %collective-permute-done.6 = f32[136,128]{1,0:T(8,128)S(1)} collective-permute-done((f32[136,128]{1,0:T(8,128)S(1)}, f32[136,128]{1,0:T(8,128)S(1)}, u32[]{:S(2)}, u32[]{:S(2)}) %collective-permute-start.6) | collective-permute-done | bytes 69664 | tf_op jit(solution)/shard_map/ppermute | solution.py:17
  19.0 2.3 %collective-permute-done.5 = f32[136,128]{1,0:T(8,128)S(1)} collective-permute-done((f32[136,128]{1,0:T(8,128)S(1)}, f32[136,128]{1,0:T(8,128)S(1)}, u32[]{:S(2)}, u32[]{:S(2)}) %collective-permute-start.5) | collective-permute-done | bytes 69664 | tf_op jit(solution)/shard_map/ppermute | solution.py:17
  21.3 0.1 collective-permute-done.4
  21.4 1.5 %collective-permute-start.8 = (f32[136,128]{1,0:T(8,128)S(1)}, f32[136,128]{1,0:T(8,128)S(1)}, u32[]{:S(2)}, u32[]{:S(2)}) collective-permute-start(f32[136,128]{1,0:T(8,128)S(1)} %add_add_fusion.sums_ref.same_ref), channel_id=1, source_target_pairs={{0,2},{2,0},{4,6},{6,4},{8,10},{10,8},{12,14},{14,12},{16,18},{18,... | collective-permute-start | bytes 208904 | tf_op jit(solution)/shard_map/ppermute | solution.py:17
  22.9 1.9 %collective-permute-start.7 = (f32[256,128]{1,0:T(8,128)S(1)}, f32[256,128]{1,0:T(8,128)S(1)}, u32[]{:S(2)}, u32[]{:S(2)}) collective-permute-start(f32[256,128]{1,0:T(8,128)S(1)} %factor.1.kept_ref), channel_id=1, source_target_pairs={{0,1},{1,0},{2,3},{3,2},{4,5},{5,4},{6,7},{7,6},{8,9},{9,8},{10,11... | collective-permute-start | bytes 393224 | tf_op jit(solution)/shard_map/ppermute | solution.py:17
  24.8 0.9 %collective-permute-done.8.other_ref = f32[136,128]{1,0:T(8,128)S(1)} collective-permute-done((f32[136,128]{1,0:T(8,128)S(1)}, f32[136,128]{1,0:T(8,128)S(1)}, u32[]{:S(2)}, u32[]{:S(2)}) %collective-permute-start.8) | collective-permute-done | bytes 69664 | tf_op jit(solution)/shard_map/ppermute | solution.py:17
  25.7 0.1 collective-permute-done.7.recv_ref
  25.8 1.2 %collective-permute-done.9.across_ref = f32[136,128]{1,0:T(8,128)S(1)} collective-permute-done((f32[136,128]{1,0:T(8,128)S(1)}, f32[136,128]{1,0:T(8,128)S(1)}, u32[]{:S(2)}, u32[]{:S(2)}) %collective-permute-start.9) | collective-permute-done | bytes 69664 | tf_op jit(solution)/shard_map/ppermute | solution.py:17
  27.0 1.7 %finish.1 = (f32[256,128]{1,0:T(8,128)}, bf16[2048,128]{1,0:T(8,128)(2,1)}) custom-call(f32[8,8,128]{2,1,0:T(8,128)S(1)} %get-tuple-element.13.factor_ref, bf16[2048,128]{1,0:T(8,128)(2,1)S(1)} %bitcast.10, bf16[2048,256]{1,0:T(8,128)(2,1)S(1)} %spread.1.lead_ref, f32[256,128]{1,0:T(8,128)S(1)} %factor.1.kept_ref, ...), custom_call_target="tpu_custom_call" | custom-call | tf_op jit(solution)/shard_map/finish/pallas_call | solution.py:367
  (9 shorter events, 0.1 us)
Async XLA Ops:
  0.6 2.5 %collective-permute-start = (bf16[2048,128]{1,0:T(8,128)(2,1)}, bf16[2048,128]{1,0:T(8,128)(2,1)S(1)}, u32[]{:S(2)}, u32[]{:S(2)}) collective-permute-start(bf16[2048,128]{1,0:T(8,128)(2,1)} %bitcast.7), channel_id=1, source_target_pairs={{0,1},{1,0},{2,3},{3,2},{4,5},{5,4},{6,7},{7,6},{8,9},{9,8},{10,11... | collective-permute-start | bytes 1572872 | tf_op jit(solution)/shard_map/ppermute | solution.py:17
  1.1 1.0 %copy-start = (bf16[1024,1,2,128]{3,2,1,0:T(2,128)(2,1)S(1)}, bf16[1024,1,2,128]{3,2,1,0:T(2,128)(2,1)}, u32[]{:S(2)}) copy-start(bf16[1024,1,2,128]{3,2,1,0:T(2,128)(2,1)} %param.2) | copy-start | bytes 1572868
  2.2 0.7 %copy-start.2 = (f32[2,2,2]{2,1,0:T(2,128)S(1)}, f32[2,2,2]{2,1,0:T(2,128)}, u32[]{:S(2)}) copy-start(f32[2,2,2]{2,1,0:T(2,128)} %scale_ref.1) | copy-start | bytes 100
  3.1 13.4 %copy-start.1 = (bf16[1024,1,2,128]{3,2,1,0:T(2,128)(2,1)S(1)}, bf16[1024,1,2,128]{3,2,1,0:T(2,128)(2,1)}, u32[]{:S(2)}) copy-start(bf16[1024,1,2,128]{3,2,1,0:T(2,128)(2,1)} %param.2) | copy-start | bytes 1572868
  3.6 6.2 %collective-permute-start.2 = (f32[136,128]{1,0:T(8,128)S(1)}, f32[136,128]{1,0:T(8,128)S(1)}, u32[]{:S(2)}, u32[]{:S(2)}) collective-permute-start(f32[136,128]{1,0:T(8,128)S(1)} %get-tuple-element.16), channel_id=1, source_target_pairs={{0,4},{2,6},{4,0},{6,2},{8,12},{10,14},{12,8},{14,10},{16,20},{18,... | collective-permute-start | bytes 208904 | tf_op jit(solution)/shard_map/ppermute | solution.py:17
  6.3 5.6 %collective-permute-start.3 = (f32[136,128]{1,0:T(8,128)S(1)}, f32[136,128]{1,0:T(8,128)S(1)}, u32[]{:S(2)}, u32[]{:S(2)}) collective-permute-start(f32[136,128]{1,0:T(8,128)S(1)} %get-tuple-element.17), channel_id=1, source_target_pairs={{0,6},{2,4},{4,2},{6,0},{8,14},{10,12},{12,10},{14,8},{16,22},{18,... | collective-permute-start | bytes 208904 | tf_op jit(solution)/shard_map/ppermute | solution.py:17
  7.8 4.3 %collective-permute-start.1 = (f32[136,128]{1,0:T(8,128)S(1)}, f32[136,128]{1,0:T(8,128)S(1)}, u32[]{:S(2)}, u32[]{:S(2)}) collective-permute-start(f32[136,128]{1,0:T(8,128)S(1)} %get-tuple-element.17), channel_id=1, source_target_pairs={{0,2},{2,0},{4,6},{6,4},{8,10},{10,8},{12,14},{14,12},{16,18},{18,... | collective-permute-start | bytes 208904 | tf_op jit(solution)/shard_map/ppermute | solution.py:17
  12.1 6.8 %collective-permute-start.6 = (f32[136,128]{1,0:T(8,128)S(1)}, f32[136,128]{1,0:T(8,128)S(1)}, u32[]{:S(2)}, u32[]{:S(2)}) collective-permute-start(f32[136,128]{1,0:T(8,128)S(1)} %add_add_fusion.1), channel_id=1, source_target_pairs={{0,24},{2,26},{4,28},{6,30},{8,16},{10,18},{12,20},{14,22},{16,8},... | collective-permute-start | bytes 208904 | tf_op jit(solution)/shard_map/ppermute | solution.py:17
  15.8 5.5 %collective-permute-start.5 = (f32[136,128]{1,0:T(8,128)S(1)}, f32[136,128]{1,0:T(8,128)S(1)}, u32[]{:S(2)}, u32[]{:S(2)}) collective-permute-start(f32[136,128]{1,0:T(8,128)S(1)} %add_add_fusion.1), channel_id=1, source_target_pairs={{0,16},{2,18},{4,20},{6,22},{8,24},{10,26},{12,28},{14,30},{16,0},... | collective-permute-start | bytes 208904 | tf_op jit(solution)/shard_map/ppermute | solution.py:17
  15.8 5.6 %collective-permute-start.4 = (f32[136,128]{1,0:T(8,128)S(1)}, f32[136,128]{1,0:T(8,128)S(1)}, u32[]{:S(2)}, u32[]{:S(2)}) collective-permute-start(f32[136,128]{1,0:T(8,128)S(1)} %add_add_fusion.1), channel_id=1, source_target_pairs={{0,8},{2,10},{4,12},{6,14},{8,0},{10,2},{12,4},{14,6},{16,24},{18,... | collective-permute-start | bytes 208904 | tf_op jit(solution)/shard_map/ppermute | solution.py:17
  21.4 4.4 %collective-permute-start.8 = (f32[136,128]{1,0:T(8,128)S(1)}, f32[136,128]{1,0:T(8,128)S(1)}, u32[]{:S(2)}, u32[]{:S(2)}) collective-permute-start(f32[136,128]{1,0:T(8,128)S(1)} %add_add_fusion.sums_ref.same_ref), channel_id=1, source_target_pairs={{0,2},{2,0},{4,6},{6,4},{8,10},{10,8},{12,14},{14,12},{16,18},{18,... | collective-permute-start | bytes 208904 | tf_op jit(solution)/shard_map/ppermute | solution.py:17
  22.9 2.9 %collective-permute-start.7 = (f32[256,128]{1,0:T(8,128)S(1)}, f32[256,128]{1,0:T(8,128)S(1)}, u32[]{:S(2)}, u32[]{:S(2)}) collective-permute-start(f32[256,128]{1,0:T(8,128)S(1)} %factor.1.kept_ref), channel_id=1, source_target_pairs={{0,1},{1,0},{2,3},{3,2},{4,5},{5,4},{6,7},{7,6},{8,9},{9,8},{10,11... | collective-permute-start | bytes 393224 | tf_op jit(solution)/shard_map/ppermute | solution.py:17
  25.7 1.3 %collective-permute-start.9 = (f32[136,128]{1,0:T(8,128)S(1)}, f32[136,128]{1,0:T(8,128)S(1)}, u32[]{:S(2)}, u32[]{:S(2)}) collective-permute-start(f32[136,128]{1,0:T(8,128)S(1)} %collective-permute-done.8.other_ref), channel_id=1, source_target_pairs={{0,1},{1,0},{2,3},{3,2},{4,5},{5,4},{6,7},{7,6},{8,9},{9,8},{10,11... | collective-permute-start | bytes 208904 | tf_op jit(solution)/shard_map/ppermute | solution.py:17

commit v8 on v7

--- a/solution.py
+++ b/solution.py
@@ -25,6 +25,25 @@
         found.append((stride, radix))
         stride *= radix
     return found
+
+
+def order(phases, parity):
+    if parity == 0 and len({radix for _, radix in phases}) == 1:
+        return phases[::-1]
+    return phases
+
+
+def hop(x, n_rows, n_cols, offset, turn=0):
+    pairs = []
+    for row in range(n_rows):
+        for col in range(n_cols):
+            pairs.append((row * n_cols + col, (row ^ offset(col % 2)) * n_cols + (col ^ turn)))
+    return lax.ppermute(x, ("rows", "cols"), pairs)
+
+
+def half_digit(phases, parity):
+    even, odd = [(lax.axis_index("rows") // order(phases, p)[0][0]) % 2 for p in range(2)]
+    return jnp.where(parity == 0, even, odd)
 
 
 def among_pairs(x, count, mine, root):
@@ -184,12 +203,12 @@
     own_ref[...] = jnp.where(odd == 1, first, last)
 
 
-def products_kernel(rounds, nblock, factor_ref, first_ref, own_ref, recv_ref, *rest):
+def products_kernel(rounds, nblock, phases, factor_ref, first_ref, own_ref, recv_ref, *rest):
     lead_ref = rest[:-4] if len(rest) == 4 else (*rest[:2], rest[-1])
     same_ref, other_ref, wide, cross = rest if len(rest) == 4 else rest[2:-1]
     group = lax.axis_index("cols")
     odd = group % 2
-    digit = lax.axis_index("rows") % 2
+    digit = half_digit(phases, odd)
     width = recv_ref.shape[1]
     points = own_ref.shape[0] // nblock
     half = width // 2
@@ -231,7 +250,7 @@
         out_ref[:, r * width : (r + 1) * width] = jnp.where(rows == r, moved, 0.0).astype(BF16)
 
 
-def factor_kernel(sums_ref, out_ref):
+def factor_kernel(sums_ref, inverse_ref, block_ref):
     width = sums_ref.shape[1]
     height = width // 2 + 8
     group = lax.axis_index("cols")
@@ -239,38 +258,37 @@
     @pl.when(group == 1)
     def _():
         gram = unpack(sums_ref[:height, :])
-        out_ref[width:, :] = gram
+        block_ref[...] = gram
         rows = [gram[8 * i : 8 * i + 8, :] for i in range(width // 8)]
         for i, row in enumerate(lower_inverse(rows, width)):
-            out_ref[8 * i : 8 * i + 8, :] = row
+            inverse_ref[8 * i : 8 * i + 8, :] = row
 
     @pl.when(group != 1)
     def _():
-        out_ref[:width, :] = jnp.zeros((width, width), F32)
-        out_ref[width : width + height, :] = sums_ref[:height, :]
-        out_ref[width + height :, :] = jnp.zeros((width - height, width), F32)
+        inverse_ref[...] = jnp.zeros((width, width), F32)
+        block_ref[:height, :] = sums_ref[:height, :]
+        block_ref[height:, :] = jnp.zeros((width - height, width), F32)
 
 
 def finish_kernel(
-    rounds, nblock, root, chunks, factor_ref, z_ref, lead_ref, kept_ref, recv_ref, same_ref, other_ref, across_ref,
-    coef_ref, out_ref, cross, coef, held, sems,
+    rounds, nblock, phases, root, chunks, factor_ref, z_ref, lead_ref, kept_ref, recv_ref, same_ref, gathered_ref, block_ref, across_ref,
+    coef_ref, out_ref, mine, theirs, coef, held, sems,
 ):
     group = lax.axis_index("cols")
     odd = group % 2 == 1
-    digit = lax.axis_index("rows") % 2
     width = z_ref.shape[1]
     half = width // 2
     height = half + 8
-    for place, own_ref, theirs in ((digit, same_ref, recv_ref[width : width + half, :]), (1 - digit, other_ref, across_ref[:half, :])):
-        at = pl.ds(pl.multiple_of(place * half, half), half)
-        gram = recv_ref[pl.ds(pl.multiple_of(width + place * half, half), half), :]
-        mine = own_ref[height:, :]
-        theirs = jnp.where(group == 0, gram, theirs)
-        cross[at, :width] = jnp.where(odd, mine, theirs)
-        cross[at, width:] = jnp.where(odd, theirs, mine)
-    inverse = jnp.where(odd, kept_ref[:width, :], recv_ref[:width, :])
+    own_digit, pair_digit = half_digit(phases, group % 2), half_digit(phases, 1 - group % 2)
+    for own_rows, pair_rows, other in ((same_ref[height:, :], block_ref[:half, :], 0), (gathered_ref[height:, :], across_ref[:half, :], 1)):
+        mine[pl.ds(pl.multiple_of((own_digit ^ other) * half, half), half), :] = own_rows
+        theirs[pl.ds(pl.multiple_of((pair_digit ^ other) * half, half), half), :] = pair_rows
+    own_block = mine[...]
+    pair_block = jnp.where(group == 0, block_ref[...], theirs[...])
+    cross = jnp.concatenate([jnp.where(odd, own_block, pair_block), jnp.where(odd, pair_block, own_block)], axis=1)
+    inverse = jnp.where(odd, kept_ref[...], recv_ref[...])
     across = inverse.T
-    raw = product(inverse, cross[...])
+    raw = product(inverse, cross)
     for r in range(rounds):
         coef[pl.ds(r, width, stride=rounds), :] = raw[:, r * width : (r + 1) * width] * (1.0 / root)
     copies = [pltpu.make_async_copy(coef, coef_ref, sems.at[chunks])]
@@ -323,7 +341,7 @@
     )(scales, z)
     extra = () if n_cols == 2 else leads
     sent = pl.pallas_call(
-        functools.partial(products_kernel, rounds, nblock),
+        functools.partial(products_kernel, rounds, nblock, phases),
         out_shape=[jax.ShapeDtypeStruct((payload, width), F32)] * 2,
         in_specs=[VMEM] * (4 + len(extra)),
         out_specs=[VMEM] * 2,
@@ -333,9 +351,11 @@
         name="products",
     )(factors, first, own, recv, *extra)
     sums = sent[0]
-    for step, (hop, base) in enumerate(phases):
+    for step, (_, base) in enumerate(phases):
         source = sent if step == 0 else [sums] * 2
-        others = [partner(source[b % 2], "rows", n_rows, b * hop) for b in range(1, base)]
+        others = [
+            hop(source[b % 2], n_rows, n_cols, lambda parity: b * order(phases, parity)[step][0]) for b in range(1, base)
+        ]
         if step == len(phases) - 1:
             lead = pl.pallas_call(
                 functools.partial(spread_kernel, rounds),
@@ -348,39 +368,41 @@
             *others, lead = lax.optimization_barrier((*others, lead))
         for other in others:
             sums = sums + other
-    gathered = partner(sums, "rows", n_rows, 1)
-    factored = pl.pallas_call(
+    height = width // 2 + 8
+    beside = lambda parity: order(phases, parity)[0][0]
+    gathered = hop(sums, n_rows, n_cols, beside)
+    inverse, block = pl.pallas_call(
         factor_kernel,
-        out_shape=jax.ShapeDtypeStruct((2 * width, width), F32),
+        out_shape=[jax.ShapeDtypeStruct((width, width), F32)] * 2,
         in_specs=[VMEM],
-        out_specs=VMEM,
+        out_specs=[VMEM] * 2,
         compiler_params=params,
         cost_estimate=pl.CostEstimate(flops=1 << 30, bytes_accessed=1 << 23, transcendentals=0),
         name="factor",
     )(sums)
-    if n_cols > 2:
-        shared = among_pairs(factored[:width], n_cols, group, 1)
-        factored = jnp.concatenate([shared, factored[width:]], axis=0)
-    crossed = partner(gathered, "cols", n_cols, 1)
-    swapped = partner(factored, "cols", n_cols, 1)
+    inverse = among_pairs(inverse, n_cols, group, 1)
+    swapped = partner(inverse, "cols", n_cols, 1)
+    blocks = partner(block, "cols", n_cols, 1)
+    crossed = hop(block[:height], n_rows, n_cols, beside, 1)
     chunks = 2 * nblock
     coef, updated = pl.pallas_call(
-        functools.partial(finish_kernel, rounds, nblock, root, chunks),
+        functools.partial(finish_kernel, rounds, nblock, phases, root, chunks),
         out_shape=[
             jax.ShapeDtypeStruct((width * rounds, width), F32),
             jax.ShapeDtypeStruct((long, width), BF16),
         ],
-        in_specs=[VMEM] * 8,
+        in_specs=[VMEM] * 9,
         out_specs=[pl.BlockSpec(memory_space=pl.ANY)] * 2,
         scratch_shapes=[
-            pltpu.VMEM((width, rounds * width), F32),
+            pltpu.VMEM((width, width), F32),
+            pltpu.VMEM((width, width), F32),
             pltpu.VMEM((width * rounds, width), F32),
             pltpu.VMEM((long, width), BF16),
             pltpu.SemaphoreType.DMA((chunks + 1,)),
         ],
         compiler_params=params,
         name="finish",
-    )(factors, z, lead, factored, swapped, sums, gathered, crossed)
+    )(factors, z, lead, inverse, swapped, sums, gathered, blocks, crossed)
     return coef.reshape(width, 1, rounds, width), updated.reshape(snapshots.shape)
 
 

time: 28.9 us -> 28.6 us (0.990)
  starting transfers between devices: 12.7 us -> 12.4 us
    ppermute x10 -> x3, waiting for transfers between devices: 10.6 us -> 0.01 us  [partner(): return lax.ppermute(x, axis, [(i, i ^ offset) for i in range(count)])]
    ppermute x0 -> x8, waiting for transfers between devices: none -> 10.6 us  [hop(): return lax.ppermute(x, ('rows', 'cols'), pairs)]
    ppermute x10 -> x3, starting transfers between devices: 12.7 us -> 2.55 us  [partner(): return lax.ppermute(x, axis, [(i, i ^ offset) for i in range(count)])]
    ppermute x0 -> x8, starting transfers between devices: none -> 9.89 us  [hop(): return lax.ppermute(x, ('rows', 'cols'), pairs)]
  transfers between devices with their start and end apart: 10 -> 11, of which waited for: 9 -> 7; matrix products, arithmetic and copies ran while one was open for 0% -> 0% of each run, Pallas kernels for 3% -> 3%
where the time goes in v8:
time: 28.6 us; the launch traced here: 28.4 us
  starting transfers between devices  12.4 us (43%)
  waiting for transfers between devices  10.6 us (37%)
  Pallas kernels  2.91 us (10%)
  local copies, waits for them, and re-layouts  1.73 us (6%)
  between operations  0.7 us (2%)
    ppermute x8, waiting for transfers between devices, hop(): return lax.ppermute(x, ('rows', 'cols'), pairs)  10.6 us
    ppermute x8, starting transfers between devices, hop(): return lax.ppermute(x, ('rows', 'cols'), pairs)  9.89 us
    ppermute x3, starting transfers between devices, partner(): return lax.ppermute(x, axis, [(i, i ^ offset) for i in range(count)])  2.55 us
    unnamed x6, local copies, waits for them, and re-layouts  1.73 us
    pallas_call x1, Pallas kernels, shards(): pl.pallas_call(functools.partial(finish_kernel, rounds, nblock, phases, r...  1.7 us
  transfers between devices with their start and end apart: 11, of which 7 were waited for; matrix products, arithmetic and copies ran while one was open for 0% of the time, Pallas kernels for 3%

profile of v8, /device:TPU:0, one launch (start us, length us, event | category | flops | bytes accessed | tf_op | source)
XLA Modules:
  0.0 28.4 jit_solution(12559748239046191862)
XLA Ops:
  0.6 0.5 %collective-permute-start = (bf16[2048,128]{1,0:T(8,128)(2,1)}, bf16[2048,128]{1,0:T(8,128)(2,1)S(1)}, u32[]{:S(2)}, u32[]{:S(2)}) collective-permute-start(bf16[2048,128]{1,0:T(8,128)(2,1)} %bitcast.7), channel_id=1, source_target_pairs={{0,1},{1,0},{2,3},{3,2},{4,5},{5,4},{6,7},{7,6},{8,9},{9,8},{10,11... | collective-permute-start | bytes 1572872 | tf_op jit(solution)/shard_map/ppermute | solution.py:17
  1.1 1.0 %copy-done = bf16[1024,1,2,128]{3,2,1,0:T(2,128)(2,1)S(1)} copy-done((bf16[1024,1,2,128]{3,2,1,0:T(2,128)(2,1)S(1)}, bf16[1024,1,2,128]{3,2,1,0:T(2,128)(2,1)}, u32[]{:S(2)}) %copy-start) | copy-done | bytes 524312
  2.2 0.7 %copy-done.2 = f32[2,2,2]{2,1,0:T(2,128)S(1)} copy-done((f32[2,2,2]{2,1,0:T(2,128)S(1)}, f32[2,2,2]{2,1,0:T(2,128)}, u32[]{:S(2)}) %copy-start.2) | copy-done | bytes 56
  2.9 0.2 split.1
  3.1 0.5 %products.1 = (f32[136,128]{1,0:T(8,128)S(1)}, f32[136,128]{1,0:T(8,128)S(1)}) custom-call(f32[8,8,128]{2,1,0:T(8,128)S(1)} %get-tuple-element.15.factor_ref, bf16[1024,128]{1,0:T(8,128)(2,1)S(1)} %get-tuple-element.16.first_ref, bf16[1024,128]{1,0:T(8,128)(2,1)S(1)} %get-tuple-element.17.own_ref, bf16[2048,128]{1,0:T(8,128)(2,1)S(1)} %collective-permute-done.recv_ref.odd_ref), custom_call_target="tpu_custom_call" | custom-call | tf_op jit(solution)/shard_map/products/pallas_call | solution.py:343
  3.6 3.8 %collective-permute-start.2 = (f32[136,128]{1,0:T(8,128)S(1)}, f32[136,128]{1,0:T(8,128)S(1)}, u32[]{:S(2)}, u32[]{:S(2)}) collective-permute-start(f32[136,128]{1,0:T(8,128)S(1)} %get-tuple-element.18), channel_id=1, source_target_pairs={{0,16},{1,5},{2,18},{3,7},{4,20},{5,1},{6,22},{7,3},{8,24},{9,13},... | collective-permute-start | bytes 208904 | tf_op jit(solution)/shard_map/ppermute | solution.py:41
  7.4 1.3 %collective-permute-start.3 = (f32[136,128]{1,0:T(8,128)S(1)}, f32[136,128]{1,0:T(8,128)S(1)}, u32[]{:S(2)}, u32[]{:S(2)}) collective-permute-start(f32[136,128]{1,0:T(8,128)S(1)} %get-tuple-element.19), channel_id=1, source_target_pairs={{0,24},{1,7},{2,26},{3,5},{4,28},{5,3},{6,30},{7,1},{8,16},{9,15},... | collective-permute-start | bytes 208904 | tf_op jit(solution)/shard_map/ppermute | solution.py:41
  8.8 0.2 collective-permute-start.1
  9.0 0.7 %collective-permute-done.2 = f32[136,128]{1,0:T(8,128)S(1)} collective-permute-done((f32[136,128]{1,0:T(8,128)S(1)}, f32[136,128]{1,0:T(8,128)S(1)}, u32[]{:S(2)}, u32[]{:S(2)}) %collective-permute-start.2) | collective-permute-done | bytes 69664 | tf_op jit(solution)/shard_map/ppermute | solution.py:41
  9.7 3.9 %collective-permute-done.3 = f32[136,128]{1,0:T(8,128)S(1)} collective-permute-done((f32[136,128]{1,0:T(8,128)S(1)}, f32[136,128]{1,0:T(8,128)S(1)}, u32[]{:S(2)}, u32[]{:S(2)}) %collective-permute-start.3) | collective-permute-done | bytes 69664 | tf_op jit(solution)/shard_map/ppermute | solution.py:41
  13.6 0.2 collective-permute-done.1
  13.8 2.5 %collective-permute-start.6 = (f32[136,128]{1,0:T(8,128)S(1)}, f32[136,128]{1,0:T(8,128)S(1)}, u32[]{:S(2)}, u32[]{:S(2)}) collective-permute-start(f32[136,128]{1,0:T(8,128)S(1)} %add_add_fusion.1), channel_id=1, source_target_pairs={{0,6},{1,25},{2,4},{3,27},{4,2},{5,29},{6,0},{7,31},{8,14},{9,17},... | collective-permute-start | bytes 208904 | tf_op jit(solution)/shard_map/ppermute | solution.py:41
  16.3 0.5 %collective-permute-start.5 = (f32[136,128]{1,0:T(8,128)S(1)}, f32[136,128]{1,0:T(8,128)S(1)}, u32[]{:S(2)}, u32[]{:S(2)}) collective-permute-start(f32[136,128]{1,0:T(8,128)S(1)} %add_add_fusion.1), channel_id=1, source_target_pairs={{0,4},{1,17},{2,6},{3,19},{4,0},{5,21},{6,2},{7,23},{8,12},{9,25},... | collective-permute-start | bytes 208904 | tf_op jit(solution)/shard_map/ppermute | solution.py:41
  16.8 0.5 %collective-permute-start.4 = (f32[136,128]{1,0:T(8,128)S(1)}, f32[136,128]{1,0:T(8,128)S(1)}, u32[]{:S(2)}, u32[]{:S(2)}) collective-permute-start(f32[136,128]{1,0:T(8,128)S(1)} %add_add_fusion.1), channel_id=1, source_target_pairs={{0,2},{1,9},{2,0},{3,11},{4,6},{5,13},{6,4},{7,15},{8,10},{9,1},{1... | collective-permute-start | bytes 208904 | tf_op jit(solution)/shard_map/ppermute | solution.py:41
  17.4 0.5 %spread.1.lead_ref = bf16[2048,256]{1,0:T(8,128)(2,1)S(1)} custom-call(bf16[2048,128]{1,0:T(8,128)(2,1)S(1)} %bitcast.9, bf16[2048,128]{1,0:T(8,128)(2,1)S(1)} %collective-permute-done.recv_ref.odd_ref), custom_call_target="tpu_custom_call" | custom-call | tf_op jit(solution)/shard_map/spread/pallas_call | solution.py:360
  17.9 1.2 %collective-permute-done.6 = f32[136,128]{1,0:T(8,128)S(1)} collective-permute-done((f32[136,128]{1,0:T(8,128)S(1)}, f32[136,128]{1,0:T(8,128)S(1)}, u32[]{:S(2)}, u32[]{:S(2)}) %collective-permute-start.6) | collective-permute-done | bytes 69664 | tf_op jit(solution)/shard_map/ppermute | solution.py:41
  19.1 1.5 %collective-permute-done.5 = f32[136,128]{1,0:T(8,128)S(1)} collective-permute-done((f32[136,128]{1,0:T(8,128)S(1)}, f32[136,128]{1,0:T(8,128)S(1)}, u32[]{:S(2)}, u32[]{:S(2)}) %collective-permute-start.5) | collective-permute-done | bytes 69664 | tf_op jit(solution)/shard_map/ppermute | solution.py:41
  20.7 0.5 %collective-permute-done.4 = f32[136,128]{1,0:T(8,128)S(1)} collective-permute-done((f32[136,128]{1,0:T(8,128)S(1)}, f32[136,128]{1,0:T(8,128)S(1)}, u32[]{:S(2)}, u32[]{:S(2)}) %collective-permute-start.4) | collective-permute-done | bytes 69664 | tf_op jit(solution)/shard_map/ppermute | solution.py:41
  21.2 0.1 collective-permute-start.8
  21.3 2.0 %collective-permute-start.7 = (f32[128,128]{1,0:T(8,128)S(1)}, f32[128,128]{1,0:T(8,128)S(1)}, u32[]{:S(2)}, u32[]{:S(2)}) collective-permute-start(f32[128,128]{1,0:T(8,128)S(1)} %get-tuple-element.24.kept_ref), channel_id=1, source_target_pairs={{0,1},{1,0},{2,3},{3,2},{4,5},{5,4},{6,7},{7,6},{8,9},{9,8},{10,11... | collective-permute-start | bytes 196616 | tf_op jit(solution)/shard_map/ppermute | solution.py:17
  23.2 0.1 collective-permute-start.9
  23.3 0.9 %collective-permute-start.10 = (f32[72,128]{1,0:T(8,128)S(1)}, f32[72,128]{1,0:T(8,128)S(1)}, u32[]{:S(2)}, u32[]{:S(2)}) collective-permute-start(f32[72,128]{1,0:T(8,128)S(1)} %slice.3), channel_id=1, source_target_pairs={{0,9},{1,2},{2,11},{3,0},{4,13},{5,6},{6,15},{7,4},{8,1},{9,10},{1... | collective-permute-start | bytes 110600 | tf_op jit(solution)/shard_map/ppermute | solution.py:41
  24.2 2.5 %collective-permute-done.10.across_ref = f32[72,128]{1,0:T(8,128)S(1)} collective-permute-done((f32[72,128]{1,0:T(8,128)S(1)}, f32[72,128]{1,0:T(8,128)S(1)}, u32[]{:S(2)}, u32[]{:S(2)}) %collective-permute-start.10) | collective-permute-done | bytes 36896 | tf_op jit(solution)/shard_map/ppermute | solution.py:41
  26.7 1.7 %finish.1 = (f32[256,128]{1,0:T(8,128)}, bf16[2048,128]{1,0:T(8,128)(2,1)}) custom-call(f32[8,8,128]{2,1,0:T(8,128)S(1)} %get-tuple-element.15.factor_ref, bf16[2048,128]{1,0:T(8,128)(2,1)S(1)} %bitcast.10, bf16[2048,256]{1,0:T(8,128)(2,1)S(1)} %spread.1.lead_ref, f32[128,128]{1,0:T(8,128)S(1)} %get-tuple-element.24.kept_ref, ...), custom_call_target="tpu_custom_call" | custom-call | tf_op jit(solution)/shard_map/finish/pallas_call | solution.py:388
  (12 shorter events, 0.1 us)
Async XLA Ops:
  0.6 2.5 %collective-permute-start = (bf16[2048,128]{1,0:T(8,128)(2,1)}, bf16[2048,128]{1,0:T(8,128)(2,1)S(1)}, u32[]{:S(2)}, u32[]{:S(2)}) collective-permute-start(bf16[2048,128]{1,0:T(8,128)(2,1)} %bitcast.7), channel_id=1, source_target_pairs={{0,1},{1,0},{2,3},{3,2},{4,5},{5,4},{6,7},{7,6},{8,9},{9,8},{10,11... | collective-permute-start | bytes 1572872 | tf_op jit(solution)/shard_map/ppermute | solution.py:17
  1.1 1.0 %copy-start = (bf16[1024,1,2,128]{3,2,1,0:T(2,128)(2,1)S(1)}, bf16[1024,1,2,128]{3,2,1,0:T(2,128)(2,1)}, u32[]{:S(2)}) copy-start(bf16[1024,1,2,128]{3,2,1,0:T(2,128)(2,1)} %param.2) | copy-start | bytes 1572868
  2.2 0.7 %copy-start.2 = (f32[2,2,2]{2,1,0:T(2,128)S(1)}, f32[2,2,2]{2,1,0:T(2,128)}, u32[]{:S(2)}) copy-start(f32[2,2,2]{2,1,0:T(2,128)} %scale_ref.1) | copy-start | bytes 100
  3.1 14.3 %copy-start.1 = (bf16[1024,1,2,128]{3,2,1,0:T(2,128)(2,1)S(1)}, bf16[1024,1,2,128]{3,2,1,0:T(2,128)(2,1)}, u32[]{:S(2)}) copy-start(bf16[1024,1,2,128]{3,2,1,0:T(2,128)(2,1)} %param.2) | copy-start | bytes 1572868
  3.6 6.1 %collective-permute-start.2 = (f32[136,128]{1,0:T(8,128)S(1)}, f32[136,128]{1,0:T(8,128)S(1)}, u32[]{:S(2)}, u32[]{:S(2)}) collective-permute-start(f32[136,128]{1,0:T(8,128)S(1)} %get-tuple-element.18), channel_id=1, source_target_pairs={{0,16},{1,5},{2,18},{3,7},{4,20},{5,1},{6,22},{7,3},{8,24},{9,13},... | collective-permute-start | bytes 208904 | tf_op jit(solution)/shard_map/ppermute | solution.py:41
  7.4 6.2 %collective-permute-start.3 = (f32[136,128]{1,0:T(8,128)S(1)}, f32[136,128]{1,0:T(8,128)S(1)}, u32[]{:S(2)}, u32[]{:S(2)}) collective-permute-start(f32[136,128]{1,0:T(8,128)S(1)} %get-tuple-element.19), channel_id=1, source_target_pairs={{0,24},{1,7},{2,26},{3,5},{4,28},{5,3},{6,30},{7,1},{8,16},{9,15},... | collective-permute-start | bytes 208904 | tf_op jit(solution)/shard_map/ppermute | solution.py:41
  8.8 5.1 %collective-permute-start.1 = (f32[136,128]{1,0:T(8,128)S(1)}, f32[136,128]{1,0:T(8,128)S(1)}, u32[]{:S(2)}, u32[]{:S(2)}) collective-permute-start(f32[136,128]{1,0:T(8,128)S(1)} %get-tuple-element.19), channel_id=1, source_target_pairs={{0,8},{1,3},{2,10},{3,1},{4,12},{5,7},{6,14},{7,5},{8,0},{9,11},{1... | collective-permute-start | bytes 208904 | tf_op jit(solution)/shard_map/ppermute | solution.py:41
  13.8 5.3 %collective-permute-start.6 = (f32[136,128]{1,0:T(8,128)S(1)}, f32[136,128]{1,0:T(8,128)S(1)}, u32[]{:S(2)}, u32[]{:S(2)}) collective-permute-start(f32[136,128]{1,0:T(8,128)S(1)} %add_add_fusion.1), channel_id=1, source_target_pairs={{0,6},{1,25},{2,4},{3,27},{4,2},{5,29},{6,0},{7,31},{8,14},{9,17},... | collective-permute-start | bytes 208904 | tf_op jit(solution)/shard_map/ppermute | solution.py:41
  16.3 4.3 %collective-permute-start.5 = (f32[136,128]{1,0:T(8,128)S(1)}, f32[136,128]{1,0:T(8,128)S(1)}, u32[]{:S(2)}, u32[]{:S(2)}) collective-permute-start(f32[136,128]{1,0:T(8,128)S(1)} %add_add_fusion.1), channel_id=1, source_target_pairs={{0,4},{1,17},{2,6},{3,19},{4,0},{5,21},{6,2},{7,23},{8,12},{9,25},... | collective-permute-start | bytes 208904 | tf_op jit(solution)/shard_map/ppermute | solution.py:41
  16.8 4.3 %collective-permute-start.4 = (f32[136,128]{1,0:T(8,128)S(1)}, f32[136,128]{1,0:T(8,128)S(1)}, u32[]{:S(2)}, u32[]{:S(2)}) collective-permute-start(f32[136,128]{1,0:T(8,128)S(1)} %add_add_fusion.1), channel_id=1, source_target_pairs={{0,2},{1,9},{2,0},{3,11},{4,6},{5,13},{6,4},{7,15},{8,10},{9,1},{1... | collective-permute-start | bytes 208904 | tf_op jit(solution)/shard_map/ppermute | solution.py:41
  21.2 5.5 %collective-permute-start.8 = (f32[136,128]{1,0:T(8,128)S(1)}, f32[136,128]{1,0:T(8,128)S(1)}, u32[]{:S(2)}, u32[]{:S(2)}) collective-permute-start(f32[136,128]{1,0:T(8,128)S(1)} %add_add_fusion.sums_ref.same_ref), channel_id=1, source_target_pairs={{0,8},{1,3},{2,10},{3,1},{4,12},{5,7},{6,14},{7,5},{8,0},{9,11},{1... | collective-permute-start | bytes 208904 | tf_op jit(solution)/shard_map/ppermute | solution.py:41
  21.3 5.4 %collective-permute-start.7 = (f32[128,128]{1,0:T(8,128)S(1)}, f32[128,128]{1,0:T(8,128)S(1)}, u32[]{:S(2)}, u32[]{:S(2)}) collective-permute-start(f32[128,128]{1,0:T(8,128)S(1)} %get-tuple-element.24.kept_ref), channel_id=1, source_target_pairs={{0,1},{1,0},{2,3},{3,2},{4,5},{5,4},{6,7},{7,6},{8,9},{9,8},{10,11... | collective-permute-start | bytes 196616 | tf_op jit(solution)/shard_map/ppermute | solution.py:17
  23.2 3.5 %collective-permute-start.9 = (f32[128,128]{1,0:T(8,128)S(1)}, f32[128,128]{1,0:T(8,128)S(1)}, u32[]{:S(2)}, u32[]{:S(2)}) collective-permute-start(f32[128,128]{1,0:T(8,128)S(1)} %get-tuple-element.25), channel_id=1, source_target_pairs={{0,1},{1,0},{2,3},{3,2},{4,5},{5,4},{6,7},{7,6},{8,9},{9,8},{10,11... | collective-permute-start | bytes 196616 | tf_op jit(solution)/shard_map/ppermute | solution.py:17
  23.3 3.4 %collective-permute-start.10 = (f32[72,128]{1,0:T(8,128)S(1)}, f32[72,128]{1,0:T(8,128)S(1)}, u32[]{:S(2)}, u32[]{:S(2)}) collective-permute-start(f32[72,128]{1,0:T(8,128)S(1)} %slice.3), channel_id=1, source_target_pairs={{0,9},{1,2},{2,11},{3,0},{4,13},{5,6},{6,15},{7,4},{8,1},{9,10},{1... | collective-permute-start | bytes 110600 | tf_op jit(solution)/shard_map/ppermute | solution.py:41

commit v9 on v8

--- a/solution.py
+++ b/solution.py
@@ -181,11 +181,20 @@
     return jnp.broadcast_to(tile[None], (rows // 8, *tile.shape)).reshape(rows, tile.shape[1])
 
 
-def split_kernel(rounds, nblock, scale_ref, z_ref, first_ref, own_ref, factor_ref, wide):
+def split_kernel(rounds, nblock, scale_hbm, z_hbm, first_ref, own_ref, factor_ref, scale_ref, z_ref, wide, sems):
     group = lax.axis_index("cols")
     odd = group % 2
     width = z_ref.shape[1]
-    points = z_ref.shape[0] // rounds
+    span = z_ref.shape[0] // nblock
+    points = span // rounds
+    scale_copy = pltpu.make_async_copy(scale_hbm, scale_ref, sems.at[nblock])
+    scale_copy.start()
+    copies = []
+    for b in range(nblock):
+        at = slice(b * span, (b + 1) * span)
+        copies.append(pltpu.make_async_copy(z_hbm.at[at, :], z_ref.at[at, :], sems.at[b]))
+        copies[b].start()
+    scale_copy.wait()
     row = lax.broadcasted_iota(jnp.int32, (8, width), 0)
     for b in range(nblock):
         lead = jnp.broadcast_to(scale_ref[b, 0:1, 0:1], (8, width))
@@ -196,11 +205,14 @@
         factor_ref[4 * b + 1] = lead * jnp.where(odd == 1, mine[0], mine[1])
         factor_ref[4 * b + 2] = lead
         factor_ref[4 * b + 3] = jnp.where(row % rounds == 0, jnp.where(group == 0, 0.0, mine[0]), mine[1])
-    wide[...] = z_ref[...].astype(F32)
-    first = wide[pl.ds(0, points, stride=rounds), :].astype(BF16)
-    last = wide[pl.ds(1, points, stride=rounds), :].astype(BF16)
-    first_ref[...] = first
-    own_ref[...] = jnp.where(odd == 1, first, last)
+    for b in range(nblock):
+        copies[b].wait()
+        at = slice(b * span, (b + 1) * span)
+        wide[at, :] = z_ref[at, :].astype(F32)
+        first = wide[pl.ds(b * span, points, stride=rounds), :].astype(BF16)
+        last = wide[pl.ds(b * span + 1, points, stride=rounds), :].astype(BF16)
+        first_ref[b * points : (b + 1) * points, :] = first
+        own_ref[b * points : (b + 1) * points, :] = jnp.where(odd == 1, first, last)
 
 
 def products_kernel(rounds, nblock, phases, factor_ref, first_ref, own_ref, recv_ref, *rest):
@@ -238,7 +250,8 @@
         theirs = cross[pl.ds(pl.multiple_of(place * half, half), half), :]
         ref[:half, :] = jnp.where(group == 1, packed[:half, :], theirs)
         ref[half:height, :] = packed[half:, :]
-        ref[height:, :] = cross[pl.ds(pl.multiple_of(width + place * half, half), half), :]
+        ref[height : height + half, :] = cross[pl.ds(pl.multiple_of(width + place * half, half), half), :]
+        ref[height + half :, :] = jnp.zeros((8, width), F32)
 
 
 def spread_kernel(rounds, even_ref, odd_ref, out_ref):
@@ -258,7 +271,8 @@
     @pl.when(group == 1)
     def _():
         gram = unpack(sums_ref[:height, :])
-        block_ref[...] = gram
+        block_ref[:width, :] = gram
+        block_ref[width:, :] = jnp.zeros((8, width), F32)
         rows = [gram[8 * i : 8 * i + 8, :] for i in range(width // 8)]
         for i, row in enumerate(lower_inverse(rows, width)):
             inverse_ref[8 * i : 8 * i + 8, :] = row
@@ -267,7 +281,7 @@
     def _():
         inverse_ref[...] = jnp.zeros((width, width), F32)
         block_ref[:height, :] = sums_ref[:height, :]
-        block_ref[height:, :] = jnp.zeros((width - height, width), F32)
+        block_ref[height:, :] = jnp.zeros((width + 8 - height, width), F32)
 
 
 def finish_kernel(
@@ -280,9 +294,9 @@
     half = width // 2
     height = half + 8
     own_digit, pair_digit = half_digit(phases, group % 2), half_digit(phases, 1 - group % 2)
-    for own_rows, pair_rows, other in ((same_ref[height:, :], block_ref[:half, :], 0), (gathered_ref[height:, :], across_ref[:half, :], 1)):
-        mine[pl.ds(pl.multiple_of((own_digit ^ other) * half, half), half), :] = own_rows
-        theirs[pl.ds(pl.multiple_of((pair_digit ^ other) * half, half), half), :] = pair_rows
+    for own_rows, pair_rows, other in ((same_ref, block_ref, 0), (gathered_ref, across_ref, 1)):
+        mine[pl.ds(pl.multiple_of((own_digit ^ other) * half, half), half), :] = own_rows[height : height + half, :]
+        theirs[pl.ds(pl.multiple_of((pair_digit ^ other) * half, half), half), :] = pair_rows[:half, :]
     own_block = mine[...]
     pair_block = jnp.where(group == 0, block_ref[...], theirs[...])
     cross = jnp.concatenate([jnp.where(odd, own_block, pair_block), jnp.where(odd, pair_block, own_block)], axis=1)
@@ -328,17 +342,22 @@
     even = among_pairs(z, n_cols, group, 0)
     leads = (even, recv) if n_cols == 2 else (even, partner(even, "cols", n_cols, 1))
     phases = radices(n_rows)
-    payload = width + 8
+    payload = width + 16
     params = pltpu.CompilerParams(vmem_limit_bytes=48 << 20)
     first, own, factors = pl.pallas_call(
         functools.partial(split_kernel, rounds, nblock),
         out_shape=[jax.ShapeDtypeStruct((points, width), BF16)] * 2 + [jax.ShapeDtypeStruct((4 * nblock, 8, width), F32)],
-        in_specs=[VMEM] * 2,
+        in_specs=[pl.BlockSpec(memory_space=pltpu.HBM)] * 2,
         out_specs=[VMEM] * 3,
-        scratch_shapes=[pltpu.VMEM((long, width), F32)],
+        scratch_shapes=[
+            pltpu.VMEM(scales.shape, F32),
+            pltpu.VMEM((long, width), BF16),
+            pltpu.VMEM((long, width), F32),
+            pltpu.SemaphoreType.DMA((nblock + 1,)),
+        ],
         compiler_params=params,
         name="split",
-    )(scales, z)
+    )(*[pltpu.with_memory_space_constraint(x, pltpu.HBM) for x in (scales, z)])
     extra = () if n_cols == 2 else leads
     sent = pl.pallas_call(
         functools.partial(products_kernel, rounds, nblock, phases),
@@ -368,12 +387,11 @@
             *others, lead = lax.optimization_barrier((*others, lead))
         for other in others:
             sums = sums + other
-    height = width // 2 + 8
     beside = lambda parity: order(phases, parity)[0][0]
     gathered = hop(sums, n_rows, n_cols, beside)
     inverse, block = pl.pallas_call(
         factor_kernel,
-        out_shape=[jax.ShapeDtypeStruct((width, width), F32)] * 2,
+        out_shape=[jax.ShapeDtypeStruct((width + pad, width), F32) for pad in (0, 8)],
         in_specs=[VMEM],
         out_specs=[VMEM] * 2,
         compiler_params=params,
@@ -382,8 +400,8 @@
     )(sums)
     inverse = among_pairs(inverse, n_cols, group, 1)
     swapped = partner(inverse, "cols", n_cols, 1)
-    blocks = partner(block, "cols", n_cols, 1)
-    crossed = hop(block[:height], n_rows, n_cols, beside, 1)
+    blocks = partner(block[:width], "cols", n_cols, 1)
+    crossed = hop(block, n_rows, n_cols, beside, 1)
     chunks = 2 * nblock
     coef, updated = pl.pallas_call(
         functools.partial(finish_kernel, rounds, nblock, phases, root, chunks),

time: 28.6 us -> 27.9 us (0.976); the launches traced: 28.4 us -> 27.4 us
  local copies, waits for them, and re-layouts: 1.73 us -> 0.01 us
  Pallas kernels: 2.91 us -> 3.81 us
    unnamed x6 -> x2, local copies, waits for them, and re-layouts: 1.73 us -> 0.01 us
    ppermute x8, waiting for transfers between devices: 10.6 us -> 8.91 us  [hop(): return lax.ppermute(x, ('rows', 'cols'), pairs)]
    ppermute x8, starting transfers between devices: 9.89 us -> 11.4 us  [hop(): return lax.ppermute(x, ('rows', 'cols'), pairs)]
    ppermute x3, starting transfers between devices: 2.55 us -> 1.03 us  [partner(): return lax.ppermute(x, axis, [(i, i ^ offset) for i in range(count)])]
    ppermute x3, waiting for transfers between devices: 0.01 us -> 1.5 us  [partner(): return lax.ppermute(x, axis, [(i, i ^ offset) for i in range(count)])]
    pallas_call x1, Pallas kernels: 0.23 us -> 1.14 us  [shards(): pl.pallas_call(functools.partial(split_kernel, rounds, nblock), out_shape...]
  transfers between devices with their start and end apart: 11 -> 11, of which waited for: 7 -> 11; matrix products, arithmetic and copies ran while one was open for 0% -> 0% of each run, Pallas kernels for 3% -> 6%
where the time goes in v9:
time: 27.9 us; the launch traced here: 27.4 us
  starting transfers between devices  12.5 us (45%)
  waiting for transfers between devices  10.4 us (37%)
  Pallas kernels  3.81 us (14%)
  between operations  0.68 us (2%)
    ppermute x8, starting transfers between devices, hop(): return lax.ppermute(x, ('rows', 'cols'), pairs)  11.4 us
    ppermute x8, waiting for transfers between devices, hop(): return lax.ppermute(x, ('rows', 'cols'), pairs)  8.91 us
    pallas_call x1, Pallas kernels, shards(): pl.pallas_call(functools.partial(finish_kernel, rounds, nblock, phases, r...  1.69 us
    ppermute x3, waiting for transfers between devices, partner(): return lax.ppermute(x, axis, [(i, i ^ offset) for i in range(count)])  1.5 us
    pallas_call x1, Pallas kernels, shards(): pl.pallas_call(functools.partial(split_kernel, rounds, nblock), out_shape...  1.14 us
    ppermute x3, starting transfers between devices, partner(): return lax.ppermute(x, axis, [(i, i ^ offset) for i in range(count)])  1.03 us
  transfers between devices with their start and end apart: 11, of which 11 were waited for; matrix products, arithmetic and copies ran while one was open for 0% of the time, Pallas kernels for 6%

profile of v9, /device:TPU:0, one launch (start us, length us, event | category | flops | bytes accessed | tf_op | source)
XLA Modules:
  0.0 27.4 jit_solution(9173936213071258304)
XLA Ops:
  0.6 0.5 %collective-permute-start = (bf16[2048,128]{1,0:T(8,128)(2,1)}, bf16[2048,128]{1,0:T(8,128)(2,1)S(1)}, u32[]{:S(2)}, u32[]{:S(2)}) collective-permute-start(bf16[2048,128]{1,0:T(8,128)(2,1)} %bitcast.7), channel_id=1, source_target_pairs={{0,1},{1,0},{2,3},{3,2},{4,5},{5,4},{6,7},{7,6},{8,9},{9,8},{10,11... | collective-permute-start | bytes 1572872 | tf_op jit(solution)/shard_map/ppermute | solution.py:17
  1.1 1.1 %split.1 = (bf16[1024,128]{1,0:T(8,128)(2,1)S(1)}, bf16[1024,128]{1,0:T(8,128)(2,1)S(1)}, f32[8,8,128]{2,1,0:T(8,128)S(1)}) custom-call(f32[2,2,2]{2,1,0:T(2,128)} %scale_hbm.1, bf16[2048,128]{1,0:T(8,128)(2,1)} %bitcast.8), custom_call_target="tpu_custom_call" | custom-call | tf_op jit(solution)/shard_map/split/pallas_call | solution.py:347
  2.3 0.6 %collective-permute-done.recv_ref.odd_ref = bf16[2048,128]{1,0:T(8,128)(2,1)S(1)} collective-permute-done((bf16[2048,128]{1,0:T(8,128)(2,1)}, bf16[2048,128]{1,0:T(8,128)(2,1)S(1)}, u32[]{:S(2)}, u32[]{:S(2)}) %collective-permute-start) | collective-permute-done | bytes 524320 | tf_op jit(solution)/shard_map/ppermute | solution.py:17
  2.9 0.5 %products.1 = (f32[144,128]{1,0:T(8,128)S(1)}, f32[144,128]{1,0:T(8,128)S(1)}) custom-call(f32[8,8,128]{2,1,0:T(8,128)S(1)} %get-tuple-element.15.factor_ref, bf16[1024,128]{1,0:T(8,128)(2,1)S(1)} %get-tuple-element.16.first_ref, bf16[1024,128]{1,0:T(8,128)(2,1)S(1)} %get-tuple-element.17.own_ref, bf16[2048,128]{1,0:T(8,128)(2,1)S(1)} %collective-permute-done.recv_ref.odd_ref), custom_call_target="tpu_custom_call" | custom-call | tf_op jit(solution)/shard_map/products/pallas_call | solution.py:362
  3.4 4.0 %collective-permute-start.2 = (f32[144,128]{1,0:T(8,128)S(1)}, f32[144,128]{1,0:T(8,128)S(1)}, u32[]{:S(2)}, u32[]{:S(2)}) collective-permute-start(f32[144,128]{1,0:T(8,128)S(1)} %get-tuple-element.18), channel_id=1, source_target_pairs={{0,16},{1,5},{2,18},{3,7},{4,20},{5,1},{6,22},{7,3},{8,24},{9,13},... | collective-permute-start | bytes 221192 | tf_op jit(solution)/shard_map/ppermute | solution.py:41
  7.4 1.3 %collective-permute-start.3 = (f32[144,128]{1,0:T(8,128)S(1)}, f32[144,128]{1,0:T(8,128)S(1)}, u32[]{:S(2)}, u32[]{:S(2)}) collective-permute-start(f32[144,128]{1,0:T(8,128)S(1)} %get-tuple-element.19), channel_id=1, source_target_pairs={{0,24},{1,7},{2,26},{3,5},{4,28},{5,3},{6,30},{7,1},{8,16},{9,15},... | collective-permute-start | bytes 221192 | tf_op jit(solution)/shard_map/ppermute | solution.py:41
  8.7 0.2 collective-permute-start.1
  9.0 0.8 %collective-permute-done.2 = f32[144,128]{1,0:T(8,128)S(1)} collective-permute-done((f32[144,128]{1,0:T(8,128)S(1)}, f32[144,128]{1,0:T(8,128)S(1)}, u32[]{:S(2)}, u32[]{:S(2)}) %collective-permute-start.2) | collective-permute-done | bytes 73760 | tf_op jit(solution)/shard_map/ppermute | solution.py:41
  9.7 3.9 %collective-permute-done.3 = f32[144,128]{1,0:T(8,128)S(1)} collective-permute-done((f32[144,128]{1,0:T(8,128)S(1)}, f32[144,128]{1,0:T(8,128)S(1)}, u32[]{:S(2)}, u32[]{:S(2)}) %collective-permute-start.3) | collective-permute-done | bytes 73760 | tf_op jit(solution)/shard_map/ppermute | solution.py:41
  13.7 0.2 collective-permute-done.1
  13.9 2.5 %collective-permute-start.6 = (f32[144,128]{1,0:T(8,128)S(1)}, f32[144,128]{1,0:T(8,128)S(1)}, u32[]{:S(2)}, u32[]{:S(2)}) collective-permute-start(f32[144,128]{1,0:T(8,128)S(1)} %add_add_fusion.1), channel_id=1, source_target_pairs={{0,6},{1,25},{2,4},{3,27},{4,2},{5,29},{6,0},{7,31},{8,14},{9,17},... | collective-permute-start | bytes 221192 | tf_op jit(solution)/shard_map/ppermute | solution.py:41
  16.4 0.5 %collective-permute-start.5 = (f32[144,128]{1,0:T(8,128)S(1)}, f32[144,128]{1,0:T(8,128)S(1)}, u32[]{:S(2)}, u32[]{:S(2)}) collective-permute-start(f32[144,128]{1,0:T(8,128)S(1)} %add_add_fusion.1), channel_id=1, source_target_pairs={{0,4},{1,17},{2,6},{3,19},{4,0},{5,21},{6,2},{7,23},{8,12},{9,25},... | collective-permute-start | bytes 221192 | tf_op jit(solution)/shard_map/ppermute | solution.py:41
  16.9 0.5 %collective-permute-start.4 = (f32[144,128]{1,0:T(8,128)S(1)}, f32[144,128]{1,0:T(8,128)S(1)}, u32[]{:S(2)}, u32[]{:S(2)}) collective-permute-start(f32[144,128]{1,0:T(8,128)S(1)} %add_add_fusion.1), channel_id=1, source_target_pairs={{0,2},{1,9},{2,0},{3,11},{4,6},{5,13},{6,4},{7,15},{8,10},{9,1},{1... | collective-permute-start | bytes 221192 | tf_op jit(solution)/shard_map/ppermute | solution.py:41
  17.5 0.5 %spread.1.lead_ref = bf16[2048,256]{1,0:T(8,128)(2,1)S(1)} custom-call(bf16[2048,128]{1,0:T(8,128)(2,1)S(1)} %bitcast.9, bf16[2048,128]{1,0:T(8,128)(2,1)S(1)} %collective-permute-done.recv_ref.odd_ref), custom_call_target="tpu_custom_call" | custom-call | tf_op jit(solution)/shard_map/spread/pallas_call | solution.py:379
  18.0 1.3 %collective-permute-done.6 = f32[144,128]{1,0:T(8,128)S(1)} collective-permute-done((f32[144,128]{1,0:T(8,128)S(1)}, f32[144,128]{1,0:T(8,128)S(1)}, u32[]{:S(2)}, u32[]{:S(2)}) %collective-permute-start.6) | collective-permute-done | bytes 73760 | tf_op jit(solution)/shard_map/ppermute | solution.py:41
  19.2 1.5 %collective-permute-done.5 = f32[144,128]{1,0:T(8,128)S(1)} collective-permute-done((f32[144,128]{1,0:T(8,128)S(1)}, f32[144,128]{1,0:T(8,128)S(1)}, u32[]{:S(2)}, u32[]{:S(2)}) %collective-permute-start.5) | collective-permute-done | bytes 73760 | tf_op jit(solution)/shard_map/ppermute | solution.py:41
  20.8 0.5 %collective-permute-done.4 = f32[144,128]{1,0:T(8,128)S(1)} collective-permute-done((f32[144,128]{1,0:T(8,128)S(1)}, f32[144,128]{1,0:T(8,128)S(1)}, u32[]{:S(2)}, u32[]{:S(2)}) %collective-permute-start.4) | collective-permute-done | bytes 73760 | tf_op jit(solution)/shard_map/ppermute | solution.py:41
  21.4 2.2 %collective-permute-start.10 = (f32[136,128]{1,0:T(8,128)S(1)}, f32[136,128]{1,0:T(8,128)S(1)}, u32[]{:S(2)}, u32[]{:S(2)}) collective-permute-start(f32[136,128]{1,0:T(8,128)S(1)} %get-tuple-element.25), channel_id=1, source_target_pairs={{0,9},{1,2},{2,11},{3,0},{4,13},{5,6},{6,15},{7,4},{8,1},{9,10},{1... | collective-permute-start | bytes 208904 | tf_op jit(solution)/shard_map/ppermute | solution.py:41
  23.7 0.5 %collective-permute-start.7 = (f32[128,128]{1,0:T(8,128)S(1)}, f32[128,128]{1,0:T(8,128)S(1)}, u32[]{:S(2)}, u32[]{:S(2)}) collective-permute-start(f32[128,128]{1,0:T(8,128)S(1)} %get-tuple-element.24.kept_ref), channel_id=1, source_target_pairs={{0,1},{1,0},{2,3},{3,2},{4,5},{5,4},{6,7},{7,6},{8,9},{9,8},{10,11... | collective-permute-start | bytes 196616 | tf_op jit(solution)/shard_map/ppermute | solution.py:17
  24.2 0.7 %collective-permute-done.9.block_ref = f32[128,128]{1,0:T(8,128)S(1)} collective-permute-done((f32[128,128]{1,0:T(8,128)S(1)}, f32[128,128]{1,0:T(8,128)S(1)}, u32[]{:S(2)}, u32[]{:S(2)}) %collective-permute-start.9) | collective-permute-done | bytes 65568 | tf_op jit(solution)/shard_map/ppermute | solution.py:17
  24.9 0.2 collective-permute-done.7.recv_ref
  25.1 0.5 %collective-permute-done.10.across_ref = f32[136,128]{1,0:T(8,128)S(1)} collective-permute-done((f32[136,128]{1,0:T(8,128)S(1)}, f32[136,128]{1,0:T(8,128)S(1)}, u32[]{:S(2)}, u32[]{:S(2)}) %collective-permute-start.10) | collective-permute-done | bytes 69664 | tf_op jit(solution)/shard_map/ppermute | solution.py:41
  25.6 0.1 collective-permute-done.8.gathered_ref
  25.7 1.7 %finish.1 = (f32[256,128]{1,0:T(8,128)}, bf16[2048,128]{1,0:T(8,128)(2,1)}) custom-call(f32[8,8,128]{2,1,0:T(8,128)S(1)} %get-tuple-element.15.factor_ref, bf16[2048,128]{1,0:T(8,128)(2,1)S(1)} %bitcast.10, bf16[2048,256]{1,0:T(8,128)(2,1)S(1)} %spread.1.lead_ref, f32[128,128]{1,0:T(8,128)S(1)} %get-tuple-element.24.kept_ref, ...), custom_call_target="tpu_custom_call" | custom-call | tf_op jit(solution)/shard_map/finish/pallas_call | solution.py:406
  (8 shorter events, 0.2 us)
Async XLA Ops:
  0.6 2.3 %collective-permute-start = (bf16[2048,128]{1,0:T(8,128)(2,1)}, bf16[2048,128]{1,0:T(8,128)(2,1)S(1)}, u32[]{:S(2)}, u32[]{:S(2)}) collective-permute-start(bf16[2048,128]{1,0:T(8,128)(2,1)} %bitcast.7), channel_id=1, source_target_pairs={{0,1},{1,0},{2,3},{3,2},{4,5},{5,4},{6,7},{7,6},{8,9},{9,8},{10,11... | collective-permute-start | bytes 1572872 | tf_op jit(solution)/shard_map/ppermute | solution.py:17
  2.9 14.6 %copy-start = (bf16[1024,1,2,128]{3,2,1,0:T(2,128)(2,1)S(1)}, bf16[1024,1,2,128]{3,2,1,0:T(2,128)(2,1)}, u32[]{:S(2)}) copy-start(bf16[1024,1,2,128]{3,2,1,0:T(2,128)(2,1)} %param.2) | copy-start | bytes 1572868
  3.4 6.4 %collective-permute-start.2 = (f32[144,128]{1,0:T(8,128)S(1)}, f32[144,128]{1,0:T(8,128)S(1)}, u32[]{:S(2)}, u32[]{:S(2)}) collective-permute-start(f32[144,128]{1,0:T(8,128)S(1)} %get-tuple-element.18), channel_id=1, source_target_pairs={{0,16},{1,5},{2,18},{3,7},{4,20},{5,1},{6,22},{7,3},{8,24},{9,13},... | collective-permute-start | bytes 221192 | tf_op jit(solution)/shard_map/ppermute | solution.py:41
  7.4 6.3 %collective-permute-start.3 = (f32[144,128]{1,0:T(8,128)S(1)}, f32[144,128]{1,0:T(8,128)S(1)}, u32[]{:S(2)}, u32[]{:S(2)}) collective-permute-start(f32[144,128]{1,0:T(8,128)S(1)} %get-tuple-element.19), channel_id=1, source_target_pairs={{0,24},{1,7},{2,26},{3,5},{4,28},{5,3},{6,30},{7,1},{8,16},{9,15},... | collective-permute-start | bytes 221192 | tf_op jit(solution)/shard_map/ppermute | solution.py:41
  8.7 5.1 %collective-permute-start.1 = (f32[144,128]{1,0:T(8,128)S(1)}, f32[144,128]{1,0:T(8,128)S(1)}, u32[]{:S(2)}, u32[]{:S(2)}) collective-permute-start(f32[144,128]{1,0:T(8,128)S(1)} %get-tuple-element.19), channel_id=1, source_target_pairs={{0,8},{1,3},{2,10},{3,1},{4,12},{5,7},{6,14},{7,5},{8,0},{9,11},{1... | collective-permute-start | bytes 221192 | tf_op jit(solution)/shard_map/ppermute | solution.py:41
  13.9 5.3 %collective-permute-start.6 = (f32[144,128]{1,0:T(8,128)S(1)}, f32[144,128]{1,0:T(8,128)S(1)}, u32[]{:S(2)}, u32[]{:S(2)}) collective-permute-start(f32[144,128]{1,0:T(8,128)S(1)} %add_add_fusion.1), channel_id=1, source_target_pairs={{0,6},{1,25},{2,4},{3,27},{4,2},{5,29},{6,0},{7,31},{8,14},{9,17},... | collective-permute-start | bytes 221192 | tf_op jit(solution)/shard_map/ppermute | solution.py:41
  16.4 4.4 %collective-permute-start.5 = (f32[144,128]{1,0:T(8,128)S(1)}, f32[144,128]{1,0:T(8,128)S(1)}, u32[]{:S(2)}, u32[]{:S(2)}) collective-permute-start(f32[144,128]{1,0:T(8,128)S(1)} %add_add_fusion.1), channel_id=1, source_target_pairs={{0,4},{1,17},{2,6},{3,19},{4,0},{5,21},{6,2},{7,23},{8,12},{9,25},... | collective-permute-start | bytes 221192 | tf_op jit(solution)/shard_map/ppermute | solution.py:41
  16.9 4.4 %collective-permute-start.4 = (f32[144,128]{1,0:T(8,128)S(1)}, f32[144,128]{1,0:T(8,128)S(1)}, u32[]{:S(2)}, u32[]{:S(2)}) collective-permute-start(f32[144,128]{1,0:T(8,128)S(1)} %add_add_fusion.1), channel_id=1, source_target_pairs={{0,2},{1,9},{2,0},{3,11},{4,6},{5,13},{6,4},{7,15},{8,10},{9,1},{1... | collective-permute-start | bytes 221192 | tf_op jit(solution)/shard_map/ppermute | solution.py:41
  21.3 4.4 %collective-permute-start.8 = (f32[144,128]{1,0:T(8,128)S(1)}, f32[144,128]{1,0:T(8,128)S(1)}, u32[]{:S(2)}, u32[]{:S(2)}) collective-permute-start(f32[144,128]{1,0:T(8,128)S(1)} %add_add_fusion.sums_ref.same_ref), channel_id=1, source_target_pairs={{0,8},{1,3},{2,10},{3,1},{4,12},{5,7},{6,14},{7,5},{8,0},{9,11},{1... | collective-permute-start | bytes 221192 | tf_op jit(solution)/shard_map/ppermute | solution.py:41
  21.4 4.2 %collective-permute-start.10 = (f32[136,128]{1,0:T(8,128)S(1)}, f32[136,128]{1,0:T(8,128)S(1)}, u32[]{:S(2)}, u32[]{:S(2)}) collective-permute-start(f32[136,128]{1,0:T(8,128)S(1)} %get-tuple-element.25), channel_id=1, source_target_pairs={{0,9},{1,2},{2,11},{3,0},{4,13},{5,6},{6,15},{7,4},{8,1},{9,10},{1... | collective-permute-start | bytes 208904 | tf_op jit(solution)/shard_map/ppermute | solution.py:41
  23.6 1.3 %collective-permute-start.9 = (f32[128,128]{1,0:T(8,128)S(1)}, f32[128,128]{1,0:T(8,128)S(1)}, u32[]{:S(2)}, u32[]{:S(2)}) collective-permute-start(f32[128,128]{1,0:T(8,128)S(1)} %slice.3), channel_id=1, source_target_pairs={{0,1},{1,0},{2,3},{3,2},{4,5},{5,4},{6,7},{7,6},{8,9},{9,8},{10,11... | collective-permute-start | bytes 196616 | tf_op jit(solution)/shard_map/ppermute | solution.py:17
  23.7 1.4 %collective-permute-start.7 = (f32[128,128]{1,0:T(8,128)S(1)}, f32[128,128]{1,0:T(8,128)S(1)}, u32[]{:S(2)}, u32[]{:S(2)}) collective-permute-start(f32[128,128]{1,0:T(8,128)S(1)} %get-tuple-element.24.kept_ref), channel_id=1, source_target_pairs={{0,1},{1,0},{2,3},{3,2},{4,5},{5,4},{6,7},{7,6},{8,9},{9,8},{10,11... | collective-permute-start | bytes 196616 | tf_op jit(solution)/shard_map/ppermute | solution.py:17

commit v10 on v9

--- a/solution.py
+++ b/solution.py
@@ -33,11 +33,11 @@
     return phases
 
 
-def hop(x, n_rows, n_cols, offset, turn=0):
+def hop(x, n_rows, n_cols, offset):
     pairs = []
     for row in range(n_rows):
         for col in range(n_cols):
-            pairs.append((row * n_cols + col, (row ^ offset(col % 2)) * n_cols + (col ^ turn)))
+            pairs.append((row * n_cols + col, (row ^ offset(col % 2)) * n_cols + col))
     return lax.ppermute(x, ("rows", "cols"), pairs)
 
 
@@ -250,8 +250,7 @@
         theirs = cross[pl.ds(pl.multiple_of(place * half, half), half), :]
         ref[:half, :] = jnp.where(group == 1, packed[:half, :], theirs)
         ref[half:height, :] = packed[half:, :]
-        ref[height : height + half, :] = cross[pl.ds(pl.multiple_of(width + place * half, half), half), :]
-        ref[height + half :, :] = jnp.zeros((8, width), F32)
+        ref[height:, :] = cross[pl.ds(pl.multiple_of(width + place * half, half), half), :]
 
 
 def spread_kernel(rounds, even_ref, odd_ref, out_ref):
@@ -271,8 +270,7 @@
     @pl.when(group == 1)
     def _():
         gram = unpack(sums_ref[:height, :])
-        block_ref[:width, :] = gram
-        block_ref[width:, :] = jnp.zeros((8, width), F32)
+        block_ref[...] = gram
         rows = [gram[8 * i : 8 * i + 8, :] for i in range(width // 8)]
         for i, row in enumerate(lower_inverse(rows, width)):
             inverse_ref[8 * i : 8 * i + 8, :] = row
@@ -281,7 +279,7 @@
     def _():
         inverse_ref[...] = jnp.zeros((width, width), F32)
         block_ref[:height, :] = sums_ref[:height, :]
-        block_ref[height:, :] = jnp.zeros((width + 8 - height, width), F32)
+        block_ref[height:, :] = jnp.zeros((width - height, width), F32)
 
 
 def finish_kernel(
@@ -342,7 +340,7 @@
     even = among_pairs(z, n_cols, group, 0)
     leads = (even, recv) if n_cols == 2 else (even, partner(even, "cols", n_cols, 1))
     phases = radices(n_rows)
-    payload = width + 16
+    payload = width + 8
     params = pltpu.CompilerParams(vmem_limit_bytes=48 << 20)
     first, own, factors = pl.pallas_call(
         functools.partial(split_kernel, rounds, nblock),
@@ -391,7 +389,7 @@
     gathered = hop(sums, n_rows, n_cols, beside)
     inverse, block = pl.pallas_call(
         factor_kernel,
-        out_shape=[jax.ShapeDtypeStruct((width + pad, width), F32) for pad in (0, 8)],
+        out_shape=[jax.ShapeDtypeStruct((width, width), F32)] * 2,
         in_specs=[VMEM],
         out_specs=[VMEM] * 2,
         compiler_params=params,
@@ -400,8 +398,8 @@
     )(sums)
     inverse = among_pairs(inverse, n_cols, group, 1)
     swapped = partner(inverse, "cols", n_cols, 1)
-    blocks = partner(block[:width], "cols", n_cols, 1)
-    crossed = hop(block, n_rows, n_cols, beside, 1)
+    blocks = partner(block, "cols", n_cols, 1)
+    crossed = partner(gathered, "cols", n_cols, 1)
     chunks = 2 * nblock
     coef, updated = pl.pallas_call(
         functools.partial(finish_kernel, rounds, nblock, phases, root, chunks),

time: 27.9 us -> 32.6 us (1.17)
  waiting for transfers between devices: 10.4 us -> 14.2 us
  starting transfers between devices: 12.5 us -> 13.7 us
    ppermute x8 -> x7, waiting for transfers between devices: 8.91 us -> 12.4 us  [hop(): return lax.ppermute(x, ('rows', 'cols'), pairs)]
    ppermute x3 -> x4, starting transfers between devices: 1.03 us -> 4.48 us  [partner(): return lax.ppermute(x, axis, [(i, i ^ offset) for i in range(count)])]
    ppermute x8 -> x7, starting transfers between devices: 11.4 us -> 9.22 us  [hop(): return lax.ppermute(x, ('rows', 'cols'), pairs)]
    ppermute x3 -> x4, waiting for transfers between devices: 1.5 us -> 1.78 us  [partner(): return lax.ppermute(x, axis, [(i, i ^ offset) for i in range(count)])]
  transfers between devices with their start and end apart: 11 -> 11, of which waited for: 11 -> 10; matrix products, arithmetic and copies ran while one was open for 0% -> 0% of each run, Pallas kernels for 6% -> 5%
where the time goes in v10:
time: 32.6 us; the launch traced here: 32.4 us
  waiting for transfers between devices  14.2 us (44%)
  starting transfers between devices  13.7 us (42%)
  Pallas kernels  3.8 us (12%)
  between operations  0.68 us (2%)
    ppermute x7, waiting for transfers between devices, hop(): return lax.ppermute(x, ('rows', 'cols'), pairs)  12.4 us
    ppermute x7, starting transfers between devices, hop(): return lax.ppermute(x, ('rows', 'cols'), pairs)  9.22 us
    ppermute x4, starting transfers between devices, partner(): return lax.ppermute(x, axis, [(i, i ^ offset) for i in range(count)])  4.48 us
    ppermute x4, waiting for transfers between devices, partner(): return lax.ppermute(x, axis, [(i, i ^ offset) for i in range(count)])  1.78 us
    pallas_call x1, Pallas kernels, shards(): pl.pallas_call(functools.partial(finish_kernel, rounds, nblock, phases, r...  1.7 us
    pallas_call x1, Pallas kernels, shards(): pl.pallas_call(functools.partial(split_kernel, rounds, nblock), out_shape...  1.14 us
  transfers between devices with their start and end apart: 11, of which 10 were waited for; matrix products, arithmetic and copies ran while one was open for 0% of the time, Pallas kernels for 5%

profile of v10, /device:TPU:0, one launch (start us, length us, event | category | flops | bytes accessed | tf_op | source)
XLA Modules:
  0.0 32.4 jit_solution(5869973292421881116)
XLA Ops:
  0.6 0.5 %collective-permute-start = (bf16[2048,128]{1,0:T(8,128)(2,1)}, bf16[2048,128]{1,0:T(8,128)(2,1)S(1)}, u32[]{:S(2)}, u32[]{:S(2)}) collective-permute-start(bf16[2048,128]{1,0:T(8,128)(2,1)} %bitcast.7), channel_id=1, source_target_pairs={{0,1},{1,0},{2,3},{3,2},{4,5},{5,4},{6,7},{7,6},{8,9},{9,8},{10,11... | collective-permute-start | bytes 1572872 | tf_op jit(solution)/shard_map/ppermute | solution.py:17
  1.1 1.1 %split.1 = (bf16[1024,128]{1,0:T(8,128)(2,1)S(1)}, bf16[1024,128]{1,0:T(8,128)(2,1)S(1)}, f32[8,8,128]{2,1,0:T(8,128)S(1)}) custom-call(f32[2,2,2]{2,1,0:T(2,128)} %scale_hbm.1, bf16[2048,128]{1,0:T(8,128)(2,1)} %bitcast.8), custom_call_target="tpu_custom_call" | custom-call | tf_op jit(solution)/shard_map/split/pallas_call | solution.py:345
  2.3 0.6 %collective-permute-done.recv_ref.odd_ref = bf16[2048,128]{1,0:T(8,128)(2,1)S(1)} collective-permute-done((bf16[2048,128]{1,0:T(8,128)(2,1)}, bf16[2048,128]{1,0:T(8,128)(2,1)S(1)}, u32[]{:S(2)}, u32[]{:S(2)}) %collective-permute-start) | collective-permute-done | bytes 524320 | tf_op jit(solution)/shard_map/ppermute | solution.py:17
  2.9 0.5 %products.1 = (f32[136,128]{1,0:T(8,128)S(1)}, f32[136,128]{1,0:T(8,128)S(1)}) custom-call(f32[8,8,128]{2,1,0:T(8,128)S(1)} %get-tuple-element.15.factor_ref, bf16[1024,128]{1,0:T(8,128)(2,1)S(1)} %get-tuple-element.16.first_ref, bf16[1024,128]{1,0:T(8,128)(2,1)S(1)} %get-tuple-element.17.own_ref, bf16[2048,128]{1,0:T(8,128)(2,1)S(1)} %collective-permute-done.recv_ref.odd_ref), custom_call_target="tpu_custom_call" | custom-call | tf_op jit(solution)/shard_map/products/pallas_call | solution.py:360
  3.4 4.0 %collective-permute-start.2 = (f32[136,128]{1,0:T(8,128)S(1)}, f32[136,128]{1,0:T(8,128)S(1)}, u32[]{:S(2)}, u32[]{:S(2)}) collective-permute-start(f32[136,128]{1,0:T(8,128)S(1)} %get-tuple-element.18), channel_id=1, source_target_pairs={{0,16},{1,5},{2,18},{3,7},{4,20},{5,1},{6,22},{7,3},{8,24},{9,13},... | collective-permute-start | bytes 208904 | tf_op jit(solution)/shard_map/ppermute | solution.py:41
  7.4 1.3 %collective-permute-start.3 = (f32[136,128]{1,0:T(8,128)S(1)}, f32[136,128]{1,0:T(8,128)S(1)}, u32[]{:S(2)}, u32[]{:S(2)}) collective-permute-start(f32[136,128]{1,0:T(8,128)S(1)} %get-tuple-element.19), channel_id=1, source_target_pairs={{0,24},{1,7},{2,26},{3,5},{4,28},{5,3},{6,30},{7,1},{8,16},{9,15},... | collective-permute-start | bytes 208904 | tf_op jit(solution)/shard_map/ppermute | solution.py:41
  8.8 0.2 collective-permute-start.1
  9.0 0.7 %collective-permute-done.2 = f32[136,128]{1,0:T(8,128)S(1)} collective-permute-done((f32[136,128]{1,0:T(8,128)S(1)}, f32[136,128]{1,0:T(8,128)S(1)}, u32[]{:S(2)}, u32[]{:S(2)}) %collective-permute-start.2) | collective-permute-done | bytes 69664 | tf_op jit(solution)/shard_map/ppermute | solution.py:41
  9.7 3.9 %collective-permute-done.3 = f32[136,128]{1,0:T(8,128)S(1)} collective-permute-done((f32[136,128]{1,0:T(8,128)S(1)}, f32[136,128]{1,0:T(8,128)S(1)}, u32[]{:S(2)}, u32[]{:S(2)}) %collective-permute-start.3) | collective-permute-done | bytes 69664 | tf_op jit(solution)/shard_map/ppermute | solution.py:41
  13.6 0.2 collective-permute-done.1
  13.8 2.5 %collective-permute-start.6 = (f32[136,128]{1,0:T(8,128)S(1)}, f32[136,128]{1,0:T(8,128)S(1)}, u32[]{:S(2)}, u32[]{:S(2)}) collective-permute-start(f32[136,128]{1,0:T(8,128)S(1)} %add_add_fusion.1), channel_id=1, source_target_pairs={{0,6},{1,25},{2,4},{3,27},{4,2},{5,29},{6,0},{7,31},{8,14},{9,17},... | collective-permute-start | bytes 208904 | tf_op jit(solution)/shard_map/ppermute | solution.py:41
  16.3 0.5 %collective-permute-start.5 = (f32[136,128]{1,0:T(8,128)S(1)}, f32[136,128]{1,0:T(8,128)S(1)}, u32[]{:S(2)}, u32[]{:S(2)}) collective-permute-start(f32[136,128]{1,0:T(8,128)S(1)} %add_add_fusion.1), channel_id=1, source_target_pairs={{0,4},{1,17},{2,6},{3,19},{4,0},{5,21},{6,2},{7,23},{8,12},{9,25},... | collective-permute-start | bytes 208904 | tf_op jit(solution)/shard_map/ppermute | solution.py:41
  16.8 0.5 %collective-permute-start.4 = (f32[136,128]{1,0:T(8,128)S(1)}, f32[136,128]{1,0:T(8,128)S(1)}, u32[]{:S(2)}, u32[]{:S(2)}) collective-permute-start(f32[136,128]{1,0:T(8,128)S(1)} %add_add_fusion.1), channel_id=1, source_target_pairs={{0,2},{1,9},{2,0},{3,11},{4,6},{5,13},{6,4},{7,15},{8,10},{9,1},{1... | collective-permute-start | bytes 208904 | tf_op jit(solution)/shard_map/ppermute | solution.py:41
  17.4 0.5 %spread.1.lead_ref = bf16[2048,256]{1,0:T(8,128)(2,1)S(1)} custom-call(bf16[2048,128]{1,0:T(8,128)(2,1)S(1)} %bitcast.9, bf16[2048,128]{1,0:T(8,128)(2,1)S(1)} %collective-permute-done.recv_ref.odd_ref), custom_call_target="tpu_custom_call" | custom-call | tf_op jit(solution)/shard_map/spread/pallas_call | solution.py:377
  17.9 1.2 %collective-permute-done.6 = f32[136,128]{1,0:T(8,128)S(1)} collective-permute-done((f32[136,128]{1,0:T(8,128)S(1)}, f32[136,128]{1,0:T(8,128)S(1)}, u32[]{:S(2)}, u32[]{:S(2)}) %collective-permute-start.6) | collective-permute-done | bytes 69664 | tf_op jit(solution)/shard_map/ppermute | solution.py:41
  19.1 1.5 %collective-permute-done.5 = f32[136,128]{1,0:T(8,128)S(1)} collective-permute-done((f32[136,128]{1,0:T(8,128)S(1)}, f32[136,128]{1,0:T(8,128)S(1)}, u32[]{:S(2)}, u32[]{:S(2)}) %collective-permute-start.5) | collective-permute-done | bytes 69664 | tf_op jit(solution)/shard_map/ppermute | solution.py:41
  20.7 0.5 %collective-permute-done.4 = f32[136,128]{1,0:T(8,128)S(1)} collective-permute-done((f32[136,128]{1,0:T(8,128)S(1)}, f32[136,128]{1,0:T(8,128)S(1)}, u32[]{:S(2)}, u32[]{:S(2)}) %collective-permute-start.4) | collective-permute-done | bytes 69664 | tf_op jit(solution)/shard_map/ppermute | solution.py:41
  21.2 0.1 collective-permute-start.8
  21.3 4.3 %collective-permute-done.8.gathered_ref = f32[136,128]{1,0:T(8,128)S(1)} collective-permute-done((f32[136,128]{1,0:T(8,128)S(1)}, f32[136,128]{1,0:T(8,128)S(1)}, u32[]{:S(2)}, u32[]{:S(2)}) %collective-permute-start.8) | collective-permute-done | bytes 69664 | tf_op jit(solution)/shard_map/ppermute | solution.py:41
  25.6 3.9 %collective-permute-start.9 = (f32[128,128]{1,0:T(8,128)S(1)}, f32[128,128]{1,0:T(8,128)S(1)}, u32[]{:S(2)}, u32[]{:S(2)}) collective-permute-start(f32[128,128]{1,0:T(8,128)S(1)} %get-tuple-element.25), channel_id=1, source_target_pairs={{0,1},{1,0},{2,3},{3,2},{4,5},{5,4},{6,7},{7,6},{8,9},{9,8},{10,11... | collective-permute-start | bytes 196616 | tf_op jit(solution)/shard_map/ppermute | solution.py:17
  29.5 0.1 collective-permute-start.7
  29.5 0.8 %collective-permute-done.9.block_ref = f32[128,128]{1,0:T(8,128)S(1)} collective-permute-done((f32[128,128]{1,0:T(8,128)S(1)}, f32[128,128]{1,0:T(8,128)S(1)}, u32[]{:S(2)}, u32[]{:S(2)}) %collective-permute-start.9) | collective-permute-done | bytes 65568 | tf_op jit(solution)/shard_map/ppermute | solution.py:17
  30.4 0.4 %collective-permute-done.7.recv_ref = f32[128,128]{1,0:T(8,128)S(1)} collective-permute-done((f32[128,128]{1,0:T(8,128)S(1)}, f32[128,128]{1,0:T(8,128)S(1)}, u32[]{:S(2)}, u32[]{:S(2)}) %collective-permute-start.7) | collective-permute-done | bytes 65568 | tf_op jit(solution)/shard_map/ppermute | solution.py:17
  30.7 1.7 %finish.1 = (f32[256,128]{1,0:T(8,128)}, bf16[2048,128]{1,0:T(8,128)(2,1)}) custom-call(f32[8,8,128]{2,1,0:T(8,128)S(1)} %get-tuple-element.15.factor_ref, bf16[2048,128]{1,0:T(8,128)(2,1)S(1)} %bitcast.10, bf16[2048,256]{1,0:T(8,128)(2,1)S(1)} %spread.1.lead_ref, f32[128,128]{1,0:T(8,128)S(1)} %get-tuple-element.24.kept_ref, ...), custom_call_target="tpu_custom_call" | custom-call | tf_op jit(solution)/shard_map/finish/pallas_call | solution.py:404
  (7 shorter events, 0.1 us)
Async XLA Ops:
  0.6 2.3 %collective-permute-start = (bf16[2048,128]{1,0:T(8,128)(2,1)}, bf16[2048,128]{1,0:T(8,128)(2,1)S(1)}, u32[]{:S(2)}, u32[]{:S(2)}) collective-permute-start(bf16[2048,128]{1,0:T(8,128)(2,1)} %bitcast.7), channel_id=1, source_target_pairs={{0,1},{1,0},{2,3},{3,2},{4,5},{5,4},{6,7},{7,6},{8,9},{9,8},{10,11... | collective-permute-start | bytes 1572872 | tf_op jit(solution)/shard_map/ppermute | solution.py:17
  2.9 14.5 %copy-start = (bf16[1024,1,2,128]{3,2,1,0:T(2,128)(2,1)S(1)}, bf16[1024,1,2,128]{3,2,1,0:T(2,128)(2,1)}, u32[]{:S(2)}) copy-start(bf16[1024,1,2,128]{3,2,1,0:T(2,128)(2,1)} %param.2) | copy-start | bytes 1572868
  3.4 6.3 %collective-permute-start.2 = (f32[136,128]{1,0:T(8,128)S(1)}, f32[136,128]{1,0:T(8,128)S(1)}, u32[]{:S(2)}, u32[]{:S(2)}) collective-permute-start(f32[136,128]{1,0:T(8,128)S(1)} %get-tuple-element.18), channel_id=1, source_target_pairs={{0,16},{1,5},{2,18},{3,7},{4,20},{5,1},{6,22},{7,3},{8,24},{9,13},... | collective-permute-start | bytes 208904 | tf_op jit(solution)/shard_map/ppermute | solution.py:41
  7.4 6.2 %collective-permute-start.3 = (f32[136,128]{1,0:T(8,128)S(1)}, f32[136,128]{1,0:T(8,128)S(1)}, u32[]{:S(2)}, u32[]{:S(2)}) collective-permute-start(f32[136,128]{1,0:T(8,128)S(1)} %get-tuple-element.19), channel_id=1, source_target_pairs={{0,24},{1,7},{2,26},{3,5},{4,28},{5,3},{6,30},{7,1},{8,16},{9,15},... | collective-permute-start | bytes 208904 | tf_op jit(solution)/shard_map/ppermute | solution.py:41
  8.8 5.1 %collective-permute-start.1 = (f32[136,128]{1,0:T(8,128)S(1)}, f32[136,128]{1,0:T(8,128)S(1)}, u32[]{:S(2)}, u32[]{:S(2)}) collective-permute-start(f32[136,128]{1,0:T(8,128)S(1)} %get-tuple-element.19), channel_id=1, source_target_pairs={{0,8},{1,3},{2,10},{3,1},{4,12},{5,7},{6,14},{7,5},{8,0},{9,11},{1... | collective-permute-start | bytes 208904 | tf_op jit(solution)/shard_map/ppermute | solution.py:41
  13.8 5.3 %collective-permute-start.6 = (f32[136,128]{1,0:T(8,128)S(1)}, f32[136,128]{1,0:T(8,128)S(1)}, u32[]{:S(2)}, u32[]{:S(2)}) collective-permute-start(f32[136,128]{1,0:T(8,128)S(1)} %add_add_fusion.1), channel_id=1, source_target_pairs={{0,6},{1,25},{2,4},{3,27},{4,2},{5,29},{6,0},{7,31},{8,14},{9,17},... | collective-permute-start | bytes 208904 | tf_op jit(solution)/shard_map/ppermute | solution.py:41
  16.3 4.3 %collective-permute-start.5 = (f32[136,128]{1,0:T(8,128)S(1)}, f32[136,128]{1,0:T(8,128)S(1)}, u32[]{:S(2)}, u32[]{:S(2)}) collective-permute-start(f32[136,128]{1,0:T(8,128)S(1)} %add_add_fusion.1), channel_id=1, source_target_pairs={{0,4},{1,17},{2,6},{3,19},{4,0},{5,21},{6,2},{7,23},{8,12},{9,25},... | collective-permute-start | bytes 208904 | tf_op jit(solution)/shard_map/ppermute | solution.py:41
  16.8 4.3 %collective-permute-start.4 = (f32[136,128]{1,0:T(8,128)S(1)}, f32[136,128]{1,0:T(8,128)S(1)}, u32[]{:S(2)}, u32[]{:S(2)}) collective-permute-start(f32[136,128]{1,0:T(8,128)S(1)} %add_add_fusion.1), channel_id=1, source_target_pairs={{0,2},{1,9},{2,0},{3,11},{4,6},{5,13},{6,4},{7,15},{8,10},{9,1},{1... | collective-permute-start | bytes 208904 | tf_op jit(solution)/shard_map/ppermute | solution.py:41
  21.2 4.4 %collective-permute-start.8 = (f32[136,128]{1,0:T(8,128)S(1)}, f32[136,128]{1,0:T(8,128)S(1)}, u32[]{:S(2)}, u32[]{:S(2)}) collective-permute-start(f32[136,128]{1,0:T(8,128)S(1)} %add_add_fusion.sums_ref.same_ref), channel_id=1, source_target_pairs={{0,8},{1,3},{2,10},{3,1},{4,12},{5,7},{6,14},{7,5},{8,0},{9,11},{1... | collective-permute-start | bytes 208904 | tf_op jit(solution)/shard_map/ppermute | solution.py:41
  25.6 5.2 %collective-permute-start.10 = (f32[136,128]{1,0:T(8,128)S(1)}, f32[136,128]{1,0:T(8,128)S(1)}, u32[]{:S(2)}, u32[]{:S(2)}) collective-permute-start(f32[136,128]{1,0:T(8,128)S(1)} %collective-permute-done.8.gathered_ref), channel_id=1, source_target_pairs={{0,1},{1,0},{2,3},{3,2},{4,5},{5,4},{6,7},{7,6},{8,9},{9,8},{10,11... | collective-permute-start | bytes 208904 | tf_op jit(solution)/shard_map/ppermute | solution.py:17
  25.6 4.8 %collective-permute-start.9 = (f32[128,128]{1,0:T(8,128)S(1)}, f32[128,128]{1,0:T(8,128)S(1)}, u32[]{:S(2)}, u32[]{:S(2)}) collective-permute-start(f32[128,128]{1,0:T(8,128)S(1)} %get-tuple-element.25), channel_id=1, source_target_pairs={{0,1},{1,0},{2,3},{3,2},{4,5},{5,4},{6,7},{7,6},{8,9},{9,8},{10,11... | collective-permute-start | bytes 196616 | tf_op jit(solution)/shard_map/ppermute | solution.py:17
  29.5 1.3 %collective-permute-start.7 = (f32[128,128]{1,0:T(8,128)S(1)}, f32[128,128]{1,0:T(8,128)S(1)}, u32[]{:S(2)}, u32[]{:S(2)}) collective-permute-start(f32[128,128]{1,0:T(8,128)S(1)} %get-tuple-element.24.kept_ref), channel_id=1, source_target_pairs={{0,1},{1,0},{2,3},{3,2},{4,5},{5,4},{6,7},{7,6},{8,9},{9,8},{10,11... | collective-permute-start | bytes 196616 | tf_op jit(solution)/shard_map/ppermute | solution.py:17

commit v11 on v10

--- a/solution.py
+++ b/solution.py
@@ -399,7 +399,8 @@
     inverse = among_pairs(inverse, n_cols, group, 1)
     swapped = partner(inverse, "cols", n_cols, 1)
     blocks = partner(block, "cols", n_cols, 1)
-    crossed = partner(gathered, "cols", n_cols, 1)
+    gathered, _ = lax.optimization_barrier((gathered, block))
+    crossed = partner(gathered[: width // 2 + 8], "cols", n_cols, 1)
     chunks = 2 * nblock
     coef, updated = pl.pallas_call(
         functools.partial(finish_kernel, rounds, nblock, phases, root, chunks),

time: 32.6 us -> 28.6 us (0.88)
  starting transfers between devices: 13.7 us -> 11.2 us
  waiting for transfers between devices: 14.2 us -> 12.7 us
    ppermute x4, starting transfers between devices: 4.48 us -> 2.02 us  [partner(): return lax.ppermute(x, axis, [(i, i ^ offset) for i in range(count)])]
    ppermute x7, waiting for transfers between devices: 12.4 us -> 10.9 us  [hop(): return lax.ppermute(x, ('rows', 'cols'), pairs)]
  transfers between devices with their start and end apart: 11 -> 11, of which waited for: 10 -> 9; matrix products, arithmetic and copies ran while one was open for 0% -> 0% of each run, Pallas kernels for 5% -> 6%
where the time goes in v11:
time: 28.6 us; the launch traced here: 28.5 us
  waiting for transfers between devices  12.7 us (44%)
  starting transfers between devices  11.2 us (39%)
  Pallas kernels  3.82 us (13%)
  between operations  0.69 us (2%)
    ppermute x7, waiting for transfers between devices, hop(): return lax.ppermute(x, ('rows', 'cols'), pairs)  10.9 us
    ppermute x7, starting transfers between devices, hop(): return lax.ppermute(x, ('rows', 'cols'), pairs)  9.22 us
    ppermute x4, starting transfers between devices, partner(): return lax.ppermute(x, axis, [(i, i ^ offset) for i in range(count)])  2.02 us
    ppermute x4, waiting for transfers between devices, partner(): return lax.ppermute(x, axis, [(i, i ^ offset) for i in range(count)])  1.8 us
    pallas_call x1, Pallas kernels, shards(): pl.pallas_call(functools.partial(finish_kernel, rounds, nblock, phases, r...  1.69 us
    pallas_call x1, Pallas kernels, shards(): pl.pallas_call(functools.partial(split_kernel, rounds, nblock), out_shape...  1.14 us
  transfers between devices with their start and end apart: 11, of which 9 were waited for; matrix products, arithmetic and copies ran while one was open for 0% of the time, Pallas kernels for 6%

profile of v11, /device:TPU:0, one launch (start us, length us, event | category | flops | bytes accessed | tf_op | source)
XLA Modules:
  0.0 28.5 jit_solution(17429653436726654790)
XLA Ops:
  0.6 0.5 %collective-permute-start = (bf16[2048,128]{1,0:T(8,128)(2,1)}, bf16[2048,128]{1,0:T(8,128)(2,1)S(1)}, u32[]{:S(2)}, u32[]{:S(2)}) collective-permute-start(bf16[2048,128]{1,0:T(8,128)(2,1)} %bitcast.7), channel_id=1, source_target_pairs={{0,1},{1,0},{2,3},{3,2},{4,5},{5,4},{6,7},{7,6},{8,9},{9,8},{10,11... | collective-permute-start | bytes 1572872 | tf_op jit(solution)/shard_map/ppermute | solution.py:17
  1.1 1.1 %split.1 = (bf16[1024,128]{1,0:T(8,128)(2,1)S(1)}, bf16[1024,128]{1,0:T(8,128)(2,1)S(1)}, f32[8,8,128]{2,1,0:T(8,128)S(1)}) custom-call(f32[2,2,2]{2,1,0:T(2,128)} %scale_hbm.1, bf16[2048,128]{1,0:T(8,128)(2,1)} %bitcast.8), custom_call_target="tpu_custom_call" | custom-call | tf_op jit(solution)/shard_map/split/pallas_call | solution.py:345
  2.3 0.6 %collective-permute-done.recv_ref.odd_ref = bf16[2048,128]{1,0:T(8,128)(2,1)S(1)} collective-permute-done((bf16[2048,128]{1,0:T(8,128)(2,1)}, bf16[2048,128]{1,0:T(8,128)(2,1)S(1)}, u32[]{:S(2)}, u32[]{:S(2)}) %collective-permute-start) | collective-permute-done | bytes 524320 | tf_op jit(solution)/shard_map/ppermute | solution.py:17
  2.9 0.5 %products.1 = (f32[136,128]{1,0:T(8,128)S(1)}, f32[136,128]{1,0:T(8,128)S(1)}) custom-call(f32[8,8,128]{2,1,0:T(8,128)S(1)} %get-tuple-element.16.factor_ref, bf16[1024,128]{1,0:T(8,128)(2,1)S(1)} %get-tuple-element.17.first_ref, bf16[1024,128]{1,0:T(8,128)(2,1)S(1)} %get-tuple-element.18.own_ref, bf16[2048,128]{1,0:T(8,128)(2,1)S(1)} %collective-permute-done.recv_ref.odd_ref), custom_call_target="tpu_custom_call" | custom-call | tf_op jit(solution)/shard_map/products/pallas_call | solution.py:360
  3.4 4.0 %collective-permute-start.2 = (f32[136,128]{1,0:T(8,128)S(1)}, f32[136,128]{1,0:T(8,128)S(1)}, u32[]{:S(2)}, u32[]{:S(2)}) collective-permute-start(f32[136,128]{1,0:T(8,128)S(1)} %get-tuple-element.19), channel_id=1, source_target_pairs={{0,16},{1,5},{2,18},{3,7},{4,20},{5,1},{6,22},{7,3},{8,24},{9,13},... | collective-permute-start | bytes 208904 | tf_op jit(solution)/shard_map/ppermute | solution.py:41
  7.4 1.3 %collective-permute-start.3 = (f32[136,128]{1,0:T(8,128)S(1)}, f32[136,128]{1,0:T(8,128)S(1)}, u32[]{:S(2)}, u32[]{:S(2)}) collective-permute-start(f32[136,128]{1,0:T(8,128)S(1)} %get-tuple-element.20), channel_id=1, source_target_pairs={{0,24},{1,7},{2,26},{3,5},{4,28},{5,3},{6,30},{7,1},{8,16},{9,15},... | collective-permute-start | bytes 208904 | tf_op jit(solution)/shard_map/ppermute | solution.py:41
  8.8 0.2 collective-permute-start.1
  9.0 0.7 %collective-permute-done.2 = f32[136,128]{1,0:T(8,128)S(1)} collective-permute-done((f32[136,128]{1,0:T(8,128)S(1)}, f32[136,128]{1,0:T(8,128)S(1)}, u32[]{:S(2)}, u32[]{:S(2)}) %collective-permute-start.2) | collective-permute-done | bytes 69664 | tf_op jit(solution)/shard_map/ppermute | solution.py:41
  9.7 3.9 %collective-permute-done.3 = f32[136,128]{1,0:T(8,128)S(1)} collective-permute-done((f32[136,128]{1,0:T(8,128)S(1)}, f32[136,128]{1,0:T(8,128)S(1)}, u32[]{:S(2)}, u32[]{:S(2)}) %collective-permute-start.3) | collective-permute-done | bytes 69664 | tf_op jit(solution)/shard_map/ppermute | solution.py:41
  13.6 0.2 collective-permute-done.1
  13.8 2.5 %collective-permute-start.6 = (f32[136,128]{1,0:T(8,128)S(1)}, f32[136,128]{1,0:T(8,128)S(1)}, u32[]{:S(2)}, u32[]{:S(2)}) collective-permute-start(f32[136,128]{1,0:T(8,128)S(1)} %add_add_fusion.1), channel_id=1, source_target_pairs={{0,6},{1,25},{2,4},{3,27},{4,2},{5,29},{6,0},{7,31},{8,14},{9,17},... | collective-permute-start | bytes 208904 | tf_op jit(solution)/shard_map/ppermute | solution.py:41
  16.3 0.5 %collective-permute-start.5 = (f32[136,128]{1,0:T(8,128)S(1)}, f32[136,128]{1,0:T(8,128)S(1)}, u32[]{:S(2)}, u32[]{:S(2)}) collective-permute-start(f32[136,128]{1,0:T(8,128)S(1)} %add_add_fusion.1), channel_id=1, source_target_pairs={{0,4},{1,17},{2,6},{3,19},{4,0},{5,21},{6,2},{7,23},{8,12},{9,25},... | collective-permute-start | bytes 208904 | tf_op jit(solution)/shard_map/ppermute | solution.py:41
  16.8 0.5 %collective-permute-start.4 = (f32[136,128]{1,0:T(8,128)S(1)}, f32[136,128]{1,0:T(8,128)S(1)}, u32[]{:S(2)}, u32[]{:S(2)}) collective-permute-start(f32[136,128]{1,0:T(8,128)S(1)} %add_add_fusion.1), channel_id=1, source_target_pairs={{0,2},{1,9},{2,0},{3,11},{4,6},{5,13},{6,4},{7,15},{8,10},{9,1},{1... | collective-permute-start | bytes 208904 | tf_op jit(solution)/shard_map/ppermute | solution.py:41
  17.4 0.5 %spread.1.lead_ref = bf16[2048,256]{1,0:T(8,128)(2,1)S(1)} custom-call(bf16[2048,128]{1,0:T(8,128)(2,1)S(1)} %bitcast.9, bf16[2048,128]{1,0:T(8,128)(2,1)S(1)} %collective-permute-done.recv_ref.odd_ref), custom_call_target="tpu_custom_call" | custom-call | tf_op jit(solution)/shard_map/spread/pallas_call | solution.py:377
  17.9 1.2 %collective-permute-done.6 = f32[136,128]{1,0:T(8,128)S(1)} collective-permute-done((f32[136,128]{1,0:T(8,128)S(1)}, f32[136,128]{1,0:T(8,128)S(1)}, u32[]{:S(2)}, u32[]{:S(2)}) %collective-permute-start.6) | collective-permute-done | bytes 69664 | tf_op jit(solution)/shard_map/ppermute | solution.py:41
  19.1 1.5 %collective-permute-done.5 = f32[136,128]{1,0:T(8,128)S(1)} collective-permute-done((f32[136,128]{1,0:T(8,128)S(1)}, f32[136,128]{1,0:T(8,128)S(1)}, u32[]{:S(2)}, u32[]{:S(2)}) %collective-permute-start.5) | collective-permute-done | bytes 69664 | tf_op jit(solution)/shard_map/ppermute | solution.py:41
  20.7 0.5 %collective-permute-done.4 = f32[136,128]{1,0:T(8,128)S(1)} collective-permute-done((f32[136,128]{1,0:T(8,128)S(1)}, f32[136,128]{1,0:T(8,128)S(1)}, u32[]{:S(2)}, u32[]{:S(2)}) %collective-permute-start.4) | collective-permute-done | bytes 69664 | tf_op jit(solution)/shard_map/ppermute | solution.py:41
  21.2 0.1 collective-permute-start.8
  21.3 1.4 %collective-permute-start.7 = (f32[128,128]{1,0:T(8,128)S(1)}, f32[128,128]{1,0:T(8,128)S(1)}, u32[]{:S(2)}, u32[]{:S(2)}) collective-permute-start(f32[128,128]{1,0:T(8,128)S(1)} %get-tuple-element.25.kept_ref), channel_id=1, source_target_pairs={{0,1},{1,0},{2,3},{3,2},{4,5},{5,4},{6,7},{7,6},{8,9},{9,8},{10,11... | collective-permute-start | bytes 196616 | tf_op jit(solution)/shard_map/ppermute | solution.py:17
  22.7 0.1 collective-permute-start.9
  22.8 2.8 %collective-permute-done.8.gathered_ref = f32[136,128]{1,0:T(8,128)S(1)} collective-permute-done((f32[136,128]{1,0:T(8,128)S(1)}, f32[136,128]{1,0:T(8,128)S(1)}, u32[]{:S(2)}, u32[]{:S(2)}) %collective-permute-start.8) | collective-permute-done | bytes 69664 | tf_op jit(solution)/shard_map/ppermute | solution.py:41
  25.6 0.0 collective-permute-start.10
  25.6 1.2 %collective-permute-done.10.across_ref = f32[72,128]{1,0:T(8,128)S(1)} collective-permute-done((f32[72,128]{1,0:T(8,128)S(1)}, f32[72,128]{1,0:T(8,128)S(1)}, u32[]{:S(2)}, u32[]{:S(2)}) %collective-permute-start.10) | collective-permute-done | bytes 36896 | tf_op jit(solution)/shard_map/ppermute | solution.py:17
  26.8 1.7 %finish.1 = (f32[256,128]{1,0:T(8,128)}, bf16[2048,128]{1,0:T(8,128)(2,1)}) custom-call(f32[8,8,128]{2,1,0:T(8,128)S(1)} %get-tuple-element.16.factor_ref, bf16[2048,128]{1,0:T(8,128)(2,1)S(1)} %bitcast.10, bf16[2048,256]{1,0:T(8,128)(2,1)S(1)} %spread.1.lead_ref, f32[128,128]{1,0:T(8,128)S(1)} %get-tuple-element.25.kept_ref, ...), custom_call_target="tpu_custom_call" | custom-call | tf_op jit(solution)/shard_map/finish/pallas_call | solution.py:405
  (8 shorter events, 0.1 us)
Async XLA Ops:
  0.6 2.3 %collective-permute-start = (bf16[2048,128]{1,0:T(8,128)(2,1)}, bf16[2048,128]{1,0:T(8,128)(2,1)S(1)}, u32[]{:S(2)}, u32[]{:S(2)}) collective-permute-start(bf16[2048,128]{1,0:T(8,128)(2,1)} %bitcast.7), channel_id=1, source_target_pairs={{0,1},{1,0},{2,3},{3,2},{4,5},{5,4},{6,7},{7,6},{8,9},{9,8},{10,11... | collective-permute-start | bytes 1572872 | tf_op jit(solution)/shard_map/ppermute | solution.py:17
  2.9 14.5 %copy-start = (bf16[1024,1,2,128]{3,2,1,0:T(2,128)(2,1)S(1)}, bf16[1024,1,2,128]{3,2,1,0:T(2,128)(2,1)}, u32[]{:S(2)}) copy-start(bf16[1024,1,2,128]{3,2,1,0:T(2,128)(2,1)} %param.2) | copy-start | bytes 1572868
  3.4 6.3 %collective-permute-start.2 = (f32[136,128]{1,0:T(8,128)S(1)}, f32[136,128]{1,0:T(8,128)S(1)}, u32[]{:S(2)}, u32[]{:S(2)}) collective-permute-start(f32[136,128]{1,0:T(8,128)S(1)} %get-tuple-element.19), channel_id=1, source_target_pairs={{0,16},{1,5},{2,18},{3,7},{4,20},{5,1},{6,22},{7,3},{8,24},{9,13},... | collective-permute-start | bytes 208904 | tf_op jit(solution)/shard_map/ppermute | solution.py:41
  7.4 6.2 %collective-permute-start.3 = (f32[136,128]{1,0:T(8,128)S(1)}, f32[136,128]{1,0:T(8,128)S(1)}, u32[]{:S(2)}, u32[]{:S(2)}) collective-permute-start(f32[136,128]{1,0:T(8,128)S(1)} %get-tuple-element.20), channel_id=1, source_target_pairs={{0,24},{1,7},{2,26},{3,5},{4,28},{5,3},{6,30},{7,1},{8,16},{9,15},... | collective-permute-start | bytes 208904 | tf_op jit(solution)/shard_map/ppermute | solution.py:41
  8.8 5.1 %collective-permute-start.1 = (f32[136,128]{1,0:T(8,128)S(1)}, f32[136,128]{1,0:T(8,128)S(1)}, u32[]{:S(2)}, u32[]{:S(2)}) collective-permute-start(f32[136,128]{1,0:T(8,128)S(1)} %get-tuple-element.20), channel_id=1, source_target_pairs={{0,8},{1,3},{2,10},{3,1},{4,12},{5,7},{6,14},{7,5},{8,0},{9,11},{1... | collective-permute-start | bytes 208904 | tf_op jit(solution)/shard_map/ppermute | solution.py:41
  13.8 5.3 %collective-permute-start.6 = (f32[136,128]{1,0:T(8,128)S(1)}, f32[136,128]{1,0:T(8,128)S(1)}, u32[]{:S(2)}, u32[]{:S(2)}) collective-permute-start(f32[136,128]{1,0:T(8,128)S(1)} %add_add_fusion.1), channel_id=1, source_target_pairs={{0,6},{1,25},{2,4},{3,27},{4,2},{5,29},{6,0},{7,31},{8,14},{9,17},... | collective-permute-start | bytes 208904 | tf_op jit(solution)/shard_map/ppermute | solution.py:41
  16.3 4.3 %collective-permute-start.5 = (f32[136,128]{1,0:T(8,128)S(1)}, f32[136,128]{1,0:T(8,128)S(1)}, u32[]{:S(2)}, u32[]{:S(2)}) collective-permute-start(f32[136,128]{1,0:T(8,128)S(1)} %add_add_fusion.1), channel_id=1, source_target_pairs={{0,4},{1,17},{2,6},{3,19},{4,0},{5,21},{6,2},{7,23},{8,12},{9,25},... | collective-permute-start | bytes 208904 | tf_op jit(solution)/shard_map/ppermute | solution.py:41
  16.8 4.3 %collective-permute-start.4 = (f32[136,128]{1,0:T(8,128)S(1)}, f32[136,128]{1,0:T(8,128)S(1)}, u32[]{:S(2)}, u32[]{:S(2)}) collective-permute-start(f32[136,128]{1,0:T(8,128)S(1)} %add_add_fusion.1), channel_id=1, source_target_pairs={{0,2},{1,9},{2,0},{3,11},{4,6},{5,13},{6,4},{7,15},{8,10},{9,1},{1... | collective-permute-start | bytes 208904 | tf_op jit(solution)/shard_map/ppermute | solution.py:41
  21.2 4.4 %collective-permute-start.8 = (f32[136,128]{1,0:T(8,128)S(1)}, f32[136,128]{1,0:T(8,128)S(1)}, u32[]{:S(2)}, u32[]{:S(2)}) collective-permute-start(f32[136,128]{1,0:T(8,128)S(1)} %add_add_fusion.sums_ref.same_ref), channel_id=1, source_target_pairs={{0,8},{1,3},{2,10},{3,1},{4,12},{5,7},{6,14},{7,5},{8,0},{9,11},{1... | collective-permute-start | bytes 208904 | tf_op jit(solution)/shard_map/ppermute | solution.py:41
  21.3 4.3 %collective-permute-start.7 = (f32[128,128]{1,0:T(8,128)S(1)}, f32[128,128]{1,0:T(8,128)S(1)}, u32[]{:S(2)}, u32[]{:S(2)}) collective-permute-start(f32[128,128]{1,0:T(8,128)S(1)} %get-tuple-element.25.kept_ref), channel_id=1, source_target_pairs={{0,1},{1,0},{2,3},{3,2},{4,5},{5,4},{6,7},{7,6},{8,9},{9,8},{10,11... | collective-permute-start | bytes 196616 | tf_op jit(solution)/shard_map/ppermute | solution.py:17
  22.7 2.9 %collective-permute-start.9 = (f32[128,128]{1,0:T(8,128)S(1)}, f32[128,128]{1,0:T(8,128)S(1)}, u32[]{:S(2)}, u32[]{:S(2)}) collective-permute-start(f32[128,128]{1,0:T(8,128)S(1)} %get-tuple-element.26), channel_id=1, source_target_pairs={{0,1},{1,0},{2,3},{3,2},{4,5},{5,4},{6,7},{7,6},{8,9},{9,8},{10,11... | collective-permute-start | bytes 196616 | tf_op jit(solution)/shard_map/ppermute | solution.py:17
  25.6 1.2 %collective-permute-start.10 = (f32[72,128]{1,0:T(8,128)S(1)}, f32[72,128]{1,0:T(8,128)S(1)}, u32[]{:S(2)}, u32[]{:S(2)}) collective-permute-start(f32[72,128]{1,0:T(8,128)S(1)} %slice.3), channel_id=1, source_target_pairs={{0,1},{1,0},{2,3},{3,2},{4,5},{5,4},{6,7},{7,6},{8,9},{9,8},{10,11... | collective-permute-start | bytes 110600 | tf_op jit(solution)/shard_map/ppermute | solution.py:17

commit v12 on v9

--- a/solution.py
+++ b/solution.py
@@ -216,8 +216,8 @@
 
 
 def products_kernel(rounds, nblock, phases, factor_ref, first_ref, own_ref, recv_ref, *rest):
-    lead_ref = rest[:-4] if len(rest) == 4 else (*rest[:2], rest[-1])
-    same_ref, other_ref, wide, cross = rest if len(rest) == 4 else rest[2:-1]
+    lead_ref = () if len(rest) == 6 else (*rest[:2], rest[-1])
+    same_ref, other_ref, again_ref, fourth_ref, wide, cross = rest if len(rest) == 6 else rest[2:-1]
     group = lax.axis_index("cols")
     odd = group % 2
     digit = half_digit(phases, odd)
@@ -246,7 +246,7 @@
     packed = pack(out[:, :width])
     cross[:width, :] = out[:, :width]
     cross[width:, :] = out[:, width:]
-    for ref, place in ((same_ref, digit), (other_ref, 1 - digit)):
+    for ref, place in ((same_ref, digit), (other_ref, 1 - digit), (again_ref, 1 - digit), (fourth_ref, digit)):
         theirs = cross[pl.ds(pl.multiple_of(place * half, half), half), :]
         ref[:half, :] = jnp.where(group == 1, packed[:half, :], theirs)
         ref[half:height, :] = packed[half:, :]
@@ -361,9 +361,9 @@
     extra = () if n_cols == 2 else leads
     sent = pl.pallas_call(
         functools.partial(products_kernel, rounds, nblock, phases),
-        out_shape=[jax.ShapeDtypeStruct((payload, width), F32)] * 2,
+        out_shape=[jax.ShapeDtypeStruct((payload, width), F32)] * 4,
         in_specs=[VMEM] * (4 + len(extra)),
-        out_specs=[VMEM] * 2,
+        out_specs=[VMEM] * 4,
         scratch_shapes=[pltpu.VMEM((long, width), F32), pltpu.VMEM((2 * width, width), F32)]
         + [pltpu.VMEM((long, width), F32)] * (len(extra) // 2),
         compiler_params=params,
@@ -371,9 +371,9 @@
     )(factors, first, own, recv, *extra)
     sums = sent[0]
     for step, (_, base) in enumerate(phases):
-        source = sent if step == 0 else [sums] * 2
+        source = (sent[0], sent[1], sent[3], sent[2]) if step == 0 else [sums] * base
         others = [
-            hop(source[b % 2], n_rows, n_cols, lambda parity: b * order(phases, parity)[step][0]) for b in range(1, base)
+            hop(source[b], n_rows, n_cols, lambda parity: b * order(phases, parity)[step][0]) for b in (range(base - 1, 0, -1) if step == 0 else range(1, base))
         ]
         if step == len(phases) - 1:
             lead = pl.pallas_call(

time: 27.9 us -> 27.6 us (0.989)
  starting transfers between devices: 12.5 us -> 12.1 us
  waiting for transfers between devices: 10.4 us -> 10.8 us
    ppermute x8, starting transfers between devices: 11.4 us -> 11 us  [hop(): return lax.ppermute(x, ('rows', 'cols'), pairs)]
    ppermute x8, waiting for transfers between devices: 8.91 us -> 9.3 us  [hop(): return lax.ppermute(x, ('rows', 'cols'), pairs)]
  transfers between devices with their start and end apart: 11 -> 11, of which waited for: 11 -> 9; matrix products, arithmetic and copies ran while one was open for 0% -> 0% of each run, Pallas kernels for 6% -> 6%
where the time goes in v12:
time: 27.6 us; the launch traced here: 27.4 us
  starting transfers between devices  12.1 us (44%)
  waiting for transfers between devices  10.8 us (39%)
  Pallas kernels  3.8 us (14%)
  between operations  0.68 us (2%)
    ppermute x8, starting transfers between devices, hop(): return lax.ppermute(x, ('rows', 'cols'), pairs)  11 us
    ppermute x8, waiting for transfers between devices, hop(): return lax.ppermute(x, ('rows', 'cols'), pairs)  9.3 us
    pallas_call x1, Pallas kernels, shards(): pl.pallas_call(functools.partial(finish_kernel, rounds, nblock, phases, r...  1.69 us
    ppermute x3, waiting for transfers between devices, partner(): return lax.ppermute(x, axis, [(i, i ^ offset) for i in range(count)])  1.5 us
    pallas_call x1, Pallas kernels, shards(): pl.pallas_call(functools.partial(split_kernel, rounds, nblock), out_shape...  1.14 us
    ppermute x3, starting transfers between devices, partner(): return lax.ppermute(x, axis, [(i, i ^ offset) for i in range(count)])  1.03 us
  transfers between devices with their start and end apart: 11, of which 9 were waited for; matrix products, arithmetic and copies ran while one was open for 0% of the time, Pallas kernels for 6%

profile of v12, /device:TPU:0, one launch (start us, length us, event | category | flops | bytes accessed | tf_op | source)
XLA Modules:
  0.0 27.4 jit_solution(16413137835096830820)
XLA Ops:
  0.6 0.5 %collective-permute-start = (bf16[2048,128]{1,0:T(8,128)(2,1)}, bf16[2048,128]{1,0:T(8,128)(2,1)S(1)}, u32[]{:S(2)}, u32[]{:S(2)}) collective-permute-start(bf16[2048,128]{1,0:T(8,128)(2,1)} %bitcast.7), channel_id=1, source_target_pairs={{0,1},{1,0},{2,3},{3,2},{4,5},{5,4},{6,7},{7,6},{8,9},{9,8},{10,11... | collective-permute-start | bytes 1572872 | tf_op jit(solution)/shard_map/ppermute | solution.py:17
  1.1 1.1 %split.1 = (bf16[1024,128]{1,0:T(8,128)(2,1)S(1)}, bf16[1024,128]{1,0:T(8,128)(2,1)S(1)}, f32[8,8,128]{2,1,0:T(8,128)S(1)}) custom-call(f32[2,2,2]{2,1,0:T(2,128)} %scale_hbm.1, bf16[2048,128]{1,0:T(8,128)(2,1)} %bitcast.8), custom_call_target="tpu_custom_call" | custom-call | tf_op jit(solution)/shard_map/split/pallas_call | solution.py:347
  2.3 0.6 %collective-permute-done.recv_ref.odd_ref = bf16[2048,128]{1,0:T(8,128)(2,1)S(1)} collective-permute-done((bf16[2048,128]{1,0:T(8,128)(2,1)}, bf16[2048,128]{1,0:T(8,128)(2,1)S(1)}, u32[]{:S(2)}, u32[]{:S(2)}) %collective-permute-start) | collective-permute-done | bytes 524320 | tf_op jit(solution)/shard_map/ppermute | solution.py:17
  2.9 0.5 %products.1 = (f32[144,128]{1,0:T(8,128)S(1)}, f32[144,128]{1,0:T(8,128)S(1)}, f32[144,128]{1,0:T(8,128)S(1)}, f32[144,128]{1,0:T(8,128)S(1)}) custom-call(f32[8,8,128]{2,1,0:T(8,128)S(1)} %get-tuple-element.17.factor_ref, bf16[1024,128]{1,0:T(8,128)(2,1)S(1)} %get-tuple-element.18.first_ref, bf16[1024,128]{1,0:T(8,128)(2,1)S(1)} %get-tuple-element.19.own_ref, ...), custom_call_target="tpu_custom_call" | custom-call | tf_op jit(solution)/shard_map/products/pallas_call | solution.py:362
  3.4 5.0 %collective-permute-start.1 = (f32[144,128]{1,0:T(8,128)S(1)}, f32[144,128]{1,0:T(8,128)S(1)}, u32[]{:S(2)}, u32[]{:S(2)}) collective-permute-start(f32[144,128]{1,0:T(8,128)S(1)} %get-tuple-element.21), channel_id=1, source_target_pairs={{0,24},{1,7},{2,26},{3,5},{4,28},{5,3},{6,30},{7,1},{8,16},{9,15},... | collective-permute-start | bytes 221192 | tf_op jit(solution)/shard_map/ppermute | solution.py:41
  8.4 0.6 %collective-permute-start.3 = (f32[144,128]{1,0:T(8,128)S(1)}, f32[144,128]{1,0:T(8,128)S(1)}, u32[]{:S(2)}, u32[]{:S(2)}) collective-permute-start(f32[144,128]{1,0:T(8,128)S(1)} %get-tuple-element.23), channel_id=1, source_target_pairs={{0,8},{1,3},{2,10},{3,1},{4,12},{5,7},{6,14},{7,5},{8,0},{9,11},{1... | collective-permute-start | bytes 221192 | tf_op jit(solution)/shard_map/ppermute | solution.py:41
  9.1 1.8 %collective-permute-done.1 = f32[144,128]{1,0:T(8,128)S(1)} collective-permute-done((f32[144,128]{1,0:T(8,128)S(1)}, f32[144,128]{1,0:T(8,128)S(1)}, u32[]{:S(2)}, u32[]{:S(2)}) %collective-permute-start.1) | collective-permute-done | bytes 73760 | tf_op jit(solution)/shard_map/ppermute | solution.py:41
  10.9 2.8 %collective-permute-done.2 = f32[144,128]{1,0:T(8,128)S(1)} collective-permute-done((f32[144,128]{1,0:T(8,128)S(1)}, f32[144,128]{1,0:T(8,128)S(1)}, u32[]{:S(2)}, u32[]{:S(2)}) %collective-permute-start.2) | collective-permute-done | bytes 73760 | tf_op jit(solution)/shard_map/ppermute | solution.py:41
  13.7 0.0 collective-permute-done.3
  13.7 3.0 %collective-permute-start.6 = (f32[144,128]{1,0:T(8,128)S(1)}, f32[144,128]{1,0:T(8,128)S(1)}, u32[]{:S(2)}, u32[]{:S(2)}) collective-permute-start(f32[144,128]{1,0:T(8,128)S(1)} %add_add_fusion.1), channel_id=1, source_target_pairs={{0,6},{1,25},{2,4},{3,27},{4,2},{5,29},{6,0},{7,31},{8,14},{9,17},... | collective-permute-start | bytes 221192 | tf_op jit(solution)/shard_map/ppermute | solution.py:41
  16.7 0.2 collective-permute-start.5
  16.8 0.5 %collective-permute-start.4 = (f32[144,128]{1,0:T(8,128)S(1)}, f32[144,128]{1,0:T(8,128)S(1)}, u32[]{:S(2)}, u32[]{:S(2)}) collective-permute-start(f32[144,128]{1,0:T(8,128)S(1)} %add_add_fusion.1), channel_id=1, source_target_pairs={{0,2},{1,9},{2,0},{3,11},{4,6},{5,13},{6,4},{7,15},{8,10},{9,1},{1... | collective-permute-start | bytes 221192 | tf_op jit(solution)/shard_map/ppermute | solution.py:41
  17.3 0.5 %spread.1.lead_ref = bf16[2048,256]{1,0:T(8,128)(2,1)S(1)} custom-call(bf16[2048,128]{1,0:T(8,128)(2,1)S(1)} %bitcast.9, bf16[2048,128]{1,0:T(8,128)(2,1)S(1)} %collective-permute-done.recv_ref.odd_ref), custom_call_target="tpu_custom_call" | custom-call | tf_op jit(solution)/shard_map/spread/pallas_call | solution.py:379
  17.8 1.2 %collective-permute-done.6 = f32[144,128]{1,0:T(8,128)S(1)} collective-permute-done((f32[144,128]{1,0:T(8,128)S(1)}, f32[144,128]{1,0:T(8,128)S(1)}, u32[]{:S(2)}, u32[]{:S(2)}) %collective-permute-start.6) | collective-permute-done | bytes 73760 | tf_op jit(solution)/shard_map/ppermute | solution.py:41
  19.0 2.0 %collective-permute-done.5 = f32[144,128]{1,0:T(8,128)S(1)} collective-permute-done((f32[144,128]{1,0:T(8,128)S(1)}, f32[144,128]{1,0:T(8,128)S(1)}, u32[]{:S(2)}, u32[]{:S(2)}) %collective-permute-start.5) | collective-permute-done | bytes 73760 | tf_op jit(solution)/shard_map/ppermute | solution.py:41
  21.0 0.2 collective-permute-done.4
  21.2 0.7 %collective-permute-start.8 = (f32[144,128]{1,0:T(8,128)S(1)}, f32[144,128]{1,0:T(8,128)S(1)}, u32[]{:S(2)}, u32[]{:S(2)}) collective-permute-start(f32[144,128]{1,0:T(8,128)S(1)} %add_add_fusion.sums_ref.same_ref), channel_id=1, source_target_pairs={{0,8},{1,3},{2,10},{3,1},{4,12},{5,7},{6,14},{7,5},{8,0},{9,11},{1... | collective-permute-start | bytes 221192 | tf_op jit(solution)/shard_map/ppermute | solution.py:41
  21.9 1.1 %collective-permute-start.10 = (f32[136,128]{1,0:T(8,128)S(1)}, f32[136,128]{1,0:T(8,128)S(1)}, u32[]{:S(2)}, u32[]{:S(2)}) collective-permute-start(f32[136,128]{1,0:T(8,128)S(1)} %get-tuple-element.29), channel_id=1, source_target_pairs={{0,9},{1,2},{2,11},{3,0},{4,13},{5,6},{6,15},{7,4},{8,1},{9,10},{1... | collective-permute-start | bytes 208904 | tf_op jit(solution)/shard_map/ppermute | solution.py:41
  23.0 0.0 collective-permute-start.9
  23.0 0.5 %collective-permute-start.7 = (f32[128,128]{1,0:T(8,128)S(1)}, f32[128,128]{1,0:T(8,128)S(1)}, u32[]{:S(2)}, u32[]{:S(2)}) collective-permute-start(f32[128,128]{1,0:T(8,128)S(1)} %get-tuple-element.28.kept_ref), channel_id=1, source_target_pairs={{0,1},{1,0},{2,3},{3,2},{4,5},{5,4},{6,7},{7,6},{8,9},{9,8},{10,11... | collective-permute-start | bytes 196616 | tf_op jit(solution)/shard_map/ppermute | solution.py:17
  23.5 0.7 %collective-permute-done.9.block_ref = f32[128,128]{1,0:T(8,128)S(1)} collective-permute-done((f32[128,128]{1,0:T(8,128)S(1)}, f32[128,128]{1,0:T(8,128)S(1)}, u32[]{:S(2)}, u32[]{:S(2)}) %collective-permute-start.9) | collective-permute-done | bytes 65568 | tf_op jit(solution)/shard_map/ppermute | solution.py:17
  24.2 0.2 collective-permute-done.7.recv_ref
  24.4 1.3 %collective-permute-done.10.across_ref = f32[136,128]{1,0:T(8,128)S(1)} collective-permute-done((f32[136,128]{1,0:T(8,128)S(1)}, f32[136,128]{1,0:T(8,128)S(1)}, u32[]{:S(2)}, u32[]{:S(2)}) %collective-permute-start.10) | collective-permute-done | bytes 69664 | tf_op jit(solution)/shard_map/ppermute | solution.py:41
  25.7 1.7 %finish.1 = (f32[256,128]{1,0:T(8,128)}, bf16[2048,128]{1,0:T(8,128)(2,1)}) custom-call(f32[8,8,128]{2,1,0:T(8,128)S(1)} %get-tuple-element.17.factor_ref, bf16[2048,128]{1,0:T(8,128)(2,1)S(1)} %bitcast.10, bf16[2048,256]{1,0:T(8,128)(2,1)S(1)} %spread.1.lead_ref, f32[128,128]{1,0:T(8,128)S(1)} %get-tuple-element.28.kept_ref, ...), custom_call_target="tpu_custom_call" | custom-call | tf_op jit(solution)/shard_map/finish/pallas_call | solution.py:406
  (8 shorter events, 0.1 us)
Async XLA Ops:
  0.6 2.3 %collective-permute-start = (bf16[2048,128]{1,0:T(8,128)(2,1)}, bf16[2048,128]{1,0:T(8,128)(2,1)S(1)}, u32[]{:S(2)}, u32[]{:S(2)}) collective-permute-start(bf16[2048,128]{1,0:T(8,128)(2,1)} %bitcast.7), channel_id=1, source_target_pairs={{0,1},{1,0},{2,3},{3,2},{4,5},{5,4},{6,7},{7,6},{8,9},{9,8},{10,11... | collective-permute-start | bytes 1572872 | tf_op jit(solution)/shard_map/ppermute | solution.py:17
  2.9 14.4 %copy-start = (bf16[1024,1,2,128]{3,2,1,0:T(2,128)(2,1)S(1)}, bf16[1024,1,2,128]{3,2,1,0:T(2,128)(2,1)}, u32[]{:S(2)}) copy-start(bf16[1024,1,2,128]{3,2,1,0:T(2,128)(2,1)} %param.2) | copy-start | bytes 1572868
  3.4 7.5 %collective-permute-start.1 = (f32[144,128]{1,0:T(8,128)S(1)}, f32[144,128]{1,0:T(8,128)S(1)}, u32[]{:S(2)}, u32[]{:S(2)}) collective-permute-start(f32[144,128]{1,0:T(8,128)S(1)} %get-tuple-element.21), channel_id=1, source_target_pairs={{0,24},{1,7},{2,26},{3,5},{4,28},{5,3},{6,30},{7,1},{8,16},{9,15},... | collective-permute-start | bytes 221192 | tf_op jit(solution)/shard_map/ppermute | solution.py:41
  8.4 5.3 %collective-permute-start.2 = (f32[144,128]{1,0:T(8,128)S(1)}, f32[144,128]{1,0:T(8,128)S(1)}, u32[]{:S(2)}, u32[]{:S(2)}) collective-permute-start(f32[144,128]{1,0:T(8,128)S(1)} %get-tuple-element.22), channel_id=1, source_target_pairs={{0,16},{1,5},{2,18},{3,7},{4,20},{5,1},{6,22},{7,3},{8,24},{9,13},... | collective-permute-start | bytes 221192 | tf_op jit(solution)/shard_map/ppermute | solution.py:41
  8.4 5.3 %collective-permute-start.3 = (f32[144,128]{1,0:T(8,128)S(1)}, f32[144,128]{1,0:T(8,128)S(1)}, u32[]{:S(2)}, u32[]{:S(2)}) collective-permute-start(f32[144,128]{1,0:T(8,128)S(1)} %get-tuple-element.23), channel_id=1, source_target_pairs={{0,8},{1,3},{2,10},{3,1},{4,12},{5,7},{6,14},{7,5},{8,0},{9,11},{1... | collective-permute-start | bytes 221192 | tf_op jit(solution)/shard_map/ppermute | solution.py:41
  13.7 5.3 %collective-permute-start.6 = (f32[144,128]{1,0:T(8,128)S(1)}, f32[144,128]{1,0:T(8,128)S(1)}, u32[]{:S(2)}, u32[]{:S(2)}) collective-permute-start(f32[144,128]{1,0:T(8,128)S(1)} %add_add_fusion.1), channel_id=1, source_target_pairs={{0,6},{1,25},{2,4},{3,27},{4,2},{5,29},{6,0},{7,31},{8,14},{9,17},... | collective-permute-start | bytes 221192 | tf_op jit(solution)/shard_map/ppermute | solution.py:41
  16.7 4.4 %collective-permute-start.5 = (f32[144,128]{1,0:T(8,128)S(1)}, f32[144,128]{1,0:T(8,128)S(1)}, u32[]{:S(2)}, u32[]{:S(2)}) collective-permute-start(f32[144,128]{1,0:T(8,128)S(1)} %add_add_fusion.1), channel_id=1, source_target_pairs={{0,4},{1,17},{2,6},{3,19},{4,0},{5,21},{6,2},{7,23},{8,12},{9,25},... | collective-permute-start | bytes 221192 | tf_op jit(solution)/shard_map/ppermute | solution.py:41
  16.8 4.4 %collective-permute-start.4 = (f32[144,128]{1,0:T(8,128)S(1)}, f32[144,128]{1,0:T(8,128)S(1)}, u32[]{:S(2)}, u32[]{:S(2)}) collective-permute-start(f32[144,128]{1,0:T(8,128)S(1)} %add_add_fusion.1), channel_id=1, source_target_pairs={{0,2},{1,9},{2,0},{3,11},{4,6},{5,13},{6,4},{7,15},{8,10},{9,1},{1... | collective-permute-start | bytes 221192 | tf_op jit(solution)/shard_map/ppermute | solution.py:41
  21.2 4.5 %collective-permute-start.8 = (f32[144,128]{1,0:T(8,128)S(1)}, f32[144,128]{1,0:T(8,128)S(1)}, u32[]{:S(2)}, u32[]{:S(2)}) collective-permute-start(f32[144,128]{1,0:T(8,128)S(1)} %add_add_fusion.sums_ref.same_ref), channel_id=1, source_target_pairs={{0,8},{1,3},{2,10},{3,1},{4,12},{5,7},{6,14},{7,5},{8,0},{9,11},{1... | collective-permute-start | bytes 221192 | tf_op jit(solution)/shard_map/ppermute | solution.py:41
  21.9 3.8 %collective-permute-start.10 = (f32[136,128]{1,0:T(8,128)S(1)}, f32[136,128]{1,0:T(8,128)S(1)}, u32[]{:S(2)}, u32[]{:S(2)}) collective-permute-start(f32[136,128]{1,0:T(8,128)S(1)} %get-tuple-element.29), channel_id=1, source_target_pairs={{0,9},{1,2},{2,11},{3,0},{4,13},{5,6},{6,15},{7,4},{8,1},{9,10},{1... | collective-permute-start | bytes 208904 | tf_op jit(solution)/shard_map/ppermute | solution.py:41
  23.0 1.3 %collective-permute-start.9 = (f32[128,128]{1,0:T(8,128)S(1)}, f32[128,128]{1,0:T(8,128)S(1)}, u32[]{:S(2)}, u32[]{:S(2)}) collective-permute-start(f32[128,128]{1,0:T(8,128)S(1)} %slice.3), channel_id=1, source_target_pairs={{0,1},{1,0},{2,3},{3,2},{4,5},{5,4},{6,7},{7,6},{8,9},{9,8},{10,11... | collective-permute-start | bytes 196616 | tf_op jit(solution)/shard_map/ppermute | solution.py:17
  23.0 1.4 %collective-permute-start.7 = (f32[128,128]{1,0:T(8,128)S(1)}, f32[128,128]{1,0:T(8,128)S(1)}, u32[]{:S(2)}, u32[]{:S(2)}) collective-permute-start(f32[128,128]{1,0:T(8,128)S(1)} %get-tuple-element.28.kept_ref), channel_id=1, source_target_pairs={{0,1},{1,0},{2,3},{3,2},{4,5},{5,4},{6,7},{7,6},{8,9},{9,8},{10,11... | collective-permute-start | bytes 196616 | tf_op jit(solution)/shard_map/ppermute | solution.py:17

commit v13 on v12

--- a/solution.py
+++ b/solution.py
@@ -401,7 +401,7 @@
     inverse = among_pairs(inverse, n_cols, group, 1)
     swapped = partner(inverse, "cols", n_cols, 1)
     blocks = partner(block[:width], "cols", n_cols, 1)
-    crossed = hop(block, n_rows, n_cols, beside, 1)
+    crossed = hop(block, n_rows, n_cols, beside if n_cols > 2 else lambda parity: beside(0), 1)
     chunks = 2 * nblock
     coef, updated = pl.pallas_call(
         functools.partial(finish_kernel, rounds, nblock, phases, root, chunks),

time: 27.6 us -> 28.3 us (1.025)
  waiting for transfers between devices: 10.8 us -> 11.5 us
    ppermute x8, waiting for transfers between devices: 9.3 us -> 9.67 us  [hop(): return lax.ppermute(x, ('rows', 'cols'), pairs)]
where the time goes in v13:
time: 28.3 us; the launch traced here: 28.1 us
  starting transfers between devices  12.2 us (43%)
  waiting for transfers between devices  11.5 us (41%)
  Pallas kernels  3.8 us (13%)
  between operations  0.67 us (2%)
    ppermute x8, starting transfers between devices, hop(): return lax.ppermute(x, ('rows', 'cols'), pairs)  11 us
    ppermute x8, waiting for transfers between devices, hop(): return lax.ppermute(x, ('rows', 'cols'), pairs)  9.67 us
    ppermute x3, waiting for transfers between devices, partner(): return lax.ppermute(x, axis, [(i, i ^ offset) for i in range(count)])  1.78 us
    pallas_call x1, Pallas kernels, shards(): pl.pallas_call(functools.partial(finish_kernel, rounds, nblock, phases, r...  1.69 us
    pallas_call x1, Pallas kernels, shards(): pl.pallas_call(functools.partial(split_kernel, rounds, nblock), out_shape...  1.14 us
    ppermute x3, starting transfers between devices, partner(): return lax.ppermute(x, axis, [(i, i ^ offset) for i in range(count)])  1.12 us
  transfers between devices with their start and end apart: 11, of which 9 were waited for; matrix products, arithmetic and copies ran while one was open for 0% of the time, Pallas kernels for 6%

profile of v13, /device:TPU:0, one launch (start us, length us, event | category | flops | bytes accessed | tf_op | source)
XLA Modules:
  0.0 28.1 jit_solution(1916938565717725107)
XLA Ops:
  0.6 0.5 %collective-permute-start = (bf16[2048,128]{1,0:T(8,128)(2,1)}, bf16[2048,128]{1,0:T(8,128)(2,1)S(1)}, u32[]{:S(2)}, u32[]{:S(2)}) collective-permute-start(bf16[2048,128]{1,0:T(8,128)(2,1)} %bitcast.7), channel_id=1, source_target_pairs={{0,1},{1,0},{2,3},{3,2},{4,5},{5,4},{6,7},{7,6},{8,9},{9,8},{10,11... | collective-permute-start | bytes 1572872 | tf_op jit(solution)/shard_map/ppermute | solution.py:17
  1.1 1.1 %split.1 = (bf16[1024,128]{1,0:T(8,128)(2,1)S(1)}, bf16[1024,128]{1,0:T(8,128)(2,1)S(1)}, f32[8,8,128]{2,1,0:T(8,128)S(1)}) custom-call(f32[2,2,2]{2,1,0:T(2,128)} %scale_hbm.1, bf16[2048,128]{1,0:T(8,128)(2,1)} %bitcast.8), custom_call_target="tpu_custom_call" | custom-call | tf_op jit(solution)/shard_map/split/pallas_call | solution.py:347
  2.3 0.6 %collective-permute-done.recv_ref.odd_ref = bf16[2048,128]{1,0:T(8,128)(2,1)S(1)} collective-permute-done((bf16[2048,128]{1,0:T(8,128)(2,1)}, bf16[2048,128]{1,0:T(8,128)(2,1)S(1)}, u32[]{:S(2)}, u32[]{:S(2)}) %collective-permute-start) | collective-permute-done | bytes 524320 | tf_op jit(solution)/shard_map/ppermute | solution.py:17
  2.9 0.5 %products.1 = (f32[144,128]{1,0:T(8,128)S(1)}, f32[144,128]{1,0:T(8,128)S(1)}, f32[144,128]{1,0:T(8,128)S(1)}, f32[144,128]{1,0:T(8,128)S(1)}) custom-call(f32[8,8,128]{2,1,0:T(8,128)S(1)} %get-tuple-element.17.factor_ref, bf16[1024,128]{1,0:T(8,128)(2,1)S(1)} %get-tuple-element.18.first_ref, bf16[1024,128]{1,0:T(8,128)(2,1)S(1)} %get-tuple-element.19.own_ref, ...), custom_call_target="tpu_custom_call" | custom-call | tf_op jit(solution)/shard_map/products/pallas_call | solution.py:362
  3.4 5.0 %collective-permute-start.1 = (f32[144,128]{1,0:T(8,128)S(1)}, f32[144,128]{1,0:T(8,128)S(1)}, u32[]{:S(2)}, u32[]{:S(2)}) collective-permute-start(f32[144,128]{1,0:T(8,128)S(1)} %get-tuple-element.21), channel_id=1, source_target_pairs={{0,24},{1,7},{2,26},{3,5},{4,28},{5,3},{6,30},{7,1},{8,16},{9,15},... | collective-permute-start | bytes 221192 | tf_op jit(solution)/shard_map/ppermute | solution.py:41
  8.4 0.6 %collective-permute-start.3 = (f32[144,128]{1,0:T(8,128)S(1)}, f32[144,128]{1,0:T(8,128)S(1)}, u32[]{:S(2)}, u32[]{:S(2)}) collective-permute-start(f32[144,128]{1,0:T(8,128)S(1)} %get-tuple-element.23), channel_id=1, source_target_pairs={{0,8},{1,3},{2,10},{3,1},{4,12},{5,7},{6,14},{7,5},{8,0},{9,11},{1... | collective-permute-start | bytes 221192 | tf_op jit(solution)/shard_map/ppermute | solution.py:41
  9.1 1.8 %collective-permute-done.1 = f32[144,128]{1,0:T(8,128)S(1)} collective-permute-done((f32[144,128]{1,0:T(8,128)S(1)}, f32[144,128]{1,0:T(8,128)S(1)}, u32[]{:S(2)}, u32[]{:S(2)}) %collective-permute-start.1) | collective-permute-done | bytes 73760 | tf_op jit(solution)/shard_map/ppermute | solution.py:41
  10.9 2.8 %collective-permute-done.2 = f32[144,128]{1,0:T(8,128)S(1)} collective-permute-done((f32[144,128]{1,0:T(8,128)S(1)}, f32[144,128]{1,0:T(8,128)S(1)}, u32[]{:S(2)}, u32[]{:S(2)}) %collective-permute-start.2) | collective-permute-done | bytes 73760 | tf_op jit(solution)/shard_map/ppermute | solution.py:41
  13.7 0.0 collective-permute-done.3
  13.7 3.0 %collective-permute-start.6 = (f32[144,128]{1,0:T(8,128)S(1)}, f32[144,128]{1,0:T(8,128)S(1)}, u32[]{:S(2)}, u32[]{:S(2)}) collective-permute-start(f32[144,128]{1,0:T(8,128)S(1)} %add_add_fusion.1), channel_id=1, source_target_pairs={{0,6},{1,25},{2,4},{3,27},{4,2},{5,29},{6,0},{7,31},{8,14},{9,17},... | collective-permute-start | bytes 221192 | tf_op jit(solution)/shard_map/ppermute | solution.py:41
  16.7 0.2 collective-permute-start.5
  16.8 0.5 %collective-permute-start.4 = (f32[144,128]{1,0:T(8,128)S(1)}, f32[144,128]{1,0:T(8,128)S(1)}, u32[]{:S(2)}, u32[]{:S(2)}) collective-permute-start(f32[144,128]{1,0:T(8,128)S(1)} %add_add_fusion.1), channel_id=1, source_target_pairs={{0,2},{1,9},{2,0},{3,11},{4,6},{5,13},{6,4},{7,15},{8,10},{9,1},{1... | collective-permute-start | bytes 221192 | tf_op jit(solution)/shard_map/ppermute | solution.py:41
  17.3 0.5 %spread.1.lead_ref = bf16[2048,256]{1,0:T(8,128)(2,1)S(1)} custom-call(bf16[2048,128]{1,0:T(8,128)(2,1)S(1)} %bitcast.9, bf16[2048,128]{1,0:T(8,128)(2,1)S(1)} %collective-permute-done.recv_ref.odd_ref), custom_call_target="tpu_custom_call" | custom-call | tf_op jit(solution)/shard_map/spread/pallas_call | solution.py:379
  17.8 1.2 %collective-permute-done.6 = f32[144,128]{1,0:T(8,128)S(1)} collective-permute-done((f32[144,128]{1,0:T(8,128)S(1)}, f32[144,128]{1,0:T(8,128)S(1)}, u32[]{:S(2)}, u32[]{:S(2)}) %collective-permute-start.6) | collective-permute-done | bytes 73760 | tf_op jit(solution)/shard_map/ppermute | solution.py:41
  19.0 2.0 %collective-permute-done.5 = f32[144,128]{1,0:T(8,128)S(1)} collective-permute-done((f32[144,128]{1,0:T(8,128)S(1)}, f32[144,128]{1,0:T(8,128)S(1)}, u32[]{:S(2)}, u32[]{:S(2)}) %collective-permute-start.5) | collective-permute-done | bytes 73760 | tf_op jit(solution)/shard_map/ppermute | solution.py:41
  21.0 0.2 collective-permute-done.4
  21.2 0.7 %collective-permute-start.8 = (f32[144,128]{1,0:T(8,128)S(1)}, f32[144,128]{1,0:T(8,128)S(1)}, u32[]{:S(2)}, u32[]{:S(2)}) collective-permute-start(f32[144,128]{1,0:T(8,128)S(1)} %add_add_fusion.sums_ref.same_ref), channel_id=1, source_target_pairs={{0,8},{1,3},{2,10},{3,1},{4,12},{5,7},{6,14},{7,5},{8,0},{9,11},{1... | collective-permute-start | bytes 221192 | tf_op jit(solution)/shard_map/ppermute | solution.py:41
  21.9 1.1 %collective-permute-start.10 = (f32[136,128]{1,0:T(8,128)S(1)}, f32[136,128]{1,0:T(8,128)S(1)}, u32[]{:S(2)}, u32[]{:S(2)}) collective-permute-start(f32[136,128]{1,0:T(8,128)S(1)} %get-tuple-element.29), channel_id=1, source_target_pairs={{0,9},{1,8},{2,11},{3,10},{4,13},{5,12},{6,15},{7,14},{8,1},{9,0},... | collective-permute-start | bytes 208904 | tf_op jit(solution)/shard_map/ppermute | solution.py:41
  23.0 0.5 %collective-permute-start.9 = (f32[128,128]{1,0:T(8,128)S(1)}, f32[128,128]{1,0:T(8,128)S(1)}, u32[]{:S(2)}, u32[]{:S(2)}) collective-permute-start(f32[128,128]{1,0:T(8,128)S(1)} %slice.3), channel_id=1, source_target_pairs={{0,1},{1,0},{2,3},{3,2},{4,5},{5,4},{6,7},{7,6},{8,9},{9,8},{10,11... | collective-permute-start | bytes 196616 | tf_op jit(solution)/shard_map/ppermute | solution.py:17
  23.5 0.1 collective-permute-start.7
  23.6 0.8 %collective-permute-done.9.block_ref = f32[128,128]{1,0:T(8,128)S(1)} collective-permute-done((f32[128,128]{1,0:T(8,128)S(1)}, f32[128,128]{1,0:T(8,128)S(1)}, u32[]{:S(2)}, u32[]{:S(2)}) %collective-permute-start.9) | collective-permute-done | bytes 65568 | tf_op jit(solution)/shard_map/ppermute | solution.py:17
  24.4 0.4 %collective-permute-done.7.recv_ref = f32[128,128]{1,0:T(8,128)S(1)} collective-permute-done((f32[128,128]{1,0:T(8,128)S(1)}, f32[128,128]{1,0:T(8,128)S(1)}, u32[]{:S(2)}, u32[]{:S(2)}) %collective-permute-start.7) | collective-permute-done | bytes 65568 | tf_op jit(solution)/shard_map/ppermute | solution.py:17
  24.8 1.7 %collective-permute-done.10.across_ref = f32[136,128]{1,0:T(8,128)S(1)} collective-permute-done((f32[136,128]{1,0:T(8,128)S(1)}, f32[136,128]{1,0:T(8,128)S(1)}, u32[]{:S(2)}, u32[]{:S(2)}) %collective-permute-start.10) | collective-permute-done | bytes 69664 | tf_op jit(solution)/shard_map/ppermute | solution.py:41
  26.4 1.7 %finish.1 = (f32[256,128]{1,0:T(8,128)}, bf16[2048,128]{1,0:T(8,128)(2,1)}) custom-call(f32[8,8,128]{2,1,0:T(8,128)S(1)} %get-tuple-element.17.factor_ref, bf16[2048,128]{1,0:T(8,128)(2,1)S(1)} %bitcast.10, bf16[2048,256]{1,0:T(8,128)(2,1)S(1)} %spread.1.lead_ref, f32[128,128]{1,0:T(8,128)S(1)} %get-tuple-element.28.kept_ref, ...), custom_call_target="tpu_custom_call" | custom-call | tf_op jit(solution)/shard_map/finish/pallas_call | solution.py:406
  (8 shorter events, 0.1 us)
Async XLA Ops:
  0.6 2.3 %collective-permute-start = (bf16[2048,128]{1,0:T(8,128)(2,1)}, bf16[2048,128]{1,0:T(8,128)(2,1)S(1)}, u32[]{:S(2)}, u32[]{:S(2)}) collective-permute-start(bf16[2048,128]{1,0:T(8,128)(2,1)} %bitcast.7), channel_id=1, source_target_pairs={{0,1},{1,0},{2,3},{3,2},{4,5},{5,4},{6,7},{7,6},{8,9},{9,8},{10,11... | collective-permute-start | bytes 1572872 | tf_op jit(solution)/shard_map/ppermute | solution.py:17
  2.9 14.4 %copy-start = (bf16[1024,1,2,128]{3,2,1,0:T(2,128)(2,1)S(1)}, bf16[1024,1,2,128]{3,2,1,0:T(2,128)(2,1)}, u32[]{:S(2)}) copy-start(bf16[1024,1,2,128]{3,2,1,0:T(2,128)(2,1)} %param.2) | copy-start | bytes 1572868
  3.4 7.5 %collective-permute-start.1 = (f32[144,128]{1,0:T(8,128)S(1)}, f32[144,128]{1,0:T(8,128)S(1)}, u32[]{:S(2)}, u32[]{:S(2)}) collective-permute-start(f32[144,128]{1,0:T(8,128)S(1)} %get-tuple-element.21), channel_id=1, source_target_pairs={{0,24},{1,7},{2,26},{3,5},{4,28},{5,3},{6,30},{7,1},{8,16},{9,15},... | collective-permute-start | bytes 221192 | tf_op jit(solution)/shard_map/ppermute | solution.py:41
  8.4 5.3 %collective-permute-start.2 = (f32[144,128]{1,0:T(8,128)S(1)}, f32[144,128]{1,0:T(8,128)S(1)}, u32[]{:S(2)}, u32[]{:S(2)}) collective-permute-start(f32[144,128]{1,0:T(8,128)S(1)} %get-tuple-element.22), channel_id=1, source_target_pairs={{0,16},{1,5},{2,18},{3,7},{4,20},{5,1},{6,22},{7,3},{8,24},{9,13},... | collective-permute-start | bytes 221192 | tf_op jit(solution)/shard_map/ppermute | solution.py:41
  8.4 5.3 %collective-permute-start.3 = (f32[144,128]{1,0:T(8,128)S(1)}, f32[144,128]{1,0:T(8,128)S(1)}, u32[]{:S(2)}, u32[]{:S(2)}) collective-permute-start(f32[144,128]{1,0:T(8,128)S(1)} %get-tuple-element.23), channel_id=1, source_target_pairs={{0,8},{1,3},{2,10},{3,1},{4,12},{5,7},{6,14},{7,5},{8,0},{9,11},{1... | collective-permute-start | bytes 221192 | tf_op jit(solution)/shard_map/ppermute | solution.py:41
  13.7 5.3 %collective-permute-start.6 = (f32[144,128]{1,0:T(8,128)S(1)}, f32[144,128]{1,0:T(8,128)S(1)}, u32[]{:S(2)}, u32[]{:S(2)}) collective-permute-start(f32[144,128]{1,0:T(8,128)S(1)} %add_add_fusion.1), channel_id=1, source_target_pairs={{0,6},{1,25},{2,4},{3,27},{4,2},{5,29},{6,0},{7,31},{8,14},{9,17},... | collective-permute-start | bytes 221192 | tf_op jit(solution)/shard_map/ppermute | solution.py:41
  16.7 4.4 %collective-permute-start.5 = (f32[144,128]{1,0:T(8,128)S(1)}, f32[144,128]{1,0:T(8,128)S(1)}, u32[]{:S(2)}, u32[]{:S(2)}) collective-permute-start(f32[144,128]{1,0:T(8,128)S(1)} %add_add_fusion.1), channel_id=1, source_target_pairs={{0,4},{1,17},{2,6},{3,19},{4,0},{5,21},{6,2},{7,23},{8,12},{9,25},... | collective-permute-start | bytes 221192 | tf_op jit(solution)/shard_map/ppermute | solution.py:41
  16.8 4.4 %collective-permute-start.4 = (f32[144,128]{1,0:T(8,128)S(1)}, f32[144,128]{1,0:T(8,128)S(1)}, u32[]{:S(2)}, u32[]{:S(2)}) collective-permute-start(f32[144,128]{1,0:T(8,128)S(1)} %add_add_fusion.1), channel_id=1, source_target_pairs={{0,2},{1,9},{2,0},{3,11},{4,6},{5,13},{6,4},{7,15},{8,10},{9,1},{1... | collective-permute-start | bytes 221192 | tf_op jit(solution)/shard_map/ppermute | solution.py:41
  21.2 5.2 %collective-permute-start.8 = (f32[144,128]{1,0:T(8,128)S(1)}, f32[144,128]{1,0:T(8,128)S(1)}, u32[]{:S(2)}, u32[]{:S(2)}) collective-permute-start(f32[144,128]{1,0:T(8,128)S(1)} %add_add_fusion.sums_ref.same_ref), channel_id=1, source_target_pairs={{0,8},{1,3},{2,10},{3,1},{4,12},{5,7},{6,14},{7,5},{8,0},{9,11},{1... | collective-permute-start | bytes 221192 | tf_op jit(solution)/shard_map/ppermute | solution.py:41
  21.9 4.5 %collective-permute-start.10 = (f32[136,128]{1,0:T(8,128)S(1)}, f32[136,128]{1,0:T(8,128)S(1)}, u32[]{:S(2)}, u32[]{:S(2)}) collective-permute-start(f32[136,128]{1,0:T(8,128)S(1)} %get-tuple-element.29), channel_id=1, source_target_pairs={{0,9},{1,8},{2,11},{3,10},{4,13},{5,12},{6,15},{7,14},{8,1},{9,0},... | collective-permute-start | bytes 208904 | tf_op jit(solution)/shard_map/ppermute | solution.py:41
  23.0 1.4 %collective-permute-start.9 = (f32[128,128]{1,0:T(8,128)S(1)}, f32[128,128]{1,0:T(8,128)S(1)}, u32[]{:S(2)}, u32[]{:S(2)}) collective-permute-start(f32[128,128]{1,0:T(8,128)S(1)} %slice.3), channel_id=1, source_target_pairs={{0,1},{1,0},{2,3},{3,2},{4,5},{5,4},{6,7},{7,6},{8,9},{9,8},{10,11... | collective-permute-start | bytes 196616 | tf_op jit(solution)/shard_map/ppermute | solution.py:17
  23.5 1.3 %collective-permute-start.7 = (f32[128,128]{1,0:T(8,128)S(1)}, f32[128,128]{1,0:T(8,128)S(1)}, u32[]{:S(2)}, u32[]{:S(2)}) collective-permute-start(f32[128,128]{1,0:T(8,128)S(1)} %get-tuple-element.28.kept_ref), channel_id=1, source_target_pairs={{0,1},{1,0},{2,3},{3,2},{4,5},{5,4},{6,7},{7,6},{8,9},{9,8},{10,11... | collective-permute-start | bytes 196616 | tf_op jit(solution)/shard_map/ppermute | solution.py:17

commit v14 on v12

--- a/solution.py
+++ b/solution.py
@@ -250,8 +250,7 @@
         theirs = cross[pl.ds(pl.multiple_of(place * half, half), half), :]
         ref[:half, :] = jnp.where(group == 1, packed[:half, :], theirs)
         ref[half:height, :] = packed[half:, :]
-        ref[height : height + half, :] = cross[pl.ds(pl.multiple_of(width + place * half, half), half), :]
-        ref[height + half :, :] = jnp.zeros((8, width), F32)
+        ref[height:, :] = cross[pl.ds(pl.multiple_of(width + place * half, half), half), :]
 
 
 def spread_kernel(rounds, even_ref, odd_ref, out_ref):
@@ -263,29 +262,40 @@
         out_ref[:, r * width : (r + 1) * width] = jnp.where(rows == r, moved, 0.0).astype(BF16)
 
 
-def factor_kernel(sums_ref, inverse_ref, block_ref):
+def factor_kernel(sums_ref, cross_ref, *pieces):
     width = sums_ref.shape[1]
-    height = width // 2 + 8
+    half = width // 2
+    height = half + 8
     group = lax.axis_index("cols")
+    long = pieces[0].shape[0]
+    cross_ref[:height, :] = sums_ref[:height, :]
+    cross_ref[height:, :] = jnp.zeros((cross_ref.shape[0] - height, width), F32)
+
+    def put(row, value):
+        pieces[row // long][row % long : row % long + 8, :] = value
+
+    for row in range(2 * width, len(pieces) * long, 8):
+        put(row, jnp.zeros((8, width), F32))
 
     @pl.when(group == 1)
     def _():
         gram = unpack(sums_ref[:height, :])
-        block_ref[:width, :] = gram
-        block_ref[width:, :] = jnp.zeros((8, width), F32)
         rows = [gram[8 * i : 8 * i + 8, :] for i in range(width // 8)]
+        for i, row in enumerate(rows):
+            put(width + 8 * i, row)
         for i, row in enumerate(lower_inverse(rows, width)):
-            inverse_ref[8 * i : 8 * i + 8, :] = row
+            put(8 * i, row)
 
     @pl.when(group != 1)
     def _():
-        inverse_ref[...] = jnp.zeros((width, width), F32)
-        block_ref[:height, :] = sums_ref[:height, :]
-        block_ref[height:, :] = jnp.zeros((width + 8 - height, width), F32)
+        for row in range(0, 2 * width, 8):
+            at = row - width
+            put(row, sums_ref[at : at + 8, :] if 0 <= at < half else jnp.zeros((8, width), F32))
 
 
 def finish_kernel(
-    rounds, nblock, phases, root, chunks, factor_ref, z_ref, lead_ref, kept_ref, recv_ref, same_ref, gathered_ref, block_ref, across_ref,
+    rounds, nblock, phases, root, chunks, factor_ref, z_ref, lead_ref, same_ref, gathered_ref, across_ref, kept_0, kept_1,
+    kept_2, swapped_0, swapped_1, swapped_2,
     coef_ref, out_ref, mine, theirs, coef, held, sems,
 ):
     group = lax.axis_index("cols")
@@ -294,13 +304,18 @@
     half = width // 2
     height = half + 8
     own_digit, pair_digit = half_digit(phases, group % 2), half_digit(phases, 1 - group % 2)
-    for own_rows, pair_rows, other in ((same_ref, block_ref, 0), (gathered_ref, across_ref, 1)):
-        mine[pl.ds(pl.multiple_of((own_digit ^ other) * half, half), half), :] = own_rows[height : height + half, :]
-        theirs[pl.ds(pl.multiple_of((pair_digit ^ other) * half, half), half), :] = pair_rows[:half, :]
+    swapped = jnp.concatenate([swapped_0[...], swapped_1[...], swapped_2[...]], axis=0)
+    kept = jnp.concatenate([kept_0[...], kept_1[...], kept_2[...]], axis=0)[:width, :]
+    gram = swapped[width : 2 * width, :]
+    start = gathered_ref.shape[0] - half
+    pieces = ((same_ref[height:, :], gram[:half, :], 0), (gathered_ref[start:, :], across_ref[:half, :], 1))
+    for own_rows, pair_rows, other in pieces:
+        mine[pl.ds(pl.multiple_of((own_digit ^ other) * half, half), half), :] = own_rows
+        theirs[pl.ds(pl.multiple_of((pair_digit ^ other) * half, half), half), :] = pair_rows
     own_block = mine[...]
-    pair_block = jnp.where(group == 0, block_ref[...], theirs[...])
+    pair_block = jnp.where(group == 0, gram, theirs[...])
     cross = jnp.concatenate([jnp.where(odd, own_block, pair_block), jnp.where(odd, pair_block, own_block)], axis=1)
-    inverse = jnp.where(odd, kept_ref[...], recv_ref[...])
+    inverse = jnp.where(odd, kept, swapped[:width, :])
     across = inverse.T
     raw = product(inverse, cross)
     for r in range(rounds):
@@ -342,7 +357,7 @@
     even = among_pairs(z, n_cols, group, 0)
     leads = (even, recv) if n_cols == 2 else (even, partner(even, "cols", n_cols, 1))
     phases = radices(n_rows)
-    payload = width + 16
+    payload = width + 8
     params = pltpu.CompilerParams(vmem_limit_bytes=48 << 20)
     first, own, factors = pl.pallas_call(
         functools.partial(split_kernel, rounds, nblock),
@@ -388,19 +403,22 @@
         for other in others:
             sums = sums + other
     beside = lambda parity: order(phases, parity)[0][0]
-    gathered = hop(sums, n_rows, n_cols, beside)
-    inverse, block = pl.pallas_call(
+    long_piece = 2 * width // 3 // 8 * 8 + 8
+    gathered = hop(sums[payload - long_piece - 16 :], n_rows, n_cols, beside)
+    block, *factored = pl.pallas_call(
         factor_kernel,
-        out_shape=[jax.ShapeDtypeStruct((width + pad, width), F32) for pad in (0, 8)],
+        out_shape=[jax.ShapeDtypeStruct((long_piece + pad, width), F32) for pad in (8, 0, 0, 0)],
         in_specs=[VMEM],
-        out_specs=[VMEM] * 2,
+        out_specs=[VMEM] * 4,
         compiler_params=params,
         cost_estimate=pl.CostEstimate(flops=1 << 30, bytes_accessed=1 << 23, transcendentals=0),
         name="factor",
     )(sums)
-    inverse = among_pairs(inverse, n_cols, group, 1)
-    swapped = partner(inverse, "cols", n_cols, 1)
-    blocks = partner(block[:width], "cols", n_cols, 1)
+    if n_cols > 2:
+        joined = jnp.concatenate(factored, axis=0)
+        joined = jnp.concatenate([among_pairs(joined[:width], n_cols, group, 1), joined[width:]], axis=0)
+        factored = [joined[i * long_piece : (i + 1) * long_piece] for i in range(3)]
+    swapped = [partner(x, "cols", n_cols, 1) for x in factored]
     crossed = hop(block, n_rows, n_cols, beside, 1)
     chunks = 2 * nblock
     coef, updated = pl.pallas_call(
@@ -409,7 +427,7 @@
             jax.ShapeDtypeStruct((width * rounds, width), F32),
             jax.ShapeDtypeStruct((long, width), BF16),
         ],
-        in_specs=[VMEM] * 9,
+        in_specs=[VMEM] * 12,
         out_specs=[pl.BlockSpec(memory_space=pl.ANY)] * 2,
         scratch_shapes=[
             pltpu.VMEM((width, width), F32),
@@ -420,7 +438,7 @@
         ],
         compiler_params=params,
         name="finish",
-    )(factors, z, lead, inverse, swapped, sums, gathered, blocks, crossed)
+    )(factors, z, lead, sums, gathered, crossed, *factored, *swapped)
     return coef.reshape(width, 1, rounds, width), updated.reshape(snapshots.shape)
 
 

time: 27.6 us -> 27.2 us (0.986)
    ppermute x8, waiting for transfers between devices: 9.3 us -> 8.85 us  [hop(): return lax.ppermute(x, ('rows', 'cols'), pairs)]
    ppermute x3 -> x4, waiting for transfers between devices: 1.5 us -> 1.82 us  [partner(): return lax.ppermute(x, axis, [(i, i ^ offset) for i in range(count)])]
    ppermute x3 -> x4, starting transfers between devices: 1.03 us -> 1.03 us  [partner(): return lax.ppermute(x, axis, [(i, i ^ offset) for i in range(count)])]
  transfers between devices with their start and end apart: 11 -> 12, of which waited for: 9 -> 11; matrix products, arithmetic and copies ran while one was open for 0% -> 0% of each run, Pallas kernels for 6% -> 6%
where the time goes in v14:
time: 27.2 us; the launch traced here: 27.1 us
  starting transfers between devices  11.9 us (44%)
  waiting for transfers between devices  10.7 us (39%)
  Pallas kernels  3.8 us (14%)
  between operations  0.68 us (2%)
    ppermute x8, starting transfers between devices, hop(): return lax.ppermute(x, ('rows', 'cols'), pairs)  10.8 us
    ppermute x8, waiting for transfers between devices, hop(): return lax.ppermute(x, ('rows', 'cols'), pairs)  8.85 us
    ppermute x4, waiting for transfers between devices, partner(): return lax.ppermute(x, axis, [(i, i ^ offset) for i in range(count)])  1.82 us
    pallas_call x1, Pallas kernels, shards(): pl.pallas_call(functools.partial(finish_kernel, rounds, nblock, phases, r...  1.69 us
    pallas_call x1, Pallas kernels, shards(): pl.pallas_call(functools.partial(split_kernel, rounds, nblock), out_shape...  1.14 us
    ppermute x4, starting transfers between devices, partner(): return lax.ppermute(x, axis, [(i, i ^ offset) for i in range(count)])  1.03 us
  transfers between devices with their start and end apart: 12, of which 11 were waited for; matrix products, arithmetic and copies ran while one was open for 0% of the time, Pallas kernels for 6%

profile of v14, /device:TPU:0, one launch (start us, length us, event | category | flops | bytes accessed | tf_op | source)
XLA Modules:
  0.0 27.1 jit_solution(17373093554952485058)
XLA Ops:
  0.6 0.5 %collective-permute-start = (bf16[2048,128]{1,0:T(8,128)(2,1)}, bf16[2048,128]{1,0:T(8,128)(2,1)S(1)}, u32[]{:S(2)}, u32[]{:S(2)}) collective-permute-start(bf16[2048,128]{1,0:T(8,128)(2,1)} %bitcast.7), channel_id=1, source_target_pairs={{0,1},{1,0},{2,3},{3,2},{4,5},{5,4},{6,7},{7,6},{8,9},{9,8},{10,11... | collective-permute-start | bytes 1572872 | tf_op jit(solution)/shard_map/ppermute | solution.py:17
  1.1 1.1 %split.1 = (bf16[1024,128]{1,0:T(8,128)(2,1)S(1)}, bf16[1024,128]{1,0:T(8,128)(2,1)S(1)}, f32[8,8,128]{2,1,0:T(8,128)S(1)}) custom-call(f32[2,2,2]{2,1,0:T(2,128)} %scale_hbm.1, bf16[2048,128]{1,0:T(8,128)(2,1)} %bitcast.8), custom_call_target="tpu_custom_call" | custom-call | tf_op jit(solution)/shard_map/split/pallas_call | solution.py:362
  2.3 0.6 %collective-permute-done.recv_ref.odd_ref = bf16[2048,128]{1,0:T(8,128)(2,1)S(1)} collective-permute-done((bf16[2048,128]{1,0:T(8,128)(2,1)}, bf16[2048,128]{1,0:T(8,128)(2,1)S(1)}, u32[]{:S(2)}, u32[]{:S(2)}) %collective-permute-start) | collective-permute-done | bytes 524320 | tf_op jit(solution)/shard_map/ppermute | solution.py:17
  2.9 0.5 %products.1 = (f32[136,128]{1,0:T(8,128)S(1)}, f32[136,128]{1,0:T(8,128)S(1)}, f32[136,128]{1,0:T(8,128)S(1)}, f32[136,128]{1,0:T(8,128)S(1)}) custom-call(f32[8,8,128]{2,1,0:T(8,128)S(1)} %get-tuple-element.19.factor_ref, bf16[1024,128]{1,0:T(8,128)(2,1)S(1)} %get-tuple-element.20.first_ref, bf16[1024,128]{1,0:T(8,128)(2,1)S(1)} %get-tuple-element.21.own_ref, ...), custom_call_target="tpu_custom_call" | custom-call | tf_op jit(solution)/shard_map/products/pallas_call | solution.py:377
  3.4 5.0 %collective-permute-start.1 = (f32[136,128]{1,0:T(8,128)S(1)}, f32[136,128]{1,0:T(8,128)S(1)}, u32[]{:S(2)}, u32[]{:S(2)}) collective-permute-start(f32[136,128]{1,0:T(8,128)S(1)} %get-tuple-element.23), channel_id=1, source_target_pairs={{0,24},{1,7},{2,26},{3,5},{4,28},{5,3},{6,30},{7,1},{8,16},{9,15},... | collective-permute-start | bytes 208904 | tf_op jit(solution)/shard_map/ppermute | solution.py:41
  8.4 0.6 %collective-permute-start.3 = (f32[136,128]{1,0:T(8,128)S(1)}, f32[136,128]{1,0:T(8,128)S(1)}, u32[]{:S(2)}, u32[]{:S(2)}) collective-permute-start(f32[136,128]{1,0:T(8,128)S(1)} %get-tuple-element.25), channel_id=1, source_target_pairs={{0,8},{1,3},{2,10},{3,1},{4,12},{5,7},{6,14},{7,5},{8,0},{9,11},{1... | collective-permute-start | bytes 208904 | tf_op jit(solution)/shard_map/ppermute | solution.py:41
  9.1 1.8 %collective-permute-done.1 = f32[136,128]{1,0:T(8,128)S(1)} collective-permute-done((f32[136,128]{1,0:T(8,128)S(1)}, f32[136,128]{1,0:T(8,128)S(1)}, u32[]{:S(2)}, u32[]{:S(2)}) %collective-permute-start.1) | collective-permute-done | bytes 69664 | tf_op jit(solution)/shard_map/ppermute | solution.py:41
  10.8 2.8 %collective-permute-done.2 = f32[136,128]{1,0:T(8,128)S(1)} collective-permute-done((f32[136,128]{1,0:T(8,128)S(1)}, f32[136,128]{1,0:T(8,128)S(1)}, u32[]{:S(2)}, u32[]{:S(2)}) %collective-permute-start.2) | collective-permute-done | bytes 69664 | tf_op jit(solution)/shard_map/ppermute | solution.py:41
  13.7 3.0 %collective-permute-start.6 = (f32[136,128]{1,0:T(8,128)S(1)}, f32[136,128]{1,0:T(8,128)S(1)}, u32[]{:S(2)}, u32[]{:S(2)}) collective-permute-start(f32[136,128]{1,0:T(8,128)S(1)} %add_add_fusion.1), channel_id=1, source_target_pairs={{0,6},{1,25},{2,4},{3,27},{4,2},{5,29},{6,0},{7,31},{8,14},{9,17},... | collective-permute-start | bytes 208904 | tf_op jit(solution)/shard_map/ppermute | solution.py:41
  16.6 0.2 collective-permute-start.5
  16.8 0.4 %collective-permute-start.4 = (f32[136,128]{1,0:T(8,128)S(1)}, f32[136,128]{1,0:T(8,128)S(1)}, u32[]{:S(2)}, u32[]{:S(2)}) collective-permute-start(f32[136,128]{1,0:T(8,128)S(1)} %add_add_fusion.1), channel_id=1, source_target_pairs={{0,2},{1,9},{2,0},{3,11},{4,6},{5,13},{6,4},{7,15},{8,10},{9,1},{1... | collective-permute-start | bytes 208904 | tf_op jit(solution)/shard_map/ppermute | solution.py:41
  17.3 0.5 %spread.1.lead_ref = bf16[2048,256]{1,0:T(8,128)(2,1)S(1)} custom-call(bf16[2048,128]{1,0:T(8,128)(2,1)S(1)} %bitcast.9, bf16[2048,128]{1,0:T(8,128)(2,1)S(1)} %collective-permute-done.recv_ref.odd_ref), custom_call_target="tpu_custom_call" | custom-call | tf_op jit(solution)/shard_map/spread/pallas_call | solution.py:394
  17.8 1.2 %collective-permute-done.6 = f32[136,128]{1,0:T(8,128)S(1)} collective-permute-done((f32[136,128]{1,0:T(8,128)S(1)}, f32[136,128]{1,0:T(8,128)S(1)}, u32[]{:S(2)}, u32[]{:S(2)}) %collective-permute-start.6) | collective-permute-done | bytes 69664 | tf_op jit(solution)/shard_map/ppermute | solution.py:41
  18.9 2.0 %collective-permute-done.5 = f32[136,128]{1,0:T(8,128)S(1)} collective-permute-done((f32[136,128]{1,0:T(8,128)S(1)}, f32[136,128]{1,0:T(8,128)S(1)}, u32[]{:S(2)}, u32[]{:S(2)}) %collective-permute-start.5) | collective-permute-done | bytes 69664 | tf_op jit(solution)/shard_map/ppermute | solution.py:41
  20.9 0.2 collective-permute-done.4
  21.2 0.5 %collective-permute-start.7 = (f32[104,128]{1,0:T(8,128)S(1)}, f32[104,128]{1,0:T(8,128)S(1)}, u32[]{:S(2)}, u32[]{:S(2)}) collective-permute-start(f32[104,128]{1,0:T(8,128)S(1)} %slice.4), channel_id=1, source_target_pairs={{0,8},{1,3},{2,10},{3,1},{4,12},{5,7},{6,14},{7,5},{8,0},{9,11},{1... | collective-permute-start | bytes 159752 | tf_op jit(solution)/shard_map/ppermute | solution.py:41
  21.7 1.0 %collective-permute-start.8 = (f32[96,128]{1,0:T(8,128)S(1)}, f32[96,128]{1,0:T(8,128)S(1)}, u32[]{:S(2)}, u32[]{:S(2)}) collective-permute-start(f32[96,128]{1,0:T(8,128)S(1)} %get-tuple-element.30), channel_id=1, source_target_pairs={{0,9},{1,2},{2,11},{3,0},{4,13},{5,6},{6,15},{7,4},{8,1},{9,10},{1... | collective-permute-start | bytes 147464 | tf_op jit(solution)/shard_map/ppermute | solution.py:41
  22.7 0.5 %collective-permute-start.10 = (f32[88,128]{1,0:T(8,128)S(1)}, f32[88,128]{1,0:T(8,128)S(1)}, u32[]{:S(2)}, u32[]{:S(2)}) collective-permute-start(f32[88,128]{1,0:T(8,128)S(1)} %get-tuple-element.32.kept_1), channel_id=1, source_target_pairs={{0,1},{1,0},{2,3},{3,2},{4,5},{5,4},{6,7},{7,6},{8,9},{9,8},{10,11... | collective-permute-start | bytes 135176 | tf_op jit(solution)/shard_map/ppermute | solution.py:17
  23.3 0.7 %collective-permute-done.9.swapped_0 = f32[88,128]{1,0:T(8,128)S(1)} collective-permute-done((f32[88,128]{1,0:T(8,128)S(1)}, f32[88,128]{1,0:T(8,128)S(1)}, u32[]{:S(2)}, u32[]{:S(2)}) %collective-permute-start.9) | collective-permute-done | bytes 45088 | tf_op jit(solution)/shard_map/ppermute | solution.py:17
  24.0 0.2 collective-permute-done.10.swapped_1
  24.1 0.3 %collective-permute-done.11.swapped_2 = f32[88,128]{1,0:T(8,128)S(1)} collective-permute-done((f32[88,128]{1,0:T(8,128)S(1)}, f32[88,128]{1,0:T(8,128)S(1)}, u32[]{:S(2)}, u32[]{:S(2)}) %collective-permute-start.11) | collective-permute-done | bytes 45088 | tf_op jit(solution)/shard_map/ppermute | solution.py:17
  24.5 0.8 %collective-permute-done.8.across_ref = f32[96,128]{1,0:T(8,128)S(1)} collective-permute-done((f32[96,128]{1,0:T(8,128)S(1)}, f32[96,128]{1,0:T(8,128)S(1)}, u32[]{:S(2)}, u32[]{:S(2)}) %collective-permute-start.8) | collective-permute-done | bytes 49184 | tf_op jit(solution)/shard_map/ppermute | solution.py:41
  25.3 0.1 collective-permute-done.7.gathered_ref
  25.4 1.7 %finish.1 = (f32[256,128]{1,0:T(8,128)}, bf16[2048,128]{1,0:T(8,128)(2,1)}) custom-call(f32[8,8,128]{2,1,0:T(8,128)S(1)} %get-tuple-element.19.factor_ref, bf16[2048,128]{1,0:T(8,128)(2,1)S(1)} %bitcast.10, bf16[2048,256]{1,0:T(8,128)(2,1)S(1)} %spread.1.lead_ref, f32[136,128]{1,0:T(8,128)S(1)} %add_add_fusion.sums_ref.same_ref, ...), custom_call_target="tpu_custom_call" | custom-call | tf_op jit(solution)/shard_map/finish/pallas_call | solution.py:424
  (10 shorter events, 0.1 us)
Async XLA Ops:
  0.6 2.3 %collective-permute-start = (bf16[2048,128]{1,0:T(8,128)(2,1)}, bf16[2048,128]{1,0:T(8,128)(2,1)S(1)}, u32[]{:S(2)}, u32[]{:S(2)}) collective-permute-start(bf16[2048,128]{1,0:T(8,128)(2,1)} %bitcast.7), channel_id=1, source_target_pairs={{0,1},{1,0},{2,3},{3,2},{4,5},{5,4},{6,7},{7,6},{8,9},{9,8},{10,11... | collective-permute-start | bytes 1572872 | tf_op jit(solution)/shard_map/ppermute | solution.py:17
  2.9 14.4 %copy-start = (bf16[1024,1,2,128]{3,2,1,0:T(2,128)(2,1)S(1)}, bf16[1024,1,2,128]{3,2,1,0:T(2,128)(2,1)}, u32[]{:S(2)}) copy-start(bf16[1024,1,2,128]{3,2,1,0:T(2,128)(2,1)} %param.2) | copy-start | bytes 1572868
  3.4 7.4 %collective-permute-start.1 = (f32[136,128]{1,0:T(8,128)S(1)}, f32[136,128]{1,0:T(8,128)S(1)}, u32[]{:S(2)}, u32[]{:S(2)}) collective-permute-start(f32[136,128]{1,0:T(8,128)S(1)} %get-tuple-element.23), channel_id=1, source_target_pairs={{0,24},{1,7},{2,26},{3,5},{4,28},{5,3},{6,30},{7,1},{8,16},{9,15},... | collective-permute-start | bytes 208904 | tf_op jit(solution)/shard_map/ppermute | solution.py:41
  8.4 5.2 %collective-permute-start.2 = (f32[136,128]{1,0:T(8,128)S(1)}, f32[136,128]{1,0:T(8,128)S(1)}, u32[]{:S(2)}, u32[]{:S(2)}) collective-permute-start(f32[136,128]{1,0:T(8,128)S(1)} %get-tuple-element.24), channel_id=1, source_target_pairs={{0,16},{1,5},{2,18},{3,7},{4,20},{5,1},{6,22},{7,3},{8,24},{9,13},... | collective-permute-start | bytes 208904 | tf_op jit(solution)/shard_map/ppermute | solution.py:41
  8.4 5.2 %collective-permute-start.3 = (f32[136,128]{1,0:T(8,128)S(1)}, f32[136,128]{1,0:T(8,128)S(1)}, u32[]{:S(2)}, u32[]{:S(2)}) collective-permute-start(f32[136,128]{1,0:T(8,128)S(1)} %get-tuple-element.25), channel_id=1, source_target_pairs={{0,8},{1,3},{2,10},{3,1},{4,12},{5,7},{6,14},{7,5},{8,0},{9,11},{1... | collective-permute-start | bytes 208904 | tf_op jit(solution)/shard_map/ppermute | solution.py:41
  13.7 5.3 %collective-permute-start.6 = (f32[136,128]{1,0:T(8,128)S(1)}, f32[136,128]{1,0:T(8,128)S(1)}, u32[]{:S(2)}, u32[]{:S(2)}) collective-permute-start(f32[136,128]{1,0:T(8,128)S(1)} %add_add_fusion.1), channel_id=1, source_target_pairs={{0,6},{1,25},{2,4},{3,27},{4,2},{5,29},{6,0},{7,31},{8,14},{9,17},... | collective-permute-start | bytes 208904 | tf_op jit(solution)/shard_map/ppermute | solution.py:41
  16.6 4.3 %collective-permute-start.5 = (f32[136,128]{1,0:T(8,128)S(1)}, f32[136,128]{1,0:T(8,128)S(1)}, u32[]{:S(2)}, u32[]{:S(2)}) collective-permute-start(f32[136,128]{1,0:T(8,128)S(1)} %add_add_fusion.1), channel_id=1, source_target_pairs={{0,4},{1,17},{2,6},{3,19},{4,0},{5,21},{6,2},{7,23},{8,12},{9,25},... | collective-permute-start | bytes 208904 | tf_op jit(solution)/shard_map/ppermute | solution.py:41
  16.8 4.3 %collective-permute-start.4 = (f32[136,128]{1,0:T(8,128)S(1)}, f32[136,128]{1,0:T(8,128)S(1)}, u32[]{:S(2)}, u32[]{:S(2)}) collective-permute-start(f32[136,128]{1,0:T(8,128)S(1)} %add_add_fusion.1), channel_id=1, source_target_pairs={{0,2},{1,9},{2,0},{3,11},{4,6},{5,13},{6,4},{7,15},{8,10},{9,1},{1... | collective-permute-start | bytes 208904 | tf_op jit(solution)/shard_map/ppermute | solution.py:41
  21.2 4.2 %collective-permute-start.7 = (f32[104,128]{1,0:T(8,128)S(1)}, f32[104,128]{1,0:T(8,128)S(1)}, u32[]{:S(2)}, u32[]{:S(2)}) collective-permute-start(f32[104,128]{1,0:T(8,128)S(1)} %slice.4), channel_id=1, source_target_pairs={{0,8},{1,3},{2,10},{3,1},{4,12},{5,7},{6,14},{7,5},{8,0},{9,11},{1... | collective-permute-start | bytes 159752 | tf_op jit(solution)/shard_map/ppermute | solution.py:41
  21.7 3.6 %collective-permute-start.8 = (f32[96,128]{1,0:T(8,128)S(1)}, f32[96,128]{1,0:T(8,128)S(1)}, u32[]{:S(2)}, u32[]{:S(2)}) collective-permute-start(f32[96,128]{1,0:T(8,128)S(1)} %get-tuple-element.30), channel_id=1, source_target_pairs={{0,9},{1,2},{2,11},{3,0},{4,13},{5,6},{6,15},{7,4},{8,1},{9,10},{1... | collective-permute-start | bytes 147464 | tf_op jit(solution)/shard_map/ppermute | solution.py:41
  22.7 1.2 %collective-permute-start.9 = (f32[88,128]{1,0:T(8,128)S(1)}, f32[88,128]{1,0:T(8,128)S(1)}, u32[]{:S(2)}, u32[]{:S(2)}) collective-permute-start(f32[88,128]{1,0:T(8,128)S(1)} %get-tuple-element.31.kept_0), channel_id=1, source_target_pairs={{0,1},{1,0},{2,3},{3,2},{4,5},{5,4},{6,7},{7,6},{8,9},{9,8},{10,11... | collective-permute-start | bytes 135176 | tf_op jit(solution)/shard_map/ppermute | solution.py:17
  22.7 1.4 %collective-permute-start.10 = (f32[88,128]{1,0:T(8,128)S(1)}, f32[88,128]{1,0:T(8,128)S(1)}, u32[]{:S(2)}, u32[]{:S(2)}) collective-permute-start(f32[88,128]{1,0:T(8,128)S(1)} %get-tuple-element.32.kept_1), channel_id=1, source_target_pairs={{0,1},{1,0},{2,3},{3,2},{4,5},{5,4},{6,7},{7,6},{8,9},{9,8},{10,11... | collective-permute-start | bytes 135176 | tf_op jit(solution)/shard_map/ppermute | solution.py:17
  23.3 1.2 %collective-permute-start.11 = (f32[88,128]{1,0:T(8,128)S(1)}, f32[88,128]{1,0:T(8,128)S(1)}, u32[]{:S(2)}, u32[]{:S(2)}) collective-permute-start(f32[88,128]{1,0:T(8,128)S(1)} %get-tuple-element.33.kept_2), channel_id=1, source_target_pairs={{0,1},{1,0},{2,3},{3,2},{4,5},{5,4},{6,7},{7,6},{8,9},{9,8},{10,11... | collective-permute-start | bytes 135176 | tf_op jit(solution)/shard_map/ppermute | solution.py:17

commit v15 on v14

--- a/solution.py
+++ b/solution.py
@@ -419,7 +419,7 @@
         joined = jnp.concatenate([among_pairs(joined[:width], n_cols, group, 1), joined[width:]], axis=0)
         factored = [joined[i * long_piece : (i + 1) * long_piece] for i in range(3)]
     swapped = [partner(x, "cols", n_cols, 1) for x in factored]
-    crossed = hop(block, n_rows, n_cols, beside, 1)
+    crossed = hop(block, n_rows, n_cols, lambda parity: 0 if parity == 1 and n_cols == 2 else beside(parity), 1)
     chunks = 2 * nblock
     coef, updated = pl.pallas_call(
         functools.partial(finish_kernel, rounds, nblock, phases, root, chunks),

time: 27.2 us -> 27.2 us (level)
  transfers between devices with their start and end apart: 12 -> 12, of which waited for: 11 -> 10; matrix products, arithmetic and copies ran while one was open for 0% -> 0% of each run, Pallas kernels for 6% -> 6%
where the time goes in v15:
time: 27.2 us; the launch traced here: 27.1 us
  starting transfers between devices  11.9 us (44%)
  waiting for transfers between devices  10.7 us (39%)
  Pallas kernels  3.8 us (14%)
  between operations  0.68 us (2%)
    ppermute x8, starting transfers between devices, hop(): return lax.ppermute(x, ('rows', 'cols'), pairs)  10.8 us
    ppermute x8, waiting for transfers between devices, hop(): return lax.ppermute(x, ('rows', 'cols'), pairs)  8.85 us
    ppermute x4, waiting for transfers between devices, partner(): return lax.ppermute(x, axis, [(i, i ^ offset) for i in range(count)])  1.82 us
    pallas_call x1, Pallas kernels, shards(): pl.pallas_call(functools.partial(finish_kernel, rounds, nblock, phases, r...  1.69 us
    pallas_call x1, Pallas kernels, shards(): pl.pallas_call(functools.partial(split_kernel, rounds, nblock), out_shape...  1.14 us
    ppermute x4, starting transfers between devices, partner(): return lax.ppermute(x, axis, [(i, i ^ offset) for i in range(count)])  1.03 us
  transfers between devices with their start and end apart: 12, of which 10 were waited for; matrix products, arithmetic and copies ran while one was open for 0% of the time, Pallas kernels for 6%

profile of v15, /device:TPU:0, one launch (start us, length us, event | category | flops | bytes accessed | tf_op | source)
XLA Modules:
  0.0 27.1 jit_solution(5470243868022178860)
XLA Ops:
  0.6 0.5 %collective-permute-start = (bf16[2048,128]{1,0:T(8,128)(2,1)}, bf16[2048,128]{1,0:T(8,128)(2,1)S(1)}, u32[]{:S(2)}, u32[]{:S(2)}) collective-permute-start(bf16[2048,128]{1,0:T(8,128)(2,1)} %bitcast.7), channel_id=1, source_target_pairs={{0,1},{1,0},{2,3},{3,2},{4,5},{5,4},{6,7},{7,6},{8,9},{9,8},{10,11... | collective-permute-start | bytes 1572872 | tf_op jit(solution)/shard_map/ppermute | solution.py:17
  1.1 1.1 %split.1 = (bf16[1024,128]{1,0:T(8,128)(2,1)S(1)}, bf16[1024,128]{1,0:T(8,128)(2,1)S(1)}, f32[8,8,128]{2,1,0:T(8,128)S(1)}) custom-call(f32[2,2,2]{2,1,0:T(2,128)} %scale_hbm.1, bf16[2048,128]{1,0:T(8,128)(2,1)} %bitcast.8), custom_call_target="tpu_custom_call" | custom-call | tf_op jit(solution)/shard_map/split/pallas_call | solution.py:362
  2.3 0.6 %collective-permute-done.recv_ref.odd_ref = bf16[2048,128]{1,0:T(8,128)(2,1)S(1)} collective-permute-done((bf16[2048,128]{1,0:T(8,128)(2,1)}, bf16[2048,128]{1,0:T(8,128)(2,1)S(1)}, u32[]{:S(2)}, u32[]{:S(2)}) %collective-permute-start) | collective-permute-done | bytes 524320 | tf_op jit(solution)/shard_map/ppermute | solution.py:17
  2.9 0.5 %products.1 = (f32[136,128]{1,0:T(8,128)S(1)}, f32[136,128]{1,0:T(8,128)S(1)}, f32[136,128]{1,0:T(8,128)S(1)}, f32[136,128]{1,0:T(8,128)S(1)}) custom-call(f32[8,8,128]{2,1,0:T(8,128)S(1)} %get-tuple-element.19.factor_ref, bf16[1024,128]{1,0:T(8,128)(2,1)S(1)} %get-tuple-element.20.first_ref, bf16[1024,128]{1,0:T(8,128)(2,1)S(1)} %get-tuple-element.21.own_ref, ...), custom_call_target="tpu_custom_call" | custom-call | tf_op jit(solution)/shard_map/products/pallas_call | solution.py:377
  3.4 5.0 %collective-permute-start.1 = (f32[136,128]{1,0:T(8,128)S(1)}, f32[136,128]{1,0:T(8,128)S(1)}, u32[]{:S(2)}, u32[]{:S(2)}) collective-permute-start(f32[136,128]{1,0:T(8,128)S(1)} %get-tuple-element.23), channel_id=1, source_target_pairs={{0,24},{1,7},{2,26},{3,5},{4,28},{5,3},{6,30},{7,1},{8,16},{9,15},... | collective-permute-start | bytes 208904 | tf_op jit(solution)/shard_map/ppermute | solution.py:41
  8.4 0.6 %collective-permute-start.3 = (f32[136,128]{1,0:T(8,128)S(1)}, f32[136,128]{1,0:T(8,128)S(1)}, u32[]{:S(2)}, u32[]{:S(2)}) collective-permute-start(f32[136,128]{1,0:T(8,128)S(1)} %get-tuple-element.25), channel_id=1, source_target_pairs={{0,8},{1,3},{2,10},{3,1},{4,12},{5,7},{6,14},{7,5},{8,0},{9,11},{1... | collective-permute-start | bytes 208904 | tf_op jit(solution)/shard_map/ppermute | solution.py:41
  9.1 1.8 %collective-permute-done.1 = f32[136,128]{1,0:T(8,128)S(1)} collective-permute-done((f32[136,128]{1,0:T(8,128)S(1)}, f32[136,128]{1,0:T(8,128)S(1)}, u32[]{:S(2)}, u32[]{:S(2)}) %collective-permute-start.1) | collective-permute-done | bytes 69664 | tf_op jit(solution)/shard_map/ppermute | solution.py:41
  10.8 2.8 %collective-permute-done.2 = f32[136,128]{1,0:T(8,128)S(1)} collective-permute-done((f32[136,128]{1,0:T(8,128)S(1)}, f32[136,128]{1,0:T(8,128)S(1)}, u32[]{:S(2)}, u32[]{:S(2)}) %collective-permute-start.2) | collective-permute-done | bytes 69664 | tf_op jit(solution)/shard_map/ppermute | solution.py:41
  13.7 3.0 %collective-permute-start.6 = (f32[136,128]{1,0:T(8,128)S(1)}, f32[136,128]{1,0:T(8,128)S(1)}, u32[]{:S(2)}, u32[]{:S(2)}) collective-permute-start(f32[136,128]{1,0:T(8,128)S(1)} %add_add_fusion.1), channel_id=1, source_target_pairs={{0,6},{1,25},{2,4},{3,27},{4,2},{5,29},{6,0},{7,31},{8,14},{9,17},... | collective-permute-start | bytes 208904 | tf_op jit(solution)/shard_map/ppermute | solution.py:41
  16.6 0.2 collective-permute-start.5
  16.8 0.4 %collective-permute-start.4 = (f32[136,128]{1,0:T(8,128)S(1)}, f32[136,128]{1,0:T(8,128)S(1)}, u32[]{:S(2)}, u32[]{:S(2)}) collective-permute-start(f32[136,128]{1,0:T(8,128)S(1)} %add_add_fusion.1), channel_id=1, source_target_pairs={{0,2},{1,9},{2,0},{3,11},{4,6},{5,13},{6,4},{7,15},{8,10},{9,1},{1... | collective-permute-start | bytes 208904 | tf_op jit(solution)/shard_map/ppermute | solution.py:41
  17.3 0.5 %spread.1.lead_ref = bf16[2048,256]{1,0:T(8,128)(2,1)S(1)} custom-call(bf16[2048,128]{1,0:T(8,128)(2,1)S(1)} %bitcast.9, bf16[2048,128]{1,0:T(8,128)(2,1)S(1)} %collective-permute-done.recv_ref.odd_ref), custom_call_target="tpu_custom_call" | custom-call | tf_op jit(solution)/shard_map/spread/pallas_call | solution.py:394
  17.8 1.2 %collective-permute-done.6 = f32[136,128]{1,0:T(8,128)S(1)} collective-permute-done((f32[136,128]{1,0:T(8,128)S(1)}, f32[136,128]{1,0:T(8,128)S(1)}, u32[]{:S(2)}, u32[]{:S(2)}) %collective-permute-start.6) | collective-permute-done | bytes 69664 | tf_op jit(solution)/shard_map/ppermute | solution.py:41
  18.9 2.0 %collective-permute-done.5 = f32[136,128]{1,0:T(8,128)S(1)} collective-permute-done((f32[136,128]{1,0:T(8,128)S(1)}, f32[136,128]{1,0:T(8,128)S(1)}, u32[]{:S(2)}, u32[]{:S(2)}) %collective-permute-start.5) | collective-permute-done | bytes 69664 | tf_op jit(solution)/shard_map/ppermute | solution.py:41
  20.9 0.2 collective-permute-done.4
  21.2 0.5 %collective-permute-start.7 = (f32[104,128]{1,0:T(8,128)S(1)}, f32[104,128]{1,0:T(8,128)S(1)}, u32[]{:S(2)}, u32[]{:S(2)}) collective-permute-start(f32[104,128]{1,0:T(8,128)S(1)} %slice.4), channel_id=1, source_target_pairs={{0,8},{1,3},{2,10},{3,1},{4,12},{5,7},{6,14},{7,5},{8,0},{9,11},{1... | collective-permute-start | bytes 159752 | tf_op jit(solution)/shard_map/ppermute | solution.py:41
  21.7 1.0 %collective-permute-start.8 = (f32[96,128]{1,0:T(8,128)S(1)}, f32[96,128]{1,0:T(8,128)S(1)}, u32[]{:S(2)}, u32[]{:S(2)}) collective-permute-start(f32[96,128]{1,0:T(8,128)S(1)} %get-tuple-element.30), channel_id=1, source_target_pairs={{0,9},{1,0},{2,11},{3,2},{4,13},{5,4},{6,15},{7,6},{8,1},{9,8},{10... | collective-permute-start | bytes 147464 | tf_op jit(solution)/shard_map/ppermute | solution.py:41
  22.7 0.5 %collective-permute-start.10 = (f32[88,128]{1,0:T(8,128)S(1)}, f32[88,128]{1,0:T(8,128)S(1)}, u32[]{:S(2)}, u32[]{:S(2)}) collective-permute-start(f32[88,128]{1,0:T(8,128)S(1)} %get-tuple-element.32.kept_1), channel_id=1, source_target_pairs={{0,1},{1,0},{2,3},{3,2},{4,5},{5,4},{6,7},{7,6},{8,9},{9,8},{10,11... | collective-permute-start | bytes 135176 | tf_op jit(solution)/shard_map/ppermute | solution.py:17
  23.3 0.7 %collective-permute-done.9.swapped_0 = f32[88,128]{1,0:T(8,128)S(1)} collective-permute-done((f32[88,128]{1,0:T(8,128)S(1)}, f32[88,128]{1,0:T(8,128)S(1)}, u32[]{:S(2)}, u32[]{:S(2)}) %collective-permute-start.9) | collective-permute-done | bytes 45088 | tf_op jit(solution)/shard_map/ppermute | solution.py:17
  24.0 0.2 collective-permute-done.10.swapped_1
  24.1 0.3 %collective-permute-done.11.swapped_2 = f32[88,128]{1,0:T(8,128)S(1)} collective-permute-done((f32[88,128]{1,0:T(8,128)S(1)}, f32[88,128]{1,0:T(8,128)S(1)}, u32[]{:S(2)}, u32[]{:S(2)}) %collective-permute-start.11) | collective-permute-done | bytes 45088 | tf_op jit(solution)/shard_map/ppermute | solution.py:17
  24.5 0.0 collective-permute-done.8.across_ref
  24.5 0.9 %collective-permute-done.7.gathered_ref = f32[104,128]{1,0:T(8,128)S(1)} collective-permute-done((f32[104,128]{1,0:T(8,128)S(1)}, f32[104,128]{1,0:T(8,128)S(1)}, u32[]{:S(2)}, u32[]{:S(2)}) %collective-permute-start.7) | collective-permute-done | bytes 53280 | tf_op jit(solution)/shard_map/ppermute | solution.py:41
  25.4 1.7 %finish.1 = (f32[256,128]{1,0:T(8,128)}, bf16[2048,128]{1,0:T(8,128)(2,1)}) custom-call(f32[8,8,128]{2,1,0:T(8,128)S(1)} %get-tuple-element.19.factor_ref, bf16[2048,128]{1,0:T(8,128)(2,1)S(1)} %bitcast.10, bf16[2048,256]{1,0:T(8,128)(2,1)S(1)} %spread.1.lead_ref, f32[136,128]{1,0:T(8,128)S(1)} %add_add_fusion.sums_ref.same_ref, ...), custom_call_target="tpu_custom_call" | custom-call | tf_op jit(solution)/shard_map/finish/pallas_call | solution.py:424
  (10 shorter events, 0.1 us)
Async XLA Ops:
  0.6 2.3 %collective-permute-start = (bf16[2048,128]{1,0:T(8,128)(2,1)}, bf16[2048,128]{1,0:T(8,128)(2,1)S(1)}, u32[]{:S(2)}, u32[]{:S(2)}) collective-permute-start(bf16[2048,128]{1,0:T(8,128)(2,1)} %bitcast.7), channel_id=1, source_target_pairs={{0,1},{1,0},{2,3},{3,2},{4,5},{5,4},{6,7},{7,6},{8,9},{9,8},{10,11... | collective-permute-start | bytes 1572872 | tf_op jit(solution)/shard_map/ppermute | solution.py:17
  2.9 14.4 %copy-start = (bf16[1024,1,2,128]{3,2,1,0:T(2,128)(2,1)S(1)}, bf16[1024,1,2,128]{3,2,1,0:T(2,128)(2,1)}, u32[]{:S(2)}) copy-start(bf16[1024,1,2,128]{3,2,1,0:T(2,128)(2,1)} %param.2) | copy-start | bytes 1572868
  3.4 7.4 %collective-permute-start.1 = (f32[136,128]{1,0:T(8,128)S(1)}, f32[136,128]{1,0:T(8,128)S(1)}, u32[]{:S(2)}, u32[]{:S(2)}) collective-permute-start(f32[136,128]{1,0:T(8,128)S(1)} %get-tuple-element.23), channel_id=1, source_target_pairs={{0,24},{1,7},{2,26},{3,5},{4,28},{5,3},{6,30},{7,1},{8,16},{9,15},... | collective-permute-start | bytes 208904 | tf_op jit(solution)/shard_map/ppermute | solution.py:41
  8.4 5.2 %collective-permute-start.2 = (f32[136,128]{1,0:T(8,128)S(1)}, f32[136,128]{1,0:T(8,128)S(1)}, u32[]{:S(2)}, u32[]{:S(2)}) collective-permute-start(f32[136,128]{1,0:T(8,128)S(1)} %get-tuple-element.24), channel_id=1, source_target_pairs={{0,16},{1,5},{2,18},{3,7},{4,20},{5,1},{6,22},{7,3},{8,24},{9,13},... | collective-permute-start | bytes 208904 | tf_op jit(solution)/shard_map/ppermute | solution.py:41
  8.4 5.2 %collective-permute-start.3 = (f32[136,128]{1,0:T(8,128)S(1)}, f32[136,128]{1,0:T(8,128)S(1)}, u32[]{:S(2)}, u32[]{:S(2)}) collective-permute-start(f32[136,128]{1,0:T(8,128)S(1)} %get-tuple-element.25), channel_id=1, source_target_pairs={{0,8},{1,3},{2,10},{3,1},{4,12},{5,7},{6,14},{7,5},{8,0},{9,11},{1... | collective-permute-start | bytes 208904 | tf_op jit(solution)/shard_map/ppermute | solution.py:41
  13.7 5.3 %collective-permute-start.6 = (f32[136,128]{1,0:T(8,128)S(1)}, f32[136,128]{1,0:T(8,128)S(1)}, u32[]{:S(2)}, u32[]{:S(2)}) collective-permute-start(f32[136,128]{1,0:T(8,128)S(1)} %add_add_fusion.1), channel_id=1, source_target_pairs={{0,6},{1,25},{2,4},{3,27},{4,2},{5,29},{6,0},{7,31},{8,14},{9,17},... | collective-permute-start | bytes 208904 | tf_op jit(solution)/shard_map/ppermute | solution.py:41
  16.6 4.3 %collective-permute-start.5 = (f32[136,128]{1,0:T(8,128)S(1)}, f32[136,128]{1,0:T(8,128)S(1)}, u32[]{:S(2)}, u32[]{:S(2)}) collective-permute-start(f32[136,128]{1,0:T(8,128)S(1)} %add_add_fusion.1), channel_id=1, source_target_pairs={{0,4},{1,17},{2,6},{3,19},{4,0},{5,21},{6,2},{7,23},{8,12},{9,25},... | collective-permute-start | bytes 208904 | tf_op jit(solution)/shard_map/ppermute | solution.py:41
  16.8 4.3 %collective-permute-start.4 = (f32[136,128]{1,0:T(8,128)S(1)}, f32[136,128]{1,0:T(8,128)S(1)}, u32[]{:S(2)}, u32[]{:S(2)}) collective-permute-start(f32[136,128]{1,0:T(8,128)S(1)} %add_add_fusion.1), channel_id=1, source_target_pairs={{0,2},{1,9},{2,0},{3,11},{4,6},{5,13},{6,4},{7,15},{8,10},{9,1},{1... | collective-permute-start | bytes 208904 | tf_op jit(solution)/shard_map/ppermute | solution.py:41
  21.2 4.2 %collective-permute-start.7 = (f32[104,128]{1,0:T(8,128)S(1)}, f32[104,128]{1,0:T(8,128)S(1)}, u32[]{:S(2)}, u32[]{:S(2)}) collective-permute-start(f32[104,128]{1,0:T(8,128)S(1)} %slice.4), channel_id=1, source_target_pairs={{0,8},{1,3},{2,10},{3,1},{4,12},{5,7},{6,14},{7,5},{8,0},{9,11},{1... | collective-permute-start | bytes 159752 | tf_op jit(solution)/shard_map/ppermute | solution.py:41
  21.7 2.8 %collective-permute-start.8 = (f32[96,128]{1,0:T(8,128)S(1)}, f32[96,128]{1,0:T(8,128)S(1)}, u32[]{:S(2)}, u32[]{:S(2)}) collective-permute-start(f32[96,128]{1,0:T(8,128)S(1)} %get-tuple-element.30), channel_id=1, source_target_pairs={{0,9},{1,0},{2,11},{3,2},{4,13},{5,4},{6,15},{7,6},{8,1},{9,8},{10... | collective-permute-start | bytes 147464 | tf_op jit(solution)/shard_map/ppermute | solution.py:41
  22.7 1.2 %collective-permute-start.9 = (f32[88,128]{1,0:T(8,128)S(1)}, f32[88,128]{1,0:T(8,128)S(1)}, u32[]{:S(2)}, u32[]{:S(2)}) collective-permute-start(f32[88,128]{1,0:T(8,128)S(1)} %get-tuple-element.31.kept_0), channel_id=1, source_target_pairs={{0,1},{1,0},{2,3},{3,2},{4,5},{5,4},{6,7},{7,6},{8,9},{9,8},{10,11... | collective-permute-start | bytes 135176 | tf_op jit(solution)/shard_map/ppermute | solution.py:17
  22.7 1.4 %collective-permute-start.10 = (f32[88,128]{1,0:T(8,128)S(1)}, f32[88,128]{1,0:T(8,128)S(1)}, u32[]{:S(2)}, u32[]{:S(2)}) collective-permute-start(f32[88,128]{1,0:T(8,128)S(1)} %get-tuple-element.32.kept_1), channel_id=1, source_target_pairs={{0,1},{1,0},{2,3},{3,2},{4,5},{5,4},{6,7},{7,6},{8,9},{9,8},{10,11... | collective-permute-start | bytes 135176 | tf_op jit(solution)/shard_map/ppermute | solution.py:17
  23.3 1.2 %collective-permute-start.11 = (f32[88,128]{1,0:T(8,128)S(1)}, f32[88,128]{1,0:T(8,128)S(1)}, u32[]{:S(2)}, u32[]{:S(2)}) collective-permute-start(f32[88,128]{1,0:T(8,128)S(1)} %get-tuple-element.33.kept_2), channel_id=1, source_target_pairs={{0,1},{1,0},{2,3},{3,2},{4,5},{5,4},{6,7},{7,6},{8,9},{9,8},{10,11... | collective-permute-start | bytes 135176 | tf_op jit(solution)/shard_map/ppermute | solution.py:17

commit v16 on v15

--- a/solution.py
+++ b/solution.py
@@ -420,7 +420,7 @@
         factored = [joined[i * long_piece : (i + 1) * long_piece] for i in range(3)]
     swapped = [partner(x, "cols", n_cols, 1) for x in factored]
     crossed = hop(block, n_rows, n_cols, lambda parity: 0 if parity == 1 and n_cols == 2 else beside(parity), 1)
-    chunks = 2 * nblock
+    chunks = 4 * nblock
     coef, updated = pl.pallas_call(
         functools.partial(finish_kernel, rounds, nblock, phases, root, chunks),
         out_shape=[

time: 27.2 us -> 27.2 us (level)
  no operation moved by 1% of the time
where the time goes in v16:
time: 27.2 us; the launch traced here: 27.1 us
  starting transfers between devices  11.9 us (44%)
  waiting for transfers between devices  10.7 us (39%)
  Pallas kernels  3.79 us (14%)
  between operations  0.68 us (2%)
    ppermute x8, starting transfers between devices, hop(): return lax.ppermute(x, ('rows', 'cols'), pairs)  10.8 us
    ppermute x8, waiting for transfers between devices, hop(): return lax.ppermute(x, ('rows', 'cols'), pairs)  8.85 us
    ppermute x4, waiting for transfers between devices, partner(): return lax.ppermute(x, axis, [(i, i ^ offset) for i in range(count)])  1.82 us
    pallas_call x1, Pallas kernels, shards(): pl.pallas_call(functools.partial(finish_kernel, rounds, nblock, phases, r...  1.68 us
    pallas_call x1, Pallas kernels, shards(): pl.pallas_call(functools.partial(split_kernel, rounds, nblock), out_shape...  1.14 us
    ppermute x4, starting transfers between devices, partner(): return lax.ppermute(x, axis, [(i, i ^ offset) for i in range(count)])  1.03 us
  transfers between devices with their start and end apart: 12, of which 10 were waited for; matrix products, arithmetic and copies ran while one was open for 0% of the time, Pallas kernels for 6%

profile of v16, /device:TPU:0, one launch (start us, length us, event | category | flops | bytes accessed | tf_op | source)
XLA Modules:
  0.0 27.1 jit_solution(6533540083154432393)
XLA Ops:
  0.6 0.5 %collective-permute-start = (bf16[2048,128]{1,0:T(8,128)(2,1)}, bf16[2048,128]{1,0:T(8,128)(2,1)S(1)}, u32[]{:S(2)}, u32[]{:S(2)}) collective-permute-start(bf16[2048,128]{1,0:T(8,128)(2,1)} %bitcast.7), channel_id=1, source_target_pairs={{0,1},{1,0},{2,3},{3,2},{4,5},{5,4},{6,7},{7,6},{8,9},{9,8},{10,11... | collective-permute-start | bytes 1572872 | tf_op jit(solution)/shard_map/ppermute | solution.py:17
  1.1 1.1 %split.1 = (bf16[1024,128]{1,0:T(8,128)(2,1)S(1)}, bf16[1024,128]{1,0:T(8,128)(2,1)S(1)}, f32[8,8,128]{2,1,0:T(8,128)S(1)}) custom-call(f32[2,2,2]{2,1,0:T(2,128)} %scale_hbm.1, bf16[2048,128]{1,0:T(8,128)(2,1)} %bitcast.8), custom_call_target="tpu_custom_call" | custom-call | tf_op jit(solution)/shard_map/split/pallas_call | solution.py:362
  2.3 0.6 %collective-permute-done.recv_ref.odd_ref = bf16[2048,128]{1,0:T(8,128)(2,1)S(1)} collective-permute-done((bf16[2048,128]{1,0:T(8,128)(2,1)}, bf16[2048,128]{1,0:T(8,128)(2,1)S(1)}, u32[]{:S(2)}, u32[]{:S(2)}) %collective-permute-start) | collective-permute-done | bytes 524320 | tf_op jit(solution)/shard_map/ppermute | solution.py:17
  2.9 0.5 %products.1 = (f32[136,128]{1,0:T(8,128)S(1)}, f32[136,128]{1,0:T(8,128)S(1)}, f32[136,128]{1,0:T(8,128)S(1)}, f32[136,128]{1,0:T(8,128)S(1)}) custom-call(f32[8,8,128]{2,1,0:T(8,128)S(1)} %get-tuple-element.19.factor_ref, bf16[1024,128]{1,0:T(8,128)(2,1)S(1)} %get-tuple-element.20.first_ref, bf16[1024,128]{1,0:T(8,128)(2,1)S(1)} %get-tuple-element.21.own_ref, ...), custom_call_target="tpu_custom_call" | custom-call | tf_op jit(solution)/shard_map/products/pallas_call | solution.py:377
  3.4 5.0 %collective-permute-start.1 = (f32[136,128]{1,0:T(8,128)S(1)}, f32[136,128]{1,0:T(8,128)S(1)}, u32[]{:S(2)}, u32[]{:S(2)}) collective-permute-start(f32[136,128]{1,0:T(8,128)S(1)} %get-tuple-element.23), channel_id=1, source_target_pairs={{0,24},{1,7},{2,26},{3,5},{4,28},{5,3},{6,30},{7,1},{8,16},{9,15},... | collective-permute-start | bytes 208904 | tf_op jit(solution)/shard_map/ppermute | solution.py:41
  8.4 0.6 %collective-permute-start.3 = (f32[136,128]{1,0:T(8,128)S(1)}, f32[136,128]{1,0:T(8,128)S(1)}, u32[]{:S(2)}, u32[]{:S(2)}) collective-permute-start(f32[136,128]{1,0:T(8,128)S(1)} %get-tuple-element.25), channel_id=1, source_target_pairs={{0,8},{1,3},{2,10},{3,1},{4,12},{5,7},{6,14},{7,5},{8,0},{9,11},{1... | collective-permute-start | bytes 208904 | tf_op jit(solution)/shard_map/ppermute | solution.py:41
  9.1 1.8 %collective-permute-done.1 = f32[136,128]{1,0:T(8,128)S(1)} collective-permute-done((f32[136,128]{1,0:T(8,128)S(1)}, f32[136,128]{1,0:T(8,128)S(1)}, u32[]{:S(2)}, u32[]{:S(2)}) %collective-permute-start.1) | collective-permute-done | bytes 69664 | tf_op jit(solution)/shard_map/ppermute | solution.py:41
  10.8 2.8 %collective-permute-done.2 = f32[136,128]{1,0:T(8,128)S(1)} collective-permute-done((f32[136,128]{1,0:T(8,128)S(1)}, f32[136,128]{1,0:T(8,128)S(1)}, u32[]{:S(2)}, u32[]{:S(2)}) %collective-permute-start.2) | collective-permute-done | bytes 69664 | tf_op jit(solution)/shard_map/ppermute | solution.py:41
  13.7 3.0 %collective-permute-start.6 = (f32[136,128]{1,0:T(8,128)S(1)}, f32[136,128]{1,0:T(8,128)S(1)}, u32[]{:S(2)}, u32[]{:S(2)}) collective-permute-start(f32[136,128]{1,0:T(8,128)S(1)} %add_add_fusion.1), channel_id=1, source_target_pairs={{0,6},{1,25},{2,4},{3,27},{4,2},{5,29},{6,0},{7,31},{8,14},{9,17},... | collective-permute-start | bytes 208904 | tf_op jit(solution)/shard_map/ppermute | solution.py:41
  16.6 0.2 collective-permute-start.5
  16.8 0.4 %collective-permute-start.4 = (f32[136,128]{1,0:T(8,128)S(1)}, f32[136,128]{1,0:T(8,128)S(1)}, u32[]{:S(2)}, u32[]{:S(2)}) collective-permute-start(f32[136,128]{1,0:T(8,128)S(1)} %add_add_fusion.1), channel_id=1, source_target_pairs={{0,2},{1,9},{2,0},{3,11},{4,6},{5,13},{6,4},{7,15},{8,10},{9,1},{1... | collective-permute-start | bytes 208904 | tf_op jit(solution)/shard_map/ppermute | solution.py:41
  17.3 0.5 %spread.1.lead_ref = bf16[2048,256]{1,0:T(8,128)(2,1)S(1)} custom-call(bf16[2048,128]{1,0:T(8,128)(2,1)S(1)} %bitcast.9, bf16[2048,128]{1,0:T(8,128)(2,1)S(1)} %collective-permute-done.recv_ref.odd_ref), custom_call_target="tpu_custom_call" | custom-call | tf_op jit(solution)/shard_map/spread/pallas_call | solution.py:394
  17.8 1.2 %collective-permute-done.6 = f32[136,128]{1,0:T(8,128)S(1)} collective-permute-done((f32[136,128]{1,0:T(8,128)S(1)}, f32[136,128]{1,0:T(8,128)S(1)}, u32[]{:S(2)}, u32[]{:S(2)}) %collective-permute-start.6) | collective-permute-done | bytes 69664 | tf_op jit(solution)/shard_map/ppermute | solution.py:41
  18.9 2.0 %collective-permute-done.5 = f32[136,128]{1,0:T(8,128)S(1)} collective-permute-done((f32[136,128]{1,0:T(8,128)S(1)}, f32[136,128]{1,0:T(8,128)S(1)}, u32[]{:S(2)}, u32[]{:S(2)}) %collective-permute-start.5) | collective-permute-done | bytes 69664 | tf_op jit(solution)/shard_map/ppermute | solution.py:41
  20.9 0.2 collective-permute-done.4
  21.2 0.5 %collective-permute-start.7 = (f32[104,128]{1,0:T(8,128)S(1)}, f32[104,128]{1,0:T(8,128)S(1)}, u32[]{:S(2)}, u32[]{:S(2)}) collective-permute-start(f32[104,128]{1,0:T(8,128)S(1)} %slice.4), channel_id=1, source_target_pairs={{0,8},{1,3},{2,10},{3,1},{4,12},{5,7},{6,14},{7,5},{8,0},{9,11},{1... | collective-permute-start | bytes 159752 | tf_op jit(solution)/shard_map/ppermute | solution.py:41
  21.7 1.0 %collective-permute-start.8 = (f32[96,128]{1,0:T(8,128)S(1)}, f32[96,128]{1,0:T(8,128)S(1)}, u32[]{:S(2)}, u32[]{:S(2)}) collective-permute-start(f32[96,128]{1,0:T(8,128)S(1)} %get-tuple-element.30), channel_id=1, source_target_pairs={{0,9},{1,0},{2,11},{3,2},{4,13},{5,4},{6,15},{7,6},{8,1},{9,8},{10... | collective-permute-start | bytes 147464 | tf_op jit(solution)/shard_map/ppermute | solution.py:41
  22.7 0.5 %collective-permute-start.10 = (f32[88,128]{1,0:T(8,128)S(1)}, f32[88,128]{1,0:T(8,128)S(1)}, u32[]{:S(2)}, u32[]{:S(2)}) collective-permute-start(f32[88,128]{1,0:T(8,128)S(1)} %get-tuple-element.32.kept_1), channel_id=1, source_target_pairs={{0,1},{1,0},{2,3},{3,2},{4,5},{5,4},{6,7},{7,6},{8,9},{9,8},{10,11... | collective-permute-start | bytes 135176 | tf_op jit(solution)/shard_map/ppermute | solution.py:17
  23.3 0.7 %collective-permute-done.9.swapped_0 = f32[88,128]{1,0:T(8,128)S(1)} collective-permute-done((f32[88,128]{1,0:T(8,128)S(1)}, f32[88,128]{1,0:T(8,128)S(1)}, u32[]{:S(2)}, u32[]{:S(2)}) %collective-permute-start.9) | collective-permute-done | bytes 45088 | tf_op jit(solution)/shard_map/ppermute | solution.py:17
  24.0 0.2 collective-permute-done.10.swapped_1
  24.1 0.3 %collective-permute-done.11.swapped_2 = f32[88,128]{1,0:T(8,128)S(1)} collective-permute-done((f32[88,128]{1,0:T(8,128)S(1)}, f32[88,128]{1,0:T(8,128)S(1)}, u32[]{:S(2)}, u32[]{:S(2)}) %collective-permute-start.11) | collective-permute-done | bytes 45088 | tf_op jit(solution)/shard_map/ppermute | solution.py:17
  24.5 0.0 collective-permute-done.8.across_ref
  24.5 0.9 %collective-permute-done.7.gathered_ref = f32[104,128]{1,0:T(8,128)S(1)} collective-permute-done((f32[104,128]{1,0:T(8,128)S(1)}, f32[104,128]{1,0:T(8,128)S(1)}, u32[]{:S(2)}, u32[]{:S(2)}) %collective-permute-start.7) | collective-permute-done | bytes 53280 | tf_op jit(solution)/shard_map/ppermute | solution.py:41
  25.4 1.7 %finish.1 = (f32[256,128]{1,0:T(8,128)}, bf16[2048,128]{1,0:T(8,128)(2,1)}) custom-call(f32[8,8,128]{2,1,0:T(8,128)S(1)} %get-tuple-element.19.factor_ref, bf16[2048,128]{1,0:T(8,128)(2,1)S(1)} %bitcast.10, bf16[2048,256]{1,0:T(8,128)(2,1)S(1)} %spread.1.lead_ref, f32[136,128]{1,0:T(8,128)S(1)} %add_add_fusion.sums_ref.same_ref, ...), custom_call_target="tpu_custom_call" | custom-call | tf_op jit(solution)/shard_map/finish/pallas_call | solution.py:424
  (10 shorter events, 0.1 us)
Async XLA Ops:
  0.6 2.3 %collective-permute-start = (bf16[2048,128]{1,0:T(8,128)(2,1)}, bf16[2048,128]{1,0:T(8,128)(2,1)S(1)}, u32[]{:S(2)}, u32[]{:S(2)}) collective-permute-start(bf16[2048,128]{1,0:T(8,128)(2,1)} %bitcast.7), channel_id=1, source_target_pairs={{0,1},{1,0},{2,3},{3,2},{4,5},{5,4},{6,7},{7,6},{8,9},{9,8},{10,11... | collective-permute-start | bytes 1572872 | tf_op jit(solution)/shard_map/ppermute | solution.py:17
  2.9 14.4 %copy-start = (bf16[1024,1,2,128]{3,2,1,0:T(2,128)(2,1)S(1)}, bf16[1024,1,2,128]{3,2,1,0:T(2,128)(2,1)}, u32[]{:S(2)}) copy-start(bf16[1024,1,2,128]{3,2,1,0:T(2,128)(2,1)} %param.2) | copy-start | bytes 1572868
  3.4 7.4 %collective-permute-start.1 = (f32[136,128]{1,0:T(8,128)S(1)}, f32[136,128]{1,0:T(8,128)S(1)}, u32[]{:S(2)}, u32[]{:S(2)}) collective-permute-start(f32[136,128]{1,0:T(8,128)S(1)} %get-tuple-element.23), channel_id=1, source_target_pairs={{0,24},{1,7},{2,26},{3,5},{4,28},{5,3},{6,30},{7,1},{8,16},{9,15},... | collective-permute-start | bytes 208904 | tf_op jit(solution)/shard_map/ppermute | solution.py:41
  8.4 5.2 %collective-permute-start.2 = (f32[136,128]{1,0:T(8,128)S(1)}, f32[136,128]{1,0:T(8,128)S(1)}, u32[]{:S(2)}, u32[]{:S(2)}) collective-permute-start(f32[136,128]{1,0:T(8,128)S(1)} %get-tuple-element.24), channel_id=1, source_target_pairs={{0,16},{1,5},{2,18},{3,7},{4,20},{5,1},{6,22},{7,3},{8,24},{9,13},... | collective-permute-start | bytes 208904 | tf_op jit(solution)/shard_map/ppermute | solution.py:41
  8.4 5.2 %collective-permute-start.3 = (f32[136,128]{1,0:T(8,128)S(1)}, f32[136,128]{1,0:T(8,128)S(1)}, u32[]{:S(2)}, u32[]{:S(2)}) collective-permute-start(f32[136,128]{1,0:T(8,128)S(1)} %get-tuple-element.25), channel_id=1, source_target_pairs={{0,8},{1,3},{2,10},{3,1},{4,12},{5,7},{6,14},{7,5},{8,0},{9,11},{1... | collective-permute-start | bytes 208904 | tf_op jit(solution)/shard_map/ppermute | solution.py:41
  13.7 5.3 %collective-permute-start.6 = (f32[136,128]{1,0:T(8,128)S(1)}, f32[136,128]{1,0:T(8,128)S(1)}, u32[]{:S(2)}, u32[]{:S(2)}) collective-permute-start(f32[136,128]{1,0:T(8,128)S(1)} %add_add_fusion.1), channel_id=1, source_target_pairs={{0,6},{1,25},{2,4},{3,27},{4,2},{5,29},{6,0},{7,31},{8,14},{9,17},... | collective-permute-start | bytes 208904 | tf_op jit(solution)/shard_map/ppermute | solution.py:41
  16.6 4.3 %collective-permute-start.5 = (f32[136,128]{1,0:T(8,128)S(1)}, f32[136,128]{1,0:T(8,128)S(1)}, u32[]{:S(2)}, u32[]{:S(2)}) collective-permute-start(f32[136,128]{1,0:T(8,128)S(1)} %add_add_fusion.1), channel_id=1, source_target_pairs={{0,4},{1,17},{2,6},{3,19},{4,0},{5,21},{6,2},{7,23},{8,12},{9,25},... | collective-permute-start | bytes 208904 | tf_op jit(solution)/shard_map/ppermute | solution.py:41
  16.8 4.3 %collective-permute-start.4 = (f32[136,128]{1,0:T(8,128)S(1)}, f32[136,128]{1,0:T(8,128)S(1)}, u32[]{:S(2)}, u32[]{:S(2)}) collective-permute-start(f32[136,128]{1,0:T(8,128)S(1)} %add_add_fusion.1), channel_id=1, source_target_pairs={{0,2},{1,9},{2,0},{3,11},{4,6},{5,13},{6,4},{7,15},{8,10},{9,1},{1... | collective-permute-start | bytes 208904 | tf_op jit(solution)/shard_map/ppermute | solution.py:41
  21.2 4.2 %collective-permute-start.7 = (f32[104,128]{1,0:T(8,128)S(1)}, f32[104,128]{1,0:T(8,128)S(1)}, u32[]{:S(2)}, u32[]{:S(2)}) collective-permute-start(f32[104,128]{1,0:T(8,128)S(1)} %slice.4), channel_id=1, source_target_pairs={{0,8},{1,3},{2,10},{3,1},{4,12},{5,7},{6,14},{7,5},{8,0},{9,11},{1... | collective-permute-start | bytes 159752 | tf_op jit(solution)/shard_map/ppermute | solution.py:41
  21.7 2.8 %collective-permute-start.8 = (f32[96,128]{1,0:T(8,128)S(1)}, f32[96,128]{1,0:T(8,128)S(1)}, u32[]{:S(2)}, u32[]{:S(2)}) collective-permute-start(f32[96,128]{1,0:T(8,128)S(1)} %get-tuple-element.30), channel_id=1, source_target_pairs={{0,9},{1,0},{2,11},{3,2},{4,13},{5,4},{6,15},{7,6},{8,1},{9,8},{10... | collective-permute-start | bytes 147464 | tf_op jit(solution)/shard_map/ppermute | solution.py:41
  22.7 1.2 %collective-permute-start.9 = (f32[88,128]{1,0:T(8,128)S(1)}, f32[88,128]{1,0:T(8,128)S(1)}, u32[]{:S(2)}, u32[]{:S(2)}) collective-permute-start(f32[88,128]{1,0:T(8,128)S(1)} %get-tuple-element.31.kept_0), channel_id=1, source_target_pairs={{0,1},{1,0},{2,3},{3,2},{4,5},{5,4},{6,7},{7,6},{8,9},{9,8},{10,11... | collective-permute-start | bytes 135176 | tf_op jit(solution)/shard_map/ppermute | solution.py:17
  22.7 1.4 %collective-permute-start.10 = (f32[88,128]{1,0:T(8,128)S(1)}, f32[88,128]{1,0:T(8,128)S(1)}, u32[]{:S(2)}, u32[]{:S(2)}) collective-permute-start(f32[88,128]{1,0:T(8,128)S(1)} %get-tuple-element.32.kept_1), channel_id=1, source_target_pairs={{0,1},{1,0},{2,3},{3,2},{4,5},{5,4},{6,7},{7,6},{8,9},{9,8},{10,11... | collective-permute-start | bytes 135176 | tf_op jit(solution)/shard_map/ppermute | solution.py:17
  23.3 1.2 %collective-permute-start.11 = (f32[88,128]{1,0:T(8,128)S(1)}, f32[88,128]{1,0:T(8,128)S(1)}, u32[]{:S(2)}, u32[]{:S(2)}) collective-permute-start(f32[88,128]{1,0:T(8,128)S(1)} %get-tuple-element.33.kept_2), channel_id=1, source_target_pairs={{0,1},{1,0},{2,3},{3,2},{4,5},{5,4},{6,7},{7,6},{8,9},{9,8},{10,11... | collective-permute-start | bytes 135176 | tf_op jit(solution)/shard_map/ppermute | solution.py:17

commit v17 on v15

--- a/solution.py
+++ b/solution.py
@@ -28,7 +28,7 @@
 
 
 def order(phases, parity):
-    if parity == 0 and len({radix for _, radix in phases}) == 1:
+    if parity == 1 and len({radix for _, radix in phases}) == 1:
         return phases[::-1]
     return phases
 

time: 27.2 us -> 27.1 us (level)
  starting transfers between devices: 11.9 us -> 11.5 us
    ppermute x8, starting transfers between devices: 10.8 us -> 10.4 us  [hop(): return lax.ppermute(x, ('rows', 'cols'), pairs)]
where the time goes in v17:
time: 27.1 us; the launch traced here: 26.9 us
  starting transfers between devices  11.5 us (42%)
  waiting for transfers between devices  10.9 us (40%)
  Pallas kernels  3.8 us (14%)
  between operations  0.68 us (3%)
    ppermute x8, starting transfers between devices, hop(): return lax.ppermute(x, ('rows', 'cols'), pairs)  10.4 us
    ppermute x8, waiting for transfers between devices, hop(): return lax.ppermute(x, ('rows', 'cols'), pairs)  9.1 us
    ppermute x4, waiting for transfers between devices, partner(): return lax.ppermute(x, axis, [(i, i ^ offset) for i in range(count)])  1.82 us
    pallas_call x1, Pallas kernels, shards(): pl.pallas_call(functools.partial(finish_kernel, rounds, nblock, phases, r...  1.69 us
    pallas_call x1, Pallas kernels, shards(): pl.pallas_call(functools.partial(split_kernel, rounds, nblock), out_shape...  1.14 us
    ppermute x4, starting transfers between devices, partner(): return lax.ppermute(x, axis, [(i, i ^ offset) for i in range(count)])  1.03 us
  transfers between devices with their start and end apart: 12, of which 10 were waited for; matrix products, arithmetic and copies ran while one was open for 0% of the time, Pallas kernels for 6%

profile of v17, /device:TPU:0, one launch (start us, length us, event | category | flops | bytes accessed | tf_op | source)
XLA Modules:
  0.0 26.9 jit_solution(12882633675107721151)
XLA Ops:
  0.6 0.5 %collective-permute-start = (bf16[2048,128]{1,0:T(8,128)(2,1)}, bf16[2048,128]{1,0:T(8,128)(2,1)S(1)}, u32[]{:S(2)}, u32[]{:S(2)}) collective-permute-start(bf16[2048,128]{1,0:T(8,128)(2,1)} %bitcast.7), channel_id=1, source_target_pairs={{0,1},{1,0},{2,3},{3,2},{4,5},{5,4},{6,7},{7,6},{8,9},{9,8},{10,11... | collective-permute-start | bytes 1572872 | tf_op jit(solution)/shard_map/ppermute | solution.py:17
  1.1 1.1 %split.1 = (bf16[1024,128]{1,0:T(8,128)(2,1)S(1)}, bf16[1024,128]{1,0:T(8,128)(2,1)S(1)}, f32[8,8,128]{2,1,0:T(8,128)S(1)}) custom-call(f32[2,2,2]{2,1,0:T(2,128)} %scale_hbm.1, bf16[2048,128]{1,0:T(8,128)(2,1)} %bitcast.8), custom_call_target="tpu_custom_call" | custom-call | tf_op jit(solution)/shard_map/split/pallas_call | solution.py:362
  2.3 0.6 %collective-permute-done.recv_ref.odd_ref = bf16[2048,128]{1,0:T(8,128)(2,1)S(1)} collective-permute-done((bf16[2048,128]{1,0:T(8,128)(2,1)}, bf16[2048,128]{1,0:T(8,128)(2,1)S(1)}, u32[]{:S(2)}, u32[]{:S(2)}) %collective-permute-start) | collective-permute-done | bytes 524320 | tf_op jit(solution)/shard_map/ppermute | solution.py:17
  2.9 0.5 %products.1 = (f32[136,128]{1,0:T(8,128)S(1)}, f32[136,128]{1,0:T(8,128)S(1)}, f32[136,128]{1,0:T(8,128)S(1)}, f32[136,128]{1,0:T(8,128)S(1)}) custom-call(f32[8,8,128]{2,1,0:T(8,128)S(1)} %get-tuple-element.19.factor_ref, bf16[1024,128]{1,0:T(8,128)(2,1)S(1)} %get-tuple-element.20.first_ref, bf16[1024,128]{1,0:T(8,128)(2,1)S(1)} %get-tuple-element.21.own_ref, ...), custom_call_target="tpu_custom_call" | custom-call | tf_op jit(solution)/shard_map/products/pallas_call | solution.py:377
  3.4 3.9 %collective-permute-start.1 = (f32[136,128]{1,0:T(8,128)S(1)}, f32[136,128]{1,0:T(8,128)S(1)}, u32[]{:S(2)}, u32[]{:S(2)}) collective-permute-start(f32[136,128]{1,0:T(8,128)S(1)} %get-tuple-element.23), channel_id=1, source_target_pairs={{0,6},{1,25},{2,4},{3,27},{4,2},{5,29},{6,0},{7,31},{8,14},{9,17},... | collective-permute-start | bytes 208904 | tf_op jit(solution)/shard_map/ppermute | solution.py:41
  7.3 0.5 %collective-permute-start.2 = (f32[136,128]{1,0:T(8,128)S(1)}, f32[136,128]{1,0:T(8,128)S(1)}, u32[]{:S(2)}, u32[]{:S(2)}) collective-permute-start(f32[136,128]{1,0:T(8,128)S(1)} %get-tuple-element.24), channel_id=1, source_target_pairs={{0,4},{1,17},{2,6},{3,19},{4,0},{5,21},{6,2},{7,23},{8,12},{9,25},... | collective-permute-start | bytes 208904 | tf_op jit(solution)/shard_map/ppermute | solution.py:41
  7.8 0.1 collective-permute-start.3
  7.9 1.6 %collective-permute-done.1 = f32[136,128]{1,0:T(8,128)S(1)} collective-permute-done((f32[136,128]{1,0:T(8,128)S(1)}, f32[136,128]{1,0:T(8,128)S(1)}, u32[]{:S(2)}, u32[]{:S(2)}) %collective-permute-start.1) | collective-permute-done | bytes 69664 | tf_op jit(solution)/shard_map/ppermute | solution.py:41
  9.5 2.0 %collective-permute-done.2 = f32[136,128]{1,0:T(8,128)S(1)} collective-permute-done((f32[136,128]{1,0:T(8,128)S(1)}, f32[136,128]{1,0:T(8,128)S(1)}, u32[]{:S(2)}, u32[]{:S(2)}) %collective-permute-start.2) | collective-permute-done | bytes 69664 | tf_op jit(solution)/shard_map/ppermute | solution.py:41
  11.6 0.5 %collective-permute-done.3 = f32[136,128]{1,0:T(8,128)S(1)} collective-permute-done((f32[136,128]{1,0:T(8,128)S(1)}, f32[136,128]{1,0:T(8,128)S(1)}, u32[]{:S(2)}, u32[]{:S(2)}) %collective-permute-start.3) | collective-permute-done | bytes 69664 | tf_op jit(solution)/shard_map/ppermute | solution.py:41
  12.1 3.7 %collective-permute-start.6 = (f32[136,128]{1,0:T(8,128)S(1)}, f32[136,128]{1,0:T(8,128)S(1)}, u32[]{:S(2)}, u32[]{:S(2)}) collective-permute-start(f32[136,128]{1,0:T(8,128)S(1)} %add_add_fusion.1), channel_id=1, source_target_pairs={{0,24},{1,7},{2,26},{3,5},{4,28},{5,3},{6,30},{7,1},{8,16},{9,15},... | collective-permute-start | bytes 208904 | tf_op jit(solution)/shard_map/ppermute | solution.py:41
  15.8 0.8 %collective-permute-start.4 = (f32[136,128]{1,0:T(8,128)S(1)}, f32[136,128]{1,0:T(8,128)S(1)}, u32[]{:S(2)}, u32[]{:S(2)}) collective-permute-start(f32[136,128]{1,0:T(8,128)S(1)} %add_add_fusion.1), channel_id=1, source_target_pairs={{0,8},{1,3},{2,10},{3,1},{4,12},{5,7},{6,14},{7,5},{8,0},{9,11},{1... | collective-permute-start | bytes 208904 | tf_op jit(solution)/shard_map/ppermute | solution.py:41
  16.6 0.5 %spread.1.lead_ref = bf16[2048,256]{1,0:T(8,128)(2,1)S(1)} custom-call(bf16[2048,128]{1,0:T(8,128)(2,1)S(1)} %bitcast.9, bf16[2048,128]{1,0:T(8,128)(2,1)S(1)} %collective-permute-done.recv_ref.odd_ref), custom_call_target="tpu_custom_call" | custom-call | tf_op jit(solution)/shard_map/spread/pallas_call | solution.py:394
  17.0 1.2 %collective-permute-done.6 = f32[136,128]{1,0:T(8,128)S(1)} collective-permute-done((f32[136,128]{1,0:T(8,128)S(1)}, f32[136,128]{1,0:T(8,128)S(1)}, u32[]{:S(2)}, u32[]{:S(2)}) %collective-permute-start.6) | collective-permute-done | bytes 69664 | tf_op jit(solution)/shard_map/ppermute | solution.py:41
  18.3 2.7 %collective-permute-done.5 = f32[136,128]{1,0:T(8,128)S(1)} collective-permute-done((f32[136,128]{1,0:T(8,128)S(1)}, f32[136,128]{1,0:T(8,128)S(1)}, u32[]{:S(2)}, u32[]{:S(2)}) %collective-permute-start.5) | collective-permute-done | bytes 69664 | tf_op jit(solution)/shard_map/ppermute | solution.py:41
  21.0 0.6 %collective-permute-start.7 = (f32[104,128]{1,0:T(8,128)S(1)}, f32[104,128]{1,0:T(8,128)S(1)}, u32[]{:S(2)}, u32[]{:S(2)}) collective-permute-start(f32[104,128]{1,0:T(8,128)S(1)} %slice.4), channel_id=1, source_target_pairs={{0,2},{1,9},{2,0},{3,11},{4,6},{5,13},{6,4},{7,15},{8,10},{9,1},{1... | collective-permute-start | bytes 159752 | tf_op jit(solution)/shard_map/ppermute | solution.py:41
  21.6 0.9 %collective-permute-start.8 = (f32[96,128]{1,0:T(8,128)S(1)}, f32[96,128]{1,0:T(8,128)S(1)}, u32[]{:S(2)}, u32[]{:S(2)}) collective-permute-start(f32[96,128]{1,0:T(8,128)S(1)} %get-tuple-element.30), channel_id=1, source_target_pairs={{0,3},{1,0},{2,1},{3,2},{4,7},{5,4},{6,5},{7,6},{8,11},{9,8},{10,9... | collective-permute-start | bytes 147464 | tf_op jit(solution)/shard_map/ppermute | solution.py:41
  22.5 0.5 %collective-permute-start.10 = (f32[88,128]{1,0:T(8,128)S(1)}, f32[88,128]{1,0:T(8,128)S(1)}, u32[]{:S(2)}, u32[]{:S(2)}) collective-permute-start(f32[88,128]{1,0:T(8,128)S(1)} %get-tuple-element.32.kept_1), channel_id=1, source_target_pairs={{0,1},{1,0},{2,3},{3,2},{4,5},{5,4},{6,7},{7,6},{8,9},{9,8},{10,11... | collective-permute-start | bytes 135176 | tf_op jit(solution)/shard_map/ppermute | solution.py:17
  23.0 0.7 %collective-permute-done.9.swapped_0 = f32[88,128]{1,0:T(8,128)S(1)} collective-permute-done((f32[88,128]{1,0:T(8,128)S(1)}, f32[88,128]{1,0:T(8,128)S(1)}, u32[]{:S(2)}, u32[]{:S(2)}) %collective-permute-start.9) | collective-permute-done | bytes 45088 | tf_op jit(solution)/shard_map/ppermute | solution.py:17
  23.7 0.2 collective-permute-done.10.swapped_1
  23.9 0.3 %collective-permute-done.11.swapped_2 = f32[88,128]{1,0:T(8,128)S(1)} collective-permute-done((f32[88,128]{1,0:T(8,128)S(1)}, f32[88,128]{1,0:T(8,128)S(1)}, u32[]{:S(2)}, u32[]{:S(2)}) %collective-permute-start.11) | collective-permute-done | bytes 45088 | tf_op jit(solution)/shard_map/ppermute | solution.py:17
  24.2 0.0 collective-permute-done.8.across_ref
  24.2 1.0 %collective-permute-done.7.gathered_ref = f32[104,128]{1,0:T(8,128)S(1)} collective-permute-done((f32[104,128]{1,0:T(8,128)S(1)}, f32[104,128]{1,0:T(8,128)S(1)}, u32[]{:S(2)}, u32[]{:S(2)}) %collective-permute-start.7) | collective-permute-done | bytes 53280 | tf_op jit(solution)/shard_map/ppermute | solution.py:41
  25.2 1.7 %finish.1 = (f32[256,128]{1,0:T(8,128)}, bf16[2048,128]{1,0:T(8,128)(2,1)}) custom-call(f32[8,8,128]{2,1,0:T(8,128)S(1)} %get-tuple-element.19.factor_ref, bf16[2048,128]{1,0:T(8,128)(2,1)S(1)} %bitcast.10, bf16[2048,256]{1,0:T(8,128)(2,1)S(1)} %spread.1.lead_ref, f32[136,128]{1,0:T(8,128)S(1)} %add_add_fusion.sums_ref.same_ref, ...), custom_call_target="tpu_custom_call" | custom-call | tf_op jit(solution)/shard_map/finish/pallas_call | solution.py:424
  (10 shorter events, 0.1 us)
Async XLA Ops:
  0.6 2.3 %collective-permute-start = (bf16[2048,128]{1,0:T(8,128)(2,1)}, bf16[2048,128]{1,0:T(8,128)(2,1)S(1)}, u32[]{:S(2)}, u32[]{:S(2)}) collective-permute-start(bf16[2048,128]{1,0:T(8,128)(2,1)} %bitcast.7), channel_id=1, source_target_pairs={{0,1},{1,0},{2,3},{3,2},{4,5},{5,4},{6,7},{7,6},{8,9},{9,8},{10,11... | collective-permute-start | bytes 1572872 | tf_op jit(solution)/shard_map/ppermute | solution.py:17
  2.9 13.7 %copy-start = (bf16[1024,1,2,128]{3,2,1,0:T(2,128)(2,1)S(1)}, bf16[1024,1,2,128]{3,2,1,0:T(2,128)(2,1)}, u32[]{:S(2)}) copy-start(bf16[1024,1,2,128]{3,2,1,0:T(2,128)(2,1)} %param.2) | copy-start | bytes 1572868
  3.4 6.2 %collective-permute-start.1 = (f32[136,128]{1,0:T(8,128)S(1)}, f32[136,128]{1,0:T(8,128)S(1)}, u32[]{:S(2)}, u32[]{:S(2)}) collective-permute-start(f32[136,128]{1,0:T(8,128)S(1)} %get-tuple-element.23), channel_id=1, source_target_pairs={{0,6},{1,25},{2,4},{3,27},{4,2},{5,29},{6,0},{7,31},{8,14},{9,17},... | collective-permute-start | bytes 208904 | tf_op jit(solution)/shard_map/ppermute | solution.py:41
  7.3 4.3 %collective-permute-start.2 = (f32[136,128]{1,0:T(8,128)S(1)}, f32[136,128]{1,0:T(8,128)S(1)}, u32[]{:S(2)}, u32[]{:S(2)}) collective-permute-start(f32[136,128]{1,0:T(8,128)S(1)} %get-tuple-element.24), channel_id=1, source_target_pairs={{0,4},{1,17},{2,6},{3,19},{4,0},{5,21},{6,2},{7,23},{8,12},{9,25},... | collective-permute-start | bytes 208904 | tf_op jit(solution)/shard_map/ppermute | solution.py:41
  7.8 4.3 %collective-permute-start.3 = (f32[136,128]{1,0:T(8,128)S(1)}, f32[136,128]{1,0:T(8,128)S(1)}, u32[]{:S(2)}, u32[]{:S(2)}) collective-permute-start(f32[136,128]{1,0:T(8,128)S(1)} %get-tuple-element.25), channel_id=1, source_target_pairs={{0,2},{1,9},{2,0},{3,11},{4,6},{5,13},{6,4},{7,15},{8,10},{9,1},{1... | collective-permute-start | bytes 208904 | tf_op jit(solution)/shard_map/ppermute | solution.py:41
  12.1 6.2 %collective-permute-start.6 = (f32[136,128]{1,0:T(8,128)S(1)}, f32[136,128]{1,0:T(8,128)S(1)}, u32[]{:S(2)}, u32[]{:S(2)}) collective-permute-start(f32[136,128]{1,0:T(8,128)S(1)} %add_add_fusion.1), channel_id=1, source_target_pairs={{0,24},{1,7},{2,26},{3,5},{4,28},{5,3},{6,30},{7,1},{8,16},{9,15},... | collective-permute-start | bytes 208904 | tf_op jit(solution)/shard_map/ppermute | solution.py:41
  15.8 5.2 %collective-permute-start.5 = (f32[136,128]{1,0:T(8,128)S(1)}, f32[136,128]{1,0:T(8,128)S(1)}, u32[]{:S(2)}, u32[]{:S(2)}) collective-permute-start(f32[136,128]{1,0:T(8,128)S(1)} %add_add_fusion.1), channel_id=1, source_target_pairs={{0,16},{1,5},{2,18},{3,7},{4,20},{5,1},{6,22},{7,3},{8,24},{9,13},... | collective-permute-start | bytes 208904 | tf_op jit(solution)/shard_map/ppermute | solution.py:41
  15.8 5.2 %collective-permute-start.4 = (f32[136,128]{1,0:T(8,128)S(1)}, f32[136,128]{1,0:T(8,128)S(1)}, u32[]{:S(2)}, u32[]{:S(2)}) collective-permute-start(f32[136,128]{1,0:T(8,128)S(1)} %add_add_fusion.1), channel_id=1, source_target_pairs={{0,8},{1,3},{2,10},{3,1},{4,12},{5,7},{6,14},{7,5},{8,0},{9,11},{1... | collective-permute-start | bytes 208904 | tf_op jit(solution)/shard_map/ppermute | solution.py:41
  21.0 4.2 %collective-permute-start.7 = (f32[104,128]{1,0:T(8,128)S(1)}, f32[104,128]{1,0:T(8,128)S(1)}, u32[]{:S(2)}, u32[]{:S(2)}) collective-permute-start(f32[104,128]{1,0:T(8,128)S(1)} %slice.4), channel_id=1, source_target_pairs={{0,2},{1,9},{2,0},{3,11},{4,6},{5,13},{6,4},{7,15},{8,10},{9,1},{1... | collective-permute-start | bytes 159752 | tf_op jit(solution)/shard_map/ppermute | solution.py:41
  21.6 2.6 %collective-permute-start.8 = (f32[96,128]{1,0:T(8,128)S(1)}, f32[96,128]{1,0:T(8,128)S(1)}, u32[]{:S(2)}, u32[]{:S(2)}) collective-permute-start(f32[96,128]{1,0:T(8,128)S(1)} %get-tuple-element.30), channel_id=1, source_target_pairs={{0,3},{1,0},{2,1},{3,2},{4,7},{5,4},{6,5},{7,6},{8,11},{9,8},{10,9... | collective-permute-start | bytes 147464 | tf_op jit(solution)/shard_map/ppermute | solution.py:41
  22.5 1.2 %collective-permute-start.9 = (f32[88,128]{1,0:T(8,128)S(1)}, f32[88,128]{1,0:T(8,128)S(1)}, u32[]{:S(2)}, u32[]{:S(2)}) collective-permute-start(f32[88,128]{1,0:T(8,128)S(1)} %get-tuple-element.31.kept_0), channel_id=1, source_target_pairs={{0,1},{1,0},{2,3},{3,2},{4,5},{5,4},{6,7},{7,6},{8,9},{9,8},{10,11... | collective-permute-start | bytes 135176 | tf_op jit(solution)/shard_map/ppermute | solution.py:17
  22.5 1.4 %collective-permute-start.10 = (f32[88,128]{1,0:T(8,128)S(1)}, f32[88,128]{1,0:T(8,128)S(1)}, u32[]{:S(2)}, u32[]{:S(2)}) collective-permute-start(f32[88,128]{1,0:T(8,128)S(1)} %get-tuple-element.32.kept_1), channel_id=1, source_target_pairs={{0,1},{1,0},{2,3},{3,2},{4,5},{5,4},{6,7},{7,6},{8,9},{9,8},{10,11... | collective-permute-start | bytes 135176 | tf_op jit(solution)/shard_map/ppermute | solution.py:17
  23.0 1.2 %collective-permute-start.11 = (f32[88,128]{1,0:T(8,128)S(1)}, f32[88,128]{1,0:T(8,128)S(1)}, u32[]{:S(2)}, u32[]{:S(2)}) collective-permute-start(f32[88,128]{1,0:T(8,128)S(1)} %get-tuple-element.33.kept_2), channel_id=1, source_target_pairs={{0,1},{1,0},{2,3},{3,2},{4,5},{5,4},{6,7},{7,6},{8,9},{9,8},{10,11... | collective-permute-start | bytes 135176 | tf_op jit(solution)/shard_map/ppermute | solution.py:17
